TPU v7x, 32 devices: a whole 2x2x4 slice. The times are simulated.
32 devices in a mesh: head: 2 (over x), blk: 16 (over z, y, core).
Axes of the slice: x: 2, y: 2, z: 4, core: 2. Of those that a mesh axis runs over, the one named last changes fastest.
Arguments:
- tokens: bfloat16 [4, 2048, 1536], P('head', 'blk'), may hold values from -6 to 6
- gain_attn: bfloat16 [1536], P(('head', 'blk')), may hold values from 0.5 to 1.5
- w_query: bfloat16 [1536, 1536], P(('head', 'blk')), may hold values from -0.15625 to 0.15625
- w_key: bfloat16 [1536, 512], P(('head', 'blk')), may hold values from -0.15625 to 0.15625
- w_value: bfloat16 [1536, 512], P(('head', 'blk')), may hold values from -0.15625 to 0.15625
- w_out: bfloat16 [1536, 1536], P(('head', 'blk')), may hold values from -6 to 6
- gain_moe: bfloat16 [1536], P(('head', 'blk')), may hold values from 0.5 to 1.5
- w_router: bfloat16 [1536, 16], P(('head', 'blk')), may hold values from -0.15625 to 0.15625
- w_gate: bfloat16 [16, 1536, 512], P('blk'), may hold values from -0.15625 to 0.15625
- w_up: bfloat16 [16, 1536, 512], P('blk'), may hold values from -0.15625 to 0.15625
- w_down: bfloat16 [16, 512, 1536], P('blk'), may hold values from -0.75 to 0.75
- routes: int32 [4, 2048, 8], P('head', 'blk'), may hold values from 0 to 15, all different within a row; in each aligned block of 128 rows (0 to 127, 128 to 255, ..., all dimensions but the last counted through in order) at most 96 rows name the same one
- grad_out: float32 [4, 2048, 1536], P('head', 'blk'), may hold values from -6 to 6
Outputs:
- out: float32 [4, 2048, 1536], P('head', 'blk')
- grad_tokens: float32 [4, 2048, 1536], P('head', 'blk')
- grad_gain_attn: float32 [1536], P(('head', 'blk'))
- grad_w_query: float32 [1536, 1536], P(('head', 'blk'))
- grad_w_key: float32 [1536, 512], P(('head', 'blk'))
- grad_w_value: float32 [1536, 512], P(('head', 'blk'))
- grad_w_out: float32 [1536, 1536], P(('head', 'blk'))
- grad_gain_moe: float32 [1536], P(('head', 'blk'))
- grad_w_router: float32 [1536, 16], P(('head', 'blk'))
- grad_w_gate: float32 [16, 1536, 512], P('blk')
- grad_w_up: float32 [16, 1536, 512], P('blk')
- grad_w_down: float32 [16, 512, 1536], P('blk')
Inputs may be any that keep to these rules, and one draw needn't show every extreme that they name: `routes`: each token names 8 different experts. In each aligned block of 128 rows (the positions of one sequence on one device), no expert is named by more than 96 rows, and in some block one expert is named by exactly 96 rows.
All inputs are finite; a program needn't handle non-finite values.
Results may differ from a plain program's by a relative error of at most 0.02.
Values may be sent and summed in bfloat16 or wider, within the bound.
No kernel may reach another device: no remote copies, remote signals or barrier semaphores. Data moves between devices by JAX's collectives and lax.ppermute only.
A program may use at most 320 MiB of HBM per device.

v0:
```python
import jax
import jax.numpy as jnp
from jax import lax
from jax.sharding import PartitionSpec as P

HDIM = 64
TOP = 8
BLOCK = 256


highest = lax.Precision.HIGHEST
theta_base = 10000.0
norm_eps = 1e-06
masked_score = -1e30
seq_block = 2


def rope_tables(positions, half_width):
    index_float = jnp.arange(half_width, dtype=jnp.float32)
    frequency = theta_base ** (-2.0 * index_float / (2 * half_width))
    angles = positions.astype(jnp.float32)[:, None] * frequency[None, :]
    return (jnp.cos(angles), jnp.sin(angles))


def rotate(values, cosine, sine):
    half_width = values.shape[-1] // 2
    first_half = values[..., :half_width]
    second_half = values[..., half_width:]
    cosine = cosine[:, None, :]
    sine = sine[:, None, :]
    return jnp.concatenate(
        [first_half * cosine - second_half * sine, second_half * cosine + first_half * sine],
        axis=-1,
    )


def rms_scale(values):
    return lax.rsqrt(jnp.mean(values * values, axis=-1, keepdims=True) + norm_eps)


def norm_back(values, inverse, gain, d_normed):
    unit_values = values * inverse
    scaled = d_normed * gain
    d_gain = jnp.sum(d_normed * unit_values, axis=0)
    d_values = inverse * (
        scaled - unit_values * jnp.mean(scaled * unit_values, axis=-1, keepdims=True)
    )
    return (d_values, d_gain)


def masked_scores(query_group, key_group, allowed, score_scale):
    scores = (
        jnp.einsum("sihgd,skhd->shgik", query_group, key_group, preferred_element_type=jnp.float32)
        * score_scale
    )
    return jnp.where(allowed, scores, masked_score)


def attend_forward(query_group, key_group, value_group, allowed, score_scale):
    scores = masked_scores(query_group, key_group, allowed, score_scale)
    maximum = jnp.max(scores, axis=-1, keepdims=True)
    exponent = jnp.exp(scores - maximum)
    row_total = jnp.sum(exponent, axis=-1, keepdims=True)
    weights = (exponent / row_total).astype(jnp.bfloat16)
    attended = jnp.einsum(
        "shgik,skhd->sihgd", weights, value_group, preferred_element_type=jnp.float32
    )
    return (attended, (maximum + jnp.log(row_total))[..., 0])


def attend_backward(query_group, key_group, value_group, d_group, log_total, allowed, score_scale):
    scores = masked_scores(query_group, key_group, allowed, score_scale)
    probs = jnp.exp(scores - log_total[..., None])
    d_probs = jnp.einsum(
        "sihgd,skhd->shgik", d_group, value_group, preferred_element_type=jnp.float32
    )
    delta = jnp.sum(probs * d_probs, axis=-1, keepdims=True)
    d_scores = (probs * (d_probs - delta)).astype(jnp.bfloat16)
    d_query = (
        jnp.einsum("shgik,skhd->sihgd", d_scores, key_group, preferred_element_type=jnp.float32)
        * score_scale
    )
    d_key = (
        jnp.einsum("shgik,sihgd->skhd", d_scores, query_group, preferred_element_type=jnp.float32)
        * score_scale
    )
    d_value = jnp.einsum(
        "shgik,sihgd->skhd", probs.astype(jnp.bfloat16), d_group, preferred_element_type=jnp.float32
    )
    return (d_query, d_key, d_value)


def local(
    tokens,
    gain_attn,
    w_query,
    w_key,
    w_value,
    w_out,
    gain_moe,
    w_router,
    w_gate,
    w_up,
    w_down,
    routes,
    grad_out,
):
    seq_local, shard, width = tokens.shape
    token_rows = seq_local * shard
    blk_index = lax.axis_index("blk")
    score_scale = HDIM ** (-0.5)
    full_query, full_key, full_value, full_out, full_router, gain_one, gain_two = (
        lax.all_gather(w_query, ("head", "blk"), axis=0, tiled=True),
        lax.all_gather(w_key, ("head", "blk"), axis=0, tiled=True),
        lax.all_gather(w_value, ("head", "blk"), axis=0, tiled=True),
        lax.all_gather(w_out, ("head", "blk"), axis=0, tiled=True),
        lax.all_gather(w_router, ("head", "blk"), axis=0, tiled=True),
        lax.all_gather(gain_attn, ("head", "blk"), axis=0, tiled=True),
        lax.all_gather(gain_moe, ("head", "blk"), axis=0, tiled=True),
    )
    experts = full_router.shape[1]
    most_rows = min(shard, max(2, 3 * shard * TOP // (2 * experts)))
    capacity = seq_local * most_rows
    residual = tokens.astype(jnp.float32).reshape(token_rows, width)
    inverse_one = rms_scale(residual)
    gain_first = gain_one.astype(jnp.float32)
    normed = (residual * inverse_one * gain_first).astype(jnp.bfloat16)
    positions = blk_index * shard + jnp.arange(shard, dtype=jnp.int32)
    cosine, sine = rope_tables(positions, HDIM // 2)
    lin_query = jnp.dot(normed, full_query, preferred_element_type=jnp.float32).reshape(
        seq_local, shard, -1, HDIM
    )
    lin_key = jnp.dot(normed, full_key, preferred_element_type=jnp.float32).reshape(
        seq_local, shard, -1, HDIM
    )
    query_tok = rotate(lin_query, cosine, sine).astype(jnp.bfloat16).reshape(seq_local, shard, -1)
    key_tok = rotate(lin_key, cosine, sine).astype(jnp.bfloat16).reshape(seq_local, shard, -1)
    value_tok = (
        jnp.dot(normed, full_value, preferred_element_type=jnp.float32)
        .astype(jnp.bfloat16)
        .reshape(seq_local, shard, -1)
    )
    blk_count = lax.axis_size("blk")
    seq_total = blk_count * shard
    query_head, key_head, value_head = (
        lax.all_to_all(query_tok, "head", split_axis=2, concat_axis=0, tiled=True),
        lax.all_to_all(key_tok, "head", split_axis=2, concat_axis=0, tiled=True),
        lax.all_to_all(value_tok, "head", split_axis=2, concat_axis=0, tiled=True),
    )
    keys_all, values_all = (
        lax.all_gather(key_head, "blk", axis=1, tiled=True),
        lax.all_gather(value_head, "blk", axis=1, tiled=True),
    )
    seq_count = query_head.shape[0]
    kv_local = key_head.shape[2] // HDIM
    group_size = query_head.shape[2] // key_head.shape[2]
    key_pos = jnp.arange(seq_total, dtype=jnp.int32)
    allowed = key_pos[None, :] // BLOCK <= positions[:, None] // BLOCK
    outer = seq_count // seq_block
    query_groups = query_head.reshape(outer, seq_block, shard, kv_local, group_size, HDIM)
    key_groups = keys_all.reshape(outer, seq_block, seq_total, kv_local, HDIM)
    value_groups = values_all.reshape(outer, seq_block, seq_total, kv_local, HDIM)

    def forward_group(grouped):
        return attend_forward(grouped[0], grouped[1], grouped[2], allowed, score_scale)

    attended_head, log_total = lax.map(forward_group, (query_groups, key_groups, value_groups))
    attended_low = attended_head.reshape(seq_count, shard, -1).astype(jnp.bfloat16)
    attended_tok = lax.all_to_all(
        attended_low, "head", split_axis=0, concat_axis=2, tiled=True
    ).reshape(token_rows, -1)
    branch = jnp.dot(attended_tok, full_out, preferred_element_type=jnp.float32)
    middle = residual + branch
    inverse_two = rms_scale(middle)
    gain_second = gain_two.astype(jnp.float32)
    normed_two = (middle * inverse_two * gain_second).astype(jnp.bfloat16)
    logits = jnp.dot(normed_two, full_router, preferred_element_type=jnp.float32)
    routes_tok = routes.reshape(token_rows, TOP)
    expert_ids = jnp.arange(experts, dtype=jnp.int32)
    chosen_mask = routes_tok[:, :, None] == expert_ids[None, None, :]
    chosen = jnp.sum(jnp.where(chosen_mask, logits[:, None, :], 0.0), axis=-1)
    gates = jax.nn.softmax(chosen, axis=-1)
    routes_flat = routes.reshape(seq_local, shard * TOP)
    member = (routes_flat[:, :, None] == expert_ids[None, None, :]).astype(jnp.int32)
    ranks = jnp.sum(member * (jnp.cumsum(member, axis=1) - 1), axis=-1)
    slot_index = jnp.arange(seq_local, dtype=jnp.int32)[:, None] * most_rows + ranks
    destination = (routes_flat * capacity + slot_index).reshape(token_rows, TOP)
    assign_count = token_rows * TOP
    assign_of_slot = (
        jnp.full((experts * capacity,), assign_count, jnp.int32)
        .at[destination.reshape(-1)]
        .set(jnp.arange(assign_count, dtype=jnp.int32))
    )
    token_of_slot = assign_of_slot // TOP
    padded_normed = jnp.concatenate([normed_two, jnp.zeros((1, width), jnp.bfloat16)], axis=0)
    send_rows = padded_normed[token_of_slot].reshape(experts, capacity, width)
    arrived = lax.all_to_all(send_rows, "blk", split_axis=0, concat_axis=0, tiled=True).reshape(
        -1, width
    )
    gate_lin = jnp.dot(arrived, w_gate[0], preferred_element_type=jnp.float32)
    up_lin = jnp.dot(arrived, w_up[0], preferred_element_type=jnp.float32)
    hidden = (jax.nn.silu(gate_lin) * up_lin).astype(jnp.bfloat16)
    expert_out = (
        jnp.dot(hidden, w_down[0], preferred_element_type=jnp.float32)
        .astype(jnp.bfloat16)
        .reshape(-1, capacity, width)
    )
    returned = lax.all_to_all(expert_out, "blk", split_axis=0, concat_axis=0, tiled=True).reshape(
        experts * capacity, width
    )
    routed_out = returned[destination].astype(jnp.float32)
    mixed = jnp.sum(gates[:, :, None] * routed_out, axis=1)
    out = (middle + mixed).reshape(seq_local, shard, width)
    d_out = grad_out.reshape(token_rows, width)
    gates_pad = jnp.concatenate([gates.reshape(-1), jnp.zeros((1,), jnp.float32)])
    d_out_pad = jnp.concatenate([d_out, jnp.zeros((1, width), jnp.float32)], axis=0)
    grad_send = (
        (gates_pad[assign_of_slot][:, None] * d_out_pad[token_of_slot])
        .astype(jnp.bfloat16)
        .reshape(experts, capacity, width)
    )
    grad_arrived = lax.all_to_all(
        grad_send, "blk", split_axis=0, concat_axis=0, tiled=True
    ).reshape(-1, width)
    d_hidden = jnp.einsum("sd,fd->sf", grad_arrived, w_down[0], preferred_element_type=jnp.float32)
    sigma = jax.nn.sigmoid(gate_lin)
    d_gate = (d_hidden * up_lin * sigma * (1.0 + gate_lin * (1.0 - sigma))).astype(jnp.bfloat16)
    d_up = (d_hidden * (gate_lin * sigma)).astype(jnp.bfloat16)
    grad_gate_part = jnp.einsum("sd,sf->df", arrived, d_gate, preferred_element_type=jnp.float32)
    grad_up_part = jnp.einsum("sd,sf->df", arrived, d_up, preferred_element_type=jnp.float32)
    grad_down_part = jnp.einsum(
        "sf,sd->fd", hidden, grad_arrived, preferred_element_type=jnp.float32
    )
    d_rows = (
        jnp.einsum("sf,df->sd", d_gate, w_gate[0], preferred_element_type=jnp.float32)
        + jnp.einsum("sf,df->sd", d_up, w_up[0], preferred_element_type=jnp.float32)
    ).astype(jnp.bfloat16)
    grad_back = lax.all_to_all(
        d_rows.reshape(-1, capacity, width), "blk", split_axis=0, concat_axis=0, tiled=True
    ).reshape(experts * capacity, width)
    grad_gate_sum, grad_up_sum, grad_down_sum = (
        lax.psum(grad_gate_part.astype(jnp.bfloat16), "head").astype(jnp.float32),
        lax.psum(grad_up_part.astype(jnp.bfloat16), "head").astype(jnp.float32),
        lax.psum(grad_down_part.astype(jnp.bfloat16), "head").astype(jnp.float32),
    )
    d_normed_experts = jnp.sum(grad_back[destination].astype(jnp.float32), axis=1)
    d_gates = jnp.sum(d_out[:, None, :] * routed_out, axis=-1)
    d_chosen = gates * (d_gates - jnp.sum(gates * d_gates, axis=-1, keepdims=True))
    d_logits = jnp.sum(jnp.where(chosen_mask, d_chosen[:, :, None], 0.0), axis=1)
    grad_router = jnp.dot(normed_two.astype(jnp.float32).T, d_logits, precision=highest)
    d_normed_two = d_normed_experts + jnp.dot(
        d_logits, full_router.astype(jnp.float32).T, precision=highest
    )
    d_mid_norm, grad_gain_second = norm_back(middle, inverse_two, gain_second, d_normed_two)
    d_mid = d_out + d_mid_norm
    d_branch = d_mid.astype(jnp.bfloat16)
    grad_out_proj = jnp.einsum(
        "rq,rd->qd", attended_tok, d_branch, preferred_element_type=jnp.float32
    )
    d_attended = jnp.einsum(
        "rd,qd->rq", d_branch, full_out, preferred_element_type=jnp.float32
    ).astype(jnp.bfloat16)
    d_head = lax.all_to_all(
        d_attended.reshape(seq_local, shard, -1), "head", split_axis=2, concat_axis=0, tiled=True
    )
    key_back, value_back = (
        lax.all_gather(key_head, "blk", axis=1, tiled=True),
        lax.all_gather(value_head, "blk", axis=1, tiled=True),
    )
    key_back_groups = key_back.reshape(outer, seq_block, seq_total, kv_local, HDIM)
    value_back_groups = value_back.reshape(outer, seq_block, seq_total, kv_local, HDIM)
    d_groups = d_head.reshape(outer, seq_block, shard, kv_local, group_size, HDIM)

    def backward_group(grouped):
        return attend_backward(
            grouped[0], grouped[1], grouped[2], grouped[3], grouped[4], allowed, score_scale
        )

    d_query, d_key_part, d_value_part = lax.map(
        backward_group, (query_groups, key_back_groups, value_back_groups, d_groups, log_total)
    )
    d_key_part = d_key_part.reshape(seq_count, seq_total, -1)
    d_value_part = d_value_part.reshape(seq_count, seq_total, -1)
    d_key_own, d_value_own = (
        lax.psum_scatter(
            d_key_part.astype(jnp.bfloat16), "blk", scatter_dimension=1, tiled=True
        ).astype(jnp.float32),
        lax.psum_scatter(
            d_value_part.astype(jnp.bfloat16), "blk", scatter_dimension=1, tiled=True
        ).astype(jnp.float32),
    )
    d_query_lin = (
        rotate(d_query.reshape(seq_count, shard, -1, HDIM), cosine, -sine)
        .astype(jnp.bfloat16)
        .reshape(seq_count, shard, -1)
    )
    d_key_lin = (
        rotate(d_key_own.reshape(seq_count, shard, -1, HDIM), cosine, -sine)
        .astype(jnp.bfloat16)
        .reshape(seq_count, shard, -1)
    )
    d_value_lin = d_value_own.astype(jnp.bfloat16)
    d_query_tok, d_key_tok, d_value_tok = (
        lax.all_to_all(d_query_lin, "head", split_axis=0, concat_axis=2, tiled=True),
        lax.all_to_all(d_key_lin, "head", split_axis=0, concat_axis=2, tiled=True),
        lax.all_to_all(d_value_lin, "head", split_axis=0, concat_axis=2, tiled=True),
    )
    d_query_tok = d_query_tok.reshape(token_rows, -1)
    d_key_tok = d_key_tok.reshape(token_rows, -1)
    d_value_tok = d_value_tok.reshape(token_rows, -1)
    grad_query_part = jnp.einsum(
        "rd,rq->dq", normed, d_query_tok, preferred_element_type=jnp.float32
    )
    grad_key_part = jnp.einsum("rd,rq->dq", normed, d_key_tok, preferred_element_type=jnp.float32)
    grad_value_part = jnp.einsum(
        "rd,rq->dq", normed, d_value_tok, preferred_element_type=jnp.float32
    )
    d_normed = (
        jnp.einsum("rq,dq->rd", d_query_tok, full_query, preferred_element_type=jnp.float32)
        + jnp.einsum("rq,dq->rd", d_key_tok, full_key, preferred_element_type=jnp.float32)
        + jnp.einsum("rq,dq->rd", d_value_tok, full_value, preferred_element_type=jnp.float32)
    )
    d_tok_norm, grad_gain_first = norm_back(residual, inverse_one, gain_first, d_normed)
    grad_tokens = (d_mid + d_tok_norm).reshape(seq_local, shard, width)
    shard_query, shard_key, shard_value, shard_out, shard_router, shard_gain_one, shard_gain_two = (
        lax.psum_scatter(grad_query_part, ("head", "blk"), scatter_dimension=0, tiled=True),
        lax.psum_scatter(grad_key_part, ("head", "blk"), scatter_dimension=0, tiled=True),
        lax.psum_scatter(grad_value_part, ("head", "blk"), scatter_dimension=0, tiled=True),
        lax.psum_scatter(grad_out_proj, ("head", "blk"), scatter_dimension=0, tiled=True),
        lax.psum_scatter(grad_router, ("head", "blk"), scatter_dimension=0, tiled=True),
        lax.psum_scatter(grad_gain_first, ("head", "blk"), scatter_dimension=0, tiled=True),
        lax.psum_scatter(grad_gain_second, ("head", "blk"), scatter_dimension=0, tiled=True),
    )
    return (
        out,
        grad_tokens,
        shard_gain_one,
        shard_query,
        shard_key,
        shard_value,
        shard_out,
        shard_gain_two,
        shard_router,
        grad_gate_sum[None],
        grad_up_sum[None],
        grad_down_sum[None],
    )


def solution(mesh):
    placed = (
        P("head", "blk", None),
        P(("head", "blk")),
        P(("head", "blk"), None),
        P(("head", "blk"), None),
        P(("head", "blk"), None),
        P(("head", "blk"), None),
        P(("head", "blk")),
        P(("head", "blk"), None),
        P("blk", None, None),
        P("blk", None, None),
        P("blk", None, None),
        P("head", "blk", None),
        P("head", "blk", None),
    )
    return jax.shard_map(
        local,
        mesh=mesh,
        in_specs=placed,
        out_specs=(
            P("head", "blk", None),
            P("head", "blk", None),
            P(("head", "blk")),
            P(("head", "blk"), None),
            P(("head", "blk"), None),
            P(("head", "blk"), None),
            P(("head", "blk"), None),
            P(("head", "blk")),
            P(("head", "blk"), None),
            P("blk", None, None),
            P("blk", None, None),
            P("blk", None, None),
        ),
        check_vma=False,
    )
```

profile of v0, /device:TPU:0, one launch (start us, length us, event | category | flops | bytes accessed | tf_op | source)
XLA Modules:
  0.0 2469.6 jit_solution(6601209752102984705)
XLA Ops:
  11.2 42.1 %all-reduce.7 = (bf16[1536]{0:T(1024)(128)(2,1)S(1)}, bf16[1536]{0:T(1024)(128)(2,1)}) all-reduce(bf16[1536]{0:T(1024)(128)(2,1)S(1)} %dynamic-update-slice, bf16[1536]{0:T(1024)(128)(2,1)S(1)} %dynamic-update-slice.1), channel_id=1, replica_groups=mesh['head'=2,'blk'=16] {'head','blk'}, use_global_device_ids=true, to_apply=%add.2 | all-reduce | flops 3072 | bytes 12288
  56.1 12.6 all-gather.8.cloned.1.call-done
  81.0 44.3 %all-gather.12.cloned.1.call-done = bf16[1536,512]{1,0:T(8,128)(2,1)} async-done(((bf16[48,512]{1,0:T(8,128)(2,1)}), bf16[1536,512]{1,0:T(8,128)(2,1)}) %all-gather.12.cloned.1.call-update) | async-done | bytes 1572880 | tf_op jit(solution)/shard_map/all_gather | solution.py:114
  150.3 40.5 %all-gather.16.cloned.1.call-done = bf16[1536,1536]{1,0:T(8,128)(2,1)} async-done(((bf16[48,1536]{1,0:T(8,128)(2,1)}), bf16[1536,1536]{1,0:T(8,128)(2,1)}) %all-gather.16.cloned.1.call-update) | async-done | bytes 4718608 | tf_op jit(solution)/shard_map/all_gather | solution.py:113
  223.9 18.3 all-gather.10.cloned.1.call-done
  248.5 45.2 %all-gather.14.cloned.1.call-done = bf16[4,2048,256]{2,1,0:T(8,128)(2,1)} async-done(((bf16[4,128,256]{2,1,0:T(8,128)(2,1)}), bf16[4,2048,256]{2,1,0:T(8,128)(2,1)}) %all-gather.14.cloned.1.call-update) | async-done | bytes 4194320 | tf_op jit(solution)/shard_map/all_gather | solution.py:151
  300.0 76.2 %while.30 = (s32[]{:T(128)}, bf16[2,2,128,4,3,64]{2,5,4,3,1,0:T(8,128)(2,1)}, f32[2,2,4,3,128]{4,3,2,1,0:T(4,128)S(1)}, bf16[2,2,2048,4,64]{2,4,3,1,0:T(8,128)(2...) while((s32[]{:T(128)}, ...), condition=%wide.region_4.5_spmd.clone.clone, body=%wide.region_1.4_spmd.clone.sunk.clone | while | flops 1686369280 | bytes 98826872 | solution.py:167
  300.3 13.6 fusion.186
  325.2 12.4 fusion.188
  338.0 14.4 fusion.186
  352.3 11.5 fusion.187
  363.8 12.4 fusion.188
  403.6 14.7 gather_fusion
  423.2 233.0 %all-gather = bf16[32,48,16]{1,2,0:T(8,128)(2,1)S(1)} all-gather(bf16[1,48,16]{1,2,0:T(8,128)(2,1)S(1)} %bitcast.470), channel_id=1, replica_groups=mesh['head'=2,'blk'=16] {'head','blk'}, dimensions={0}, use_global_device_ids=true | all-gather | bytes 50688 | tf_op jit(solution)/shard_map/all_gather | solution.py:117
  658.0 15.9 gather_fusion.3
  675.7 17.4 gather_fusion.2
  693.2 11.4 multiply_convert_fusion
  730.0 148.1 %all-to-all-done.6 = bf16[16,192,1536]{2,1,0:T(8,128)(2,1)} async-done(((bf16[16,192,1536]{2,1,0:T(8,128)(2,1)}), bf16[16,192,1536]{2,1,0:T(8,128)(2,1)}, u32[]{:S(2)}, u32[]{:S(2)}) %all-to-all-start.6) | async-done | bytes 9437216 | tf_op jit(solution)/shard_map/all_to_all | solution.py:222
  878.1 14.6 multiply_convert_fusion.1
  900.3 40.9 %all-to-all-start.5 = ((bf16[16,192,1536]{2,1,0:T(8,128)(2,1)}), bf16[16,192,1536]{2,1,0:T(8,128)(2,1)}, u32[]{:S(2)}, u32[]{:S(2)}) async-start(bf16[16,192,1536]{2,1,0:T(8,128)(2,1)} %bitcast.426), calls=%async_computation.5 | async-start | bytes 18874368 | tf_op jit(solution)/shard_map/all_to_all | solution.py:208
  941.2 11.4 fusion.80
  952.6 11.6 add_convert_fusion
  964.2 145.9 %all-to-all-done.5 = bf16[16,192,1536]{2,1,0:T(8,128)(2,1)} async-done(((bf16[16,192,1536]{2,1,0:T(8,128)(2,1)}), bf16[16,192,1536]{2,1,0:T(8,128)(2,1)}, u32[]{:S(2)}, u32[]{:S(2)}) %all-to-all-start.5) | async-done | bytes 9437216 | tf_op jit(solution)/shard_map/all_to_all | solution.py:208
  1110.0 40.9 %all-to-all-start.7 = ((bf16[16,192,1536]{2,1,0:T(8,128)(2,1)}), bf16[16,192,1536]{2,1,0:T(8,128)(2,1)}, u32[]{:S(2)}, u32[]{:S(2)}) async-start(bf16[16,192,1536]{2,1,0:T(8,128)(2,1)} %bitcast.425), calls=%async_computation.7 | async-start | bytes 18874368 | tf_op jit(solution)/shard_map/all_to_all | solution.py:238
  1151.4 18.3 gather_fusion.1
  1169.7 16.5 fusion.69
  1186.4 133.3 %all-to-all-done.7 = bf16[16,192,1536]{2,1,0:T(8,128)(2,1)} async-done(((bf16[16,192,1536]{2,1,0:T(8,128)(2,1)}), bf16[16,192,1536]{2,1,0:T(8,128)(2,1)}, u32[]{:S(2)}, u32[]{:S(2)}) %all-to-all-start.7) | async-done | bytes 9437216 | tf_op jit(solution)/shard_map/all_to_all | solution.py:238
  1319.7 18.6 gather_fusion.4
  1357.2 12.1 all-to-all-done.8
  1369.5 168.4 %while.31 = (s32[]{:T(128)}, f32[2,2,128,4,3,64]{2,5,4,3,1,0:T(8,128)}, bf16[2,2,2048,4,64]{2,4,3,1,0:T(8,128)(2,1)}, bf16[2,2,2048,4,64]{2,4,3,1,0:T(8,128)(2,1...) while((s32[]{:T(128)}, ...), condition=%wide.region_21.22_spmd.clone.clone, body=%wide.region_19.21_spmd.clone.sunk.clone | while | flops 4122407936 | bytes 286631648 | solution.py:279
  1370.0 13.4 fusion.197
  1383.4 12.2 bitcast_dynamic-update-slice_fusion.11
  1395.7 22.2 fusion.198
  1417.9 18.5 fusion.199
  1454.1 13.4 fusion.197
  1467.5 12.2 bitcast_dynamic-update-slice_fusion.11
  1479.7 22.2 fusion.198
  1501.9 18.5 fusion.199
  1592.1 65.9 %reduce-scatter.24.cloned.1.call-done = bf16[128,1024]{1,0:T(8,128)(2,1)} async-done(((bf16[2048,1024]{1,0:T(8,128)(2,1)}), bf16[128,1024]{1,0:T(8,128)(2,1)}) %reduce-scatter.24.cloned.1.call-update) | async-done | bytes 262160
  1671.3 62.5 %reduce-scatter.22.cloned.1.call-done = bf16[128,1024]{1,0:T(8,128)(2,1)} async-done(((bf16[2048,1024]{1,0:T(8,128)(2,1)}), bf16[128,1024]{1,0:T(8,128)(2,1)}) %reduce-scatter.22.cloned.1.call-update) | async-done | bytes 262160
  1754.3 22.0 all_to_all.149
  1782.3 81.4 %all-reduce.11.cloned.1.call-done = (bf16[1,1536,512]{2,1,0:T(8,128)(2,1)}, bf16[1,1536,512]{2,1,0:T(8,128)(2,1)}, bf16[1,512,1536]{2,1,0:T(8,128)(2,1)}) async-done(((bf16[1,1536,512]{2,1,0:T(8,128)(2,1)}, bf16[1,1536,512]{2,1,0:T(8,128)(2,1)}, bf16[1,512,1536]{2,1,0:T(8,128)(2,1)}), (bf16[1,1536,512]{2,1,0:T(8,128)(2,1)}, bf16[1,1536,512]{2,1,0:T(8,128)(2,1)}, ...) | async-done | bytes 4718608 | tf_op jit(solution)/shard_map/psum | solution.py:242
  1871.6 93.4 %reduce-scatter.26.cloned.1.call-done = f32[48,16]{1,0:T(8,128)} async-done(((f32[1536,16]{1,0:T(8,128)}), f32[48,16]{1,0:T(8,128)}) %reduce-scatter.26.cloned.1.call-update) | async-done | bytes 3088
  1973.8 40.3 %all-reduce.6 = (f32[1536]{0:T(1024)S(1)}, f32[1536]{0:T(1024)S(1)}) all-reduce(f32[1536]{0:T(1024)S(1)} %get-tuple-element.178, f32[1536]{0:T(1024)S(1)} %copy-done.48), channel_id=4, replica_groups=mesh['head'=2,'blk'=16] {'head','blk'}, use_global_device_ids=true, to_apply=%region_26.27.clone | all-reduce | flops 3072 | bytes 24576
  2018.7 53.6 %reduce-scatter.18.cloned.1.call-done = f32[48,512]{1,0:T(8,128)} async-done(((f32[1536,512]{1,0:T(8,128)}), f32[48,512]{1,0:T(8,128)}) %reduce-scatter.18.cloned.1.call-update) | async-done | bytes 98320 | tf_op jit(solution)/shard_map/reduce_scatter | solution.py:328
  2072.2 107.1 %reduce-scatter.16.cloned.1.call-done = f32[48,512]{1,0:T(8,128)} async-done(((f32[1536,512]{1,0:T(8,128)}), f32[48,512]{1,0:T(8,128)}) %reduce-scatter.16.cloned.1.call-update) | async-done | bytes 98320 | tf_op jit(solution)/shard_map/reduce_scatter | solution.py:327
  2179.3 141.8 %reduce-scatter.20.cloned.1.call-done = f32[48,1536]{1,0:T(8,128)} async-done(((f32[1536,1536]{1,0:T(8,128)}), f32[48,1536]{1,0:T(8,128)}) %reduce-scatter.20.cloned.1.call-update) | async-done | bytes 294928 | tf_op jit(solution)/shard_map/reduce_scatter | solution.py:329
  2321.1 141.5 %reduce-scatter.14.cloned.1.call-done = f32[48,1536]{1,0:T(8,128)} async-done(((f32[1536,1536]{1,0:T(8,128)}), f32[48,1536]{1,0:T(8,128)}) %reduce-scatter.14.cloned.1.call-update) | async-done | bytes 294928 | tf_op jit(solution)/shard_map/reduce_scatter | solution.py:326
  (339 shorter events, 339.9 us)
Async XLA Ops:
  7.2 871.0 %copy-start = (bf16[1,512,1536]{2,1,0:T(8,128)(2,1)S(1)}, bf16[1,512,1536]{2,1,0:T(8,128)(2,1)}, u32[]{:S(2)}) copy-start(bf16[1,512,1536]{2,1,0:T(8,128)(2,1)} %param.27) | copy-start | bytes 4718596
  7.2 73.6 %copy-start.7 = (bf16[2,128,1536]{2,1,0:T(8,128)(2,1)S(1)}, bf16[2,128,1536]{2,1,0:T(8,128)(2,1)}, u32[]{:S(2)}) copy-start(bf16[2,128,1536]{2,1,0:T(8,128)(2,1)} %param.17) | copy-start | bytes 2359300
  7.2 61.4 %all-gather.8.cloned.1.call-start = ((), (), s32[]{:S(2)}) async-start(), calls=%async_computation.19 | async-start | bytes 1622016 | tf_op jit(solution)/shard_map/all_gather | solution.py:115
  7.9 117.4 %all-gather.12.cloned.1.call-start = ((), (), s32[]{:S(2)}) async-start(), calls=%async_computation.21 | async-start | bytes 1622016 | tf_op jit(solution)/shard_map/all_gather | solution.py:114
  8.7 182.1 %all-gather.16.cloned.1.call-start = ((), (), s32[]{:S(2)}) async-start(), calls=%async_computation.23 | async-start | bytes 4866048 | tf_op jit(solution)/shard_map/all_gather | solution.py:113
  9.4 232.7 %all-gather.10.cloned.1.call-start = ((), (), s32[]{:S(2)}) async-start(), calls=%async_computation.20 | async-start | bytes 4456448 | tf_op jit(solution)/shard_map/all_gather | solution.py:152
  53.3 27.7 %copy-start.33 = (f32[1536]{0:T(1024)}, f32[1536]{0:T(1024)S(1)}, u32[]{:S(2)}) copy-start(f32[1536]{0:T(1024)S(1)} %convert_element_type.135) | copy-start | bytes 18436
  79.9 213.8 %all-gather.14.cloned.1.call-start = ((), (), s32[]{:S(2)}) async-start(), calls=%async_computation.22 | async-start | bytes 4456448 | tf_op jit(solution)/shard_map/all_gather | solution.py:151
  80.7 120.2 %copy-start.31 = (f32[128,32]{0,1:T(8,128)}, f32[128,32]{0,1:T(8,128)S(1)}, u32[]{:S(2)}) copy-start(f32[128,32]{0,1:T(8,128)S(1)} %get-tuple-element.246) | copy-start | bytes 49156
  81.0 116.4 %copy-start.15 = (bf16[2,128,1536]{2,1,0:T(8,128)(2,1)}, bf16[2,128,1536]{2,1,0:T(8,128)(2,1)S(1)}, u32[]{:S(2)}) copy-start(bf16[2,128,1536]{2,1,0:T(8,128)(2,1)S(1)} %multiply_convert_fusion.5) | copy-start | bytes 2359300
  139.6 257.6 %all-gather.18.cloned.1.call-start = ((), (), s32[]{:S(2)}) async-start(), calls=%async_computation.24 | async-start | bytes 4866048 | tf_op jit(solution)/shard_map/all_gather | solution.py:116
  140.2 57.2 %copy-start.57 = (s32[2]{0:T(128)}, s32[2]{0:T(128)S(1)}, u32[]{:S(2)}) copy-start(s32[2]{0:T(128)S(1)} %iota_multiply_fusion) | copy-start | bytes 28
  150.2 47.2 %copy-start.44 = (s32[2,1024]{1,0:T(2,128)}, s32[2,1024]{1,0:T(2,128)S(1)}, u32[]{:S(2)}) copy-start(s32[2,1024]{1,0:T(2,128)S(1)} %fusion.91) | copy-start | bytes 24580
  208.6 15.2 all-to-all-start.2
  300.0 80.8 %copy-start.49 = (s32[2048,1]{0,1:T(1,128)S(1)}, s32[2048,1]{0,1:T(1,128)}, u32[]{:S(2)}) copy-start(s32[2048,1]{0,1:T(1,128)} %mul.422) | copy-start | bytes 24580
  300.0 80.8 %copy-start.50 = (s32[1,1,2,1024]{3,1,2,0:T(1,128)S(1)}, s32[1,1,2,1024]{3,1,2,0:T(1,128)}, u32[]{:S(2)}) copy-start(s32[1,1,2,1024]{3,1,2,0:T(1,128)} %copy.313) | copy-start | bytes 24580
  300.0 80.8 %copy-start.56 = (bf16[1536]{0:T(1024)(128)(2,1)S(1)}, bf16[1536]{0:T(1024)(128)(2,1)}, u32[]{:S(2)}) copy-start(bf16[1536]{0:T(1024)(128)(2,1)} %get-tuple-element.221) | copy-start | bytes 9220
  376.2 25.0 %copy-start.4 = (bf16[2,2,128,4,3,64]{2,5,4,3,1,0:T(8,128)(2,1)}, bf16[2,2,128,4,3,64]{2,5,4,3,1,0:T(8,128)(2,1)S(1)}, u32[]{:S(2)}) copy-start(bf16[2,2,128,4,3,64]{2,5,4,3,1,0:T(8,128)(2,1)S(1)} %get-tuple-element.500) | copy-start | bytes 2359300
  376.2 25.0 %copy-start.29 = (s32[2048]{0:T(1024)}, s32[2048]{0:T(1024)S(1)}, u32[]{:S(2)}) copy-start(s32[2048]{0:T(1024)S(1)} %get-tuple-element.544) | copy-start | bytes 24580
  376.3 25.0 %copy-start.35 = (f32[2,2,4,3,128]{4,3,2,1,0:T(4,128)}, f32[2,2,4,3,128]{4,3,2,1,0:T(4,128)S(1)}, u32[]{:S(2)}) copy-start(f32[2,2,4,3,128]{4,3,2,1,0:T(4,128)S(1)} %get-tuple-element.453) | copy-start | bytes 73732
  376.3 15.8 all-to-all-start.3
  418.3 286.3 %all-to-all-start.4 = ((bf16[16,192,1536]{2,1,0:T(8,128)(2,1)}), bf16[16,192,1536]{2,1,0:T(8,128)(2,1)}, u32[]{:S(2)}, u32[]{:S(2)}) async-start(bf16[16,192,1536]{2,1,0:T(8,128)(2,1)} %bitcast.413), calls=%async_computation.4 | async-start | bytes 18874368 | tf_op jit(solution)/shard_map/all_to_all | solution.py:197
  704.6 173.6 %all-to-all-start.6 = ((bf16[16,192,1536]{2,1,0:T(8,128)(2,1)}), bf16[16,192,1536]{2,1,0:T(8,128)(2,1)}, u32[]{:S(2)}, u32[]{:S(2)}) async-start(bf16[16,192,1536]{2,1,0:T(8,128)(2,1)} %multiply_convert_fusion), calls=%async_computation.6 | async-start | bytes 18874368 | tf_op jit(solution)/shard_map/all_to_all | solution.py:222
  900.3 209.8 %all-to-all-start.5 = ((bf16[16,192,1536]{2,1,0:T(8,128)(2,1)}), bf16[16,192,1536]{2,1,0:T(8,128)(2,1)}, u32[]{:S(2)}, u32[]{:S(2)}) async-start(bf16[16,192,1536]{2,1,0:T(8,128)(2,1)} %bitcast.426), calls=%async_computation.5 | async-start | bytes 18874368 | tf_op jit(solution)/shard_map/all_to_all | solution.py:208
  1110.0 40.9 %copy-start.45 = (s32[2,1024]{1,0:T(2,128)S(1)}, s32[2,1024]{1,0:T(2,128)}, u32[]{:S(2)}) copy-start(s32[2,1024]{1,0:T(2,128)} %copy-done.44) | copy-start | bytes 24580
  1110.0 41.1 %copy-start.58 = (s32[2]{0:T(128)S(1)}, s32[2]{0:T(128)}, u32[]{:S(2)}) copy-start(s32[2]{0:T(128)} %copy-done.57) | copy-start | bytes 28
  1110.0 209.7 %all-to-all-start.7 = ((bf16[16,192,1536]{2,1,0:T(8,128)(2,1)}), bf16[16,192,1536]{2,1,0:T(8,128)(2,1)}, u32[]{:S(2)}, u32[]{:S(2)}) async-start(bf16[16,192,1536]{2,1,0:T(8,128)(2,1)} %bitcast.425), calls=%async_computation.7 | async-start | bytes 18874368 | tf_op jit(solution)/shard_map/all_to_all | solution.py:238
  1186.4 159.1 %copy-start.39 = (f32[256,16]{0,1:T(8,128)}, f32[256,16]{0,1:T(8,128)S(1)}, u32[]{:S(2)}) copy-start(f32[256,16]{0,1:T(8,128)S(1)} %select_reduce_fusion) | copy-start | bytes 49156
  1353.6 15.7 all-to-all-start.8
  1357.2 300.9 %reduce-scatter.24.cloned.1.call-start = ((), (), s32[]{:S(2)}) async-start(), calls=%async_computation.30 | async-start | bytes 4456448
  1417.9 23.1 copy-start.23
  1501.9 23.1 copy-start.23
  1550.6 183.2 %reduce-scatter.22.cloned.1.call-start = ((), (), s32[]{:S(2)}) async-start(), calls=%async_computation.29 | async-start | bytes 4456448
  1563.4 300.3 %all-reduce.11.cloned.1.call-start = ((), (), s32[]{:S(2)}) async-start(), calls=%async_computation.32 | async-start | bytes 9437184 | tf_op jit(solution)/shard_map/psum | solution.py:242
  1592.1 71.3 %copy-start.18 = (bf16[256,1536]{1,0:T(8,128)(2,1)S(1)}, bf16[256,1536]{1,0:T(8,128)(2,1)}, u32[]{:S(2)}) copy-start(bf16[256,1536]{1,0:T(8,128)(2,1)} %copy-done.17) | copy-start | bytes 2359300
  1592.1 71.4 %copy-start.40 = (f32[256,16]{0,1:T(8,128)S(1)}, f32[256,16]{0,1:T(8,128)}, u32[]{:S(2)}) copy-start(f32[256,16]{0,1:T(8,128)} %copy-done.39) | copy-start | bytes 49156
  1592.1 76.8 %copy-start.16 = (bf16[2,128,1536]{2,1,0:T(8,128)(2,1)S(1)}, bf16[2,128,1536]{2,1,0:T(8,128)(2,1)}, u32[]{:S(2)}) copy-start(bf16[2,128,1536]{2,1,0:T(8,128)(2,1)} %copy-done.15) | copy-start | bytes 2359300
  1659.9 8.6 all-to-all-start.11
  1663.4 301.6 %reduce-scatter.26.cloned.1.call-start = ((), (), s32[]{:S(2)}) async-start(), calls=%async_computation.31 | async-start | bytes 811008
  1665.3 407.0 %reduce-scatter.18.cloned.1.call-start = ((), (), s32[]{:S(2)}) async-start(), calls=%async_computation.27 | async-start | bytes 3244032 | tf_op jit(solution)/shard_map/reduce_scatter | solution.py:328
  1668.8 66.3 %copy-start.21 = (bf16[32,8,2,256]{3,1,2,0:T(8,128)(2,1)}, bf16[32,8,2,256]{3,1,2,0:T(8,128)(2,1)S(1)}, u32[]{:S(2)}) copy-start(bf16[32,8,2,256]{3,1,2,0:T(8,128)(2,1)S(1)} %copy.318) | copy-start | bytes 786436
  1668.9 66.4 %copy-start.32 = (f32[128,32]{0,1:T(8,128)S(1)}, f32[128,32]{0,1:T(8,128)}, u32[]{:S(2)}) copy-start(f32[128,32]{0,1:T(8,128)} %copy-done.31) | copy-start | bytes 49156
  1668.9 66.4 %copy-start.41 = (f32[128,32]{0,1:T(8,128)S(1)}, f32[128,32]{0,1:T(8,128)}, u32[]{:S(2)}) copy-start(f32[128,32]{0,1:T(8,128)} %get-tuple-element.244) | copy-start | bytes 49156
  1671.2 508.1 %reduce-scatter.16.cloned.1.call-start = ((), (), s32[]{:S(2)}) async-start(), calls=%async_computation.26 | async-start | bytes 3244032 | tf_op jit(solution)/shard_map/reduce_scatter | solution.py:327
  1747.5 573.7 %reduce-scatter.20.cloned.1.call-start = ((), (), s32[]{:S(2)}) async-start(), calls=%async_computation.28 | async-start | bytes 9732096 | tf_op jit(solution)/shard_map/reduce_scatter | solution.py:329
  1752.6 710.0 %reduce-scatter.14.cloned.1.call-start = ((), (), s32[]{:S(2)}) async-start(), calls=%async_computation.25 | async-start | bytes 9732096 | tf_op jit(solution)/shard_map/reduce_scatter | solution.py:326
  1871.6 98.5 %copy-start.19 = (bf16[1536,512]{1,0:T(8,128)(2,1)S(1)}, bf16[1536,512]{1,0:T(8,128)(2,1)}, u32[]{:S(2)}) copy-start(bf16[1536,512]{1,0:T(8,128)(2,1)} %all-gather.12.cloned.1.call-done) | copy-start | bytes 4718596
  1971.9 490.8 %copy-start.1 = (bf16[1,512,1536]{2,1,0:T(8,128)(2,1)S(1)}, bf16[1,512,1536]{2,1,0:T(8,128)(2,1)}, u32[]{:S(2)}) copy-start(bf16[1,512,1536]{2,1,0:T(8,128)(2,1)} %param.27) | copy-start | bytes 4718596
  (46 other events, 419.3 us)
Sparse Core Ops, SparseCore 0:
  10.9 57.6 all-gather.7
  71.5 53.7 all-gather.11
  128.3 62.4 all-gather.15
  193.4 48.7 all-gather.9
  244.7 48.9 all-gather.13
  296.5 62.0 all-gather.17
  1550.7 107.2 reduce-scatter.23
  1661.9 71.8 reduce-scatter.21
  1737.0 126.7 all-reduce.10
  1868.7 96.2 reduce-scatter.25
  1971.0 101.2 reduce-scatter.17
  2078.1 101.1 reduce-scatter.15
  2185.8 135.2 reduce-scatter.19
  2327.5 135.1 reduce-scatter.13
where the time goes:
time: 2480 us; the launch traced here: 2470 us
  waiting for transfers between devices  1360 us (55%)
  blocking collectives  362 us (15%)
  matrix products  307 us (12%)
  local copies, waits for them, and re-layouts  188 us (8%)
  other arithmetic  125 us (5%)
  starting transfers between devices  107 us (4%)
    all_gather x1, blocking collectives, local(): lax.all_gather(w_router, ('head', 'blk'), axis=0, tiled=True)  233 us
    unnamed x17, waiting for transfers between devices  225 us
    all_to_all x1, waiting for transfers between devices, local(): lax.all_to_all(grad_send, 'blk', split_axis=0, concat_axis=0, tiled=True)  148 us
    all_to_all x1, waiting for transfers between devices, local(): lax.all_to_all(expert_out, 'blk', split_axis=0, concat_axis=0, tiled=True)  146 us
    reduce_scatter x1, waiting for transfers between devices, local(): lax.psum_scatter(grad_out_proj, ('head', 'blk'), scatter_dimension=0, til...  142 us
    reduce_scatter x1, waiting for transfers between devices, local(): lax.psum_scatter(grad_query_part, ('head', 'blk'), scatter_dimension=0, t...  141 us
    all_to_all x1, waiting for transfers between devices, local(): lax.all_to_all(d_rows.reshape(-1, capacity, width), 'blk', split_axis=0,...  133 us
    reduce_scatter x1, waiting for transfers between devices, local(): lax.psum_scatter(grad_key_part, ('head', 'blk'), scatter_dimension=0, til...  107 us
  transfers between devices with their start and end apart: 22, of which 20 were waited for; matrix products, arithmetic and copies ran while one was open for 15% of the time, Pallas kernels for 0%

commit v1 on v0

v1 whole, which is shorter than its diff:
```python
import functools

import jax
import jax.numpy as jnp
from jax import lax
from jax.experimental import pallas as pl
from jax.experimental.pallas import tpu as pltpu
from jax.sharding import PartitionSpec as P

HDIM = 64
TOP = 8
BLOCK = 256
LANES = 128

highest = lax.Precision.HIGHEST
theta_base = 10000.0
norm_eps = 1e-06


def rope_tables(positions, half_width):
    index_float = jnp.arange(half_width, dtype=jnp.float32)
    frequency = theta_base ** (-2.0 * index_float / (2 * half_width))
    angles = positions.astype(jnp.float32)[:, None] * frequency[None, :]
    return (jnp.cos(angles), jnp.sin(angles))


def rms_scale(values):
    return lax.rsqrt(jnp.mean(values * values, axis=-1, keepdims=True) + norm_eps)


def norm_back(values, inverse, gain, d_normed):
    unit_values = values * inverse
    scaled = d_normed * gain
    d_gain = jnp.sum(d_normed * unit_values, axis=0)
    d_values = inverse * (
        scaled - unit_values * jnp.mean(scaled * unit_values, axis=-1, keepdims=True)
    )
    return (d_values, d_gain)


def matmul(left, right):
    return jnp.dot(left, right, preferred_element_type=jnp.float32)


def matmul_nt(left, right):
    return lax.dot_general(left, right, (((1,), (1,)), ((), ())), preferred_element_type=jnp.float32)


def matmul_tn(left, right):
    return lax.dot_general(left, right, (((0,), (0,)), ((), ())), preferred_element_type=jnp.float32)


def wide(block, group):
    flipped = block.T
    return jnp.concatenate([flipped[h*HDIM:(h+1)*HDIM] for h in range(group)], axis=1)

def tall(block, group):
    return jnp.concatenate([block[:, h*HDIM:(h+1)*HDIM] for h in range(group)], axis=0)

def narrow(values, group, rows):
    return jnp.concatenate([values[:, h*rows:(h+1)*rows] for h in range(group)], axis=0).T

def forward_kernel(group, qkv_ref, att_ref, flat_ref, lse_ref, key_sc, val_sc, acc_sc):
    i = pl.program_id(0)
    lanes = group*HDIM
    @pl.when(i == 0)
    def _():
        key_sc[...] = qkv_ref[:, lanes:lanes+HDIM]
        val_sc[...] = qkv_ref[:, lanes+HDIM:lanes+2*HDIM].T
    rows = pl.ds(pl.multiple_of(i*BLOCK, BLOCK), BLOCK)
    query = wide(qkv_ref[rows, :lanes], group) * jnp.bfloat16(HDIM**-0.5)
    acc_sc[...] = jnp.zeros_like(acc_sc)
    def step(j, carry):
        top, total = carry
        here = pl.ds(pl.multiple_of(j*BLOCK, BLOCK), BLOCK)
        scores = jnp.dot(key_sc[here, :], query, preferred_element_type=jnp.float32)
        new_top = jnp.maximum(top, jnp.max(scores, axis=0, keepdims=True))
        probs = jnp.exp(scores - new_top)
        fade = jnp.exp(top - new_top)
        acc_sc[...] = acc_sc[...]*fade + jnp.dot(val_sc[:, here], probs.astype(jnp.bfloat16), preferred_element_type=jnp.float32)
        return new_top, total*fade + jnp.sum(probs, axis=0, keepdims=True)
    width = group*BLOCK
    top, total = lax.fori_loop(0, i+1, step, (jnp.full((1,width), -1e30, jnp.float32), jnp.zeros((1,width), jnp.float32)))
    result = acc_sc[...] / total
    flat_ref[0] = result
    att_ref[...] = narrow(result.astype(jnp.bfloat16), group, BLOCK)
    lse_ref[0] = top + jnp.log(total)

def attend_forward(qkv, group):
    total = qkv.shape[0]; steps = total//BLOCK; lanes = group*HDIM; width = group*BLOCK
    return pl.pallas_call(
        functools.partial(forward_kernel, group),
        grid=(steps,),
        in_specs=[pl.BlockSpec((total, lanes+2*HDIM), lambda i: (0,0))],
        out_specs=[pl.BlockSpec((BLOCK, lanes), lambda i: (i,0)),
                   pl.BlockSpec((1, HDIM, width), lambda i: (i,0,0)),
                   pl.BlockSpec((1,1,width), lambda i: (i,0,0))],
        out_shape=[jax.ShapeDtypeStruct((total, lanes), jnp.bfloat16),
                   jax.ShapeDtypeStruct((steps,HDIM,width), jnp.float32),
                   jax.ShapeDtypeStruct((steps,1,width), jnp.float32)],
        scratch_shapes=[pltpu.VMEM((total,HDIM), jnp.bfloat16), pltpu.VMEM((HDIM,total), jnp.bfloat16), pltpu.VMEM((HDIM,width), jnp.float32)],
        compiler_params=pltpu.CompilerParams(dimension_semantics=("arbitrary",)),
        name="attend_forward",
    )(qkv)

def unrotate(values, cosine, sine):
    a, b = values[:HDIM//2], values[HDIM//2:]
    return jnp.concatenate([a*cosine + b*sine, b*cosine - a*sine], axis=0)

def backward_kernel(group, steps, qkv_ref, grad_ref, flat_ref, lse_ref, cos_ref, sin_ref, out_ref, key_sc, keyt_sc, val_sc, dq_sc, dk_sc, dv_sc):
    i = pl.program_id(0)
    lanes = group*HDIM
    scale = HDIM**-0.5
    @pl.when(i == 0)
    def _():
        key = qkv_ref[:, lanes:lanes+HDIM]
        key_sc[...] = key
        keyt_sc[...] = key.T
        val_sc[...] = qkv_ref[:, lanes+HDIM:lanes+2*HDIM]
        dk_sc[...] = jnp.zeros_like(dk_sc)
        dv_sc[...] = jnp.zeros_like(dv_sc)
    rows = pl.ds(pl.multiple_of(i*BLOCK, BLOCK), BLOCK)
    block = qkv_ref[rows, :lanes] * jnp.bfloat16(scale)
    query_w, query_t = wide(block, group), tall(block, group)
    grad = grad_ref[...]
    grad_w, grad_t = wide(grad, group), tall(grad, group)
    lse = lse_ref[0]
    delta = jnp.sum(grad_w.astype(jnp.float32)*flat_ref[0], axis=0, keepdims=True)
    dq_sc[...] = jnp.zeros_like(dq_sc)
    def step(j, carry):
        here = pl.ds(pl.multiple_of(j*BLOCK, BLOCK), BLOCK)
        scores = jnp.dot(key_sc[here,:], query_w, preferred_element_type=jnp.float32)
        probs = jnp.exp(scores - lse)
        dprobs = jnp.dot(val_sc[here,:], grad_w, preferred_element_type=jnp.float32)
        dv_sc[here,:] += jnp.dot(probs.astype(jnp.bfloat16), grad_t, preferred_element_type=jnp.float32)
        dscores = (probs*(dprobs-delta)).astype(jnp.bfloat16)
        dk_sc[here,:] += jnp.dot(dscores, query_t, preferred_element_type=jnp.float32)
        dq_sc[...] += jnp.dot(keyt_sc[:,here], dscores, preferred_element_type=jnp.float32)
        return carry
    lax.fori_loop(0, i+1, step, 0)
    cosine, sine = cos_ref[:, rows], sin_ref[:, rows]
    pieces = [unrotate(dq_sc[:, h*BLOCK:(h+1)*BLOCK]*scale, cosine, sine).astype(jnp.bfloat16) for h in range(group)]
    out_ref[rows, :lanes] = jnp.concatenate(pieces, axis=0).T
    @pl.when(i == steps-1)
    def _():
        def finish(j, carry):
            here = pl.ds(pl.multiple_of(j*BLOCK, BLOCK), BLOCK)
            turned = unrotate(dk_sc[here,:].T, cos_ref[:,here], sin_ref[:,here]).astype(jnp.bfloat16)
            both = jnp.concatenate([turned, dv_sc[here,:].astype(jnp.bfloat16).T], axis=0).T
            out_ref[here, lanes:lanes+2*HDIM] = both
            return carry
        lax.fori_loop(0, steps, finish, 0)

def attend_backward(qkv, grad, flat, lse, cosine, sine, group):
    total = qkv.shape[0]; steps = total//BLOCK; lanes = group*HDIM; width = group*BLOCK
    return pl.pallas_call(
        functools.partial(backward_kernel, group, steps),
        grid=(steps,),
        in_specs=[pl.BlockSpec((total, lanes+2*HDIM), lambda i: (0,0)),
                  pl.BlockSpec((BLOCK, lanes), lambda i: (i,0)),
                  pl.BlockSpec((1, HDIM, width), lambda i: (i,0,0)),
                  pl.BlockSpec((1,1,width), lambda i: (i,0,0)),
                  pl.BlockSpec((HDIM//2, total), lambda i: (0,0)),
                  pl.BlockSpec((HDIM//2, total), lambda i: (0,0))],
        out_specs=pl.BlockSpec((total, lanes+2*HDIM), lambda i: (0,0)),
        out_shape=jax.ShapeDtypeStruct((total, lanes+2*HDIM), jnp.bfloat16),
        scratch_shapes=[pltpu.VMEM((total,HDIM), jnp.bfloat16), pltpu.VMEM((HDIM,total), jnp.bfloat16), pltpu.VMEM((total,HDIM), jnp.bfloat16),
                        pltpu.VMEM((HDIM,width), jnp.float32), pltpu.VMEM((total,HDIM), jnp.float32), pltpu.VMEM((total,HDIM), jnp.float32)],
        compiler_params=pltpu.CompilerParams(dimension_semantics=("arbitrary",)),
        name="attend_backward",
    )(qkv, grad, flat, lse, cosine, sine)

def expert_kernel(
    parts, rows, width, experts, steps, chained, index_ref, *refs
):
    blocks = refs[:parts]
    grads = refs[parts : 2 * parts]
    router_ref, gate_ref, up_ref, down_ref = refs[2 * parts : 2 * parts + 4]
    refs = refs[2 * parts + 4 + (5 if chained else 0) :]
    mixed_ref, back_ref, rows_ref, grads_ref, d_gate_ref, d_up_ref, hidden_ref = refs[:7]
    gates_sc, d_gates_sc, mixed_sc, back_sc = refs[7:]
    step = pl.program_id(0)
    lane = lax.broadcasted_iota(jnp.int32, (rows, LANES), 1)

    @pl.when(step == 0)
    def _():
        part = rows // parts
        for k in range(parts):
            here = pl.ds(k * part, part)
            rows_ref[here, :] = blocks[k][...]
            grads_ref[here, :] = grads[k][:, :width]
            logits = jnp.dot(blocks[k][...], router_ref[...], preferred_element_type=jnp.float32)
            logits = jnp.where(grads[k][:, width:].astype(jnp.float32) > 0.5, logits, -1e30)
            weight = jnp.exp(logits - jnp.max(logits, axis=1, keepdims=True))
            gates_sc[here, :] = weight / jnp.sum(weight, axis=1, keepdims=True)
        d_gates_sc[...] = jnp.zeros_like(d_gates_sc)

    expert = index_ref[step * 2 // steps]
    own = lane == expert
    gate = jnp.sum(jnp.where(own, gates_sc[...], 0.0), axis=1, keepdims=True)
    block = rows_ref[...]
    gate_lin = jnp.dot(block, gate_ref[0], preferred_element_type=jnp.float32)
    up_lin = jnp.dot(block, up_ref[0], preferred_element_type=jnp.float32)
    d_hidden = matmul_nt(grads_ref[...], down_ref[0])
    sigma = 1.0 / (1.0 + jnp.exp(-gate_lin))
    active = gate_lin * sigma
    hidden = active * up_lin
    d_gates_sc[...] += jnp.where(own, jnp.sum(hidden * d_hidden, axis=1, keepdims=True), 0.0)
    hidden = (gate * hidden).astype(jnp.bfloat16)
    d_hidden = gate * d_hidden
    d_gate = (d_hidden * up_lin * sigma * (1.0 + gate_lin * (1.0 - sigma))).astype(jnp.bfloat16)
    d_up = (d_hidden * active).astype(jnp.bfloat16)
    hidden_ref[...] = hidden
    d_gate_ref[...] = d_gate
    d_up_ref[...] = d_up
    mixed = jnp.dot(hidden, down_ref[0], preferred_element_type=jnp.float32)
    back = matmul_nt(d_gate, gate_ref[0]) + matmul_nt(d_up, up_ref[0])

    @pl.when(step == 0)
    def _():
        mixed_sc[...] = mixed
        back_sc[...] = back

    @pl.when(step > 0)
    def _():
        mixed_sc[...] += mixed
        back_sc[...] += back

    @pl.when(step == steps - 1)
    def _():
        mixed_ref[...] = mixed_sc[...].astype(jnp.bfloat16)
        back_ref[:, :width] = back_sc[...].astype(jnp.bfloat16)
        d_gates = d_gates_sc[...]
        high = d_gates.astype(jnp.bfloat16).astype(jnp.float32)
        low = pltpu.roll(d_gates - high, experts, 1)
        back_ref[:, width:] = jnp.where(lane < experts, high, low).astype(jnp.bfloat16)


def expert_rows(index, experts, blocks, grads, router, gate, up, down, slot, total, buffers):
    parts = len(blocks)
    part, width = blocks[0].shape
    rows = parts * part
    units = gate.shape[2]
    tile = 256
    tiles = units // tile
    steps = 2 * tiles
    whole = lambda *shape: pl.BlockSpec(shape, lambda i, ids: (0,) * len(shape))
    activation = pl.BlockSpec((rows, tile), lambda i, ids: (slot, i))
    kept = pl.BlockSpec((rows, width), lambda i, ids: (slot, 0))
    chained = buffers is not None
    shapes = [
        jax.ShapeDtypeStruct((rows, width), jnp.bfloat16),
        jax.ShapeDtypeStruct((rows, width + LANES), jnp.bfloat16),
        jax.ShapeDtypeStruct((total, width), jnp.bfloat16),
        jax.ShapeDtypeStruct((total, width), jnp.bfloat16),
    ] + [jax.ShapeDtypeStruct((total, 2 * units), jnp.bfloat16)] * 3
    inputs = [index, *blocks, *grads, router, gate, up, down] + (list(buffers) if chained else [])
    first = 1 + 2 * parts + 4
    return pl.pallas_call(
        functools.partial(expert_kernel, parts, rows, width, experts, steps, chained),
        grid_spec=pltpu.PrefetchScalarGridSpec(
            num_scalar_prefetch=1,
            grid=(steps,),
            in_specs=[whole(part, width)] * parts
            + [whole(part, width + LANES)] * parts
            + [
                whole(width, LANES),
                pl.BlockSpec((1, width, tile), lambda i, ids: (i // tiles, 0, i % tiles)),
                pl.BlockSpec((1, width, tile), lambda i, ids: (i // tiles, 0, i % tiles)),
                pl.BlockSpec((1, tile, width), lambda i, ids: (i // tiles, i % tiles, 0)),
            ]
            + ([pl.BlockSpec(memory_space=pl.ANY)] * 5 if chained else []),
            out_specs=[
                whole(rows, width),
                whole(rows, width + LANES),
                kept,
                kept,
                activation,
                activation,
                activation,
            ],
            scratch_shapes=[
                pltpu.VMEM((rows, LANES), jnp.float32),
                pltpu.VMEM((rows, LANES), jnp.float32),
                pltpu.VMEM((rows, width), jnp.float32),
                pltpu.VMEM((rows, width), jnp.float32),
            ],
        ),
        out_shape=shapes,
        input_output_aliases={first + k: 2 + k for k in range(5)} if chained else {},
        compiler_params=pltpu.CompilerParams(dimension_semantics=("arbitrary",)),
        cost_estimate=pl.CostEstimate(
            flops=rows * width * units * 24,
            bytes_accessed=12 * width * units + 20 * rows * width,
            transcendentals=rows * units * 2,
        ),
        name="expert_rows",
    )(*inputs)


def gather_dense(values):
    return lax.all_gather(values, ("head", "blk"), axis=0, tiled=True)


def scatter_dense(values):
    return lax.psum_scatter(
        values.astype(jnp.bfloat16), ("head", "blk"), scatter_dimension=0, tiled=True
    ).astype(jnp.float32)


def exchange(values):
    return lax.all_to_all(values, "blk", split_axis=0, concat_axis=0, tiled=True)


def sum_heads(values):
    if lax.axis_size("head") == 2:
        other = lax.ppermute(values, "head", [(0, 1), (1, 0)])
        return values.astype(jnp.float32) + other.astype(jnp.float32)
    return lax.psum(values, "head").astype(jnp.float32)


def partner(values):
    count = lax.axis_size("blk")
    return lax.ppermute(values, "blk", [(k, k ^ 1) for k in range(count)])


def ring_steps():
    count = lax.axis_size("blk")
    half = count // 4
    order = [2 * k for k in range(half)] + [2 * k + 1 for k in reversed(range(half))]
    onward, back = [], []
    for place, chip in enumerate(order):
        following = order[(place + 1) % len(order)]
        for core in range(2):
            onward.append((2 * chip + core, 2 * following + core))
            back.append((2 * following + core, 2 * chip + core))
    send_on = lambda values: lax.ppermute(values, "blk", onward)
    send_back = lambda values: lax.ppermute(values, "blk", back)
    return len(order), send_on, send_back


def ring_gather(values):
    length, send_on, send_back = ring_steps()
    half = values.shape[0] // 2
    behind = ahead = values
    pairs = []
    for _ in range(length // 2 - 1):
        behind, ahead = send_on(behind), send_back(ahead)
        pairs.append((behind, ahead))
    return pairs, (send_on(behind[:half]), send_back(ahead[half:]))


def ring_scatter(own, pairs, opposite):
    length, send_on, send_back = ring_steps()
    half = own.shape[0] // 2
    onward, back = send_on(opposite[:half]), send_back(opposite[half:])
    onward = jnp.pad(onward, ((0, half), (0, 0)))
    back = jnp.pad(back, ((half, 0), (0, 0)))
    for behind, ahead in reversed(pairs):
        onward = send_on(onward + ahead)
        back = send_back(back + behind)
    wide = own.astype(jnp.float32)
    return wide + onward.astype(jnp.float32) + back.astype(jnp.float32)


def with_lanes(values, extra):
    rows = values.shape[0]
    spare = jnp.zeros((rows, LANES - extra.shape[1]), values.dtype)
    return jnp.concatenate([values, extra.astype(values.dtype), spare], axis=1)


def add_lanes(padded, extra):
    rows, columns = padded.shape
    spread = ((0, 0), (columns - LANES, LANES - extra.shape[1]))
    return padded + jnp.pad(extra, spread)


def local(
    tokens,
    gain_attn,
    w_query,
    w_key,
    w_value,
    w_out,
    gain_moe,
    w_router,
    w_gate,
    w_up,
    w_down,
    routes,
    grad_out,
):
    seq_local, shard, width = tokens.shape
    token_rows = seq_local * shard
    blk_index = lax.axis_index("blk")
    blk_count = lax.axis_size("blk")
    seq_total = blk_count * shard
    part_rows = w_query.shape[0]
    groups = w_key.shape[1] // HDIM
    group = w_query.shape[1] // w_key.shape[1]
    lanes = group * HDIM
    span = lanes + 2 * HDIM
    pairs = seq_local * groups
    copies = blk_count // pairs
    experts = w_router.shape[1]
    units = w_gate.shape[2]

    mixed_weights = jnp.concatenate(
        [
            w_query.reshape(part_rows, groups, lanes),
            w_key.reshape(part_rows, groups, HDIM),
            w_value.reshape(part_rows, groups, HDIM),
        ],
        axis=2,
    ).reshape(part_rows, groups * span)
    full_mixed = gather_dense(with_lanes(mixed_weights, gain_attn[:, None]))
    full_out = gather_dense(
        with_lanes(w_out, jnp.concatenate([w_router, gain_moe[:, None]], axis=1))
    )
    router = full_out[:, width:]
    full_router = router[:, :experts]
    router = jnp.where(jnp.arange(LANES)[None, :] < experts, router, jnp.bfloat16(0.0))
    gain_first = full_mixed[:, groups * span].astype(jnp.float32)
    gain_second = full_out[:, width + experts].astype(jnp.float32)

    expert_ids = jnp.arange(experts, dtype=jnp.int32)
    routes_tok = routes.reshape(token_rows, TOP)
    chosen = jnp.any(routes_tok[:, :, None] == expert_ids[None, None, :], axis=1)
    d_out = grad_out.reshape(token_rows, width)
    grads_own = with_lanes(d_out.astype(jnp.bfloat16), chosen)
    grads_pairs, grads_opposite = ring_gather(grads_own)
    both_gate = jnp.concatenate([w_gate, partner(w_gate)], axis=0)
    both_up = jnp.concatenate([w_up, partner(w_up)], axis=0)
    both_down = jnp.concatenate([w_down, partner(w_down)], axis=0)

    residual = tokens.astype(jnp.float32).reshape(token_rows, width)
    inverse_one = rms_scale(residual)
    normed = (residual * inverse_one * gain_first).astype(jnp.bfloat16)
    positions = blk_index * shard + jnp.arange(shard, dtype=jnp.int32)
    cosine, sine = rope_tables(positions, HDIM // 2)
    turned = (jnp.arange(groups * (group + 2)) % (group + 2) < group + 1)[None, None, :, None]
    cosine = jnp.where(turned, cosine[None, :, None, :], 1.0)
    sine = jnp.where(turned, sine[None, :, None, :], 0.0)
    linear = matmul(normed, full_mixed)[:, : groups * span].reshape(seq_local, shard, -1, HDIM)
    first, second = linear[..., : HDIM // 2], linear[..., HDIM // 2 :]
    packed = jnp.concatenate(
        [first * cosine - second * sine, second * cosine + first * sine], axis=-1
    ).astype(jnp.bfloat16)

    def to_pairs(values, columns):
        values = values.reshape(seq_local, shard, groups, columns)
        values = values.transpose(0, 2, 1, 3).reshape(pairs, 1, shard, columns)
        values = jnp.broadcast_to(values, (pairs, copies, shard, columns))
        return exchange(values.reshape(blk_count, shard, columns)).reshape(seq_total, columns)

    def to_tokens(values, columns):
        values = exchange(values.reshape(blk_count, shard, columns))
        values = values.reshape(pairs, copies, shard, columns)[:, 0]
        values = values.reshape(seq_local, groups, shard, columns).transpose(0, 2, 1, 3)
        return values.reshape(token_rows, groups * columns)

    pair_qkv = to_pairs(packed, span)
    pair_attended, flat, log_total = attend_forward(pair_qkv, group)
    attended = to_tokens(pair_attended, lanes)
    middle = residual + matmul(attended, full_out)[:, :width]
    inverse_two = rms_scale(middle)
    normed_two = (middle * inverse_two * gain_second).astype(jnp.bfloat16)
    logits = matmul(normed_two, full_router)
    gates = jax.nn.softmax(jnp.where(chosen, logits, -jnp.inf), axis=-1)

    blocks_pairs, blocks_opposite = ring_gather(normed_two)
    total = blk_count // 2 * token_rows
    ids = jnp.stack([blk_index, blk_index ^ 1]).astype(jnp.int32)

    def apply_experts(blocks, grads, slot, buffers):
        return expert_rows(
            ids, experts, blocks, grads, router, both_gate, both_up, both_down, slot, total, buffers
        )

    ring_pairs = len(blocks_pairs)
    mixed_own, back_own, *buffers = apply_experts(
        [normed_two], [grads_own], 2 * ring_pairs, None
    )
    mixed_pairs, back_pairs = [], []
    for k in range(ring_pairs):
        mixed, back, *buffers = apply_experts(blocks_pairs[k], grads_pairs[k], k, buffers)
        mixed_pairs.append((mixed[:token_rows], mixed[token_rows:]))
        back_pairs.append((back[:token_rows], back[token_rows:]))
    mixed_opposite, back_opposite, *buffers = apply_experts(
        blocks_opposite, grads_opposite, 2 * ring_pairs + 1, buffers
    )
    rows_all, grads_all, d_gate_all, d_up_all, hidden_all = buffers
    back_sum = ring_scatter(back_own, back_pairs, back_opposite)
    mixed_sum = ring_scatter(mixed_own, mixed_pairs, mixed_opposite)
    out = (middle + mixed_sum).reshape(seq_local, shard, width)

    def expert_sum(left, right, swap):
        other = matmul_tn(*((left[:, units:], right) if swap else (left, right[:, units:])))
        mine = matmul_tn(*((left[:, :units], right) if swap else (left, right[:, :units])))
        mine = mine + partner(other.astype(jnp.bfloat16)).astype(jnp.float32)
        return sum_heads(mine.astype(jnp.bfloat16))

    grad_gate_sum = expert_sum(rows_all, d_gate_all, False)
    grad_up_sum = expert_sum(rows_all, d_up_all, False)
    grad_down_sum = expert_sum(hidden_all, grads_all, True)

    d_gates = back_sum[:, width : width + experts] + back_sum[:, width + experts : width + 2 * experts]
    d_logits = gates * (d_gates - jnp.sum(gates * d_gates, axis=-1, keepdims=True))
    grad_router = jnp.dot(normed_two.astype(jnp.float32).T, d_logits, precision=highest)
    d_normed_two = back_sum[:, :width] + jnp.dot(
        d_logits, full_router.astype(jnp.float32).T, precision=highest
    )
    d_mid_norm, grad_gain_second = norm_back(middle, inverse_two, gain_second, d_normed_two)
    d_mid = d_out + d_mid_norm
    d_branch = jnp.pad(d_mid.astype(jnp.bfloat16), ((0, 0), (0, LANES)))
    d_attended = matmul_nt(d_branch, full_out).astype(jnp.bfloat16)
    pair_grad = to_pairs(d_attended, lanes)
    pair_cosine, pair_sine = rope_tables(jnp.arange(seq_total, dtype=jnp.int32), HDIM // 2)
    pair_d = attend_backward(
        pair_qkv, pair_grad, flat, log_total, pair_cosine.T, pair_sine.T, group
    )
    early = scatter_dense(
        add_lanes(
            matmul_tn(attended, d_branch),
            jnp.concatenate([grad_router, grad_gain_second[:, None]], axis=1),
        )
    )
    d_linear = jnp.pad(to_tokens(pair_d, span), ((0, 0), (0, LANES)))
    d_normed = matmul_nt(d_linear, full_mixed)
    d_tok_norm, grad_gain_first = norm_back(residual, inverse_one, gain_first, d_normed)
    grad_tokens = (d_mid + d_tok_norm).reshape(seq_local, shard, width)
    late = scatter_dense(add_lanes(matmul_tn(normed, d_linear), grad_gain_first[:, None]))
    late_mixed = late[:, : groups * span].reshape(part_rows, groups, span)
    return (
        out,
        grad_tokens,
        late[:, groups * span],
        late_mixed[:, :, :lanes].reshape(part_rows, -1),
        late_mixed[:, :, lanes : lanes + HDIM].reshape(part_rows, -1),
        late_mixed[:, :, lanes + HDIM :].reshape(part_rows, -1),
        early[:, :width],
        early[:, width + experts],
        early[:, width : width + experts],
        grad_gate_sum[None],
        grad_up_sum[None],
        grad_down_sum[None],
    )


def solution(mesh):
    placed = (
        P("head", "blk", None),
        P(("head", "blk")),
        P(("head", "blk"), None),
        P(("head", "blk"), None),
        P(("head", "blk"), None),
        P(("head", "blk"), None),
        P(("head", "blk")),
        P(("head", "blk"), None),
        P("blk", None, None),
        P("blk", None, None),
        P("blk", None, None),
        P("head", "blk", None),
        P("head", "blk", None),
    )
    return jax.shard_map(
        local,
        mesh=mesh,
        in_specs=placed,
        out_specs=(
            P("head", "blk", None),
            P("head", "blk", None),
            P(("head", "blk")),
            P(("head", "blk"), None),
            P(("head", "blk"), None),
            P(("head", "blk"), None),
            P(("head", "blk"), None),
            P(("head", "blk")),
            P(("head", "blk"), None),
            P("blk", None, None),
            P("blk", None, None),
            P("blk", None, None),
        ),
        check_vma=False,
    )
```

time: 2480 us -> 811 us (0.33)
  waiting for transfers between devices: 1360 us -> 372 us
  blocking collectives: 362 us -> 43.5 us
  matrix products: 307 us -> 63.4 us
  Pallas kernels: 0 us -> 143 us
  local copies, waits for them, and re-layouts: 188 us -> 57.4 us
  other arithmetic: 125 us -> 31 us
  starting transfers between devices: 107 us -> 81.1 us
    reduce_scatter x4 -> x2, waiting for transfers between devices: 444 us -> 0.01 us  [scatter_dense(): lax.psum_scatter(values.astype(jnp.bfloat16), ('head', 'blk'), scatter_di...]
    all_to_all x8 -> x3, waiting for transfers between devices: 454 us -> 16.8 us  [exchange(): lax.all_to_all(values, 'blk', split_axis=0, concat_axis=0, tiled=True)]
    ppermute x0 -> x41, waiting for transfers between devices: none -> 278 us  [the longest x16 164 us: ring_steps(): send_on = lambda values: lax.ppermute(values, 'blk', onward)]
    dot_general x36 -> x13, matrix products: 304 us -> 52.1 us  [the longest x8 33.3 us: matmul_tn(): lax.dot_general(left, right, (((0,), (0,)), ((), ())), preferred_element_...]
    all_gather x1 -> x0, blocking collectives: 233 us -> none  [local(): lax.all_gather(w_router, ('head', 'blk'), axis=0, tiled=True)]
    unnamed x17 -> x4, waiting for transfers between devices: 225 us -> 0.07 us
    pallas_call x0 -> x7, Pallas kernels: none -> 143 us  [the longest x5 91.1 us: expert_rows(): pl.pallas_call(functools.partial(expert_kernel, parts, rows, width, exper...]
    all_to_all x8 -> x3, starting transfers between devices: 107 us -> 15.2 us  [exchange(): lax.all_to_all(values, 'blk', split_axis=0, concat_axis=0, tiled=True)]
  transfers between devices with their start and end apart: 22 -> 48, of which waited for: 20 -> 24; matrix products, arithmetic and copies ran while one was open for 15% -> 16% of each run, Pallas kernels for 0% -> 16%
where the time goes in v1:
time: 811 us; the launch traced here: 806 us
  waiting for transfers between devices  372 us (46%)
  Pallas kernels  143 us (18%)
  starting transfers between devices  81.1 us (10%)
  matrix products  63.4 us (8%)
  local copies, waits for them, and re-layouts  57.4 us (7%)
  blocking collectives  43.5 us (5%)
  other arithmetic  31 us (4%)
  between operations  14.8 us (2%)
    ppermute x16, waiting for transfers between devices, ring_steps(): send_on = lambda values: lax.ppermute(values, 'blk', onward)  164 us
    ppermute x3, waiting for transfers between devices, sum_heads(): other = lax.ppermute(values, 'head', [(0, 1), (1, 0)])  109 us
    pallas_call x5, Pallas kernels, expert_rows(): pl.pallas_call(functools.partial(expert_kernel, parts, rows, width, exper...  91.1 us
    all_gather x2, waiting for transfers between devices, gather_dense(): return lax.all_gather(values, ('head', 'blk'), axis=0, tiled=True)  77 us
    all_to_all x1, blocking collectives, exchange(): lax.all_to_all(values, 'blk', split_axis=0, concat_axis=0, tiled=True)  43.5 us
    ppermute x16, starting transfers between devices, ring_steps(): send_on = lambda values: lax.ppermute(values, 'blk', onward)  36.8 us
    dot_general x8, matrix products, matmul_tn(): lax.dot_general(left, right, (((0,), (0,)), ((), ())), preferred_element_...  33.3 us
    pallas_call x1, Pallas kernels, attend_backward(): pl.pallas_call(functools.partial(backward_kernel, group, steps), grid=(st...  29.2 us
  transfers between devices with their start and end apart: 48, of which 24 were waited for; matrix products, arithmetic and copies ran while one was open for 16% of the time, Pallas kernels for 16%

profile of v1, /device:TPU:0, one launch (start us, length us, event | category | flops | bytes accessed | tf_op | source)
XLA Modules:
  0.0 805.9 jit_solution(14923820275946935612)
XLA Ops:
  14.1 77.0 %all-gather.3.cloned.1.call-done = bf16[1536,2688]{1,0:T(8,128)(2,1)} async-done(((bf16[48,2688]{1,0:T(8,128)(2,1)}), bf16[1536,2688]{1,0:T(8,128)(2,1)}) %all-gather.3.cloned.1.call-update) | async-done | bytes 8257552 | tf_op jit(solution)/shard_map/all_gather | solution.py:302
  93.4 7.9 fusion
  101.3 3.1 reshape.235
  110.0 4.5 all-to-all-start
  117.7 55.3 %collective-permute-done.11.refs_2_ = bf16[256,1664]{1,0:T(8,128)(2,1)} collective-permute-done((bf16[256,1664]{1,0:T(8,128)(2,1)S(1)}, bf16[256,1664]{1,0:T(8,128)(2,1)}, u32[]{:S(2)}, u32[]{:S(2)}) %collective-permute-start.11) | collective-permute-done | bytes 852000 | tf_op jit(solution)/shard_map/ppermute | solution.py:337
  173.0 11.0 %collective-permute-start.12 = (bf16[256,1664]{1,0:T(8,128)(2,1)}, bf16[256,1664]{1,0:T(8,128)(2,1)}, u32[]{:S(2)}, u32[]{:S(2)}) collective-permute-start(bf16[256,1664]{1,0:T(8,128)(2,1)} %collective-permute-done.11.refs_2_), channel_id=1, source_target_pairs={{0,4},{1,5},{4,8},{5,9},{8,12},{9,13},{12,14},{13,15},{14,10},{15,... | collective-permute-start | bytes 2555912 | tf_op jit(solution)/shard_map/ppermute | solution.py:337
  185.6 2.5 copy.106
  188.1 22.5 %attend_forward.1 = (bf16[2048,192]{1,0:T(8,128)(2,1)}, f32[8,64,768]{2,1,0:T(8,128)}, f32[8,1,768]{2,1,0:T(1,128)}) custom-call(bf16[2048,320]{1,0:T(8,128)(2,1)} %bitcast.85), custom_call_target="tpu_custom_call" | custom-call | tf_op jit(solution)/shard_map/attend_forward/pallas_call | solution.py:91
  212.9 6.3 all-to-all-start.1
  219.5 2.7 constant_dynamic-update-slice_fusion.3
  227.9 2.6 constant_dynamic-update-slice_fusion.2.refs_4_.refs_6_
  230.6 2.6 constant_dynamic-update-slice_fusion.4.refs_5_.refs_7_
  233.2 18.0 %collective-permute-done.13.refs_2_ = bf16[256,1664]{1,0:T(8,128)(2,1)S(1)} collective-permute-done((bf16[256,1664]{1,0:T(8,128)(2,1)}, bf16[256,1664]{1,0:T(8,128)(2,1)S(1)}, u32[]{:S(2)}, u32[]{:S(2)}) %collective-permute-start.13) | collective-permute-done | bytes 852000 | tf_op jit(solution)/shard_map/ppermute | solution.py:337
  252.0 5.9 collective-permute-start.14
  263.0 4.1 multiply_reduce_fusion.4
  273.6 13.3 %expert_rows.5 = (bf16[256,1536]{1,0:T(8,128)(2,1)}, bf16[256,1664]{1,0:T(8,128)(2,1)}, bf16[2048,1536]{1,0:T(8,128)(2,1)}, bf16[2048,1536]{1,0:T(8,128)(2,1)}, ...) custom-call(s32[2]{0:T(128)} %pad_add_fusion.index_ref, ...), custom_call_target="tpu_custom_call" | custom-call | flops 4831838208 | bytes 17301504 | tf_op jit(solution)/shard_map/expert_rows/pallas_call | solution.py:259
  291.2 21.5 %expert_rows.6 = (bf16[512,1536]{1,0:T(8,128)(2,1)}, bf16[512,1664]{1,0:T(8,128)(2,1)}, bf16[2048,1536]{1,0:T(8,128)(2,1)}, bf16[2048,1536]{1,0:T(8,128)(2,1)}, ...) custom-call(s32[2]{0:T(128)} %pad_add_fusion.index_ref, ...), custom_call_target="tpu_custom_call", output_to_operand_aliasing={{2}: (9, {}), {3}: (10, {}), {4}: (11, {}), {5}: (12, {}), ... | custom-call | flops 9663676416 | bytes 25165824 | tf_op jit(solution)/shard_map/expert_rows/pallas_call | solution.py:259
  313.4 12.3 %collective-permute-start.9 = (bf16[256,1536]{1,0:T(8,128)(2,1)}, bf16[256,1536]{1,0:T(8,128)(2,1)}, u32[]{:S(2)}, u32[]{:S(2)}) collective-permute-start(bf16[256,1536]{1,0:T(8,128)(2,1)} %collective-permute-done.8.refs_1_), channel_id=1, source_target_pairs={{4,0},{5,1},{8,4},{9,5},{12,8},{13,9},{14,12},{15,13},{10,14},{11,... | collective-permute-start | bytes 2359304 | tf_op jit(solution)/shard_map/ppermute | solution.py:338
  325.7 21.6 %expert_rows.7 = (bf16[512,1536]{1,0:T(8,128)(2,1)}, bf16[512,1664]{1,0:T(8,128)(2,1)}, bf16[2048,1536]{1,0:T(8,128)(2,1)}, bf16[2048,1536]{1,0:T(8,128)(2,1)}, ...) custom-call(s32[2]{0:T(128)} %pad_add_fusion.index_ref, ...), custom_call_target="tpu_custom_call", output_to_operand_aliasing={{2}: (9, {}), {3}: (10, {}), {4}: (11, {}), {5}: (12, {}), ... | custom-call | flops 9663676416 | bytes 25165824 | tf_op jit(solution)/shard_map/expert_rows/pallas_call | solution.py:259
  352.9 21.5 %expert_rows.8 = (bf16[512,1536]{1,0:T(8,128)(2,1)}, bf16[512,1664]{1,0:T(8,128)(2,1)}, bf16[2048,1536]{1,0:T(8,128)(2,1)}, bf16[2048,1536]{1,0:T(8,128)(2,1)}, ...) custom-call(s32[2]{0:T(128)} %pad_add_fusion.index_ref, ...), custom_call_target="tpu_custom_call", output_to_operand_aliasing={{2}: (9, {}), {3}: (10, {}), {4}: (11, {}), {5}: (12, {}), ... | custom-call | flops 9663676416 | bytes 25165824 | tf_op jit(solution)/shard_map/expert_rows/pallas_call | solution.py:259
  375.4 13.2 %expert_rows.9 = (bf16[256,1536]{1,0:T(8,128)(2,1)}, bf16[256,1664]{1,0:T(8,128)(2,1)}, bf16[2048,1536]{1,0:T(8,128)(2,1)}, bf16[2048,1536]{1,0:T(8,128)(2,1)}, ...) custom-call(s32[2]{0:T(128)} %pad_add_fusion.index_ref, ...), custom_call_target="tpu_custom_call", output_to_operand_aliasing={{2}: (9, {}), {3}: (10, {}), {4}: (11, {}), {5}: (12, {}), ... | custom-call | flops 4831838208 | bytes 17301504 | tf_op jit(solution)/shard_map/expert_rows/pallas_call | solution.py:259
  395.2 7.4 collective-permute-done.27
  405.6 5.5 collective-permute-done.19
  414.0 15.3 %collective-permute-done.28 = bf16[256,1664]{1,0:T(8,128)(2,1)S(1)} collective-permute-done((bf16[256,1664]{1,0:T(8,128)(2,1)S(1)}, bf16[256,1664]{1,0:T(8,128)(2,1)S(1)}, u32[]{:S(2)}, u32[]{:S(2)}) %collective-permute-start.28) | collective-permute-done | bytes 852000 | tf_op jit(solution)/shard_map/ppermute | solution.py:337
  432.3 13.9 %collective-permute-done.20 = bf16[256,1536]{1,0:T(8,128)(2,1)S(1)} collective-permute-done((bf16[256,1536]{1,0:T(8,128)(2,1)S(1)}, bf16[256,1536]{1,0:T(8,128)(2,1)S(1)}, u32[]{:S(2)}, u32[]{:S(2)}) %collective-permute-start.20) | collective-permute-done | bytes 786464 | tf_op jit(solution)/shard_map/ppermute | solution.py:337
  449.1 15.4 %collective-permute-done.29 = bf16[256,1664]{1,0:T(8,128)(2,1)S(1)} collective-permute-done((bf16[256,1664]{1,0:T(8,128)(2,1)S(1)}, bf16[256,1664]{1,0:T(8,128)(2,1)S(1)}, u32[]{:S(2)}, u32[]{:S(2)}) %collective-permute-start.29) | collective-permute-done | bytes 852000 | tf_op jit(solution)/shard_map/ppermute | solution.py:337
  469.2 12.1 %collective-permute-done.21 = bf16[256,1536]{1,0:T(8,128)(2,1)S(1)} collective-permute-done((bf16[256,1536]{1,0:T(8,128)(2,1)S(1)}, bf16[256,1536]{1,0:T(8,128)(2,1)S(1)}, u32[]{:S(2)}, u32[]{:S(2)}) %collective-permute-start.21) | collective-permute-done | bytes 786464 | tf_op jit(solution)/shard_map/ppermute | solution.py:337
  485.6 13.9 %collective-permute-done.30 = bf16[256,1664]{1,0:T(8,128)(2,1)S(1)} collective-permute-done((bf16[256,1664]{1,0:T(8,128)(2,1)S(1)}, bf16[256,1664]{1,0:T(8,128)(2,1)S(1)}, u32[]{:S(2)}, u32[]{:S(2)}) %collective-permute-start.30) | collective-permute-done | bytes 852000 | tf_op jit(solution)/shard_map/ppermute | solution.py:337
  500.8 3.4 multiply_reduce_fusion
  507.3 5.2 collective-permute-done.22
  512.9 5.0 fusion.38
  518.8 3.8 add_convert_fusion.1
  523.7 4.1 convolution_convert_fusion.3
  529.3 4.3 all-to-all-start.2
  535.5 16.8 %all-to-all-done.2 = bf16[16,128,192]{1,2,0:T(8,128)(2,1)S(1)} async-done(((bf16[16,128,192]{1,2,0:T(8,128)(2,1)}), bf16[16,128,192]{1,2,0:T(8,128)(2,1)S(1)}, u32[]{:S(2)}, u32[]{:S(2)}) %all-to-all-start.2) | async-done | bytes 786464 | tf_op jit(solution)/shard_map/all_to_all | solution.py:312
  553.6 29.2 %attend_backward.1 = bf16[2048,320]{1,0:T(8,128)(2,1)} custom-call(bf16[2048,320]{1,0:T(8,128)(2,1)} %bitcast.86, bf16[2048,192]{1,0:T(8,128)(2,1)} %bitcast.91, f32[8,64,768]{2,1,0:T(8,128)} %get-tuple-element.81.flat_ref, f32[8,1,768]{2,1,0:T(1,128)} %get-tuple-element.82.lse_ref, f32[32,2048]{1,0:T(8,128)} %get-tuple-element.176.cos_ref, ...), custom_call_target="tpu_custom_call" | custom-call | tf_op jit(solution)/shard_map/attend_backward/pallas_call | solution.py:156
  584.7 43.5 %all_to_all.20 = bf16[16,128,320]{1,2,0:T(8,128)(2,1)S(1)} all-to-all(bf16[16,128,320]{1,2,0:T(8,128)(2,1)S(1)} %copy.117), channel_id=1, replica_groups=mesh['head'=2,'blk'=16] {'blk'}, dimensions={0} | all-to-all | bytes 2621440 | tf_op jit(solution)/shard_map/all_to_all | solution.py:312
  629.8 7.1 multiply_reduce_fusion.1
  637.2 4.9 add_convert_fusion
  642.1 7.0 convolution_convert_fusion
  651.2 3.5 convolution_convert_fusion.1
  654.8 3.5 convolution_convert_fusion.2
  658.8 3.5 fusion.6
  663.9 3.7 fusion.5
  668.2 3.5 fusion.4
  673.2 29.6 %collective-permute-done.40 = bf16[512,1536]{1,0:T(8,128)(2,1)S(1)} collective-permute-done((bf16[512,1536]{1,0:T(8,128)(2,1)S(1)}, bf16[512,1536]{1,0:T(8,128)(2,1)S(1)}, u32[]{:S(2)}, u32[]{:S(2)}) %collective-permute-start.40) | collective-permute-done | bytes 1572896 | tf_op jit(solution)/shard_map/ppermute | solution.py:317
  704.9 43.2 %collective-permute-done.38 = bf16[1536,512]{1,0:T(8,128)(2,1)S(1)} collective-permute-done((bf16[1536,512]{1,0:T(8,128)(2,1)S(1)}, bf16[1536,512]{1,0:T(8,128)(2,1)S(1)}, u32[]{:S(2)}, u32[]{:S(2)}) %collective-permute-start.38) | collective-permute-done | bytes 1572896 | tf_op jit(solution)/shard_map/ppermute | solution.py:317
  750.3 36.2 %collective-permute-done.36 = bf16[1536,512]{1,0:T(8,128)(2,1)S(1)} collective-permute-done((bf16[1536,512]{1,0:T(8,128)(2,1)S(1)}, bf16[1536,512]{1,0:T(8,128)(2,1)S(1)}, u32[]{:S(2)}, u32[]{:S(2)}) %collective-permute-start.36) | collective-permute-done | bytes 1572896 | tf_op jit(solution)/shard_map/ppermute | solution.py:317
  (259 shorter events, 117.1 us)
Async XLA Ops:
  7.2 83.8 %all-gather.3.cloned.1.call-start = ((), (), s32[]{:S(2)}) async-start(), calls=%async_computation.6 | async-start | bytes 8515584 | tf_op jit(solution)/shard_map/all_gather | solution.py:302
  11.6 248.1 %all-gather.5.cloned.1.call-start = ((), (), s32[]{:S(2)}) async-start(), calls=%async_computation.7 | async-start | bytes 5271552 | tf_op jit(solution)/shard_map/all_gather | solution.py:302
  110.0 75.6 %all-to-all-start = ((bf16[16,128,320]{1,2,0:T(8,128)(2,1)}), bf16[16,128,320]{1,2,0:T(8,128)(2,1)}, u32[]{:S(2)}, u32[]{:S(2)}) async-start(bf16[16,128,320]{1,2,0:T(8,128)(2,1)} %bitcast.5), calls=%async_computation | async-start | bytes 2621440 | tf_op jit(solution)/shard_map/all_to_all | solution.py:312
  115.1 57.9 %collective-permute-start.11 = (bf16[256,1664]{1,0:T(8,128)(2,1)S(1)}, bf16[256,1664]{1,0:T(8,128)(2,1)}, u32[]{:S(2)}, u32[]{:S(2)}) collective-permute-start(bf16[256,1664]{1,0:T(8,128)(2,1)S(1)} %concatenate.32.refs_1_), channel_id=1, source_target_pairs={{0,4},{1,5},{4,8},{5,9},{8,12},{9,13},{12,14},{13,15},{14,10},{15,... | collective-permute-start | bytes 2555912 | tf_op jit(solution)/shard_map/ppermute | solution.py:337
  116.9 67.1 %collective-permute-start.15 = (bf16[256,1664]{1,0:T(8,128)(2,1)S(1)}, bf16[256,1664]{1,0:T(8,128)(2,1)}, u32[]{:S(2)}, u32[]{:S(2)}) collective-permute-start(bf16[256,1664]{1,0:T(8,128)(2,1)S(1)} %concatenate.32.refs_1_), channel_id=1, source_target_pairs={{4,0},{5,1},{8,4},{9,5},{12,8},{13,9},{14,12},{15,13},{10,14},{11,... | collective-permute-start | bytes 2555912 | tf_op jit(solution)/shard_map/ppermute | solution.py:338
  117.2 109.2 %collective-permute-start = (bf16[1,1536,512]{2,1,0:T(8,128)(2,1)}, bf16[1,1536,512]{2,1,0:T(8,128)(2,1)}, u32[]{:S(2)}, u32[]{:S(2)}) collective-permute-start(bf16[1,1536,512]{2,1,0:T(8,128)(2,1)} %param.21), channel_id=1, source_target_pairs={{0,1},{1,0},{2,3},{3,2},{4,5},{5,4},{6,7},{7,6},{8,9},{9,8},{10,11... | collective-permute-start | bytes 4718600 | tf_op jit(solution)/shard_map/ppermute | solution.py:324
  117.2 110.7 %collective-permute-start.1 = (bf16[1,1536,512]{2,1,0:T(8,128)(2,1)}, bf16[1,1536,512]{2,1,0:T(8,128)(2,1)}, u32[]{:S(2)}, u32[]{:S(2)}) collective-permute-start(bf16[1,1536,512]{2,1,0:T(8,128)(2,1)} %param.22), channel_id=1, source_target_pairs={{0,1},{1,0},{2,3},{3,2},{4,5},{5,4},{6,7},{7,6},{8,9},{9,8},{10,11... | collective-permute-start | bytes 4718600 | tf_op jit(solution)/shard_map/ppermute | solution.py:324
  117.7 112.9 %collective-permute-start.2 = (bf16[1,512,1536]{2,1,0:T(8,128)(2,1)}, bf16[1,512,1536]{2,1,0:T(8,128)(2,1)}, u32[]{:S(2)}, u32[]{:S(2)}) collective-permute-start(bf16[1,512,1536]{2,1,0:T(8,128)(2,1)} %param.23), channel_id=1, source_target_pairs={{0,1},{1,0},{2,3},{3,2},{4,5},{5,4},{6,7},{7,6},{8,9},{9,8},{10,11... | collective-permute-start | bytes 4718600 | tf_op jit(solution)/shard_map/ppermute | solution.py:324
  173.0 50.6 %collective-permute-start.12 = (bf16[256,1664]{1,0:T(8,128)(2,1)}, bf16[256,1664]{1,0:T(8,128)(2,1)}, u32[]{:S(2)}, u32[]{:S(2)}) collective-permute-start(bf16[256,1664]{1,0:T(8,128)(2,1)} %collective-permute-done.11.refs_2_), channel_id=1, source_target_pairs={{0,4},{1,5},{4,8},{5,9},{8,12},{9,13},{12,14},{13,15},{14,10},{15,... | collective-permute-start | bytes 2555912 | tf_op jit(solution)/shard_map/ppermute | solution.py:337
  184.0 41.6 %collective-permute-start.16 = (bf16[256,1664]{1,0:T(8,128)(2,1)}, bf16[256,1664]{1,0:T(8,128)(2,1)}, u32[]{:S(2)}, u32[]{:S(2)}) collective-permute-start(bf16[256,1664]{1,0:T(8,128)(2,1)} %collective-permute-done.15.refs_3_), channel_id=1, source_target_pairs={{4,0},{5,1},{8,4},{9,5},{12,8},{13,9},{14,12},{15,13},{10,14},{11,... | collective-permute-start | bytes 2555912 | tf_op jit(solution)/shard_map/ppermute | solution.py:338
  212.9 48.2 %all-to-all-start.1 = ((bf16[16,128,192]{1,2,0:T(8,128)(2,1)}), bf16[16,128,192]{1,2,0:T(8,128)(2,1)}, u32[]{:S(2)}, u32[]{:S(2)}) async-start(bf16[16,128,192]{1,2,0:T(8,128)(2,1)} %copy.107), calls=%async_computation.1 | async-start | bytes 1572864 | tf_op jit(solution)/shard_map/all_to_all | solution.py:312
  219.2 571.0 %reduce-scatter.5.cloned.1.call-start = ((), (), s32[]{:S(2)}) async-start(), calls=%async_computation.9 | async-start | bytes 5271552 | tf_op jit(solution)/shard_map/reduce_scatter | solution.py:306
  223.7 27.6 %collective-permute-start.13 = (bf16[256,1664]{1,0:T(8,128)(2,1)}, bf16[256,1664]{1,0:T(8,128)(2,1)S(1)}, u32[]{:S(2)}, u32[]{:S(2)}) collective-permute-start(bf16[256,1664]{1,0:T(8,128)(2,1)} %collective-permute-done.12.refs_2_), channel_id=1, source_target_pairs={{0,4},{1,5},{4,8},{5,9},{8,12},{9,13},{12,14},{13,15},{14,10},{15,... | collective-permute-start | bytes 2555912 | tf_op jit(solution)/shard_map/ppermute | solution.py:337
  225.6 32.3 %collective-permute-start.17 = (bf16[256,1664]{1,0:T(8,128)(2,1)}, bf16[256,1664]{1,0:T(8,128)(2,1)S(1)}, u32[]{:S(2)}, u32[]{:S(2)}) collective-permute-start(bf16[256,1664]{1,0:T(8,128)(2,1)} %collective-permute-done.16.refs_3_), channel_id=1, source_target_pairs={{4,0},{5,1},{8,4},{9,5},{12,8},{13,9},{14,12},{15,13},{10,14},{11,... | collective-permute-start | bytes 2555912 | tf_op jit(solution)/shard_map/ppermute | solution.py:338
  252.0 122.4 %collective-permute-start.14 = (bf16[128,1664]{1,0:T(8,128)(2,1)}, bf16[128,1664]{1,0:T(8,128)(2,1)S(1)}, u32[]{:S(2)}, u32[]{:S(2)}) collective-permute-start(bf16[128,1664]{1,0:T(8,128)(2,1)} %slice.192), channel_id=1, source_target_pairs={{0,4},{1,5},{4,8},{5,9},{8,12},{9,13},{12,14},{13,15},{14,10},{15,... | collective-permute-start | bytes 1277960 | tf_op jit(solution)/shard_map/ppermute | solution.py:337
  259.7 114.7 %collective-permute-start.18 = (bf16[128,1664]{1,0:T(8,128)(2,1)}, bf16[128,1664]{1,0:T(8,128)(2,1)S(1)}, u32[]{:S(2)}, u32[]{:S(2)}) collective-permute-start(bf16[128,1664]{1,0:T(8,128)(2,1)} %slice.193), channel_id=1, source_target_pairs={{4,0},{5,1},{8,4},{9,5},{12,8},{13,9},{14,12},{15,13},{10,14},{11,... | collective-permute-start | bytes 1277960 | tf_op jit(solution)/shard_map/ppermute | solution.py:338
  268.4 20.7 %collective-permute-start.3 = (bf16[256,1536]{1,0:T(8,128)(2,1)}, bf16[256,1536]{1,0:T(8,128)(2,1)}, u32[]{:S(2)}, u32[]{:S(2)}) collective-permute-start(bf16[256,1536]{1,0:T(8,128)(2,1)} %multiply_convert_fusion.refs_0_), channel_id=1, source_target_pairs={{0,4},{1,5},{4,8},{5,9},{8,12},{9,13},{12,14},{13,15},{14,10},{15,... | collective-permute-start | bytes 2359304 | tf_op jit(solution)/shard_map/ppermute | solution.py:337
  270.8 19.0 %collective-permute-start.7 = (bf16[256,1536]{1,0:T(8,128)(2,1)}, bf16[256,1536]{1,0:T(8,128)(2,1)}, u32[]{:S(2)}, u32[]{:S(2)}) collective-permute-start(bf16[256,1536]{1,0:T(8,128)(2,1)} %multiply_convert_fusion.refs_0_), channel_id=1, source_target_pairs={{4,0},{5,1},{8,4},{9,5},{12,8},{13,9},{14,12},{15,13},{10,14},{11,... | collective-permute-start | bytes 2359304 | tf_op jit(solution)/shard_map/ppermute | solution.py:338
  289.1 23.5 %collective-permute-start.4 = (bf16[256,1536]{1,0:T(8,128)(2,1)}, bf16[256,1536]{1,0:T(8,128)(2,1)}, u32[]{:S(2)}, u32[]{:S(2)}) collective-permute-start(bf16[256,1536]{1,0:T(8,128)(2,1)} %collective-permute-done.3.refs_0_), channel_id=1, source_target_pairs={{0,4},{1,5},{4,8},{5,9},{8,12},{9,13},{12,14},{13,15},{14,10},{15,... | collective-permute-start | bytes 2359304 | tf_op jit(solution)/shard_map/ppermute | solution.py:337
  289.8 23.6 %collective-permute-start.8 = (bf16[256,1536]{1,0:T(8,128)(2,1)}, bf16[256,1536]{1,0:T(8,128)(2,1)}, u32[]{:S(2)}, u32[]{:S(2)}) collective-permute-start(bf16[256,1536]{1,0:T(8,128)(2,1)} %collective-permute-done.7.refs_1_), channel_id=1, source_target_pairs={{4,0},{5,1},{8,4},{9,5},{12,8},{13,9},{14,12},{15,13},{10,14},{11,... | collective-permute-start | bytes 2359304 | tf_op jit(solution)/shard_map/ppermute | solution.py:338
  312.7 38.2 %collective-permute-start.5 = (bf16[256,1536]{1,0:T(8,128)(2,1)}, bf16[256,1536]{1,0:T(8,128)(2,1)}, u32[]{:S(2)}, u32[]{:S(2)}) collective-permute-start(bf16[256,1536]{1,0:T(8,128)(2,1)} %collective-permute-done.4.refs_0_), channel_id=1, source_target_pairs={{0,4},{1,5},{4,8},{5,9},{8,12},{9,13},{12,14},{13,15},{14,10},{15,... | collective-permute-start | bytes 2359304 | tf_op jit(solution)/shard_map/ppermute | solution.py:337
  313.4 34.0 %collective-permute-start.9 = (bf16[256,1536]{1,0:T(8,128)(2,1)}, bf16[256,1536]{1,0:T(8,128)(2,1)}, u32[]{:S(2)}, u32[]{:S(2)}) collective-permute-start(bf16[256,1536]{1,0:T(8,128)(2,1)} %collective-permute-done.8.refs_1_), channel_id=1, source_target_pairs={{4,0},{5,1},{8,4},{9,5},{12,8},{13,9},{14,12},{15,13},{10,14},{11,... | collective-permute-start | bytes 2359304 | tf_op jit(solution)/shard_map/ppermute | solution.py:338
  349.1 25.3 %collective-permute-start.10 = (bf16[128,1536]{1,0:T(8,128)(2,1)}, bf16[128,1536]{1,0:T(8,128)(2,1)}, u32[]{:S(2)}, u32[]{:S(2)}) collective-permute-start(bf16[128,1536]{1,0:T(8,128)(2,1)} %slice.191), channel_id=1, source_target_pairs={{4,0},{5,1},{8,4},{9,5},{12,8},{13,9},{14,12},{15,13},{10,14},{11,... | collective-permute-start | bytes 1179656 | tf_op jit(solution)/shard_map/ppermute | solution.py:338
  352.6 21.8 %collective-permute-start.6 = (bf16[128,1536]{1,0:T(8,128)(2,1)}, bf16[128,1536]{1,0:T(8,128)(2,1)}, u32[]{:S(2)}, u32[]{:S(2)}) collective-permute-start(bf16[128,1536]{1,0:T(8,128)(2,1)} %slice.190), channel_id=1, source_target_pairs={{0,4},{1,5},{4,8},{5,9},{8,12},{9,13},{12,14},{13,15},{14,10},{15,... | collective-permute-start | bytes 1179656 | tf_op jit(solution)/shard_map/ppermute | solution.py:337
  389.9 12.7 %collective-permute-start.27 = (bf16[128,1664]{1,0:T(8,128)(2,1)S(1)}, bf16[128,1664]{1,0:T(8,128)(2,1)S(1)}, u32[]{:S(2)}, u32[]{:S(2)}) collective-permute-start(bf16[128,1664]{1,0:T(8,128)(2,1)S(1)} %get-tuple-element.169), channel_id=1, source_target_pairs={{0,4},{1,5},{4,8},{5,9},{8,12},{9,13},{12,14},{13,15},{14,10},{15,... | collective-permute-start | bytes 1277960 | tf_op jit(solution)/shard_map/ppermute | solution.py:337
  390.6 12.7 %collective-permute-start.31 = (bf16[128,1664]{1,0:T(8,128)(2,1)S(1)}, bf16[128,1664]{1,0:T(8,128)(2,1)S(1)}, u32[]{:S(2)}, u32[]{:S(2)}) collective-permute-start(bf16[128,1664]{1,0:T(8,128)(2,1)S(1)} %get-tuple-element.170), channel_id=1, source_target_pairs={{4,0},{5,1},{8,4},{9,5},{12,8},{13,9},{14,12},{15,13},{10,14},{11,... | collective-permute-start | bytes 1277960 | tf_op jit(solution)/shard_map/ppermute | solution.py:338
  393.2 17.9 %collective-permute-start.19 = (bf16[128,1536]{1,0:T(8,128)(2,1)S(1)}, bf16[128,1536]{1,0:T(8,128)(2,1)S(1)}, u32[]{:S(2)}, u32[]{:S(2)}) collective-permute-start(bf16[128,1536]{1,0:T(8,128)(2,1)S(1)} %get-tuple-element.171), channel_id=1, source_target_pairs={{0,4},{1,5},{4,8},{5,9},{8,12},{9,13},{12,14},{13,15},{14,10},{15,... | collective-permute-start | bytes 1179656 | tf_op jit(solution)/shard_map/ppermute | solution.py:337
  393.8 17.9 %collective-permute-start.23 = (bf16[128,1536]{1,0:T(8,128)(2,1)S(1)}, bf16[128,1536]{1,0:T(8,128)(2,1)S(1)}, u32[]{:S(2)}, u32[]{:S(2)}) collective-permute-start(bf16[128,1536]{1,0:T(8,128)(2,1)S(1)} %get-tuple-element.172), channel_id=1, source_target_pairs={{4,0},{5,1},{8,4},{9,5},{12,8},{13,9},{14,12},{15,13},{10,14},{11,... | collective-permute-start | bytes 1179656 | tf_op jit(solution)/shard_map/ppermute | solution.py:338
  403.5 25.8 %collective-permute-start.28 = (bf16[256,1664]{1,0:T(8,128)(2,1)S(1)}, bf16[256,1664]{1,0:T(8,128)(2,1)S(1)}, u32[]{:S(2)}, u32[]{:S(2)}) collective-permute-start(bf16[256,1664]{1,0:T(8,128)(2,1)S(1)} %get-tuple-element.160), channel_id=1, source_target_pairs={{0,4},{1,5},{4,8},{5,9},{8,12},{9,13},{12,14},{13,15},{14,10},{15,... | collective-permute-start | bytes 2555912 | tf_op jit(solution)/shard_map/ppermute | solution.py:337
  405.3 24.6 %collective-permute-start.32 = (bf16[256,1664]{1,0:T(8,128)(2,1)S(1)}, bf16[256,1664]{1,0:T(8,128)(2,1)S(1)}, u32[]{:S(2)}, u32[]{:S(2)}) collective-permute-start(bf16[256,1664]{1,0:T(8,128)(2,1)S(1)} %get-tuple-element.161), channel_id=1, source_target_pairs={{4,0},{5,1},{8,4},{9,5},{12,8},{13,9},{14,12},{15,13},{10,14},{11,... | collective-permute-start | bytes 2555912 | tf_op jit(solution)/shard_map/ppermute | solution.py:338
  411.9 34.3 %collective-permute-start.20 = (bf16[256,1536]{1,0:T(8,128)(2,1)S(1)}, bf16[256,1536]{1,0:T(8,128)(2,1)S(1)}, u32[]{:S(2)}, u32[]{:S(2)}) collective-permute-start(bf16[256,1536]{1,0:T(8,128)(2,1)S(1)} %get-tuple-element.167), channel_id=1, source_target_pairs={{0,4},{1,5},{4,8},{5,9},{8,12},{9,13},{12,14},{13,15},{14,10},{15,... | collective-permute-start | bytes 2359304 | tf_op jit(solution)/shard_map/ppermute | solution.py:337
  413.7 33.1 %collective-permute-start.24 = (bf16[256,1536]{1,0:T(8,128)(2,1)S(1)}, bf16[256,1536]{1,0:T(8,128)(2,1)S(1)}, u32[]{:S(2)}, u32[]{:S(2)}) collective-permute-start(bf16[256,1536]{1,0:T(8,128)(2,1)S(1)} %get-tuple-element.168), channel_id=1, source_target_pairs={{4,0},{5,1},{8,4},{9,5},{12,8},{13,9},{14,12},{15,13},{10,14},{11,... | collective-permute-start | bytes 2359304 | tf_op jit(solution)/shard_map/ppermute | solution.py:338
  430.1 34.3 %collective-permute-start.29 = (bf16[256,1664]{1,0:T(8,128)(2,1)S(1)}, bf16[256,1664]{1,0:T(8,128)(2,1)S(1)}, u32[]{:S(2)}, u32[]{:S(2)}) collective-permute-start(bf16[256,1664]{1,0:T(8,128)(2,1)S(1)} %get-tuple-element.158), channel_id=1, source_target_pairs={{0,4},{1,5},{4,8},{5,9},{8,12},{9,13},{12,14},{13,15},{14,10},{15,... | collective-permute-start | bytes 2555912 | tf_op jit(solution)/shard_map/ppermute | solution.py:337
  432.0 33.1 %collective-permute-start.33 = (bf16[256,1664]{1,0:T(8,128)(2,1)S(1)}, bf16[256,1664]{1,0:T(8,128)(2,1)S(1)}, u32[]{:S(2)}, u32[]{:S(2)}) collective-permute-start(bf16[256,1664]{1,0:T(8,128)(2,1)S(1)} %get-tuple-element.159), channel_id=1, source_target_pairs={{4,0},{5,1},{8,4},{9,5},{12,8},{13,9},{14,12},{15,13},{10,14},{11,... | collective-permute-start | bytes 2555912 | tf_op jit(solution)/shard_map/ppermute | solution.py:338
  447.0 34.3 %collective-permute-start.21 = (bf16[256,1536]{1,0:T(8,128)(2,1)S(1)}, bf16[256,1536]{1,0:T(8,128)(2,1)S(1)}, u32[]{:S(2)}, u32[]{:S(2)}) collective-permute-start(bf16[256,1536]{1,0:T(8,128)(2,1)S(1)} %get-tuple-element.165), channel_id=1, source_target_pairs={{0,4},{1,5},{4,8},{5,9},{8,12},{9,13},{12,14},{13,15},{14,10},{15,... | collective-permute-start | bytes 2359304 | tf_op jit(solution)/shard_map/ppermute | solution.py:337
  448.8 33.1 %collective-permute-start.25 = (bf16[256,1536]{1,0:T(8,128)(2,1)S(1)}, bf16[256,1536]{1,0:T(8,128)(2,1)S(1)}, u32[]{:S(2)}, u32[]{:S(2)}) collective-permute-start(bf16[256,1536]{1,0:T(8,128)(2,1)S(1)} %get-tuple-element.166), channel_id=1, source_target_pairs={{4,0},{5,1},{8,4},{9,5},{12,8},{13,9},{14,12},{15,13},{10,14},{11,... | collective-permute-start | bytes 2359304 | tf_op jit(solution)/shard_map/ppermute | solution.py:338
  465.3 34.3 %collective-permute-start.30 = (bf16[256,1664]{1,0:T(8,128)(2,1)S(1)}, bf16[256,1664]{1,0:T(8,128)(2,1)S(1)}, u32[]{:S(2)}, u32[]{:S(2)}) collective-permute-start(bf16[256,1664]{1,0:T(8,128)(2,1)S(1)} %get-tuple-element.156), channel_id=1, source_target_pairs={{0,4},{1,5},{4,8},{5,9},{8,12},{9,13},{12,14},{13,15},{14,10},{15,... | collective-permute-start | bytes 2555912 | tf_op jit(solution)/shard_map/ppermute | solution.py:337
  467.1 33.1 %collective-permute-start.34 = (bf16[256,1664]{1,0:T(8,128)(2,1)S(1)}, bf16[256,1664]{1,0:T(8,128)(2,1)S(1)}, u32[]{:S(2)}, u32[]{:S(2)}) collective-permute-start(bf16[256,1664]{1,0:T(8,128)(2,1)S(1)} %get-tuple-element.157), channel_id=1, source_target_pairs={{4,0},{5,1},{8,4},{9,5},{12,8},{13,9},{14,12},{15,13},{10,14},{11,... | collective-permute-start | bytes 2555912 | tf_op jit(solution)/shard_map/ppermute | solution.py:338
  483.2 29.3 %collective-permute-start.22 = (bf16[256,1536]{1,0:T(8,128)(2,1)}, bf16[256,1536]{1,0:T(8,128)(2,1)}, u32[]{:S(2)}, u32[]{:S(2)}) collective-permute-start(bf16[256,1536]{1,0:T(8,128)(2,1)} %get-tuple-element.163), channel_id=1, source_target_pairs={{0,4},{1,5},{4,8},{5,9},{8,12},{9,13},{12,14},{13,15},{14,10},{15,... | collective-permute-start | bytes 2359304 | tf_op jit(solution)/shard_map/ppermute | solution.py:337
  485.0 27.9 %collective-permute-start.26 = (bf16[256,1536]{1,0:T(8,128)(2,1)}, bf16[256,1536]{1,0:T(8,128)(2,1)}, u32[]{:S(2)}, u32[]{:S(2)}) collective-permute-start(bf16[256,1536]{1,0:T(8,128)(2,1)} %get-tuple-element.164), channel_id=1, source_target_pairs={{4,0},{5,1},{8,4},{9,5},{12,8},{13,9},{14,12},{15,13},{10,14},{11,... | collective-permute-start | bytes 2359304 | tf_op jit(solution)/shard_map/ppermute | solution.py:338
  529.3 23.0 %all-to-all-start.2 = ((bf16[16,128,192]{1,2,0:T(8,128)(2,1)}), bf16[16,128,192]{1,2,0:T(8,128)(2,1)S(1)}, u32[]{:S(2)}, u32[]{:S(2)}) async-start(bf16[16,128,192]{1,2,0:T(8,128)(2,1)} %bitcast.17), calls=%async_computation.2 | async-start | bytes 1572864 | tf_op jit(solution)/shard_map/all_to_all | solution.py:312
  533.6 261.2 %reduce-scatter.3.cloned.1.call-start = ((), (), s32[]{:S(2)}) async-start(), calls=%async_computation.8 | async-start | bytes 8515584 | tf_op jit(solution)/shard_map/reduce_scatter | solution.py:306
  649.1 9.7 %collective-permute-start.39 = (bf16[512,1536]{1,0:T(8,128)(2,1)S(1)}, bf16[512,1536]{1,0:T(8,128)(2,1)S(1)}, u32[]{:S(2)}, u32[]{:S(2)}) collective-permute-start(bf16[512,1536]{1,0:T(8,128)(2,1)S(1)} %convolution_convert_fusion), channel_id=1, source_target_pairs={{0,1},{1,0},{2,3},{3,2},{4,5},{5,4},{6,7},{7,6},{8,9},{9,8},{10,11... | collective-permute-start | bytes 4718600 | tf_op jit(solution)/shard_map/ppermute | solution.py:324
  654.7 9.2 %collective-permute-start.37 = (bf16[1536,512]{1,0:T(8,128)(2,1)S(1)}, bf16[1536,512]{1,0:T(8,128)(2,1)S(1)}, u32[]{:S(2)}, u32[]{:S(2)}) collective-permute-start(bf16[1536,512]{1,0:T(8,128)(2,1)S(1)} %convolution_convert_fusion.1), channel_id=1, source_target_pairs={{0,1},{1,0},{2,3},{3,2},{4,5},{5,4},{6,7},{7,6},{8,9},{9,8},{10,11... | collective-permute-start | bytes 4718600 | tf_op jit(solution)/shard_map/ppermute | solution.py:324
  658.3 9.9 %collective-permute-start.35 = (bf16[1536,512]{1,0:T(8,128)(2,1)S(1)}, bf16[1536,512]{1,0:T(8,128)(2,1)S(1)}, u32[]{:S(2)}, u32[]{:S(2)}) collective-permute-start(bf16[1536,512]{1,0:T(8,128)(2,1)S(1)} %convolution_convert_fusion.2), channel_id=1, source_target_pairs={{0,1},{1,0},{2,3},{3,2},{4,5},{5,4},{6,7},{7,6},{8,9},{9,8},{10,11... | collective-permute-start | bytes 4718600 | tf_op jit(solution)/shard_map/ppermute | solution.py:324
  662.3 40.5 %collective-permute-start.40 = (bf16[512,1536]{1,0:T(8,128)(2,1)S(1)}, bf16[512,1536]{1,0:T(8,128)(2,1)S(1)}, u32[]{:S(2)}, u32[]{:S(2)}) collective-permute-start(bf16[512,1536]{1,0:T(8,128)(2,1)S(1)} %fusion.6), channel_id=1, source_target_pairs={{0,16},{16,0},{1,17},{17,1},{2,18},{18,2},{3,19},{19,3},{4,20},{20... | collective-permute-start | bytes 4718600 | tf_op jit(solution)/shard_map/ppermute | solution.py:317
  667.6 80.5 %collective-permute-start.38 = (bf16[1536,512]{1,0:T(8,128)(2,1)S(1)}, bf16[1536,512]{1,0:T(8,128)(2,1)S(1)}, u32[]{:S(2)}, u32[]{:S(2)}) collective-permute-start(bf16[1536,512]{1,0:T(8,128)(2,1)S(1)} %fusion.5), channel_id=1, source_target_pairs={{0,16},{16,0},{1,17},{17,1},{2,18},{18,2},{3,19},{19,3},{4,20},{20... | collective-permute-start | bytes 4718600 | tf_op jit(solution)/shard_map/ppermute | solution.py:317
  671.7 114.8 %collective-permute-start.36 = (bf16[1536,512]{1,0:T(8,128)(2,1)S(1)}, bf16[1536,512]{1,0:T(8,128)(2,1)S(1)}, u32[]{:S(2)}, u32[]{:S(2)}) collective-permute-start(bf16[1536,512]{1,0:T(8,128)(2,1)S(1)} %fusion.4), channel_id=1, source_target_pairs={{0,16},{16,0},{1,17},{17,1},{2,18},{18,2},{3,19},{19,3},{4,20},{20... | collective-permute-start | bytes 4718600 | tf_op jit(solution)/shard_map/ppermute | solution.py:317
  (43 other events, 677.3 us)
Sparse Core Ops, SparseCore 0:
  11.7 79.2 all-gather.2
  94.6 83.6 all-gather.4
  522.7 115.4 reduce-scatter.4
  644.0 143.4 reduce-scatter.2

commit v2 on v1

--- a/solution.py
+++ b/solution.py
@@ -175,10 +175,11 @@
 ):
     blocks = refs[:parts]
     grads = refs[parts : 2 * parts]
-    router_ref, gate_ref, up_ref, down_ref = refs[2 * parts : 2 * parts + 4]
-    refs = refs[2 * parts + 4 + (5 if chained else 0) :]
-    mixed_ref, back_ref, rows_ref, grads_ref, d_gate_ref, d_up_ref, hidden_ref = refs[:7]
-    gates_sc, d_gates_sc, mixed_sc, back_sc = refs[7:]
+    router_ref, lin_ref, down_ref = refs[2 * parts : 2 * parts + 3]
+    refs = refs[2 * parts + 3 + (4 if chained else 0) :]
+    mixed_ref, back_ref, rows_ref, grads_ref, d_lin_ref, hidden_ref = refs[:6]
+    gates_sc, d_gates_sc, mixed_sc, back_sc = refs[6:]
+    units = down_ref.shape[1]
     step = pl.program_id(0)
     lane = lax.broadcasted_iota(jnp.int32, (rows, LANES), 1)
 
@@ -195,12 +196,12 @@
             gates_sc[here, :] = weight / jnp.sum(weight, axis=1, keepdims=True)
         d_gates_sc[...] = jnp.zeros_like(d_gates_sc)
 
-    expert = index_ref[step * 2 // steps]
+    expert = index_ref[step]
     own = lane == expert
     gate = jnp.sum(jnp.where(own, gates_sc[...], 0.0), axis=1, keepdims=True)
     block = rows_ref[...]
-    gate_lin = jnp.dot(block, gate_ref[0], preferred_element_type=jnp.float32)
-    up_lin = jnp.dot(block, up_ref[0], preferred_element_type=jnp.float32)
+    lin = jnp.dot(block, lin_ref[0], preferred_element_type=jnp.float32)
+    gate_lin, up_lin = lin[:, :units], lin[:, units:]
     d_hidden = matmul_nt(grads_ref[...], down_ref[0])
     sigma = 1.0 / (1.0 + jnp.exp(-gate_lin))
     active = gate_lin * sigma
@@ -211,10 +212,10 @@
     d_gate = (d_hidden * up_lin * sigma * (1.0 + gate_lin * (1.0 - sigma))).astype(jnp.bfloat16)
     d_up = (d_hidden * active).astype(jnp.bfloat16)
     hidden_ref[...] = hidden
-    d_gate_ref[...] = d_gate
-    d_up_ref[...] = d_up
+    d_lin = jnp.concatenate([d_gate, d_up], axis=1)
+    d_lin_ref[...] = d_lin
     mixed = jnp.dot(hidden, down_ref[0], preferred_element_type=jnp.float32)
-    back = matmul_nt(d_gate, gate_ref[0]) + matmul_nt(d_up, up_ref[0])
+    back = matmul_nt(d_lin, lin_ref[0])
 
     @pl.when(step == 0)
     def _():
@@ -236,16 +237,14 @@
         back_ref[:, width:] = jnp.where(lane < experts, high, low).astype(jnp.bfloat16)
 
 
-def expert_rows(index, experts, blocks, grads, router, gate, up, down, slot, total, buffers):
+def expert_rows(index, experts, blocks, grads, router, lin, down, slot, total, buffers):
     parts = len(blocks)
     part, width = blocks[0].shape
     rows = parts * part
-    units = gate.shape[2]
-    tile = 256
-    tiles = units // tile
-    steps = 2 * tiles
+    units = down.shape[1]
+    steps = 2
     whole = lambda *shape: pl.BlockSpec(shape, lambda i, ids: (0,) * len(shape))
-    activation = pl.BlockSpec((rows, tile), lambda i, ids: (slot, i))
+    columns = lambda count: pl.BlockSpec((rows, count), lambda i, ids: (slot, i))
     kept = pl.BlockSpec((rows, width), lambda i, ids: (slot, 0))
     chained = buffers is not None
     shapes = [
@@ -253,9 +252,11 @@
         jax.ShapeDtypeStruct((rows, width + LANES), jnp.bfloat16),
         jax.ShapeDtypeStruct((total, width), jnp.bfloat16),
         jax.ShapeDtypeStruct((total, width), jnp.bfloat16),
-    ] + [jax.ShapeDtypeStruct((total, 2 * units), jnp.bfloat16)] * 3
-    inputs = [index, *blocks, *grads, router, gate, up, down] + (list(buffers) if chained else [])
-    first = 1 + 2 * parts + 4
+        jax.ShapeDtypeStruct((total, 4 * units), jnp.bfloat16),
+        jax.ShapeDtypeStruct((total, 2 * units), jnp.bfloat16),
+    ]
+    inputs = [index, *blocks, *grads, router, lin, down] + (list(buffers) if chained else [])
+    first = 1 + 2 * parts + 3
     return pl.pallas_call(
         functools.partial(expert_kernel, parts, rows, width, experts, steps, chained),
         grid_spec=pltpu.PrefetchScalarGridSpec(
@@ -265,19 +266,17 @@
             + [whole(part, width + LANES)] * parts
             + [
                 whole(width, LANES),
-                pl.BlockSpec((1, width, tile), lambda i, ids: (i // tiles, 0, i % tiles)),
-                pl.BlockSpec((1, width, tile), lambda i, ids: (i // tiles, 0, i % tiles)),
-                pl.BlockSpec((1, tile, width), lambda i, ids: (i // tiles, i % tiles, 0)),
+                pl.BlockSpec((1, width, 2 * units), lambda i, ids: (i, 0, 0)),
+                pl.BlockSpec((1, units, width), lambda i, ids: (i, 0, 0)),
             ]
-            + ([pl.BlockSpec(memory_space=pl.ANY)] * 5 if chained else []),
+            + ([pl.BlockSpec(memory_space=pl.ANY)] * 4 if chained else []),
             out_specs=[
                 whole(rows, width),
                 whole(rows, width + LANES),
                 kept,
                 kept,
-                activation,
-                activation,
-                activation,
+                columns(2 * units),
+                columns(units),
             ],
             scratch_shapes=[
                 pltpu.VMEM((rows, LANES), jnp.float32),
@@ -287,7 +286,7 @@
             ],
         ),
         out_shape=shapes,
-        input_output_aliases={first + k: 2 + k for k in range(5)} if chained else {},
+        input_output_aliases={first + k: 2 + k for k in range(4)} if chained else {},
         compiler_params=pltpu.CompilerParams(dimension_semantics=("arbitrary",)),
         cost_estimate=pl.CostEstimate(
             flops=rows * width * units * 24,
@@ -302,12 +301,6 @@
     return lax.all_gather(values, ("head", "blk"), axis=0, tiled=True)
 
 
-def scatter_dense(values):
-    return lax.psum_scatter(
-        values.astype(jnp.bfloat16), ("head", "blk"), scatter_dimension=0, tiled=True
-    ).astype(jnp.float32)
-
-
 def exchange(values):
     return lax.all_to_all(values, "blk", split_axis=0, concat_axis=0, tiled=True)
 
@@ -324,10 +317,17 @@
     return lax.ppermute(values, "blk", [(k, k ^ 1) for k in range(count)])
 
 
+def after(values, *earlier):
+    return lax.optimization_barrier((values, earlier))[0]
+
+
+def ring_order():
+    half = lax.axis_size("blk") // 4
+    return [2 * k for k in range(half)] + [2 * k + 1 for k in reversed(range(half))]
+
+
 def ring_steps():
-    count = lax.axis_size("blk")
-    half = count // 4
-    order = [2 * k for k in range(half)] + [2 * k + 1 for k in reversed(range(half))]
+    order = ring_order()
     onward, back = [], []
     for place, chip in enumerate(order):
         following = order[(place + 1) % len(order)]
@@ -350,17 +350,80 @@
     return pairs, (send_on(behind[:half]), send_back(ahead[half:]))
 
 
-def ring_scatter(own, pairs, opposite):
-    length, send_on, send_back = ring_steps()
-    half = own.shape[0] // 2
-    onward, back = send_on(opposite[:half]), send_back(opposite[half:])
-    onward = jnp.pad(onward, ((0, half), (0, 0)))
-    back = jnp.pad(back, ((half, 0), (0, 0)))
-    for behind, ahead in reversed(pairs):
-        onward = send_on(onward + ahead)
-        back = send_back(back + behind)
-    wide = own.astype(jnp.float32)
-    return wide + onward.astype(jnp.float32) + back.astype(jnp.float32)
+class RingSum:
+    def __init__(self, own, pairs, opposite, axis=0):
+        _, self.send_on, self.send_back = ring_steps()
+        self.own, self.pairs, self.axis = own, list(reversed(pairs)), axis
+        self.half = own.shape[axis] // 2
+        self.onward = lax.slice_in_dim(opposite, 0, self.half, axis=axis)
+        self.back = lax.slice_in_dim(opposite, self.half, 2 * self.half, axis=axis)
+        self.hop = 0
+
+    def send(self, *hold):
+        if self.hop > 0:
+            behind, ahead = self.pairs[self.hop - 1]
+            self.onward, self.back = self.onward + ahead, self.back + behind
+        if hold:
+            self.onward, self.back = after((self.onward, self.back), hold)
+        self.onward, self.back = self.send_on(self.onward), self.send_back(self.back)
+        return self
+
+    def land(self, *filler):
+        if filler:
+            self.onward, self.back = after((self.onward, self.back), filler)
+        if self.hop == 0:
+            spread = [(0, 0), (0, 0)]
+            spread[self.axis] = (0, self.half)
+            self.onward = jnp.pad(self.onward, spread)
+            spread[self.axis] = (self.half, 0)
+            self.back = jnp.pad(self.back, spread)
+        self.hop += 1
+        return self
+
+    def total(self):
+        while self.hop <= len(self.pairs):
+            self.send().land()
+        wide = self.own.astype(jnp.float32)
+        return wide + self.onward.astype(jnp.float32) + self.back.astype(jnp.float32)
+
+
+def scatter_dense(values):
+    return lax.psum_scatter(
+        values, ("head", "blk"), scatter_dimension=0, tiled=True
+    ).astype(jnp.float32)
+
+
+def dense_scatter(values):
+    heads = lax.axis_size("head")
+    chips = lax.axis_size("blk") // 2
+    rows = values.shape[0] // (2 * heads * chips)
+    columns = values.shape[1]
+    grid = values.reshape(heads, chips, 2, rows, columns)
+    index = lax.axis_index("blk")
+    head = lax.axis_index("head")
+    chip, turns = index // 2, chips // 2
+    place = jnp.where(chip % 2 == 0, chip // 2, chips - 1 - chip // 2)
+    parts = grid[:, :, 0], grid[:, :, 1]
+    even = index % 2 == 0
+    away = jnp.where(even, parts[1], parts[0])
+    mine = jnp.where(even, parts[0], parts[1]) + partner(away)
+
+    def block(offset):
+        target = (place + offset) % chips
+        chip = jnp.where(target < turns, 2 * target, 2 * (chips - 1 - target) + 1)
+        piece = lax.dynamic_slice(mine, (0, chip, 0, 0), (heads, 1, rows, columns))
+        return piece.reshape(heads * rows, columns)
+
+    pairs = [(block(-k), block(k)) for k in range(1, chips // 2)]
+    total = RingSum(block(0), pairs, block(chips // 2)).total().astype(jnp.bfloat16)
+    share = lambda turn: lax.dynamic_slice(
+        total, ((head + turn) % heads * rows, 0), (rows, columns)
+    )
+    result = share(0).astype(jnp.float32)
+    for turn in range(1, heads):
+        moved = [(k, (k + turn) % heads) for k in range(heads)]
+        result = result + lax.ppermute(share(turn), "head", moved).astype(jnp.float32)
+    return result
 
 
 def with_lanes(values, extra):
@@ -429,8 +492,9 @@
     d_out = grad_out.reshape(token_rows, width)
     grads_own = with_lanes(d_out.astype(jnp.bfloat16), chosen)
     grads_pairs, grads_opposite = ring_gather(grads_own)
-    both_gate = jnp.concatenate([w_gate, partner(w_gate)], axis=0)
-    both_up = jnp.concatenate([w_up, partner(w_up)], axis=0)
+    full_mixed = after(full_mixed, grads_pairs[:2])
+    w_lin = jnp.concatenate([w_gate, w_up], axis=2)
+    both_lin = jnp.concatenate([w_lin, partner(w_lin)], axis=0)
     both_down = jnp.concatenate([w_down, partner(w_down)], axis=0)
 
     residual = tokens.astype(jnp.float32).reshape(token_rows, width)
@@ -474,7 +538,7 @@
 
     def apply_experts(blocks, grads, slot, buffers):
         return expert_rows(
-            ids, experts, blocks, grads, router, both_gate, both_up, both_down, slot, total, buffers
+            ids, experts, blocks, grads, router, both_lin, both_down, slot, total, buffers
         )
 
     ring_pairs = len(blocks_pairs)
@@ -489,20 +553,26 @@
     mixed_opposite, back_opposite, *buffers = apply_experts(
         blocks_opposite, grads_opposite, 2 * ring_pairs + 1, buffers
     )
-    rows_all, grads_all, d_gate_all, d_up_all, hidden_all = buffers
-    back_sum = ring_scatter(back_own, back_pairs, back_opposite)
-    mixed_sum = ring_scatter(mixed_own, mixed_pairs, mixed_opposite)
-    out = (middle + mixed_sum).reshape(seq_local, shard, width)
-
-    def expert_sum(left, right, swap):
-        other = matmul_tn(*((left[:, units:], right) if swap else (left, right[:, units:])))
-        mine = matmul_tn(*((left[:, :units], right) if swap else (left, right[:, :units])))
-        mine = mine + partner(other.astype(jnp.bfloat16)).astype(jnp.float32)
-        return sum_heads(mine.astype(jnp.bfloat16))
-
-    grad_gate_sum = expert_sum(rows_all, d_gate_all, False)
-    grad_up_sum = expert_sum(rows_all, d_up_all, False)
-    grad_down_sum = expert_sum(hidden_all, grads_all, True)
+    rows_all, grads_all, d_lin_all, hidden_all = buffers
+    others = [
+        matmul_tn(rows_all, d_lin_all[:, 2 * units :]).astype(jnp.bfloat16),
+        matmul_tn(hidden_all[:, units:], grads_all).astype(jnp.bfloat16),
+    ]
+    mine = [
+        matmul_tn(rows_all, d_lin_all[:, : 2 * units]),
+        matmul_tn(hidden_all[:, :units], grads_all),
+    ]
+    mine = [
+        (part + partner(other).astype(jnp.float32)).astype(jnp.bfloat16)
+        for part, other in zip(mine, others)
+    ]
+    back_ring = RingSum(back_own, back_pairs, back_opposite)
+    back_ring.send().land(others).send().land(mine)
+    back_sum = back_ring.total()
+    grad_lin_sum, grad_down_sum = [sum_heads(part) for part in mine]
+    grad_gate_sum, grad_up_sum = grad_lin_sum[:, :units], grad_lin_sum[:, units:]
+    mixed_ring = RingSum(mixed_own, mixed_pairs, mixed_opposite)
+    mixed_ring.send(back_sum)
 
     d_gates = back_sum[:, width : width + experts] + back_sum[:, width + experts : width + 2 * experts]
     d_logits = gates * (d_gates - jnp.sum(gates * d_gates, axis=-1, keepdims=True))
@@ -514,27 +584,35 @@
     d_mid = d_out + d_mid_norm
     d_branch = jnp.pad(d_mid.astype(jnp.bfloat16), ((0, 0), (0, LANES)))
     d_attended = matmul_nt(d_branch, full_out).astype(jnp.bfloat16)
+    early = add_lanes(
+        matmul_tn(attended, d_branch),
+        jnp.concatenate([grad_router, grad_gain_second[:, None]], axis=1),
+    ).astype(jnp.bfloat16)
+    d_attended = after(d_attended, early)
+    mixed_ring.land(d_attended)
     pair_grad = to_pairs(d_attended, lanes)
+    mixed_ring.send(pair_grad)
     pair_cosine, pair_sine = rope_tables(jnp.arange(seq_total, dtype=jnp.int32), HDIM // 2)
     pair_d = attend_backward(
         pair_qkv, pair_grad, flat, log_total, pair_cosine.T, pair_sine.T, group
     )
-    early = scatter_dense(
-        add_lanes(
-            matmul_tn(attended, d_branch),
-            jnp.concatenate([grad_router, grad_gain_second[:, None]], axis=1),
-        )
-    )
-    d_linear = jnp.pad(to_tokens(pair_d, span), ((0, 0), (0, LANES)))
-    d_normed = matmul_nt(d_linear, full_mixed)
+    early = scatter_dense(early)
+    mixed_ring.land(pair_d).send(pair_d)
+    d_linear = to_tokens(pair_d, span)
+    mixed_ring.land(d_linear)
+    out = (middle + mixed_ring.total()).reshape(seq_local, shard, width)
+    grad_mixed = matmul_tn(normed, d_linear).astype(jnp.bfloat16)
+    late_mixed = dense_scatter(grad_mixed).reshape(part_rows, groups, span)
+    d_normed = matmul_nt(jnp.pad(d_linear, ((0, 0), (0, LANES))), full_mixed)
     d_tok_norm, grad_gain_first = norm_back(residual, inverse_one, gain_first, d_normed)
     grad_tokens = (d_mid + d_tok_norm).reshape(seq_local, shard, width)
-    late = scatter_dense(add_lanes(matmul_tn(normed, d_linear), grad_gain_first[:, None]))
-    late_mixed = late[:, : groups * span].reshape(part_rows, groups, span)
+    late_gain = dense_scatter(
+        jnp.pad(grad_gain_first[:, None].astype(jnp.bfloat16), ((0, 0), (0, LANES - 1)))
+    )
     return (
         out,
         grad_tokens,
-        late[:, groups * span],
+        late_gain[:, 0],
         late_mixed[:, :, :lanes].reshape(part_rows, -1),
         late_mixed[:, :, lanes : lanes + HDIM].reshape(part_rows, -1),
         late_mixed[:, :, lanes + HDIM :].reshape(part_rows, -1),

time: 811 us -> 723 us (0.89)
  waiting for transfers between devices: 372 us -> 298 us
  blocking collectives: 43.5 us -> 0 us
  starting transfers between devices: 81.1 us -> 99.1 us
  other arithmetic: 31 us -> 44.1 us
    ppermute x3 -> x2, waiting for transfers between devices: 109 us -> 0.01 us  [sum_heads(): other = lax.ppermute(values, 'head', [(0, 1), (1, 0)])]
    all_gather x2, waiting for transfers between devices: 77 us -> 27.6 us  [gather_dense(): return lax.all_gather(values, ('head', 'blk'), axis=0, tiled=True)]
    ppermute x16 -> x24, waiting for transfers between devices: 164 us -> 208 us  [ring_steps(): send_on = lambda values: lax.ppermute(values, 'blk', onward)]
    all_to_all x1 -> x0, blocking collectives: 43.5 us -> none  [exchange(): lax.all_to_all(values, 'blk', split_axis=0, concat_axis=0, tiled=True)]
    all_to_all x3 -> x4, waiting for transfers between devices: 16.8 us -> 45.2 us  [exchange(): lax.all_to_all(values, 'blk', split_axis=0, concat_axis=0, tiled=True)]
    ppermute x16 -> x24, waiting for transfers between devices: 4.58 us -> 16.7 us  [ring_steps(): send_back = lambda values: lax.ppermute(values, 'blk', back)]
    all_to_all x3 -> x4, starting transfers between devices: 15.2 us -> 26.4 us  [exchange(): lax.all_to_all(values, 'blk', split_axis=0, concat_axis=0, tiled=True)]
    add x7 -> x24, other arithmetic: 2.65 us -> 12.4 us  [the longest x18 5.61 us: send(): self.onward, self.back = (self.onward + ahead, self.back + behind)]
  transfers between devices with their start and end apart: 48 -> 65, of which waited for: 24 -> 33; matrix products, arithmetic and copies ran while one was open for 16% -> 20% of each run, Pallas kernels for 16% -> 18%
where the time goes in v2:
time: 723 us; the launch traced here: 713 us
  waiting for transfers between devices  298 us (41%)
  Pallas kernels  138 us (19%)
  starting transfers between devices  99.1 us (14%)
  matrix products  62.8 us (9%)
  local copies, waits for them, and re-layouts  55.9 us (8%)
  other arithmetic  44.1 us (6%)
  between operations  15.3 us (2%)
    ppermute x24, waiting for transfers between devices, ring_steps(): send_on = lambda values: lax.ppermute(values, 'blk', onward)  208 us
    pallas_call x5, Pallas kernels, expert_rows(): pl.pallas_call(functools.partial(expert_kernel, parts, rows, width, exper...  86.3 us
    all_to_all x4, waiting for transfers between devices, exchange(): lax.all_to_all(values, 'blk', split_axis=0, concat_axis=0, tiled=True)  45.2 us
    ppermute x24, starting transfers between devices, ring_steps(): send_on = lambda values: lax.ppermute(values, 'blk', onward)  40.3 us
    dot_general x6, matrix products, matmul_tn(): lax.dot_general(left, right, (((0,), (0,)), ((), ())), preferred_element_...  34.2 us
    pallas_call x1, Pallas kernels, attend_backward(): pl.pallas_call(functools.partial(backward_kernel, group, steps), grid=(st...  29.2 us
    all_gather x2, waiting for transfers between devices, gather_dense(): return lax.all_gather(values, ('head', 'blk'), axis=0, tiled=True)  27.6 us
    all_to_all x4, starting transfers between devices, exchange(): lax.all_to_all(values, 'blk', split_axis=0, concat_axis=0, tiled=True)  26.4 us
  transfers between devices with their start and end apart: 65, of which 33 were waited for; matrix products, arithmetic and copies ran while one was open for 20% of the time, Pallas kernels for 18%

profile of v2, /device:TPU:0, one launch (start us, length us, event | category | flops | bytes accessed | tf_op | source)
XLA Modules:
  0.0 713.3 jit_solution(9800167404373442514)
XLA Ops:
  18.6 23.2 %collective-permute-done.refs_2_ = bf16[256,1664]{1,0:T(8,128)(2,1)} collective-permute-done((bf16[256,1664]{1,0:T(8,128)(2,1)}, bf16[256,1664]{1,0:T(8,128)(2,1)}, u32[]{:S(2)}, u32[]{:S(2)}) %collective-permute-start) | collective-permute-done | bytes 852000 | tf_op jit(solution)/shard_map/ppermute | solution.py:337
  46.7 26.2 %collective-permute-done.2.refs_2_ = bf16[256,1664]{1,0:T(8,128)(2,1)} collective-permute-done((bf16[256,1664]{1,0:T(8,128)(2,1)}, bf16[256,1664]{1,0:T(8,128)(2,1)}, u32[]{:S(2)}, u32[]{:S(2)}) %collective-permute-start.2) | collective-permute-done | bytes 852000 | tf_op jit(solution)/shard_map/ppermute | solution.py:337
  75.0 27.6 %all-gather.3.cloned.1.call-done = bf16[1536,2688]{1,0:T(8,128)(2,1)} async-done(((bf16[48,2688]{1,0:T(8,128)(2,1)}), bf16[1536,2688]{1,0:T(8,128)(2,1)}) %all-gather.3.cloned.1.call-update) | async-done | bytes 8257552 | tf_op jit(solution)/shard_map/all_gather | solution.py:301
  104.1 7.9 %fusion = f32[256,2560]{0,1:T(8,128)} fusion(bf16[256,1536]{1,0:T(8,128)(2,1)S(1)} %multiply_convert_fusion.2, bf16[1536,2688]{1,0:T(8,128)(2,1)} %all-gather.3.cloned.1.call-done), kind=kOutput, calls=%fused_computation.2 | convolution fusion | flops 2013265920 | bytes 11272192 | tf_op jit(solution)/shard_map/slice | solution.py:508
  112.0 3.1 reshape.318
  120.7 4.4 all-to-all-start
  126.8 32.3 %all-to-all-done = bf16[16,128,320]{1,2,0:T(8,128)(2,1)S(1)} async-done(((bf16[16,128,320]{1,2,0:T(8,128)(2,1)}), bf16[16,128,320]{1,2,0:T(8,128)(2,1)S(1)}, u32[]{:S(2)}, u32[]{:S(2)}) %all-to-all-start) | async-done | bytes 1310752 | tf_op jit(solution)/shard_map/all_to_all | solution.py:305
  160.7 22.6 %attend_forward.1 = (bf16[2048,192]{1,0:T(8,128)(2,1)}, f32[8,64,768]{2,1,0:T(8,128)}, f32[8,1,768]{2,1,0:T(1,128)}) custom-call(bf16[2048,320]{1,0:T(8,128)(2,1)} %bitcast.167), custom_call_target="tpu_custom_call" | custom-call | tf_op jit(solution)/shard_map/attend_forward/pallas_call | solution.py:91
  185.5 11.6 %all-to-all-start.1 = ((bf16[16,128,192]{1,2,0:T(8,128)(2,1)}), bf16[16,128,192]{1,2,0:T(8,128)(2,1)}, u32[]{:S(2)}, u32[]{:S(2)}) async-start(bf16[16,128,192]{1,2,0:T(8,128)(2,1)} %copy.139), calls=%async_computation.1 | async-start | bytes 1572864 | tf_op jit(solution)/shard_map/all_to_all | solution.py:305
  203.1 26.1 %collective-permute-done.14.refs_2_ = bf16[256,1664]{1,0:T(8,128)(2,1)} collective-permute-done((bf16[256,1664]{1,0:T(8,128)(2,1)}, bf16[256,1664]{1,0:T(8,128)(2,1)}, u32[]{:S(2)}, u32[]{:S(2)}) %collective-permute-start.14) | collective-permute-done | bytes 852000 | tf_op jit(solution)/shard_map/ppermute | solution.py:337
  230.9 5.9 collective-permute-start.15
  238.6 6.1 pad_maximum_fusion.refs_3_.refs_5_
  248.1 4.1 multiply_reduce_fusion.4
  252.4 3.4 collective-permute-start.10
  257.6 12.5 %expert_rows.5 = (bf16[256,1536]{1,0:T(8,128)(2,1)}, bf16[256,1664]{1,0:T(8,128)(2,1)}, bf16[2048,1536]{1,0:T(8,128)(2,1)}, bf16[2048,1536]{1,0:T(8,128)(2,1)}, ...) custom-call(s32[2]{0:T(128)} %pad_add_fusion.index_ref, bf16[256,1536]{1,0:T(8,128)(2,1)} %copy-done.7, ...), custom_call_target="tpu_custom_call" | custom-call | flops 4831838208 | bytes 17301504 | tf_op jit(solution)/shard_map/expert_rows/pallas_call | solution.py:260
  274.9 20.5 %expert_rows.6 = (bf16[512,1536]{1,0:T(8,128)(2,1)}, bf16[512,1664]{1,0:T(8,128)(2,1)}, bf16[2048,1536]{1,0:T(8,128)(2,1)}, bf16[2048,1536]{1,0:T(8,128)(2,1)}, ...) custom-call(s32[2]{0:T(128)} %pad_add_fusion.index_ref, ...), custom_call_target="tpu_custom_call", output_to_operand_aliasing={{2}: (8, {}), {3}: (9, {}), {4}: (10, {}), {5}: (11, {})} | custom-call | flops 9663676416 | bytes 25165824 | tf_op jit(solution)/shard_map/expert_rows/pallas_call | solution.py:260
  297.8 20.5 %expert_rows.7 = (bf16[512,1536]{1,0:T(8,128)(2,1)}, bf16[512,1664]{1,0:T(8,128)(2,1)}, bf16[2048,1536]{1,0:T(8,128)(2,1)}, bf16[2048,1536]{1,0:T(8,128)(2,1)}, ...) custom-call(s32[2]{0:T(128)} %pad_add_fusion.index_ref, ...), custom_call_target="tpu_custom_call", output_to_operand_aliasing={{2}: (8, {}), {3}: (9, {}), {4}: (10, {}), {5}: (11, {})} | custom-call | flops 9663676416 | bytes 25165824 | tf_op jit(solution)/shard_map/expert_rows/pallas_call | solution.py:260
  323.1 20.5 %expert_rows.8 = (bf16[512,1536]{1,0:T(8,128)(2,1)}, bf16[512,1664]{1,0:T(8,128)(2,1)}, bf16[2048,1536]{1,0:T(8,128)(2,1)}, bf16[2048,1536]{1,0:T(8,128)(2,1)}, ...) custom-call(s32[2]{0:T(128)} %pad_add_fusion.index_ref, ...), custom_call_target="tpu_custom_call", output_to_operand_aliasing={{2}: (8, {}), {3}: (9, {}), {4}: (10, {}), {5}: (11, {})} | custom-call | flops 9663676416 | bytes 25165824 | tf_op jit(solution)/shard_map/expert_rows/pallas_call | solution.py:260
  344.4 12.5 %expert_rows.9 = (bf16[256,1536]{1,0:T(8,128)(2,1)}, bf16[256,1664]{1,0:T(8,128)(2,1)}, bf16[2048,1536]{1,0:T(8,128)(2,1)}, bf16[2048,1536]{1,0:T(8,128)(2,1)}, ...) custom-call(s32[2]{0:T(128)} %pad_add_fusion.index_ref, ...), custom_call_target="tpu_custom_call", output_to_operand_aliasing={{2}: (8, {}), {3}: (9, {}), {4}: (10, {}), {5}: (11, {})} | custom-call | flops 4831838208 | bytes 17301504 | tf_op jit(solution)/shard_map/expert_rows/pallas_call | solution.py:260
  356.9 10.5 %fusion.10 = bf16[1536,1024]{1,0:T(8,128)(2,1)S(1)} fusion(bf16[2048,1536]{1,0:T(8,128)(2,1)} %get-tuple-element.85, bf16[2048,2048]{1,0:T(8,128)(2,1)} %get-tuple-element.86), kind=kOutput, calls=%fused_computation.17 | convolution fusion | flops 6444023808 | bytes 13631488 | tf_op jit(solution)/shard_map/dot_general | solution.py:50
  367.4 3.5 convolution_convert_fusion.1
  373.7 10.0 %collective-permute-done.18 = bf16[128,1664]{1,0:T(8,128)(2,1)S(1)} collective-permute-done((bf16[128,1664]{1,0:T(8,128)(2,1)S(1)}, bf16[128,1664]{1,0:T(8,128)(2,1)S(1)}, u32[]{:S(2)}, u32[]{:S(2)}) %collective-permute-start.18) | collective-permute-done | bytes 426016 | tf_op jit(solution)/shard_map/ppermute | solution.py:337
  386.6 4.6 fusion.13
  391.3 9.4 %add_convert_fusion.1 = bf16[1536,1024]{1,0:T(8,128)(2,1)} fusion(bf16[1536,1024]{1,0:T(8,128)(2,1)} %collective-permute-done.22, bf16[2048,1536]{1,0:T(8,128)(2,1)S(1)} %bitcast.164, bf16[2048,2048]{1,0:T(8,128)(2,1)S(1)} %bitcast.162), kind=kOutput, calls=%fused_computation.7 | convolution fusion | flops 6447169536 | bytes 16777216 | tf_op jit(solution)/shard_map/dot_general | solution.py:50
  400.7 3.6 collective-permute-done.20
  408.1 16.6 %collective-permute-done.24 = bf16[256,1664]{1,0:T(8,128)(2,1)S(1)} collective-permute-done((bf16[256,1664]{1,0:T(8,128)(2,1)S(1)}, bf16[256,1664]{1,0:T(8,128)(2,1)S(1)}, u32[]{:S(2)}, u32[]{:S(2)}) %collective-permute-start.24) | collective-permute-done | bytes 852000 | tf_op jit(solution)/shard_map/ppermute | solution.py:337
  431.7 11.4 %collective-permute-done.25 = bf16[256,1664]{1,0:T(8,128)(2,1)S(1)} collective-permute-done((bf16[256,1664]{1,0:T(8,128)(2,1)S(1)}, bf16[256,1664]{1,0:T(8,128)(2,1)S(1)}, u32[]{:S(2)}, u32[]{:S(2)}) %collective-permute-start.25) | collective-permute-done | bytes 852000 | tf_op jit(solution)/shard_map/ppermute | solution.py:337
  445.0 3.4 multiply_reduce_fusion.2
  448.7 3.5 fusion.47
  452.2 5.0 convolution_convert_fusion.2
  457.3 3.9 add_convert_fusion
  465.9 4.8 all-to-all-start.2
  477.0 12.9 %all-to-all-done.2 = bf16[16,128,192]{1,2,0:T(8,128)(2,1)} async-done(((bf16[16,128,192]{1,2,0:T(8,128)(2,1)}), bf16[16,128,192]{1,2,0:T(8,128)(2,1)}, u32[]{:S(2)}, u32[]{:S(2)}) %all-to-all-start.2) | async-done | bytes 786464 | tf_op jit(solution)/shard_map/all_to_all | solution.py:305
  492.1 29.2 %attend_backward.1 = bf16[2048,320]{1,0:T(8,128)(2,1)} custom-call(bf16[2048,320]{1,0:T(8,128)(2,1)} %bitcast.168, bf16[2048,192]{1,0:T(8,128)(2,1)} %bitcast.174, f32[8,64,768]{2,1,0:T(8,128)} %get-tuple-element.104.flat_ref, f32[8,1,768]{2,1,0:T(1,128)} %get-tuple-element.105.lse_ref, f32[32,2048]{1,0:T(8,128)} %get-tuple-element.221.cos_ref, ...), custom_call_target="tpu_custom_call" | custom-call | tf_op jit(solution)/shard_map/attend_backward/pallas_call | solution.py:156
  523.8 5.6 all-to-all-start.3
  529.5 4.0 add_bitcast_fusion
  537.6 4.3 convert_add_fusion
  541.9 3.4 slice_bitcast_fusion
  545.3 23.3 %collective-permute-done.30 = bf16[256,1536]{1,0:T(8,128)(2,1)} collective-permute-done((bf16[256,1536]{1,0:T(8,128)(2,1)S(1)}, bf16[256,1536]{1,0:T(8,128)(2,1)}, u32[]{:S(2)}, u32[]{:S(2)}) %collective-permute-start.30) | collective-permute-done | bytes 786464 | tf_op jit(solution)/shard_map/ppermute | solution.py:337
  579.3 8.6 %collective-permute-start.32 = (bf16[256,1536]{1,0:T(8,128)(2,1)}, bf16[256,1536]{1,0:T(8,128)(2,1)S(1)}, u32[]{:S(2)}, u32[]{:S(2)}) collective-permute-start(bf16[256,1536]{1,0:T(8,128)(2,1)} %get-tuple-element.109), channel_id=1, source_target_pairs={{0,4},{1,5},{4,8},{5,9},{8,12},{9,13},{12,14},{13,15},{14,10},{15,... | collective-permute-start | bytes 2359304 | tf_op jit(solution)/shard_map/ppermute | solution.py:337
  588.1 6.0 multiply_reduce_fusion
  594.5 19.4 %collective-permute-done.32 = bf16[256,1536]{1,0:T(8,128)(2,1)S(1)} collective-permute-done((bf16[256,1536]{1,0:T(8,128)(2,1)}, bf16[256,1536]{1,0:T(8,128)(2,1)S(1)}, u32[]{:S(2)}, u32[]{:S(2)}) %collective-permute-start.32) | collective-permute-done | bytes 786464 | tf_op jit(solution)/shard_map/ppermute | solution.py:337
  614.0 4.2 collective-permute-done.33
  639.5 20.4 %collective-permute-done.47 = bf16[48,2560]{1,0:T(8,128)(2,1)S(1)} collective-permute-done((bf16[48,2560]{1,0:T(8,128)(2,1)S(1)}, bf16[48,2560]{1,0:T(8,128)(2,1)S(1)}, u32[]{:S(2)}, u32[]{:S(2)}) %collective-permute-start.47) | collective-permute-done | bytes 245792 | tf_op jit(solution)/shard_map/ppermute | solution.py:337
  663.3 9.1 %collective-permute-done.48 = bf16[96,2560]{1,0:T(8,128)(2,1)S(1)} collective-permute-done((bf16[96,2560]{1,0:T(8,128)(2,1)S(1)}, bf16[96,2560]{1,0:T(8,128)(2,1)S(1)}, u32[]{:S(2)}, u32[]{:S(2)}) %collective-permute-start.48) | collective-permute-done | bytes 491552 | tf_op jit(solution)/shard_map/ppermute | solution.py:337
  674.7 9.0 %collective-permute-done.49 = bf16[96,2560]{1,0:T(8,128)(2,1)S(1)} collective-permute-done((bf16[96,2560]{1,0:T(8,128)(2,1)S(1)}, bf16[96,2560]{1,0:T(8,128)(2,1)S(1)}, u32[]{:S(2)}, u32[]{:S(2)}) %collective-permute-start.49) | collective-permute-done | bytes 491552 | tf_op jit(solution)/shard_map/ppermute | solution.py:337
  688.3 5.2 collective-permute-done.50
  694.5 3.2 collective-permute-start.55
  (310 shorter events, 149.3 us)
Async XLA Ops:
  7.2 95.4 %all-gather.3.cloned.1.call-start = ((), (), s32[]{:S(2)}) async-start(), calls=%async_computation.5 | async-start | bytes 8515584 | tf_op jit(solution)/shard_map/all_gather | solution.py:301
  11.7 233.0 %all-gather.5.cloned.1.call-start = ((), (), s32[]{:S(2)}) async-start(), calls=%async_computation.6 | async-start | bytes 5271552 | tf_op jit(solution)/shard_map/all_gather | solution.py:301
  14.7 27.1 %collective-permute-start = (bf16[256,1664]{1,0:T(8,128)(2,1)}, bf16[256,1664]{1,0:T(8,128)(2,1)}, u32[]{:S(2)}, u32[]{:S(2)}) collective-permute-start(bf16[256,1664]{1,0:T(8,128)(2,1)} %concatenate.30.refs_1_), channel_id=1, source_target_pairs={{0,4},{1,5},{4,8},{5,9},{8,12},{9,13},{12,14},{13,15},{14,10},{15,... | collective-permute-start | bytes 2555912 | tf_op jit(solution)/shard_map/ppermute | solution.py:337
  17.8 26.5 %collective-permute-start.1 = (bf16[256,1664]{1,0:T(8,128)(2,1)}, bf16[256,1664]{1,0:T(8,128)(2,1)}, u32[]{:S(2)}, u32[]{:S(2)}) collective-permute-start(bf16[256,1664]{1,0:T(8,128)(2,1)} %concatenate.30.refs_1_), channel_id=1, source_target_pairs={{4,0},{5,1},{8,4},{9,5},{12,8},{13,9},{14,12},{15,13},{10,14},{11,... | collective-permute-start | bytes 2555912 | tf_op jit(solution)/shard_map/ppermute | solution.py:338
  41.8 31.1 %collective-permute-start.2 = (bf16[256,1664]{1,0:T(8,128)(2,1)}, bf16[256,1664]{1,0:T(8,128)(2,1)}, u32[]{:S(2)}, u32[]{:S(2)}) collective-permute-start(bf16[256,1664]{1,0:T(8,128)(2,1)} %collective-permute-done.refs_2_), channel_id=1, source_target_pairs={{0,4},{1,5},{4,8},{5,9},{8,12},{9,13},{12,14},{13,15},{14,10},{15,... | collective-permute-start | bytes 2555912 | tf_op jit(solution)/shard_map/ppermute | solution.py:337
  44.3 30.7 %collective-permute-start.3 = (bf16[256,1664]{1,0:T(8,128)(2,1)}, bf16[256,1664]{1,0:T(8,128)(2,1)}, u32[]{:S(2)}, u32[]{:S(2)}) collective-permute-start(bf16[256,1664]{1,0:T(8,128)(2,1)} %collective-permute-done.1.refs_3_), channel_id=1, source_target_pairs={{4,0},{5,1},{8,4},{9,5},{12,8},{13,9},{14,12},{15,13},{10,14},{11,... | collective-permute-start | bytes 2555912 | tf_op jit(solution)/shard_map/ppermute | solution.py:338
  120.7 38.4 %all-to-all-start = ((bf16[16,128,320]{1,2,0:T(8,128)(2,1)}), bf16[16,128,320]{1,2,0:T(8,128)(2,1)S(1)}, u32[]{:S(2)}, u32[]{:S(2)}) async-start(bf16[16,128,320]{1,2,0:T(8,128)(2,1)} %bitcast.7), calls=%async_computation | async-start | bytes 2621440 | tf_op jit(solution)/shard_map/all_to_all | solution.py:305
  126.3 112.4 %collective-permute-start.4 = (bf16[1,1536,1024]{2,1,0:T(8,128)(2,1)}, bf16[1,1536,1024]{2,1,0:T(8,128)(2,1)}, u32[]{:S(2)}, u32[]{:S(2)}) collective-permute-start(bf16[1,1536,1024]{2,1,0:T(8,128)(2,1)} %constant_dynamic-update-slice_fusion), channel_id=1, source_target_pairs={{0,1},{1,0},{2,3},{3,2},{4,5},{5,4},{6,7},{7,6},{8,9},{9,8},{10,11... | collective-permute-start | bytes 9437192 | tf_op jit(solution)/shard_map/ppermute | solution.py:317
  126.7 74.8 %collective-permute-start.5 = (bf16[1,512,1536]{2,1,0:T(8,128)(2,1)}, bf16[1,512,1536]{2,1,0:T(8,128)(2,1)}, u32[]{:S(2)}, u32[]{:S(2)}) collective-permute-start(bf16[1,512,1536]{2,1,0:T(8,128)(2,1)} %param.23), channel_id=1, source_target_pairs={{0,1},{1,0},{2,3},{3,2},{4,5},{5,4},{6,7},{7,6},{8,9},{9,8},{10,11... | collective-permute-start | bytes 4718600 | tf_op jit(solution)/shard_map/ppermute | solution.py:317
  185.5 60.6 %all-to-all-start.1 = ((bf16[16,128,192]{1,2,0:T(8,128)(2,1)}), bf16[16,128,192]{1,2,0:T(8,128)(2,1)}, u32[]{:S(2)}, u32[]{:S(2)}) async-start(bf16[16,128,192]{1,2,0:T(8,128)(2,1)} %copy.139), calls=%async_computation.1 | async-start | bytes 1572864 | tf_op jit(solution)/shard_map/all_to_all | solution.py:305
  197.1 32.1 %collective-permute-start.14 = (bf16[256,1664]{1,0:T(8,128)(2,1)}, bf16[256,1664]{1,0:T(8,128)(2,1)}, u32[]{:S(2)}, u32[]{:S(2)}) collective-permute-start(bf16[256,1664]{1,0:T(8,128)(2,1)} %collective-permute-done.2.refs_2_), channel_id=1, source_target_pairs={{0,4},{1,5},{4,8},{5,9},{8,12},{9,13},{12,14},{13,15},{14,10},{15,... | collective-permute-start | bytes 2555912 | tf_op jit(solution)/shard_map/ppermute | solution.py:337
  199.0 37.8 %collective-permute-start.16 = (bf16[256,1664]{1,0:T(8,128)(2,1)}, bf16[256,1664]{1,0:T(8,128)(2,1)}, u32[]{:S(2)}, u32[]{:S(2)}) collective-permute-start(bf16[256,1664]{1,0:T(8,128)(2,1)} %collective-permute-done.3.refs_3_), channel_id=1, source_target_pairs={{4,0},{5,1},{8,4},{9,5},{12,8},{13,9},{14,12},{15,13},{10,14},{11,... | collective-permute-start | bytes 2555912 | tf_op jit(solution)/shard_map/ppermute | solution.py:338
  230.9 112.7 %collective-permute-start.15 = (bf16[128,1664]{1,0:T(8,128)(2,1)}, bf16[128,1664]{1,0:T(8,128)(2,1)}, u32[]{:S(2)}, u32[]{:S(2)}) collective-permute-start(bf16[128,1664]{1,0:T(8,128)(2,1)} %slice.235), channel_id=1, source_target_pairs={{0,4},{1,5},{4,8},{5,9},{8,12},{9,13},{12,14},{13,15},{14,10},{15,... | collective-permute-start | bytes 1277960 | tf_op jit(solution)/shard_map/ppermute | solution.py:337
  238.6 105.0 %collective-permute-start.17 = (bf16[128,1664]{1,0:T(8,128)(2,1)}, bf16[128,1664]{1,0:T(8,128)(2,1)}, u32[]{:S(2)}, u32[]{:S(2)}) collective-permute-start(bf16[128,1664]{1,0:T(8,128)(2,1)} %slice.236), channel_id=1, source_target_pairs={{4,0},{5,1},{8,4},{9,5},{12,8},{13,9},{14,12},{15,13},{10,14},{11,... | collective-permute-start | bytes 1277960 | tf_op jit(solution)/shard_map/ppermute | solution.py:338
  252.4 19.6 %collective-permute-start.10 = (bf16[256,1536]{1,0:T(8,128)(2,1)S(1)}, bf16[256,1536]{1,0:T(8,128)(2,1)}, u32[]{:S(2)}, u32[]{:S(2)}) collective-permute-start(bf16[256,1536]{1,0:T(8,128)(2,1)S(1)} %multiply_convert_fusion.1.refs_0_), channel_id=1, source_target_pairs={{4,0},{5,1},{8,4},{9,5},{12,8},{13,9},{14,12},{15,13},{10,14},{11,... | collective-permute-start | bytes 2359304 | tf_op jit(solution)/shard_map/ppermute | solution.py:338
  255.8 18.8 %collective-permute-start.6 = (bf16[256,1536]{1,0:T(8,128)(2,1)S(1)}, bf16[256,1536]{1,0:T(8,128)(2,1)}, u32[]{:S(2)}, u32[]{:S(2)}) collective-permute-start(bf16[256,1536]{1,0:T(8,128)(2,1)S(1)} %multiply_convert_fusion.1.refs_0_), channel_id=1, source_target_pairs={{0,4},{1,5},{4,8},{5,9},{8,12},{9,13},{12,14},{13,15},{14,10},{15,... | collective-permute-start | bytes 2359304 | tf_op jit(solution)/shard_map/ppermute | solution.py:337
  272.0 23.3 %collective-permute-start.11 = (bf16[256,1536]{1,0:T(8,128)(2,1)}, bf16[256,1536]{1,0:T(8,128)(2,1)}, u32[]{:S(2)}, u32[]{:S(2)}) collective-permute-start(bf16[256,1536]{1,0:T(8,128)(2,1)} %collective-permute-done.10.refs_1_), channel_id=1, source_target_pairs={{4,0},{5,1},{8,4},{9,5},{12,8},{13,9},{14,12},{15,13},{10,14},{11,... | collective-permute-start | bytes 2359304 | tf_op jit(solution)/shard_map/ppermute | solution.py:338
  274.6 22.8 %collective-permute-start.7 = (bf16[256,1536]{1,0:T(8,128)(2,1)}, bf16[256,1536]{1,0:T(8,128)(2,1)}, u32[]{:S(2)}, u32[]{:S(2)}) collective-permute-start(bf16[256,1536]{1,0:T(8,128)(2,1)} %collective-permute-done.6.refs_0_), channel_id=1, source_target_pairs={{0,4},{1,5},{4,8},{5,9},{8,12},{9,13},{12,14},{13,15},{14,10},{15,... | collective-permute-start | bytes 2359304 | tf_op jit(solution)/shard_map/ppermute | solution.py:337
  295.3 23.0 %collective-permute-start.12 = (bf16[256,1536]{1,0:T(8,128)(2,1)}, bf16[256,1536]{1,0:T(8,128)(2,1)S(1)}, u32[]{:S(2)}, u32[]{:S(2)}) collective-permute-start(bf16[256,1536]{1,0:T(8,128)(2,1)} %collective-permute-done.11.refs_1_), channel_id=1, source_target_pairs={{4,0},{5,1},{8,4},{9,5},{12,8},{13,9},{14,12},{15,13},{10,14},{11,... | collective-permute-start | bytes 2359304 | tf_op jit(solution)/shard_map/ppermute | solution.py:338
  297.4 23.8 %collective-permute-start.8 = (bf16[256,1536]{1,0:T(8,128)(2,1)}, bf16[256,1536]{1,0:T(8,128)(2,1)}, u32[]{:S(2)}, u32[]{:S(2)}) collective-permute-start(bf16[256,1536]{1,0:T(8,128)(2,1)} %collective-permute-done.7.refs_0_), channel_id=1, source_target_pairs={{0,4},{1,5},{4,8},{5,9},{8,12},{9,13},{12,14},{13,15},{14,10},{15,... | collective-permute-start | bytes 2359304 | tf_op jit(solution)/shard_map/ppermute | solution.py:337
  319.2 24.4 %collective-permute-start.13 = (bf16[128,1536]{1,0:T(8,128)(2,1)}, bf16[128,1536]{1,0:T(8,128)(2,1)S(1)}, u32[]{:S(2)}, u32[]{:S(2)}) collective-permute-start(bf16[128,1536]{1,0:T(8,128)(2,1)} %slice.234), channel_id=1, source_target_pairs={{4,0},{5,1},{8,4},{9,5},{12,8},{13,9},{14,12},{15,13},{10,14},{11,... | collective-permute-start | bytes 1179656 | tf_op jit(solution)/shard_map/ppermute | solution.py:338
  323.0 20.7 %collective-permute-start.9 = (bf16[128,1536]{1,0:T(8,128)(2,1)}, bf16[128,1536]{1,0:T(8,128)(2,1)}, u32[]{:S(2)}, u32[]{:S(2)}) collective-permute-start(bf16[128,1536]{1,0:T(8,128)(2,1)} %slice.233), channel_id=1, source_target_pairs={{0,4},{1,5},{4,8},{5,9},{8,12},{9,13},{12,14},{13,15},{14,10},{15,... | collective-permute-start | bytes 1179656 | tf_op jit(solution)/shard_map/ppermute | solution.py:337
  367.3 23.9 %collective-permute-start.22 = (bf16[1536,1024]{1,0:T(8,128)(2,1)S(1)}, bf16[1536,1024]{1,0:T(8,128)(2,1)}, u32[]{:S(2)}, u32[]{:S(2)}) collective-permute-start(bf16[1536,1024]{1,0:T(8,128)(2,1)S(1)} %fusion.10), channel_id=1, source_target_pairs={{0,1},{1,0},{2,3},{3,2},{4,5},{5,4},{6,7},{7,6},{8,9},{9,8},{10,11... | collective-permute-start | bytes 9437192 | tf_op jit(solution)/shard_map/ppermute | solution.py:317
  371.0 15.6 %collective-permute-start.23 = (bf16[512,1536]{1,0:T(8,128)(2,1)S(1)}, bf16[512,1536]{1,0:T(8,128)(2,1)S(1)}, u32[]{:S(2)}, u32[]{:S(2)}) collective-permute-start(bf16[512,1536]{1,0:T(8,128)(2,1)S(1)} %convolution_convert_fusion.1), channel_id=1, source_target_pairs={{0,1},{1,0},{2,3},{3,2},{4,5},{5,4},{6,7},{7,6},{8,9},{9,8},{10,11... | collective-permute-start | bytes 4718600 | tf_op jit(solution)/shard_map/ppermute | solution.py:317
  384.5 19.8 %collective-permute-start.20 = (bf16[256,1664]{1,0:T(8,128)(2,1)S(1)}, bf16[256,1664]{1,0:T(8,128)(2,1)S(1)}, u32[]{:S(2)}, u32[]{:S(2)}) collective-permute-start(bf16[256,1664]{1,0:T(8,128)(2,1)S(1)} %get-tuple-element.198), channel_id=1, source_target_pairs={{0,4},{1,5},{4,8},{5,9},{8,12},{9,13},{12,14},{13,15},{14,10},{15,... | collective-permute-start | bytes 2555912 | tf_op jit(solution)/shard_map/ppermute | solution.py:337
  386.3 19.5 %collective-permute-start.21 = (bf16[256,1664]{1,0:T(8,128)(2,1)S(1)}, bf16[256,1664]{1,0:T(8,128)(2,1)S(1)}, u32[]{:S(2)}, u32[]{:S(2)}) collective-permute-start(bf16[256,1664]{1,0:T(8,128)(2,1)S(1)} %get-tuple-element.197), channel_id=1, source_target_pairs={{4,0},{5,1},{8,4},{9,5},{12,8},{13,9},{14,12},{15,13},{10,14},{11,... | collective-permute-start | bytes 2555912 | tf_op jit(solution)/shard_map/ppermute | solution.py:338
  406.0 18.7 %collective-permute-start.24 = (bf16[256,1664]{1,0:T(8,128)(2,1)S(1)}, bf16[256,1664]{1,0:T(8,128)(2,1)S(1)}, u32[]{:S(2)}, u32[]{:S(2)}) collective-permute-start(bf16[256,1664]{1,0:T(8,128)(2,1)S(1)} %get-tuple-element.195), channel_id=1, source_target_pairs={{0,4},{1,5},{4,8},{5,9},{8,12},{9,13},{12,14},{13,15},{14,10},{15,... | collective-permute-start | bytes 2555912 | tf_op jit(solution)/shard_map/ppermute | solution.py:337
  406.6 18.6 %collective-permute-start.26 = (bf16[256,1664]{1,0:T(8,128)(2,1)S(1)}, bf16[256,1664]{1,0:T(8,128)(2,1)S(1)}, u32[]{:S(2)}, u32[]{:S(2)}) collective-permute-start(bf16[256,1664]{1,0:T(8,128)(2,1)S(1)} %get-tuple-element.196), channel_id=1, source_target_pairs={{4,0},{5,1},{8,4},{9,5},{12,8},{13,9},{14,12},{15,13},{10,14},{11,... | collective-permute-start | bytes 2555912 | tf_op jit(solution)/shard_map/ppermute | solution.py:338
  425.4 17.8 %collective-permute-start.25 = (bf16[256,1664]{1,0:T(8,128)(2,1)S(1)}, bf16[256,1664]{1,0:T(8,128)(2,1)S(1)}, u32[]{:S(2)}, u32[]{:S(2)}) collective-permute-start(bf16[256,1664]{1,0:T(8,128)(2,1)S(1)} %get-tuple-element.193), channel_id=1, source_target_pairs={{0,4},{1,5},{4,8},{5,9},{8,12},{9,13},{12,14},{13,15},{14,10},{15,... | collective-permute-start | bytes 2555912 | tf_op jit(solution)/shard_map/ppermute | solution.py:337
  426.1 17.8 %collective-permute-start.27 = (bf16[256,1664]{1,0:T(8,128)(2,1)S(1)}, bf16[256,1664]{1,0:T(8,128)(2,1)S(1)}, u32[]{:S(2)}, u32[]{:S(2)}) collective-permute-start(bf16[256,1664]{1,0:T(8,128)(2,1)S(1)} %get-tuple-element.194), channel_id=1, source_target_pairs={{4,0},{5,1},{8,4},{9,5},{12,8},{13,9},{14,12},{15,13},{10,14},{11,... | collective-permute-start | bytes 2555912 | tf_op jit(solution)/shard_map/ppermute | solution.py:338
  429.6 99.9 %collective-permute-start.57 = (bf16[512,1536]{1,0:T(8,128)(2,1)}, bf16[512,1536]{1,0:T(8,128)(2,1)}, u32[]{:S(2)}, u32[]{:S(2)}) collective-permute-start(bf16[512,1536]{1,0:T(8,128)(2,1)} %fusion.13), channel_id=1, source_target_pairs={{0,16},{16,0},{1,17},{17,1},{2,18},{18,2},{3,19},{19,3},{4,20},{20... | collective-permute-start | bytes 4718600 | tf_op jit(solution)/shard_map/ppermute | solution.py:310
  429.7 107.9 %collective-permute-start.56 = (bf16[1536,1024]{1,0:T(8,128)(2,1)}, bf16[1536,1024]{1,0:T(8,128)(2,1)}, u32[]{:S(2)}, u32[]{:S(2)}) collective-permute-start(bf16[1536,1024]{1,0:T(8,128)(2,1)} %add_convert_fusion.1), channel_id=1, source_target_pairs={{0,16},{16,0},{1,17},{17,1},{2,18},{18,2},{3,19},{19,3},{4,20},{20... | collective-permute-start | bytes 9437192 | tf_op jit(solution)/shard_map/ppermute | solution.py:310
  465.9 24.0 %all-to-all-start.2 = ((bf16[16,128,192]{1,2,0:T(8,128)(2,1)}), bf16[16,128,192]{1,2,0:T(8,128)(2,1)}, u32[]{:S(2)}, u32[]{:S(2)}) async-start(bf16[16,128,192]{1,2,0:T(8,128)(2,1)} %bitcast.16), calls=%async_computation.2 | async-start | bytes 1572864 | tf_op jit(solution)/shard_map/all_to_all | solution.py:305
  474.9 58.6 %collective-permute-start.28 = (bf16[128,1536]{1,0:T(8,128)(2,1)}, bf16[128,1536]{1,0:T(8,128)(2,1)}, u32[]{:S(2)}, u32[]{:S(2)}) collective-permute-start(bf16[128,1536]{1,0:T(8,128)(2,1)} %get-tuple-element.96), channel_id=1, source_target_pairs={{0,4},{1,5},{4,8},{5,9},{8,12},{9,13},{12,14},{13,15},{14,10},{15,... | collective-permute-start | bytes 1179656 | tf_op jit(solution)/shard_map/ppermute | solution.py:337
  476.8 56.7 %collective-permute-start.29 = (bf16[128,1536]{1,0:T(8,128)(2,1)S(1)}, bf16[128,1536]{1,0:T(8,128)(2,1)}, u32[]{:S(2)}, u32[]{:S(2)}) collective-permute-start(bf16[128,1536]{1,0:T(8,128)(2,1)S(1)} %get-tuple-element.97), channel_id=1, source_target_pairs={{4,0},{5,1},{8,4},{9,5},{12,8},{13,9},{14,12},{15,13},{10,14},{11,... | collective-permute-start | bytes 1179656 | tf_op jit(solution)/shard_map/ppermute | solution.py:338
  523.8 46.7 %all-to-all-start.3 = ((bf16[16,128,320]{1,2,0:T(8,128)(2,1)}), bf16[16,128,320]{1,2,0:T(8,128)(2,1)}, u32[]{:S(2)}, u32[]{:S(2)}) async-start(bf16[16,128,320]{1,2,0:T(8,128)(2,1)} %copy.149), calls=%async_computation.3 | async-start | bytes 2621440 | tf_op jit(solution)/shard_map/all_to_all | solution.py:305
  529.4 169.7 %reduce-scatter.2.cloned.1.call-start = ((), (), s32[]{:S(2)}) async-start(), calls=%async_computation.7 | async-start | bytes 5271552 | tf_op jit(solution)/shard_map/reduce_scatter | solution.py:391
  535.3 33.2 %collective-permute-start.30 = (bf16[256,1536]{1,0:T(8,128)(2,1)S(1)}, bf16[256,1536]{1,0:T(8,128)(2,1)}, u32[]{:S(2)}, u32[]{:S(2)}) collective-permute-start(bf16[256,1536]{1,0:T(8,128)(2,1)S(1)} %get-tuple-element.102), channel_id=1, source_target_pairs={{0,4},{1,5},{4,8},{5,9},{8,12},{9,13},{12,14},{13,15},{14,10},{15,... | collective-permute-start | bytes 2359304 | tf_op jit(solution)/shard_map/ppermute | solution.py:337
  537.3 33.2 %collective-permute-start.31 = (bf16[256,1536]{1,0:T(8,128)(2,1)S(1)}, bf16[256,1536]{1,0:T(8,128)(2,1)}, u32[]{:S(2)}, u32[]{:S(2)}) collective-permute-start(bf16[256,1536]{1,0:T(8,128)(2,1)S(1)} %get-tuple-element.103), channel_id=1, source_target_pairs={{4,0},{5,1},{8,4},{9,5},{12,8},{13,9},{14,12},{15,13},{10,14},{11,... | collective-permute-start | bytes 2359304 | tf_op jit(solution)/shard_map/ppermute | solution.py:338
  575.9 60.2 %collective-permute-start.46 = (bf16[2,8,48,2560]{3,2,1,0:T(8,128)(2,1)S(1)}, bf16[2,8,48,2560]{3,2,1,0:T(8,128)(2,1)S(1)}, u32[]{:S(2)}, u32[]{:S(2)}) collective-permute-start(bf16[2,8,48,2560]{3,2,1,0:T(8,128)(2,1)S(1)} %fusion.7), channel_id=1, source_target_pairs={{0,1},{1,0},{2,3},{3,2},{4,5},{5,4},{6,7},{7,6},{8,9},{9,8},{10,11... | collective-permute-start | bytes 11796488 | tf_op jit(solution)/shard_map/ppermute | solution.py:317
  579.3 34.6 %collective-permute-start.32 = (bf16[256,1536]{1,0:T(8,128)(2,1)}, bf16[256,1536]{1,0:T(8,128)(2,1)S(1)}, u32[]{:S(2)}, u32[]{:S(2)}) collective-permute-start(bf16[256,1536]{1,0:T(8,128)(2,1)} %get-tuple-element.109), channel_id=1, source_target_pairs={{0,4},{1,5},{4,8},{5,9},{8,12},{9,13},{12,14},{13,15},{14,10},{15,... | collective-permute-start | bytes 2359304 | tf_op jit(solution)/shard_map/ppermute | solution.py:337
  587.9 30.3 %collective-permute-start.33 = (bf16[256,1536]{1,0:T(8,128)(2,1)S(1)}, bf16[256,1536]{1,0:T(8,128)(2,1)S(1)}, u32[]{:S(2)}, u32[]{:S(2)}) collective-permute-start(bf16[256,1536]{1,0:T(8,128)(2,1)S(1)} %get-tuple-element.110), channel_id=1, source_target_pairs={{4,0},{5,1},{8,4},{9,5},{12,8},{13,9},{14,12},{15,13},{10,14},{11,... | collective-permute-start | bytes 2359304 | tf_op jit(solution)/shard_map/ppermute | solution.py:338
  594.5 23.9 %collective-permute-start.36 = (bf16[2,8,48,128]{3,2,1,0:T(8,128)(2,1)S(1)}, bf16[2,8,48,128]{3,2,1,0:T(8,128)(2,1)S(1)}, u32[]{:S(2)}, u32[]{:S(2)}) collective-permute-start(bf16[2,8,48,128]{3,2,1,0:T(8,128)(2,1)S(1)} %fusion.34), channel_id=1, source_target_pairs={{0,1},{1,0},{2,3},{3,2},{4,5},{5,4},{6,7},{7,6},{8,9},{9,8},{10,11... | collective-permute-start | bytes 589832 | tf_op jit(solution)/shard_map/ppermute | solution.py:317
  633.0 64.6 %collective-permute-start.34 = (bf16[256,1536]{1,0:T(8,128)(2,1)S(1)}, bf16[256,1536]{1,0:T(8,128)(2,1)S(1)}, u32[]{:S(2)}, u32[]{:S(2)}) collective-permute-start(bf16[256,1536]{1,0:T(8,128)(2,1)S(1)} %get-tuple-element.199), channel_id=1, source_target_pairs={{0,4},{1,5},{4,8},{5,9},{8,12},{9,13},{12,14},{13,15},{14,10},{15,... | collective-permute-start | bytes 2359304 | tf_op jit(solution)/shard_map/ppermute | solution.py:337
  633.8 63.8 %collective-permute-start.35 = (bf16[256,1536]{1,0:T(8,128)(2,1)S(1)}, bf16[256,1536]{1,0:T(8,128)(2,1)S(1)}, u32[]{:S(2)}, u32[]{:S(2)}) collective-permute-start(bf16[256,1536]{1,0:T(8,128)(2,1)S(1)} %get-tuple-element.200), channel_id=1, source_target_pairs={{4,0},{5,1},{8,4},{9,5},{12,8},{13,9},{14,12},{15,13},{10,14},{11,... | collective-permute-start | bytes 2359304 | tf_op jit(solution)/shard_map/ppermute | solution.py:338
  636.0 51.6 %collective-permute-start.45 = (bf16[48,128]{1,0:T(8,128)(2,1)S(1)}, bf16[48,128]{1,0:T(8,128)(2,1)S(1)}, u32[]{:S(2)}, u32[]{:S(2)}) collective-permute-start(bf16[48,128]{1,0:T(8,128)(2,1)S(1)} %constant_dynamic-slice_fusion.8), channel_id=1, source_target_pairs={{0,16},{16,0},{1,17},{17,1},{2,18},{18,2},{3,19},{19,3},{4,20},{20... | collective-permute-start | bytes 36872 | tf_op jit(solution)/shard_map/ppermute | solution.py:425
  636.8 23.0 %collective-permute-start.47 = (bf16[48,2560]{1,0:T(8,128)(2,1)S(1)}, bf16[48,2560]{1,0:T(8,128)(2,1)S(1)}, u32[]{:S(2)}, u32[]{:S(2)}) collective-permute-start(bf16[48,2560]{1,0:T(8,128)(2,1)S(1)} %get-tuple-element.189), channel_id=1, source_target_pairs={{0,4},{1,5},{4,8},{5,9},{8,12},{9,13},{12,14},{13,15},{14,10},{15,... | collective-permute-start | bytes 737288 | tf_op jit(solution)/shard_map/ppermute | solution.py:337
  638.5 23.9 %collective-permute-start.51 = (bf16[48,2560]{1,0:T(8,128)(2,1)S(1)}, bf16[48,2560]{1,0:T(8,128)(2,1)S(1)}, u32[]{:S(2)}, u32[]{:S(2)}) collective-permute-start(bf16[48,2560]{1,0:T(8,128)(2,1)S(1)} %get-tuple-element.190), channel_id=1, source_target_pairs={{4,0},{5,1},{8,4},{9,5},{12,8},{13,9},{14,12},{15,13},{10,14},{11,... | collective-permute-start | bytes 737288 | tf_op jit(solution)/shard_map/ppermute | solution.py:338
  (58 other events, 588.7 us)
Sparse Core Ops, SparseCore 0:
  11.8 90.7 all-gather.2
  106.1 75.7 all-gather.4
  535.8 126.2 reduce-scatter.1

commit v3 on v2

--- a/solution.py
+++ b/solution.py
@@ -7,6 +7,7 @@
 from jax.experimental.pallas import tpu as pltpu
 from jax.sharding import PartitionSpec as P
 
+
 HDIM = 64
 TOP = 8
 BLOCK = 256
@@ -54,22 +55,28 @@
     flipped = block.T
     return jnp.concatenate([flipped[h*HDIM:(h+1)*HDIM] for h in range(group)], axis=1)
 
+
 def tall(block, group):
     return jnp.concatenate([block[:, h*HDIM:(h+1)*HDIM] for h in range(group)], axis=0)
 
+
 def narrow(values, group, rows):
     return jnp.concatenate([values[:, h*rows:(h+1)*rows] for h in range(group)], axis=0).T
+
 
 def forward_kernel(group, qkv_ref, att_ref, flat_ref, lse_ref, key_sc, val_sc, acc_sc):
     i = pl.program_id(0)
     lanes = group*HDIM
+
     @pl.when(i == 0)
     def _():
         key_sc[...] = qkv_ref[:, lanes:lanes+HDIM]
         val_sc[...] = qkv_ref[:, lanes+HDIM:lanes+2*HDIM].T
+
     rows = pl.ds(pl.multiple_of(i*BLOCK, BLOCK), BLOCK)
     query = wide(qkv_ref[rows, :lanes], group) * jnp.bfloat16(HDIM**-0.5)
     acc_sc[...] = jnp.zeros_like(acc_sc)
+
     def step(j, carry):
         top, total = carry
         here = pl.ds(pl.multiple_of(j*BLOCK, BLOCK), BLOCK)
@@ -79,12 +86,14 @@
         fade = jnp.exp(top - new_top)
         acc_sc[...] = acc_sc[...]*fade + jnp.dot(val_sc[:, here], probs.astype(jnp.bfloat16), preferred_element_type=jnp.float32)
         return new_top, total*fade + jnp.sum(probs, axis=0, keepdims=True)
+
     width = group*BLOCK
     top, total = lax.fori_loop(0, i+1, step, (jnp.full((1,width), -1e30, jnp.float32), jnp.zeros((1,width), jnp.float32)))
     result = acc_sc[...] / total
     flat_ref[0] = result
     att_ref[...] = narrow(result.astype(jnp.bfloat16), group, BLOCK)
     lse_ref[0] = top + jnp.log(total)
+
 
 def attend_forward(qkv, group):
     total = qkv.shape[0]; steps = total//BLOCK; lanes = group*HDIM; width = group*BLOCK
@@ -103,14 +112,17 @@
         name="attend_forward",
     )(qkv)
 
+
 def unrotate(values, cosine, sine):
     a, b = values[:HDIM//2], values[HDIM//2:]
     return jnp.concatenate([a*cosine + b*sine, b*cosine - a*sine], axis=0)
+
 
 def backward_kernel(group, steps, qkv_ref, grad_ref, flat_ref, lse_ref, cos_ref, sin_ref, out_ref, key_sc, keyt_sc, val_sc, dq_sc, dk_sc, dv_sc):
     i = pl.program_id(0)
     lanes = group*HDIM
     scale = HDIM**-0.5
+
     @pl.when(i == 0)
     def _():
         key = qkv_ref[:, lanes:lanes+HDIM]
@@ -119,6 +131,7 @@
         val_sc[...] = qkv_ref[:, lanes+HDIM:lanes+2*HDIM]
         dk_sc[...] = jnp.zeros_like(dk_sc)
         dv_sc[...] = jnp.zeros_like(dv_sc)
+
     rows = pl.ds(pl.multiple_of(i*BLOCK, BLOCK), BLOCK)
     block = qkv_ref[rows, :lanes] * jnp.bfloat16(scale)
     query_w, query_t = wide(block, group), tall(block, group)
@@ -127,6 +140,7 @@
     lse = lse_ref[0]
     delta = jnp.sum(grad_w.astype(jnp.float32)*flat_ref[0], axis=0, keepdims=True)
     dq_sc[...] = jnp.zeros_like(dq_sc)
+
     def step(j, carry):
         here = pl.ds(pl.multiple_of(j*BLOCK, BLOCK), BLOCK)
         scores = jnp.dot(key_sc[here,:], query_w, preferred_element_type=jnp.float32)
@@ -137,10 +151,12 @@
         dk_sc[here,:] += jnp.dot(dscores, query_t, preferred_element_type=jnp.float32)
         dq_sc[...] += jnp.dot(keyt_sc[:,here], dscores, preferred_element_type=jnp.float32)
         return carry
+
     lax.fori_loop(0, i+1, step, 0)
     cosine, sine = cos_ref[:, rows], sin_ref[:, rows]
     pieces = [unrotate(dq_sc[:, h*BLOCK:(h+1)*BLOCK]*scale, cosine, sine).astype(jnp.bfloat16) for h in range(group)]
     out_ref[rows, :lanes] = jnp.concatenate(pieces, axis=0).T
+
     @pl.when(i == steps-1)
     def _():
         def finish(j, carry):
@@ -149,7 +165,9 @@
             both = jnp.concatenate([turned, dv_sc[here,:].astype(jnp.bfloat16).T], axis=0).T
             out_ref[here, lanes:lanes+2*HDIM] = both
             return carry
+
         lax.fori_loop(0, steps, finish, 0)
+
 
 def attend_backward(qkv, grad, flat, lse, cosine, sine, group):
     total = qkv.shape[0]; steps = total//BLOCK; lanes = group*HDIM; width = group*BLOCK
@@ -170,6 +188,7 @@
         name="attend_backward",
     )(qkv, grad, flat, lse, cosine, sine)
 
+
 def expert_kernel(
     parts, rows, width, experts, steps, chained, index_ref, *refs
 ):
@@ -177,15 +196,16 @@
     grads = refs[parts : 2 * parts]
     router_ref, lin_ref, down_ref = refs[2 * parts : 2 * parts + 3]
     refs = refs[2 * parts + 3 + (4 if chained else 0) :]
-    mixed_ref, back_ref, rows_ref, grads_ref, d_lin_ref, hidden_ref = refs[:6]
-    gates_sc, d_gates_sc, mixed_sc, back_sc = refs[6:]
+    mixed_refs, back_refs, refs = refs[:parts], refs[parts : 2 * parts], refs[2 * parts :]
+    rows_ref, grads_ref, d_lin_ref, hidden_ref = refs[:4]
+    gates_sc, d_gates_sc, mixed_sc, back_sc = refs[4:]
+    part = rows // parts
     units = down_ref.shape[1]
     step = pl.program_id(0)
     lane = lax.broadcasted_iota(jnp.int32, (rows, LANES), 1)
 
     @pl.when(step == 0)
     def _():
-        part = rows // parts
         for k in range(parts):
             here = pl.ds(k * part, part)
             rows_ref[here, :] = blocks[k][...]
@@ -209,7 +229,8 @@
     d_gates_sc[...] += jnp.where(own, jnp.sum(hidden * d_hidden, axis=1, keepdims=True), 0.0)
     hidden = (gate * hidden).astype(jnp.bfloat16)
     d_hidden = gate * d_hidden
-    d_gate = (d_hidden * up_lin * sigma * (1.0 + gate_lin * (1.0 - sigma))).astype(jnp.bfloat16)
+    slope = sigma + active - active * sigma
+    d_gate = (d_hidden * up_lin * slope).astype(jnp.bfloat16)
     d_up = (d_hidden * active).astype(jnp.bfloat16)
     hidden_ref[...] = hidden
     d_lin = jnp.concatenate([d_gate, d_up], axis=1)
@@ -229,12 +250,15 @@
 
     @pl.when(step == steps - 1)
     def _():
-        mixed_ref[...] = mixed_sc[...].astype(jnp.bfloat16)
-        back_ref[:, :width] = back_sc[...].astype(jnp.bfloat16)
         d_gates = d_gates_sc[...]
         high = d_gates.astype(jnp.bfloat16).astype(jnp.float32)
         low = pltpu.roll(d_gates - high, experts, 1)
-        back_ref[:, width:] = jnp.where(lane < experts, high, low).astype(jnp.bfloat16)
+        d_gates = jnp.where(lane < experts, high, low).astype(jnp.bfloat16)
+        for k in range(parts):
+            here = slice(k * part, (k + 1) * part)
+            mixed_refs[k][...] = mixed_sc[here, :].astype(jnp.bfloat16)
+            back_refs[k][:, :width] = back_sc[here, :].astype(jnp.bfloat16)
+            back_refs[k][:, width:] = d_gates[here]
 
 
 def expert_rows(index, experts, blocks, grads, router, lin, down, slot, total, buffers):
@@ -248,8 +272,8 @@
     kept = pl.BlockSpec((rows, width), lambda i, ids: (slot, 0))
     chained = buffers is not None
     shapes = [
-        jax.ShapeDtypeStruct((rows, width), jnp.bfloat16),
-        jax.ShapeDtypeStruct((rows, width + LANES), jnp.bfloat16),
+        *[jax.ShapeDtypeStruct((part, width), jnp.bfloat16)] * parts,
+        *[jax.ShapeDtypeStruct((part, width + LANES), jnp.bfloat16)] * parts,
         jax.ShapeDtypeStruct((total, width), jnp.bfloat16),
         jax.ShapeDtypeStruct((total, width), jnp.bfloat16),
         jax.ShapeDtypeStruct((total, 4 * units), jnp.bfloat16),
@@ -257,7 +281,7 @@
     ]
     inputs = [index, *blocks, *grads, router, lin, down] + (list(buffers) if chained else [])
     first = 1 + 2 * parts + 3
-    return pl.pallas_call(
+    results = pl.pallas_call(
         functools.partial(expert_kernel, parts, rows, width, experts, steps, chained),
         grid_spec=pltpu.PrefetchScalarGridSpec(
             num_scalar_prefetch=1,
@@ -271,8 +295,8 @@
             ]
             + ([pl.BlockSpec(memory_space=pl.ANY)] * 4 if chained else []),
             out_specs=[
-                whole(rows, width),
-                whole(rows, width + LANES),
+                *[whole(part, width)] * parts,
+                *[whole(part, width + LANES)] * parts,
                 kept,
                 kept,
                 columns(2 * units),
@@ -286,7 +310,7 @@
             ],
         ),
         out_shape=shapes,
-        input_output_aliases={first + k: 2 + k for k in range(4)} if chained else {},
+        input_output_aliases={first + k: 2 * parts + k for k in range(4)} if chained else {},
         compiler_params=pltpu.CompilerParams(dimension_semantics=("arbitrary",)),
         cost_estimate=pl.CostEstimate(
             flops=rows * width * units * 24,
@@ -295,6 +319,7 @@
         ),
         name="expert_rows",
     )(*inputs)
+    return results[:parts], results[parts : 2 * parts], results[2 * parts :]
 
 
 def gather_dense(values):
@@ -305,11 +330,12 @@
     return lax.all_to_all(values, "blk", split_axis=0, concat_axis=0, tiled=True)
 
 
-def sum_heads(values):
-    if lax.axis_size("head") == 2:
-        other = lax.ppermute(values, "head", [(0, 1), (1, 0)])
-        return values.astype(jnp.float32) + other.astype(jnp.float32)
-    return lax.psum(values, "head").astype(jnp.float32)
+def from_heads(values):
+    heads = lax.axis_size("head")
+    return [
+        lax.ppermute(values, "head", [(k, (k + turn) % heads) for k in range(heads)])
+        for turn in range(1, heads)
+    ]
 
 
 def partner(values):
@@ -347,16 +373,16 @@
     for _ in range(length // 2 - 1):
         behind, ahead = send_on(behind), send_back(ahead)
         pairs.append((behind, ahead))
-    return pairs, (send_on(behind[:half]), send_back(ahead[half:]))
+    behind, ahead = behind[:half], ahead[half:]
+    return pairs, (send_on(behind), send_back(ahead))
 
 
 class RingSum:
-    def __init__(self, own, pairs, opposite, axis=0):
+    def __init__(self, own, pairs, opposite, label, axis=0):
         _, self.send_on, self.send_back = ring_steps()
-        self.own, self.pairs, self.axis = own, list(reversed(pairs)), axis
-        self.half = own.shape[axis] // 2
-        self.onward = lax.slice_in_dim(opposite, 0, self.half, axis=axis)
-        self.back = lax.slice_in_dim(opposite, self.half, 2 * self.half, axis=axis)
+        self.own, self.pairs, self.label = own, list(reversed(pairs)), label
+        self.onward, self.back = opposite
+        self.axis = axis
         self.hop = 0
 
     def send(self, *hold):
@@ -372,10 +398,11 @@
         if filler:
             self.onward, self.back = after((self.onward, self.back), filler)
         if self.hop == 0:
+            lengths = self.onward.shape[self.axis], self.back.shape[self.axis]
             spread = [(0, 0), (0, 0)]
-            spread[self.axis] = (0, self.half)
+            spread[self.axis] = (0, lengths[1])
             self.onward = jnp.pad(self.onward, spread)
-            spread[self.axis] = (self.half, 0)
+            spread[self.axis] = (lengths[0], 0)
             self.back = jnp.pad(self.back, spread)
         self.hop += 1
         return self
@@ -387,43 +414,111 @@
         return wide + self.onward.astype(jnp.float32) + self.back.astype(jnp.float32)
 
 
-def scatter_dense(values):
-    return lax.psum_scatter(
-        values, ("head", "blk"), scatter_dimension=0, tiled=True
-    ).astype(jnp.float32)
-
-
-def dense_scatter(values):
-    heads = lax.axis_size("head")
-    chips = lax.axis_size("blk") // 2
-    rows = values.shape[0] // (2 * heads * chips)
-    columns = values.shape[1]
-    grid = values.reshape(heads, chips, 2, rows, columns)
-    index = lax.axis_index("blk")
+def head_share(values):
+    heads, rows = lax.axis_size("head"), values.shape[0] // lax.axis_size("head")
     head = lax.axis_index("head")
-    chip, turns = index // 2, chips // 2
-    place = jnp.where(chip % 2 == 0, chip // 2, chips - 1 - chip // 2)
-    parts = grid[:, :, 0], grid[:, :, 1]
-    even = index % 2 == 0
-    away = jnp.where(even, parts[1], parts[0])
-    mine = jnp.where(even, parts[0], parts[1]) + partner(away)
-
-    def block(offset):
-        target = (place + offset) % chips
-        chip = jnp.where(target < turns, 2 * target, 2 * (chips - 1 - target) + 1)
-        piece = lax.dynamic_slice(mine, (0, chip, 0, 0), (heads, 1, rows, columns))
-        return piece.reshape(heads * rows, columns)
-
-    pairs = [(block(-k), block(k)) for k in range(1, chips // 2)]
-    total = RingSum(block(0), pairs, block(chips // 2)).total().astype(jnp.bfloat16)
+    start = (0,) * (values.ndim - 1)
     share = lambda turn: lax.dynamic_slice(
-        total, ((head + turn) % heads * rows, 0), (rows, columns)
+        values, ((head + turn) % heads * rows, *start), (rows, *values.shape[1:])
     )
     result = share(0).astype(jnp.float32)
     for turn in range(1, heads):
         moved = [(k, (k + turn) % heads) for k in range(heads)]
-        result = result + lax.ppermute(share(turn), "head", moved).astype(jnp.float32)
+        other = lax.ppermute(share(turn), "head", moved)
+        result = result + other.astype(jnp.float32)
     return result
+
+
+class DenseSum:
+    def __init__(self, values, label, heads_first=False):
+        self.heads = lax.axis_size("head")
+        self.chips = lax.axis_size("blk") // 2
+        self.rows = values.shape[0] // (2 * self.heads * self.chips)
+        self.label, self.heads_first = label, heads_first
+        self.index = lax.axis_index("blk")
+        self.mine = self.core_sum(values)
+
+    def core_sum(self, values):
+        grid = values.reshape(self.heads, self.chips, 2, self.rows, values.shape[1])
+        even = self.index % 2 == 0
+        swapped = partner(jnp.where(even, grid[:, :, 1], grid[:, :, 0]))
+        return jnp.where(even, grid[:, :, 0], grid[:, :, 1]) + swapped
+
+    def append(self, values):
+        self.mine = jnp.concatenate([self.mine, self.core_sum(values)], axis=3)
+
+    def block(self, offset):
+        chip, turns = self.index // 2, self.chips // 2
+        place = jnp.where(chip % 2 == 0, chip // 2, self.chips - 1 - chip // 2)
+        target = (place + offset) % self.chips
+        chip = jnp.where(target < turns, 2 * target, 2 * (self.chips - 1 - target) + 1)
+        heads, columns = self.mine.shape[0], self.mine.shape[3]
+        piece = lax.dynamic_slice(self.mine, (0, chip, 0, 0), (heads, 1, self.rows, columns))
+        return piece.reshape(heads * self.rows, columns)
+
+    def ring(self):
+        if self.heads_first:
+            self.mine = head_share(self.mine).astype(jnp.bfloat16)
+        pairs = [(self.block(-k), self.block(k)) for k in range(1, self.chips // 2)]
+        opposite = self.block(self.chips // 2)
+        axis = 1 if self.heads_first else 0
+        half = opposite.shape[1] // 256 * 128 if axis else opposite.shape[0] // 2
+        opposite = jnp.split(opposite, [half], axis=axis)
+        return RingSum(self.block(0), pairs, opposite, self.label, axis)
+
+    def finish(self, total):
+        return total if self.heads_first else head_share(total.astype(jnp.bfloat16))
+
+    def total(self):
+        return self.finish(self.ring().total())
+
+
+def project_kernel(shard, groups, rows_ref, weight_ref, cosine_ref, sine_ref, out_ref):
+    values = jnp.dot(rows_ref[...], weight_ref[...], preferred_element_type=jnp.float32)
+    width = values.shape[1]
+    lane = lax.broadcasted_iota(jnp.int32, (shard, width), 1)
+    first = lane % HDIM < HDIM // 2
+    span = width // groups
+    for s in range(values.shape[0] // shard):
+        part = values[s * shard : (s + 1) * shard]
+        turned = jnp.where(
+            first, pltpu.roll(part, width - HDIM // 2, 1), pltpu.roll(part, HDIM // 2, 1)
+        )
+        part = (part * cosine_ref[...] + turned * sine_ref[...]).astype(jnp.bfloat16)
+        for k in range(groups):
+            out_ref[s, k] = part[:, k * span : (k + 1) * span]
+
+
+def project(normed, weights, positions, groups, group):
+    rows, width = normed.shape
+    shard = positions.shape[0]
+    span = (group + 2) * HDIM
+    cosine, sine = rope_tables(positions, HDIM // 2)
+    cosine = jnp.concatenate([cosine, cosine], axis=1)
+    sine = jnp.concatenate([-sine, sine], axis=1)
+    plain = (jnp.ones((shard, HDIM), jnp.float32), jnp.zeros((shard, HDIM), jnp.float32))
+    cosine = jnp.concatenate(([cosine] * (group + 1) + [plain[0]]) * 2, axis=1)
+    sine = jnp.concatenate(([sine] * (group + 1) + [plain[1]]) * 2, axis=1)
+    table = pl.BlockSpec((shard, 2 * span), lambda j: (0, 0))
+    return pl.pallas_call(
+        functools.partial(project_kernel, shard, 2),
+        grid=(groups // 2,),
+        in_specs=[
+            pl.BlockSpec((rows, width), lambda j: (0, 0)),
+            pl.BlockSpec((width, 2 * span), lambda j: (0, j)),
+            table,
+            table,
+        ],
+        out_specs=pl.BlockSpec((rows // shard, 2, shard, span), lambda j: (0, j, 0, 0)),
+        out_shape=jax.ShapeDtypeStruct((rows // shard, groups, shard, span), jnp.bfloat16),
+        compiler_params=pltpu.CompilerParams(dimension_semantics=("arbitrary",)),
+        cost_estimate=pl.CostEstimate(
+            flops=2 * rows * width * groups * span,
+            bytes_accessed=2 * width * groups * span,
+            transcendentals=0,
+        ),
+        name="project",
+    )(normed, weights, cosine, sine)
 
 
 def with_lanes(values, extra):
@@ -433,12 +528,12 @@
 
 
 def add_lanes(padded, extra):
-    rows, columns = padded.shape
+    _, columns = padded.shape
     spread = ((0, 0), (columns - LANES, LANES - extra.shape[1]))
     return padded + jnp.pad(extra, spread)
 
 
-def local(
+def layer(
     tokens,
     gain_attn,
     w_query,
@@ -501,19 +596,10 @@
     inverse_one = rms_scale(residual)
     normed = (residual * inverse_one * gain_first).astype(jnp.bfloat16)
     positions = blk_index * shard + jnp.arange(shard, dtype=jnp.int32)
-    cosine, sine = rope_tables(positions, HDIM // 2)
-    turned = (jnp.arange(groups * (group + 2)) % (group + 2) < group + 1)[None, None, :, None]
-    cosine = jnp.where(turned, cosine[None, :, None, :], 1.0)
-    sine = jnp.where(turned, sine[None, :, None, :], 0.0)
-    linear = matmul(normed, full_mixed)[:, : groups * span].reshape(seq_local, shard, -1, HDIM)
-    first, second = linear[..., : HDIM // 2], linear[..., HDIM // 2 :]
-    packed = jnp.concatenate(
-        [first * cosine - second * sine, second * cosine + first * sine], axis=-1
-    ).astype(jnp.bfloat16)
+    packed = project(normed, full_mixed, positions, groups, group)
 
     def to_pairs(values, columns):
-        values = values.reshape(seq_local, shard, groups, columns)
-        values = values.transpose(0, 2, 1, 3).reshape(pairs, 1, shard, columns)
+        values = values.reshape(pairs, 1, shard, columns)
         values = jnp.broadcast_to(values, (pairs, copies, shard, columns))
         return exchange(values.reshape(blk_count, shard, columns)).reshape(seq_total, columns)
 
@@ -542,37 +628,36 @@
         )
 
     ring_pairs = len(blocks_pairs)
-    mixed_own, back_own, *buffers = apply_experts(
+    mixed_own, back_own, buffers = apply_experts(
         [normed_two], [grads_own], 2 * ring_pairs, None
     )
     mixed_pairs, back_pairs = [], []
     for k in range(ring_pairs):
-        mixed, back, *buffers = apply_experts(blocks_pairs[k], grads_pairs[k], k, buffers)
-        mixed_pairs.append((mixed[:token_rows], mixed[token_rows:]))
-        back_pairs.append((back[:token_rows], back[token_rows:]))
-    mixed_opposite, back_opposite, *buffers = apply_experts(
+        mixed, back, buffers = apply_experts(blocks_pairs[k], grads_pairs[k], k, buffers)
+        mixed_pairs.append(mixed)
+        back_pairs.append(back)
+    mixed_opposite, back_opposite, buffers = apply_experts(
         blocks_opposite, grads_opposite, 2 * ring_pairs + 1, buffers
     )
     rows_all, grads_all, d_lin_all, hidden_all = buffers
+    back_ring = RingSum(back_own[0], back_pairs, back_opposite, "back")
     others = [
         matmul_tn(rows_all, d_lin_all[:, 2 * units :]).astype(jnp.bfloat16),
         matmul_tn(hidden_all[:, units:], grads_all).astype(jnp.bfloat16),
     ]
+    others = [partner(part) for part in others]
     mine = [
-        matmul_tn(rows_all, d_lin_all[:, : 2 * units]),
-        matmul_tn(hidden_all[:, :units], grads_all),
+        matmul_tn(rows_all, d_lin_all[:, : 2 * units]) + others[0].astype(jnp.float32),
+        matmul_tn(hidden_all[:, :units], grads_all) + others[1].astype(jnp.float32),
     ]
-    mine = [
-        (part + partner(other).astype(jnp.float32)).astype(jnp.bfloat16)
-        for part, other in zip(mine, others)
-    ]
-    back_ring = RingSum(back_own, back_pairs, back_opposite)
-    back_ring.send().land(others).send().land(mine)
+    mine = [part.astype(jnp.bfloat16) for part in mine]
     back_sum = back_ring.total()
-    grad_lin_sum, grad_down_sum = [sum_heads(part) for part in mine]
-    grad_gate_sum, grad_up_sum = grad_lin_sum[:, :units], grad_lin_sum[:, units:]
-    mixed_ring = RingSum(mixed_own, mixed_pairs, mixed_opposite)
-    mixed_ring.send(back_sum)
+    theirs = [from_heads(part) for part in mine]
+    mixed_ring = RingSum(mixed_own[0], mixed_pairs, mixed_opposite, "mixed")
+    (mixed_ring.onward, mixed_ring.back), back_sum = lax.optimization_barrier(
+        ((mixed_ring.onward, mixed_ring.back), back_sum)
+    )
+    mixed_ring.send()
 
     d_gates = back_sum[:, width : width + experts] + back_sum[:, width + experts : width + 2 * experts]
     d_logits = gates * (d_gates - jnp.sum(gates * d_gates, axis=-1, keepdims=True))
@@ -588,31 +673,50 @@
         matmul_tn(attended, d_branch),
         jnp.concatenate([grad_router, grad_gain_second[:, None]], axis=1),
     ).astype(jnp.bfloat16)
-    d_attended = after(d_attended, early)
-    mixed_ring.land(d_attended)
-    pair_grad = to_pairs(d_attended, lanes)
-    mixed_ring.send(pair_grad)
+    mixed_ring.land()
+    d_attended, early, mixed_ring.onward, mixed_ring.back = lax.optimization_barrier(
+        (d_attended, early, mixed_ring.onward, mixed_ring.back)
+    )
+    pair_grad = to_pairs(
+        d_attended.reshape(seq_local, shard, groups, lanes).transpose(0, 2, 1, 3), lanes
+    )
+    pair_grad, mixed_ring.onward, mixed_ring.back = lax.optimization_barrier(
+        (pair_grad, mixed_ring.onward, mixed_ring.back)
+    )
+    mixed_ring.send()
     pair_cosine, pair_sine = rope_tables(jnp.arange(seq_total, dtype=jnp.int32), HDIM // 2)
     pair_d = attend_backward(
         pair_qkv, pair_grad, flat, log_total, pair_cosine.T, pair_sine.T, group
     )
-    early = scatter_dense(early)
-    mixed_ring.land(pair_d).send(pair_d)
+    early = DenseSum(early, "early", True).total()
+    mixed_ring.land()
+    pair_d, mixed_ring.onward, mixed_ring.back = lax.optimization_barrier(
+        (pair_d, mixed_ring.onward, mixed_ring.back)
+    )
+    mixed_ring.send()
     d_linear = to_tokens(pair_d, span)
-    mixed_ring.land(d_linear)
-    out = (middle + mixed_ring.total()).reshape(seq_local, shard, width)
+    mixed_ring.land()
+    d_linear, early = lax.optimization_barrier((d_linear, early))
     grad_mixed = matmul_tn(normed, d_linear).astype(jnp.bfloat16)
-    late_mixed = dense_scatter(grad_mixed).reshape(part_rows, groups, span)
+    late = DenseSum(grad_mixed, "late", True)
     d_normed = matmul_nt(jnp.pad(d_linear, ((0, 0), (0, LANES))), full_mixed)
     d_tok_norm, grad_gain_first = norm_back(residual, inverse_one, gain_first, d_normed)
     grad_tokens = (d_mid + d_tok_norm).reshape(seq_local, shard, width)
-    late_gain = dense_scatter(
-        jnp.pad(grad_gain_first[:, None].astype(jnp.bfloat16), ((0, 0), (0, LANES - 1)))
-    )
+    late.append(jnp.pad(grad_gain_first[:, None].astype(jnp.bfloat16), ((0, 0), (0, LANES - 1))))
+    late_ring = late.ring()
+    sums = [
+        functools.reduce(jnp.add, [v.astype(jnp.float32) for v in others], part.astype(jnp.float32))
+        for part, others in zip(mine, theirs)
+    ]
+    grad_gate_sum, grad_up_sum = sums[0][:, :units], sums[0][:, units:]
+    grad_down_sum = sums[1]
+    out = (middle + mixed_ring.total()).reshape(seq_local, shard, width)
+    late = late.finish(late_ring.total())
+    late_mixed = late[:, : groups * span].reshape(part_rows, groups, span)
     return (
         out,
         grad_tokens,
-        late_gain[:, 0],
+        late[:, groups * span],
         late_mixed[:, :, :lanes].reshape(part_rows, -1),
         late_mixed[:, :, lanes : lanes + HDIM].reshape(part_rows, -1),
         late_mixed[:, :, lanes + HDIM :].reshape(part_rows, -1),
@@ -642,7 +746,7 @@
         P("head", "blk", None),
     )
     return jax.shard_map(
-        local,
+        layer,
         mesh=mesh,
         in_specs=placed,
         out_specs=(

time: 723 us -> 820 us (1.13)
  waiting for transfers between devices: 298 us -> 392 us
    ppermute x4, waiting for transfers between devices: 0.01 us -> 134 us  [the longest x2 86.4 us: from_heads(): lax.ppermute(values, 'head', [(k, (k + turn) % heads) for k in range(head...]
    ppermute x24, waiting for transfers between devices: 208 us -> 177 us  [ring_steps(): send_on = lambda values: lax.ppermute(values, 'blk', onward)]
    ppermute x24, waiting for transfers between devices: 16.7 us -> 7.73 us  [ring_steps(): send_back = lambda values: lax.ppermute(values, 'blk', back)]
  transfers between devices with their start and end apart: 65 -> 65, of which waited for: 33 -> 26; matrix products, arithmetic and copies ran while one was open for 20% -> 17% of each run, Pallas kernels for 18% -> 16%
where the time goes in v3:
time: 820 us; the launch traced here: 811 us
  waiting for transfers between devices  392 us (48%)
  Pallas kernels  146 us (18%)
  starting transfers between devices  95.2 us (12%)
  matrix products  56.1 us (7%)
  local copies, waits for them, and re-layouts  53.3 us (6%)
  other arithmetic  52.3 us (6%)
  between operations  15.5 us (2%)
    ppermute x24, waiting for transfers between devices, ring_steps(): send_on = lambda values: lax.ppermute(values, 'blk', onward)  177 us
    pallas_call x5, Pallas kernels, expert_rows(): pl.pallas_call(functools.partial(expert_kernel, parts, rows, width, exper...  86.7 us
    ppermute x2, waiting for transfers between devices, from_heads(): lax.ppermute(values, 'head', [(k, (k + turn) % heads) for k in range(head...  86.4 us
    ppermute x2, waiting for transfers between devices, head_share(): other = lax.ppermute(share(turn), 'head', moved)  47.9 us
    all_to_all x4, waiting for transfers between devices, exchange(): lax.all_to_all(values, 'blk', split_axis=0, concat_axis=0, tiled=True)  44.8 us
    ppermute x24, starting transfers between devices, ring_steps(): send_on = lambda values: lax.ppermute(values, 'blk', onward)  39.8 us
    dot_general x6, matrix products, matmul_tn(): lax.dot_general(left, right, (((0,), (0,)), ((), ())), preferred_element_...  37.9 us
    pallas_call x1, Pallas kernels, attend_backward(): pl.pallas_call(functools.partial(backward_kernel, group, steps), grid=(st...  29.2 us
  transfers between devices with their start and end apart: 65, of which 26 were waited for; matrix products, arithmetic and copies ran while one was open for 17% of the time, Pallas kernels for 16%

profile of v3, /device:TPU:0, one launch (start us, length us, event | category | flops | bytes accessed | tf_op | source)
XLA Modules:
  0.0 810.6 jit_solution(777720743446760834)
XLA Ops:
  14.6 3.1 collective-permute-start
  17.7 23.7 %collective-permute-done.refs_2_ = bf16[256,1664]{1,0:T(8,128)(2,1)} collective-permute-done((bf16[256,1664]{1,0:T(8,128)(2,1)S(1)}, bf16[256,1664]{1,0:T(8,128)(2,1)}, u32[]{:S(2)}, u32[]{:S(2)}) %collective-permute-start) | collective-permute-done | bytes 852000 | tf_op jit(solution)/shard_map/ppermute | solution.py:363
  41.4 2.6 collective-permute-start.2
  47.9 24.8 %collective-permute-done.2.refs_2_ = bf16[256,1664]{1,0:T(8,128)(2,1)} collective-permute-done((bf16[256,1664]{1,0:T(8,128)(2,1)}, bf16[256,1664]{1,0:T(8,128)(2,1)}, u32[]{:S(2)}, u32[]{:S(2)}) %collective-permute-start.2) | collective-permute-done | bytes 852000 | tf_op jit(solution)/shard_map/ppermute | solution.py:363
  74.9 28.6 %all-gather.3.cloned.1.call-done.weight_ref = bf16[1536,2688]{1,0:T(8,128)(2,1)} async-done(((bf16[48,2688]{1,0:T(8,128)(2,1)}), bf16[1536,2688]{1,0:T(8,128)(2,1)}) %all-gather.3.cloned.1.call-update) | async-done | bytes 8257552 | tf_op jit(solution)/shard_map/all_gather | solution.py:326
  105.9 7.6 project.1
  113.5 2.7 copy.184
  116.2 4.2 all-to-all-start
  122.2 32.0 %all-to-all-done = bf16[16,128,320]{1,2,0:T(8,128)(2,1)S(1)} async-done(((bf16[16,128,320]{1,2,0:T(8,128)(2,1)}), bf16[16,128,320]{1,2,0:T(8,128)(2,1)S(1)}, u32[]{:S(2)}, u32[]{:S(2)}) %all-to-all-start) | async-done | bytes 1310752 | tf_op jit(solution)/shard_map/all_to_all | solution.py:330
  155.7 22.5 %attend_forward.1 = (bf16[2048,192]{1,0:T(8,128)(2,1)}, f32[8,64,768]{2,1,0:T(8,128)}, f32[8,1,768]{2,1,0:T(1,128)}) custom-call(bf16[2048,320]{1,0:T(8,128)(2,1)} %bitcast.174), custom_call_target="tpu_custom_call" | custom-call | tf_op jit(solution)/shard_map/attend_forward/pallas_call | solution.py:100
  180.5 9.5 %all-to-all-start.1 = ((bf16[16,128,192]{1,2,0:T(8,128)(2,1)}), bf16[16,128,192]{1,2,0:T(8,128)(2,1)}, u32[]{:S(2)}, u32[]{:S(2)}) async-start(bf16[16,128,192]{1,2,0:T(8,128)(2,1)} %copy.186), calls=%async_computation.1 | async-start | bytes 1572864 | tf_op jit(solution)/shard_map/all_to_all | solution.py:330
  195.7 26.3 %collective-permute-done.14.refs_2_ = bf16[256,1664]{1,0:T(8,128)(2,1)} collective-permute-done((bf16[256,1664]{1,0:T(8,128)(2,1)}, bf16[256,1664]{1,0:T(8,128)(2,1)}, u32[]{:S(2)}, u32[]{:S(2)}) %collective-permute-start.14) | collective-permute-done | bytes 852000 | tf_op jit(solution)/shard_map/ppermute | solution.py:363
  223.9 5.9 collective-permute-start.15
  231.6 6.1 pad_maximum_fusion.refs_3_.refs_5_
  241.0 4.3 multiply_reduce_fusion.4
  245.9 3.3 collective-permute-start.10
  251.2 12.6 %expert_rows.5 = (bf16[256,1536]{1,0:T(8,128)(2,1)}, bf16[256,1664]{1,0:T(8,128)(2,1)}, bf16[2048,1536]{1,0:T(8,128)(2,1)}, bf16[2048,1536]{1,0:T(8,128)(2,1)}, ...) custom-call(s32[2]{0:T(128)} %pad_add_fusion.2.index_ref, bf16[256,1536]{1,0:T(8,128)(2,1)} %copy-done.15, ...), custom_call_target="tpu_custom_call" | custom-call | flops 4831838208 | bytes 17301504 | tf_op jit(solution)/shard_map/expert_rows/pallas_call | solution.py:284
  269.0 20.5 %expert_rows.6 = (bf16[256,1536]{1,0:T(8,128)(2,1)}, bf16[256,1536]{1,0:T(8,128)(2,1)}, bf16[256,1664]{1,0:T(8,128)(2,1)}, bf16[256,1664]{1,0:T(8,128)(2,1)}, bf...) custom-call(s32[2]{0:T(128)} %pad_add_fusion.2.index_ref, ...), custom_call_target="tpu_custom_call", output_to_operand_aliasing={{4}: (8, {}), {5}: (9, {}), {6}: (10, {}), {7}: (11, {})} | custom-call | flops 9663676416 | bytes 25165824 | tf_op jit(solution)/shard_map/expert_rows/pallas_call | solution.py:284
  291.6 20.4 %expert_rows.7 = (bf16[256,1536]{1,0:T(8,128)(2,1)}, bf16[256,1536]{1,0:T(8,128)(2,1)}, bf16[256,1664]{1,0:T(8,128)(2,1)}, bf16[256,1664]{1,0:T(8,128)(2,1)}, bf...) custom-call(s32[2]{0:T(128)} %pad_add_fusion.2.index_ref, ...), custom_call_target="tpu_custom_call", output_to_operand_aliasing={{4}: (8, {}), {5}: (9, {}), {6}: (10, {}), {7}: (11, {})} | custom-call | flops 9663676416 | bytes 25165824 | tf_op jit(solution)/shard_map/expert_rows/pallas_call | solution.py:284
  316.1 20.5 %expert_rows.8 = (bf16[256,1536]{1,0:T(8,128)(2,1)}, bf16[256,1536]{1,0:T(8,128)(2,1)}, bf16[256,1664]{1,0:T(8,128)(2,1)}, bf16[256,1664]{1,0:T(8,128)(2,1)}, bf...) custom-call(s32[2]{0:T(128)} %pad_add_fusion.2.index_ref, ...), custom_call_target="tpu_custom_call", output_to_operand_aliasing={{4}: (8, {}), {5}: (9, {}), {6}: (10, {}), {7}: (11, {})} | custom-call | flops 9663676416 | bytes 25165824 | tf_op jit(solution)/shard_map/expert_rows/pallas_call | solution.py:284
  337.4 12.7 %expert_rows.9 = (bf16[128,1536]{1,0:T(8,128)(2,1)}, bf16[128,1536]{1,0:T(8,128)(2,1)}, bf16[128,1664]{1,0:T(8,128)(2,1)}, bf16[128,1664]{1,0:T(8,128)(2,1)}, bf...) custom-call(s32[2]{0:T(128)} %pad_add_fusion.2.index_ref, ...), custom_call_target="tpu_custom_call", output_to_operand_aliasing={{4}: (8, {}), {5}: (9, {}), {6}: (10, {}), {7}: (11, {})} | custom-call | flops 4831838208 | bytes 17301504 | tf_op jit(solution)/shard_map/expert_rows/pallas_call | solution.py:284
  352.2 8.0 collective-permute-done.18
  362.6 16.7 %collective-permute-done.19 = bf16[256,1664]{1,0:T(8,128)(2,1)S(1)} collective-permute-done((bf16[256,1664]{1,0:T(8,128)(2,1)S(1)}, bf16[256,1664]{1,0:T(8,128)(2,1)S(1)}, u32[]{:S(2)}, u32[]{:S(2)}) %collective-permute-start.19) | collective-permute-done | bytes 852000 | tf_op jit(solution)/shard_map/ppermute | solution.py:363
  381.8 16.6 %collective-permute-done.20 = bf16[256,1664]{1,0:T(8,128)(2,1)S(1)} collective-permute-done((bf16[256,1664]{1,0:T(8,128)(2,1)S(1)}, bf16[256,1664]{1,0:T(8,128)(2,1)S(1)}, u32[]{:S(2)}, u32[]{:S(2)}) %collective-permute-start.20) | collective-permute-done | bytes 852000 | tf_op jit(solution)/shard_map/ppermute | solution.py:363
  403.7 10.4 %collective-permute-done.21 = bf16[256,1664]{1,0:T(8,128)(2,1)} collective-permute-done((bf16[256,1664]{1,0:T(8,128)(2,1)S(1)}, bf16[256,1664]{1,0:T(8,128)(2,1)}, u32[]{:S(2)}, u32[]{:S(2)}) %collective-permute-start.21) | collective-permute-done | bytes 852000 | tf_op jit(solution)/shard_map/ppermute | solution.py:363
  435.2 4.5 all-to-all-start.2
  439.8 3.6 bitcast_add_fusion.1
  445.6 12.8 %all-to-all-done.2 = bf16[16,128,192]{1,2,0:T(8,128)(2,1)S(1)} async-done(((bf16[16,128,192]{1,2,0:T(8,128)(2,1)}), bf16[16,128,192]{1,2,0:T(8,128)(2,1)S(1)}, u32[]{:S(2)}, u32[]{:S(2)}) %all-to-all-start.2) | async-done | bytes 786464 | tf_op jit(solution)/shard_map/all_to_all | solution.py:330
  465.5 9.8 %collective-permute-done.35 = bf16[1,8,48,1664]{3,2,1,0:T(8,128)(2,1)} collective-permute-done((bf16[1,8,48,1664]{3,2,1,0:T(8,128)(2,1)}, bf16[1,8,48,1664]{3,2,1,0:T(8,128)(2,1)}, u32[]{:S(2)}, u32[]{:S(2)}) %collective-permute-start.35) | collective-permute-done | bytes 1277984 | tf_op jit(solution)/shard_map/ppermute | solution.py:427
  479.0 8.0 collective-permute-done.36
  491.9 29.2 %attend_backward.1 = bf16[2048,320]{1,0:T(8,128)(2,1)} custom-call(bf16[2048,320]{1,0:T(8,128)(2,1)} %bitcast.175, bf16[2048,192]{1,0:T(8,128)(2,1)} %bitcast.183, f32[8,64,768]{2,1,0:T(8,128)} %get-tuple-element.106.flat_ref, f32[8,1,768]{2,1,0:T(1,128)} %get-tuple-element.107.lse_ref, f32[32,2048]{1,0:T(8,128)} %get-tuple-element.233.cos_ref, ...), custom_call_target="tpu_custom_call" | custom-call | tf_op jit(solution)/shard_map/attend_backward/pallas_call | solution.py:174
  522.0 2.6 copy.196
  524.6 3.7 all-to-all-start.3
  531.4 22.4 %collective-permute-done.38 = bf16[48,1664]{1,0:T(8,128)(2,1)S(1)} collective-permute-done((bf16[48,1664]{1,0:T(8,128)(2,1)S(1)}, bf16[48,1664]{1,0:T(8,128)(2,1)S(1)}, u32[]{:S(2)}, u32[]{:S(2)}) %collective-permute-start.38) | collective-permute-done | bytes 159776 | tf_op jit(solution)/shard_map/ppermute | solution.py:363
  553.9 10.6 %collective-permute-start.39 = (bf16[48,1664]{1,0:T(8,128)(2,1)S(1)}, bf16[48,1664]{1,0:T(8,128)(2,1)S(1)}, u32[]{:S(2)}, u32[]{:S(2)}) collective-permute-start(bf16[48,1664]{1,0:T(8,128)(2,1)S(1)} %get-tuple-element.224), channel_id=1, source_target_pairs={{0,4},{1,5},{4,8},{5,9},{8,12},{9,13},{12,14},{13,15},{14,10},{15,... | collective-permute-start | bytes 479240 | tf_op jit(solution)/shard_map/ppermute | solution.py:363
  564.5 8.0 convolution_convert_fusion.1
  574.2 6.3 convolution_convert_fusion
  580.5 6.5 select_bitcast_fusion
  587.6 8.5 %fusion.5 = bf16[1536,1024]{1,0:T(8,128)(2,1)} fusion(bf16[2048,1536]{1,0:T(8,128)(2,1)S(1)} %bitcast.165, bf16[2048,2048]{1,0:T(8,128)(2,1)S(1)} %bitcast.163), kind=kOutput, calls=%fused_computation.17 | convolution fusion | flops 6444023808 | bytes 13631488 | tf_op jit(solution)/shard_map/dot_general | solution.py:51
  596.1 7.7 multiply_reduce_fusion
  604.9 5.2 fusion.8
  615.0 8.4 %add_convert_fusion.1 = bf16[1536,1024]{1,0:T(8,128)(2,1)S(1)} fusion(bf16[1536,1024]{1,0:T(8,128)(2,1)} %collective-permute-done.55, bf16[2048,1536]{1,0:T(8,128)(2,1)S(1)} %bitcast.165, bf16[2048,2048]{1,0:T(8,128)(2,1)S(1)} %bitcast.163), kind=kOutput, calls=%fused_computation.4 | convolution fusion | flops 6447169536 | bytes 16777216 | tf_op jit(solution)/shard_map/dot_general | solution.py:51
  624.5 22.9 %collective-permute-done.58 = bf16[512,1536]{1,0:T(8,128)(2,1)S(1)} collective-permute-done((bf16[512,1536]{1,0:T(8,128)(2,1)S(1)}, bf16[512,1536]{1,0:T(8,128)(2,1)S(1)}, u32[]{:S(2)}, u32[]{:S(2)}) %collective-permute-start.58) | collective-permute-done | bytes 1572896 | tf_op jit(solution)/shard_map/ppermute | solution.py:336
  653.5 38.1 %collective-permute-done.46 = bf16[1,8,48,2688]{3,2,1,0:T(8,128)(2,1)S(1)} collective-permute-done((bf16[1,8,48,2688]{3,2,1,0:T(8,128)(2,1)S(1)}, bf16[1,8,48,2688]{3,2,1,0:T(8,128)(2,1)S(1)}, u32[]{:S(2)}, u32[]{:S(2)}) %collective-permute-start.46) | collective-permute-done | bytes 2064416 | tf_op jit(solution)/shard_map/ppermute | solution.py:427
  694.5 63.4 %collective-permute-done.56 = bf16[1536,1024]{1,0:T(8,128)(2,1)S(1)} collective-permute-done((bf16[1536,1024]{1,0:T(8,128)(2,1)S(1)}, bf16[1536,1024]{1,0:T(8,128)(2,1)S(1)}, u32[]{:S(2)}, u32[]{:S(2)}) %collective-permute-start.56) | collective-permute-done | bytes 3145760 | tf_op jit(solution)/shard_map/ppermute | solution.py:336
  764.6 3.4 slice_bitcast_fusion.2
  768.0 15.6 %collective-permute-done.48 = bf16[48,2688]{1,0:T(8,128)(2,1)S(1)} collective-permute-done((bf16[48,2688]{1,0:T(8,128)(2,1)S(1)}, bf16[48,2688]{1,0:T(8,128)(2,1)S(1)}, u32[]{:S(2)}, u32[]{:S(2)}) %collective-permute-start.48) | collective-permute-done | bytes 258080 | tf_op jit(solution)/shard_map/ppermute | solution.py:363
  789.3 2.7 collective-permute-done.49
  (359 shorter events, 145.5 us)
Async XLA Ops:
  7.2 96.3 %all-gather.3.cloned.1.call-start = ((), (), s32[]{:S(2)}) async-start(), calls=%async_computation.4 | async-start | bytes 8515584 | tf_op jit(solution)/shard_map/all_gather | solution.py:326
  12.3 225.4 %all-gather.5.cloned.1.call-start = ((), (), s32[]{:S(2)}) async-start(), calls=%async_computation.5 | async-start | bytes 5271552 | tf_op jit(solution)/shard_map/all_gather | solution.py:326
  14.6 26.8 %collective-permute-start = (bf16[256,1664]{1,0:T(8,128)(2,1)S(1)}, bf16[256,1664]{1,0:T(8,128)(2,1)}, u32[]{:S(2)}, u32[]{:S(2)}) collective-permute-start(bf16[256,1664]{1,0:T(8,128)(2,1)S(1)} %concatenate.39.refs_1_), channel_id=1, source_target_pairs={{0,4},{1,5},{4,8},{5,9},{8,12},{9,13},{12,14},{13,15},{14,10},{15,... | collective-permute-start | bytes 2555912 | tf_op jit(solution)/shard_map/ppermute | solution.py:363
  17.7 26.3 %collective-permute-start.1 = (bf16[256,1664]{1,0:T(8,128)(2,1)S(1)}, bf16[256,1664]{1,0:T(8,128)(2,1)}, u32[]{:S(2)}, u32[]{:S(2)}) collective-permute-start(bf16[256,1664]{1,0:T(8,128)(2,1)S(1)} %concatenate.39.refs_1_), channel_id=1, source_target_pairs={{4,0},{5,1},{8,4},{9,5},{12,8},{13,9},{14,12},{15,13},{10,14},{11,... | collective-permute-start | bytes 2555912 | tf_op jit(solution)/shard_map/ppermute | solution.py:364
  41.4 31.3 %collective-permute-start.2 = (bf16[256,1664]{1,0:T(8,128)(2,1)}, bf16[256,1664]{1,0:T(8,128)(2,1)}, u32[]{:S(2)}, u32[]{:S(2)}) collective-permute-start(bf16[256,1664]{1,0:T(8,128)(2,1)} %collective-permute-done.refs_2_), channel_id=1, source_target_pairs={{0,4},{1,5},{4,8},{5,9},{8,12},{9,13},{12,14},{13,15},{14,10},{15,... | collective-permute-start | bytes 2555912 | tf_op jit(solution)/shard_map/ppermute | solution.py:363
  44.0 30.9 %collective-permute-start.3 = (bf16[256,1664]{1,0:T(8,128)(2,1)}, bf16[256,1664]{1,0:T(8,128)(2,1)}, u32[]{:S(2)}, u32[]{:S(2)}) collective-permute-start(bf16[256,1664]{1,0:T(8,128)(2,1)} %collective-permute-done.1.refs_3_), channel_id=1, source_target_pairs={{4,0},{5,1},{8,4},{9,5},{12,8},{13,9},{14,12},{15,13},{10,14},{11,... | collective-permute-start | bytes 2555912 | tf_op jit(solution)/shard_map/ppermute | solution.py:364
  116.2 38.0 %all-to-all-start = ((bf16[16,128,320]{1,2,0:T(8,128)(2,1)}), bf16[16,128,320]{1,2,0:T(8,128)(2,1)S(1)}, u32[]{:S(2)}, u32[]{:S(2)}) async-start(bf16[16,128,320]{1,2,0:T(8,128)(2,1)} %copy.184), calls=%async_computation | async-start | bytes 2621440 | tf_op jit(solution)/shard_map/all_to_all | solution.py:330
  121.7 109.9 %collective-permute-start.4 = (bf16[1,1536,1024]{2,1,0:T(8,128)(2,1)}, bf16[1,1536,1024]{2,1,0:T(8,128)(2,1)}, u32[]{:S(2)}, u32[]{:S(2)}) collective-permute-start(bf16[1,1536,1024]{2,1,0:T(8,128)(2,1)} %constant_dynamic-update-slice_fusion), channel_id=1, source_target_pairs={{0,1},{1,0},{2,3},{3,2},{4,5},{5,4},{6,7},{7,6},{8,9},{9,8},{10,11... | collective-permute-start | bytes 9437192 | tf_op jit(solution)/shard_map/ppermute | solution.py:343
  122.1 72.1 %collective-permute-start.5 = (bf16[1,512,1536]{2,1,0:T(8,128)(2,1)}, bf16[1,512,1536]{2,1,0:T(8,128)(2,1)}, u32[]{:S(2)}, u32[]{:S(2)}) collective-permute-start(bf16[1,512,1536]{2,1,0:T(8,128)(2,1)} %param.23), channel_id=1, source_target_pairs={{0,1},{1,0},{2,3},{3,2},{4,5},{5,4},{6,7},{7,6},{8,9},{9,8},{10,11... | collective-permute-start | bytes 4718600 | tf_op jit(solution)/shard_map/ppermute | solution.py:343
  180.5 58.5 %all-to-all-start.1 = ((bf16[16,128,192]{1,2,0:T(8,128)(2,1)}), bf16[16,128,192]{1,2,0:T(8,128)(2,1)}, u32[]{:S(2)}, u32[]{:S(2)}) async-start(bf16[16,128,192]{1,2,0:T(8,128)(2,1)} %copy.186), calls=%async_computation.1 | async-start | bytes 1572864 | tf_op jit(solution)/shard_map/all_to_all | solution.py:330
  190.0 32.1 %collective-permute-start.14 = (bf16[256,1664]{1,0:T(8,128)(2,1)}, bf16[256,1664]{1,0:T(8,128)(2,1)}, u32[]{:S(2)}, u32[]{:S(2)}) collective-permute-start(bf16[256,1664]{1,0:T(8,128)(2,1)} %collective-permute-done.2.refs_2_), channel_id=1, source_target_pairs={{0,4},{1,5},{4,8},{5,9},{8,12},{9,13},{12,14},{13,15},{14,10},{15,... | collective-permute-start | bytes 2555912 | tf_op jit(solution)/shard_map/ppermute | solution.py:363
  191.9 37.9 %collective-permute-start.16 = (bf16[256,1664]{1,0:T(8,128)(2,1)}, bf16[256,1664]{1,0:T(8,128)(2,1)}, u32[]{:S(2)}, u32[]{:S(2)}) collective-permute-start(bf16[256,1664]{1,0:T(8,128)(2,1)} %collective-permute-done.3.refs_3_), channel_id=1, source_target_pairs={{4,0},{5,1},{8,4},{9,5},{12,8},{13,9},{14,12},{15,13},{10,14},{11,... | collective-permute-start | bytes 2555912 | tf_op jit(solution)/shard_map/ppermute | solution.py:364
  223.9 112.7 %collective-permute-start.15 = (bf16[128,1664]{1,0:T(8,128)(2,1)}, bf16[128,1664]{1,0:T(8,128)(2,1)}, u32[]{:S(2)}, u32[]{:S(2)}) collective-permute-start(bf16[128,1664]{1,0:T(8,128)(2,1)} %slice.142), channel_id=1, source_target_pairs={{0,4},{1,5},{4,8},{5,9},{8,12},{9,13},{12,14},{13,15},{14,10},{15,... | collective-permute-start | bytes 1277960 | tf_op jit(solution)/shard_map/ppermute | solution.py:363
  231.6 105.0 %collective-permute-start.17 = (bf16[128,1664]{1,0:T(8,128)(2,1)}, bf16[128,1664]{1,0:T(8,128)(2,1)}, u32[]{:S(2)}, u32[]{:S(2)}) collective-permute-start(bf16[128,1664]{1,0:T(8,128)(2,1)} %slice.143), channel_id=1, source_target_pairs={{4,0},{5,1},{8,4},{9,5},{12,8},{13,9},{14,12},{15,13},{10,14},{11,... | collective-permute-start | bytes 1277960 | tf_op jit(solution)/shard_map/ppermute | solution.py:364
  245.9 19.5 %collective-permute-start.10 = (bf16[256,1536]{1,0:T(8,128)(2,1)S(1)}, bf16[256,1536]{1,0:T(8,128)(2,1)}, u32[]{:S(2)}, u32[]{:S(2)}) collective-permute-start(bf16[256,1536]{1,0:T(8,128)(2,1)S(1)} %multiply_convert_fusion.refs_0_), channel_id=1, source_target_pairs={{4,0},{5,1},{8,4},{9,5},{12,8},{13,9},{14,12},{15,13},{10,14},{11,... | collective-permute-start | bytes 2359304 | tf_op jit(solution)/shard_map/ppermute | solution.py:364
  265.5 24.0 %collective-permute-start.11 = (bf16[256,1536]{1,0:T(8,128)(2,1)}, bf16[256,1536]{1,0:T(8,128)(2,1)}, u32[]{:S(2)}, u32[]{:S(2)}) collective-permute-start(bf16[256,1536]{1,0:T(8,128)(2,1)} %collective-permute-done.10.refs_1_), channel_id=1, source_target_pairs={{4,0},{5,1},{8,4},{9,5},{12,8},{13,9},{14,12},{15,13},{10,14},{11,... | collective-permute-start | bytes 2359304 | tf_op jit(solution)/shard_map/ppermute | solution.py:364
  268.1 23.2 %collective-permute-start.7 = (bf16[256,1536]{1,0:T(8,128)(2,1)S(1)}, bf16[256,1536]{1,0:T(8,128)(2,1)}, u32[]{:S(2)}, u32[]{:S(2)}) collective-permute-start(bf16[256,1536]{1,0:T(8,128)(2,1)S(1)} %collective-permute-done.6.refs_0_), channel_id=1, source_target_pairs={{0,4},{1,5},{4,8},{5,9},{8,12},{9,13},{12,14},{13,15},{14,10},{15,... | collective-permute-start | bytes 2359304 | tf_op jit(solution)/shard_map/ppermute | solution.py:363
  289.5 22.5 %collective-permute-start.12 = (bf16[256,1536]{1,0:T(8,128)(2,1)}, bf16[256,1536]{1,0:T(8,128)(2,1)S(1)}, u32[]{:S(2)}, u32[]{:S(2)}) collective-permute-start(bf16[256,1536]{1,0:T(8,128)(2,1)} %collective-permute-done.11.refs_1_), channel_id=1, source_target_pairs={{4,0},{5,1},{8,4},{9,5},{12,8},{13,9},{14,12},{15,13},{10,14},{11,... | collective-permute-start | bytes 2359304 | tf_op jit(solution)/shard_map/ppermute | solution.py:364
  291.3 23.3 %collective-permute-start.8 = (bf16[256,1536]{1,0:T(8,128)(2,1)}, bf16[256,1536]{1,0:T(8,128)(2,1)S(1)}, u32[]{:S(2)}, u32[]{:S(2)}) collective-permute-start(bf16[256,1536]{1,0:T(8,128)(2,1)} %collective-permute-done.7.refs_0_), channel_id=1, source_target_pairs={{0,4},{1,5},{4,8},{5,9},{8,12},{9,13},{12,14},{13,15},{14,10},{15,... | collective-permute-start | bytes 2359304 | tf_op jit(solution)/shard_map/ppermute | solution.py:363
  312.8 23.8 %collective-permute-start.13 = (bf16[128,1536]{1,0:T(8,128)(2,1)}, bf16[128,1536]{1,0:T(8,128)(2,1)S(1)}, u32[]{:S(2)}, u32[]{:S(2)}) collective-permute-start(bf16[128,1536]{1,0:T(8,128)(2,1)} %slice.141), channel_id=1, source_target_pairs={{4,0},{5,1},{8,4},{9,5},{12,8},{13,9},{14,12},{15,13},{10,14},{11,... | collective-permute-start | bytes 1179656 | tf_op jit(solution)/shard_map/ppermute | solution.py:364
  315.4 21.2 %collective-permute-start.9 = (bf16[128,1536]{1,0:T(8,128)(2,1)}, bf16[128,1536]{1,0:T(8,128)(2,1)}, u32[]{:S(2)}, u32[]{:S(2)}) collective-permute-start(bf16[128,1536]{1,0:T(8,128)(2,1)} %slice.140), channel_id=1, source_target_pairs={{0,4},{1,5},{4,8},{5,9},{8,12},{9,13},{12,14},{13,15},{14,10},{15,... | collective-permute-start | bytes 1179656 | tf_op jit(solution)/shard_map/ppermute | solution.py:363
  360.3 18.9 %collective-permute-start.19 = (bf16[256,1664]{1,0:T(8,128)(2,1)S(1)}, bf16[256,1664]{1,0:T(8,128)(2,1)S(1)}, u32[]{:S(2)}, u32[]{:S(2)}) collective-permute-start(bf16[256,1664]{1,0:T(8,128)(2,1)S(1)} %pad_add_fusion.1), channel_id=1, source_target_pairs={{0,4},{1,5},{4,8},{5,9},{8,12},{9,13},{12,14},{13,15},{14,10},{15,... | collective-permute-start | bytes 2555912 | tf_op jit(solution)/shard_map/ppermute | solution.py:363
  360.8 19.0 %collective-permute-start.23 = (bf16[256,1664]{1,0:T(8,128)(2,1)S(1)}, bf16[256,1664]{1,0:T(8,128)(2,1)S(1)}, u32[]{:S(2)}, u32[]{:S(2)}) collective-permute-start(bf16[256,1664]{1,0:T(8,128)(2,1)S(1)} %pad_add_fusion), channel_id=1, source_target_pairs={{4,0},{5,1},{8,4},{9,5},{12,8},{13,9},{14,12},{15,13},{10,14},{11,... | collective-permute-start | bytes 2555912 | tf_op jit(solution)/shard_map/ppermute | solution.py:364
  379.4 18.9 %collective-permute-start.20 = (bf16[256,1664]{1,0:T(8,128)(2,1)S(1)}, bf16[256,1664]{1,0:T(8,128)(2,1)S(1)}, u32[]{:S(2)}, u32[]{:S(2)}) collective-permute-start(bf16[256,1664]{1,0:T(8,128)(2,1)S(1)} %add.371), channel_id=1, source_target_pairs={{0,4},{1,5},{4,8},{5,9},{8,12},{9,13},{12,14},{13,15},{14,10},{15,... | collective-permute-start | bytes 2555912 | tf_op jit(solution)/shard_map/ppermute | solution.py:363
  380.0 18.9 %collective-permute-start.24 = (bf16[256,1664]{1,0:T(8,128)(2,1)S(1)}, bf16[256,1664]{1,0:T(8,128)(2,1)S(1)}, u32[]{:S(2)}, u32[]{:S(2)}) collective-permute-start(bf16[256,1664]{1,0:T(8,128)(2,1)S(1)} %add.375), channel_id=1, source_target_pairs={{4,0},{5,1},{8,4},{9,5},{12,8},{13,9},{14,12},{15,13},{10,14},{11,... | collective-permute-start | bytes 2555912 | tf_op jit(solution)/shard_map/ppermute | solution.py:364
  435.2 23.2 %all-to-all-start.2 = ((bf16[16,128,192]{1,2,0:T(8,128)(2,1)}), bf16[16,128,192]{1,2,0:T(8,128)(2,1)S(1)}, u32[]{:S(2)}, u32[]{:S(2)}) async-start(bf16[16,128,192]{1,2,0:T(8,128)(2,1)} %bitcast.14), calls=%async_computation.2 | async-start | bytes 1572864 | tf_op jit(solution)/shard_map/all_to_all | solution.py:330
  444.6 30.7 %collective-permute-start.35 = (bf16[1,8,48,1664]{3,2,1,0:T(8,128)(2,1)}, bf16[1,8,48,1664]{3,2,1,0:T(8,128)(2,1)}, u32[]{:S(2)}, u32[]{:S(2)}) collective-permute-start(bf16[1,8,48,1664]{3,2,1,0:T(8,128)(2,1)} %constant_dynamic-slice_fusion), channel_id=1, source_target_pairs={{0,16},{16,0},{1,17},{17,1},{2,18},{18,2},{3,19},{19,3},{4,20},{20... | collective-permute-start | bytes 3833864 | tf_op jit(solution)/shard_map/ppermute | solution.py:427
  462.3 58.8 %collective-permute-start.29 = (bf16[256,1536]{1,0:T(8,128)(2,1)}, bf16[256,1536]{1,0:T(8,128)(2,1)S(1)}, u32[]{:S(2)}, u32[]{:S(2)}) collective-permute-start(bf16[256,1536]{1,0:T(8,128)(2,1)} %add.383), channel_id=1, source_target_pairs={{4,0},{5,1},{8,4},{9,5},{12,8},{13,9},{14,12},{15,13},{10,14},{11,... | collective-permute-start | bytes 2359304 | tf_op jit(solution)/shard_map/ppermute | solution.py:364
  464.4 56.7 %collective-permute-start.28 = (bf16[256,1536]{1,0:T(8,128)(2,1)}, bf16[256,1536]{1,0:T(8,128)(2,1)}, u32[]{:S(2)}, u32[]{:S(2)}) collective-permute-start(bf16[256,1536]{1,0:T(8,128)(2,1)} %add.382), channel_id=1, source_target_pairs={{0,4},{1,5},{4,8},{5,9},{8,12},{9,13},{12,14},{13,15},{14,10},{15,... | collective-permute-start | bytes 2359304 | tf_op jit(solution)/shard_map/ppermute | solution.py:363
  487.8 40.5 %collective-permute-start.37 = (bf16[48,1664]{1,0:T(8,128)(2,1)}, bf16[48,1664]{1,0:T(8,128)(2,1)S(1)}, u32[]{:S(2)}, u32[]{:S(2)}) collective-permute-start(bf16[48,1664]{1,0:T(8,128)(2,1)} %get-tuple-element.228), channel_id=1, source_target_pairs={{0,4},{1,5},{4,8},{5,9},{8,12},{9,13},{12,14},{13,15},{14,10},{15,... | collective-permute-start | bytes 479240 | tf_op jit(solution)/shard_map/ppermute | solution.py:363
  488.4 40.0 %collective-permute-start.41 = (bf16[48,1664]{1,0:T(8,128)(2,1)}, bf16[48,1664]{1,0:T(8,128)(2,1)}, u32[]{:S(2)}, u32[]{:S(2)}) collective-permute-start(bf16[48,1664]{1,0:T(8,128)(2,1)} %get-tuple-element.229), channel_id=1, source_target_pairs={{4,0},{5,1},{8,4},{9,5},{12,8},{13,9},{14,12},{15,13},{10,14},{11,... | collective-permute-start | bytes 479240 | tf_op jit(solution)/shard_map/ppermute | solution.py:364
  524.6 48.0 %all-to-all-start.3 = ((bf16[16,128,320]{1,2,0:T(8,128)(2,1)}), bf16[16,128,320]{1,2,0:T(8,128)(2,1)S(1)}, u32[]{:S(2)}, u32[]{:S(2)}) async-start(bf16[16,128,320]{1,2,0:T(8,128)(2,1)} %copy.196), calls=%async_computation.3 | async-start | bytes 2621440 | tf_op jit(solution)/shard_map/all_to_all | solution.py:330
  529.3 24.5 %collective-permute-start.38 = (bf16[48,1664]{1,0:T(8,128)(2,1)S(1)}, bf16[48,1664]{1,0:T(8,128)(2,1)S(1)}, u32[]{:S(2)}, u32[]{:S(2)}) collective-permute-start(bf16[48,1664]{1,0:T(8,128)(2,1)S(1)} %get-tuple-element.226), channel_id=1, source_target_pairs={{0,4},{1,5},{4,8},{5,9},{8,12},{9,13},{12,14},{13,15},{14,10},{15,... | collective-permute-start | bytes 479240 | tf_op jit(solution)/shard_map/ppermute | solution.py:363
  531.2 22.7 %collective-permute-start.42 = (bf16[48,1664]{1,0:T(8,128)(2,1)S(1)}, bf16[48,1664]{1,0:T(8,128)(2,1)S(1)}, u32[]{:S(2)}, u32[]{:S(2)}) collective-permute-start(bf16[48,1664]{1,0:T(8,128)(2,1)S(1)} %get-tuple-element.227), channel_id=1, source_target_pairs={{4,0},{5,1},{8,4},{9,5},{12,8},{13,9},{14,12},{15,13},{10,14},{11,... | collective-permute-start | bytes 479240 | tf_op jit(solution)/shard_map/ppermute | solution.py:364
  572.5 32.3 %collective-permute-start.57 = (bf16[512,1536]{1,0:T(8,128)(2,1)}, bf16[512,1536]{1,0:T(8,128)(2,1)}, u32[]{:S(2)}, u32[]{:S(2)}) collective-permute-start(bf16[512,1536]{1,0:T(8,128)(2,1)} %convolution_convert_fusion.1), channel_id=1, source_target_pairs={{0,1},{1,0},{2,3},{3,2},{4,5},{5,4},{6,7},{7,6},{8,9},{9,8},{10,11... | collective-permute-start | bytes 4718600 | tf_op jit(solution)/shard_map/ppermute | solution.py:343
  587.0 24.2 %collective-permute-start.44 = (bf16[2,8,48,2560]{3,2,1,0:T(8,128)(2,1)}, bf16[2,8,48,2560]{3,2,1,0:T(8,128)(2,1)}, u32[]{:S(2)}, u32[]{:S(2)}) collective-permute-start(bf16[2,8,48,2560]{3,2,1,0:T(8,128)(2,1)} %select_bitcast_fusion), channel_id=1, source_target_pairs={{0,1},{1,0},{2,3},{3,2},{4,5},{5,4},{6,7},{7,6},{8,9},{9,8},{10,11... | collective-permute-start | bytes 11796488 | tf_op jit(solution)/shard_map/ppermute | solution.py:343
  596.1 18.9 %collective-permute-start.55 = (bf16[1536,1024]{1,0:T(8,128)(2,1)}, bf16[1536,1024]{1,0:T(8,128)(2,1)}, u32[]{:S(2)}, u32[]{:S(2)}) collective-permute-start(bf16[1536,1024]{1,0:T(8,128)(2,1)} %fusion.5), channel_id=1, source_target_pairs={{0,1},{1,0},{2,3},{3,2},{4,5},{5,4},{6,7},{7,6},{8,9},{9,8},{10,11... | collective-permute-start | bytes 9437192 | tf_op jit(solution)/shard_map/ppermute | solution.py:343
  610.1 37.3 %collective-permute-start.58 = (bf16[512,1536]{1,0:T(8,128)(2,1)S(1)}, bf16[512,1536]{1,0:T(8,128)(2,1)S(1)}, u32[]{:S(2)}, u32[]{:S(2)}) collective-permute-start(bf16[512,1536]{1,0:T(8,128)(2,1)S(1)} %fusion.8), channel_id=1, source_target_pairs={{0,16},{16,0},{1,17},{17,1},{2,18},{18,2},{3,19},{19,3},{4,20},{20... | collective-permute-start | bytes 4718600 | tf_op jit(solution)/shard_map/ppermute | solution.py:336
  613.9 77.7 %collective-permute-start.46 = (bf16[1,8,48,2688]{3,2,1,0:T(8,128)(2,1)S(1)}, bf16[1,8,48,2688]{3,2,1,0:T(8,128)(2,1)S(1)}, u32[]{:S(2)}, u32[]{:S(2)}) collective-permute-start(bf16[1,8,48,2688]{3,2,1,0:T(8,128)(2,1)S(1)} %fusion.14), channel_id=1, source_target_pairs={{0,16},{16,0},{1,17},{17,1},{2,18},{18,2},{3,19},{19,3},{4,20},{20... | collective-permute-start | bytes 6193160 | tf_op jit(solution)/shard_map/ppermute | solution.py:427
  623.4 134.5 %collective-permute-start.56 = (bf16[1536,1024]{1,0:T(8,128)(2,1)S(1)}, bf16[1536,1024]{1,0:T(8,128)(2,1)S(1)}, u32[]{:S(2)}, u32[]{:S(2)}) collective-permute-start(bf16[1536,1024]{1,0:T(8,128)(2,1)S(1)} %add_convert_fusion.1), channel_id=1, source_target_pairs={{0,16},{16,0},{1,17},{17,1},{2,18},{18,2},{3,19},{19,3},{4,20},{20... | collective-permute-start | bytes 9437192 | tf_op jit(solution)/shard_map/ppermute | solution.py:336
  651.0 108.4 %collective-permute-start.30 = (bf16[256,1536]{1,0:T(8,128)(2,1)S(1)}, bf16[256,1536]{1,0:T(8,128)(2,1)S(1)}, u32[]{:S(2)}, u32[]{:S(2)}) collective-permute-start(bf16[256,1536]{1,0:T(8,128)(2,1)S(1)} %add.384), channel_id=1, source_target_pairs={{0,4},{1,5},{4,8},{5,9},{8,12},{9,13},{12,14},{13,15},{14,10},{15,... | collective-permute-start | bytes 2359304 | tf_op jit(solution)/shard_map/ppermute | solution.py:363
  653.3 108.4 %collective-permute-start.32 = (bf16[256,1536]{1,0:T(8,128)(2,1)S(1)}, bf16[256,1536]{1,0:T(8,128)(2,1)S(1)}, u32[]{:S(2)}, u32[]{:S(2)}) collective-permute-start(bf16[256,1536]{1,0:T(8,128)(2,1)S(1)} %add.387), channel_id=1, source_target_pairs={{4,0},{5,1},{8,4},{9,5},{12,8},{13,9},{14,12},{15,13},{10,14},{11,... | collective-permute-start | bytes 2359304 | tf_op jit(solution)/shard_map/ppermute | solution.py:364
  692.3 70.1 %collective-permute-start.51 = (bf16[48,1408]{1,0:T(8,128)(2,1)S(1)}, bf16[48,1408]{1,0:T(8,128)(2,1)S(1)}, u32[]{:S(2)}, u32[]{:S(2)}) collective-permute-start(bf16[48,1408]{1,0:T(8,128)(2,1)S(1)} %split.19), channel_id=1, source_target_pairs={{4,0},{5,1},{8,4},{9,5},{12,8},{13,9},{14,12},{15,13},{10,14},{11,... | collective-permute-start | bytes 405512 | tf_op jit(solution)/shard_map/ppermute | solution.py:364
  694.0 68.4 %collective-permute-start.47 = (bf16[48,1280]{1,0:T(8,128)(2,1)S(1)}, bf16[48,1280]{1,0:T(8,128)(2,1)S(1)}, u32[]{:S(2)}, u32[]{:S(2)}) collective-permute-start(bf16[48,1280]{1,0:T(8,128)(2,1)S(1)} %split.18), channel_id=1, source_target_pairs={{0,4},{1,5},{4,8},{5,9},{8,12},{9,13},{12,14},{13,15},{14,10},{15,... | collective-permute-start | bytes 368648 | tf_op jit(solution)/shard_map/ppermute | solution.py:363
  759.6 28.2 %collective-permute-start.31 = (bf16[256,1536]{1,0:T(8,128)(2,1)S(1)}, bf16[256,1536]{1,0:T(8,128)(2,1)S(1)}, u32[]{:S(2)}, u32[]{:S(2)}) collective-permute-start(bf16[256,1536]{1,0:T(8,128)(2,1)S(1)} %add.385), channel_id=1, source_target_pairs={{0,4},{1,5},{4,8},{5,9},{8,12},{9,13},{12,14},{13,15},{14,10},{15,... | collective-permute-start | bytes 2359304 | tf_op jit(solution)/shard_map/ppermute | solution.py:363
  761.9 25.9 %collective-permute-start.33 = (bf16[256,1536]{1,0:T(8,128)(2,1)S(1)}, bf16[256,1536]{1,0:T(8,128)(2,1)S(1)}, u32[]{:S(2)}, u32[]{:S(2)}) collective-permute-start(bf16[256,1536]{1,0:T(8,128)(2,1)S(1)} %add.388), channel_id=1, source_target_pairs={{4,0},{5,1},{8,4},{9,5},{12,8},{13,9},{14,12},{15,13},{10,14},{11,... | collective-permute-start | bytes 2359304 | tf_op jit(solution)/shard_map/ppermute | solution.py:364
  762.5 21.1 %collective-permute-start.48 = (bf16[48,2688]{1,0:T(8,128)(2,1)S(1)}, bf16[48,2688]{1,0:T(8,128)(2,1)S(1)}, u32[]{:S(2)}, u32[]{:S(2)}) collective-permute-start(bf16[48,2688]{1,0:T(8,128)(2,1)S(1)} %get-tuple-element.222), channel_id=1, source_target_pairs={{0,4},{1,5},{4,8},{5,9},{8,12},{9,13},{12,14},{13,15},{14,10},{15,... | collective-permute-start | bytes 774152 | tf_op jit(solution)/shard_map/ppermute | solution.py:363
  764.1 21.5 %collective-permute-start.52 = (bf16[48,2688]{1,0:T(8,128)(2,1)S(1)}, bf16[48,2688]{1,0:T(8,128)(2,1)S(1)}, u32[]{:S(2)}, u32[]{:S(2)}) collective-permute-start(bf16[48,2688]{1,0:T(8,128)(2,1)S(1)} %get-tuple-element.223), channel_id=1, source_target_pairs={{4,0},{5,1},{8,4},{9,5},{12,8},{13,9},{14,12},{15,13},{10,14},{11,... | collective-permute-start | bytes 774152 | tf_op jit(solution)/shard_map/ppermute | solution.py:364
  (80 other events, 1141.2 us)
Sparse Core Ops, SparseCore 0:
  12.4 91.0 all-gather.2
  107.0 74.5 all-gather.4

commit v4 on v3

--- a/solution.py
+++ b/solution.py
@@ -322,10 +322,6 @@
     return results[:parts], results[parts : 2 * parts], results[2 * parts :]
 
 
-def gather_dense(values):
-    return lax.all_gather(values, ("head", "blk"), axis=0, tiled=True)
-
-
 def exchange(values):
     return lax.all_to_all(values, "blk", split_axis=0, concat_axis=0, tiled=True)
 
@@ -365,15 +361,16 @@
     return len(order), send_on, send_back
 
 
-def ring_gather(values):
+def ring_gather(values, axis=0):
     length, send_on, send_back = ring_steps()
-    half = values.shape[0] // 2
+    half = values.shape[axis] // 256 * 128
     behind = ahead = values
     pairs = []
     for _ in range(length // 2 - 1):
         behind, ahead = send_on(behind), send_back(ahead)
         pairs.append((behind, ahead))
-    behind, ahead = behind[:half], ahead[half:]
+    behind = lax.slice_in_dim(behind, 0, half, axis=axis)
+    ahead = lax.slice_in_dim(ahead, half, ahead.shape[axis], axis=axis)
     return pairs, (send_on(behind), send_back(ahead))
 
 
@@ -414,6 +411,64 @@
         return wide + self.onward.astype(jnp.float32) + self.back.astype(jnp.float32)
 
 
+def ring_chip(offset):
+    chips = lax.axis_size("blk") // 2
+    chip = lax.axis_index("blk") // 2
+    place = jnp.where(chip % 2 == 0, chip // 2, chips - 1 - chip // 2)
+    target = (place + offset) % chips
+    return jnp.where(target < chips // 2, 2 * target, 2 * (chips - 1 - target) + 1)
+
+
+def all_heads(values):
+    heads = lax.axis_size("head")
+    head = lax.axis_index("head")
+    place = lambda found, at: lax.dynamic_update_index_in_dim(result, found, at, 0)
+    result = jnp.zeros((heads, *values.shape), values.dtype)
+    result = place(values, head)
+    for turn in range(1, heads):
+        other = lax.ppermute(
+            values, "head", [(k, (k + turn) % heads) for k in range(heads)]
+        )
+        result = place(other, (head - turn) % heads)
+    return result
+
+
+def ring_pieces(block, axis):
+    pairs, opposite = ring_gather(block, axis)
+    found = [(0, block)]
+    for k, (behind, ahead) in enumerate(pairs):
+        found += [(-k - 1, behind), (k + 1, ahead)]
+    return found + [(len(pairs) + 1, jnp.concatenate(opposite, axis=axis))]
+
+
+def dense_gather(shard):
+    chips = lax.axis_size("blk") // 2
+    heads = lax.axis_size("head")
+    core = lax.axis_index("blk") % 2
+    rows, columns = shard.shape
+    block = all_heads(shard).reshape(heads * rows, columns)
+    full = jnp.zeros((heads, chips, 2, rows, columns), shard.dtype)
+    for offset, piece in ring_pieces(block, 1):
+        for side, part in ((core, piece), (1 - core, partner(piece))):
+            full = lax.dynamic_update_slice(
+                full, part.reshape(heads, 1, 1, rows, columns), (0, ring_chip(offset), side, 0, 0)
+            )
+    return full.reshape(-1, columns)
+
+
+def dense_gather_late(shard):
+    chips = lax.axis_size("blk") // 2
+    rows, columns = shard.shape
+    found = jnp.zeros((chips, rows, columns), shard.dtype)
+    for offset, piece in ring_pieces(shard, 1):
+        found = lax.dynamic_update_slice(found, piece[None], (ring_chip(offset), 0, 0))
+    found = all_heads(found)
+    other = partner(found)
+    even = lax.axis_index("blk") % 2 == 0
+    pair = [jnp.where(even, found, other), jnp.where(even, other, found)]
+    return jnp.stack(pair, axis=2).reshape(-1, columns)
+
+
 def head_share(values):
     heads, rows = lax.axis_size("head"), values.shape[0] // lax.axis_size("head")
     head = lax.axis_index("head")
@@ -448,10 +503,7 @@
         self.mine = jnp.concatenate([self.mine, self.core_sum(values)], axis=3)
 
     def block(self, offset):
-        chip, turns = self.index // 2, self.chips // 2
-        place = jnp.where(chip % 2 == 0, chip // 2, self.chips - 1 - chip // 2)
-        target = (place + offset) % self.chips
-        chip = jnp.where(target < turns, 2 * target, 2 * (self.chips - 1 - target) + 1)
+        chip = ring_chip(offset)
         heads, columns = self.mine.shape[0], self.mine.shape[3]
         piece = lax.dynamic_slice(self.mine, (0, chip, 0, 0), (heads, 1, self.rows, columns))
         return piece.reshape(heads * self.rows, columns)
@@ -571,8 +623,8 @@
         ],
         axis=2,
     ).reshape(part_rows, groups * span)
-    full_mixed = gather_dense(with_lanes(mixed_weights, gain_attn[:, None]))
-    full_out = gather_dense(
+    full_mixed = dense_gather(with_lanes(mixed_weights, gain_attn[:, None]))
+    full_out = dense_gather_late(
         with_lanes(w_out, jnp.concatenate([w_router, gain_moe[:, None]], axis=1))
     )
     router = full_out[:, width:]
@@ -587,10 +639,10 @@
     d_out = grad_out.reshape(token_rows, width)
     grads_own = with_lanes(d_out.astype(jnp.bfloat16), chosen)
     grads_pairs, grads_opposite = ring_gather(grads_own)
-    full_mixed = after(full_mixed, grads_pairs[:2])
     w_lin = jnp.concatenate([w_gate, w_up], axis=2)
-    both_lin = jnp.concatenate([w_lin, partner(w_lin)], axis=0)
-    both_down = jnp.concatenate([w_down, partner(w_down)], axis=0)
+    other_lin, other_down = partner(w_lin), partner(w_down)
+    both_lin = jnp.concatenate([w_lin, other_lin], axis=0)
+    both_down = jnp.concatenate([w_down, other_down], axis=0)
 
     residual = tokens.astype(jnp.float32).reshape(token_rows, width)
     inverse_one = rms_scale(residual)
@@ -612,7 +664,8 @@
     pair_qkv = to_pairs(packed, span)
     pair_attended, flat, log_total = attend_forward(pair_qkv, group)
     attended = to_tokens(pair_attended, lanes)
-    middle = residual + matmul(attended, full_out)[:, :width]
+    branch = matmul(attended, full_out)[:, :width]
+    middle = residual + branch
     inverse_two = rms_scale(middle)
     normed_two = (middle * inverse_two * gain_second).astype(jnp.bfloat16)
     logits = matmul(normed_two, full_router)

time: 820 us -> 825 us (level)
  waiting for transfers between devices: 392 us -> 364 us
  local copies, waits for them, and re-layouts: 53.3 us -> 80.8 us
  starting transfers between devices: 95.2 us -> 115 us
  between operations: 15.5 us -> 2.2 us
    all_gather x2 -> x0, waiting for transfers between devices: 28.6 us -> none  [gather_dense(): return lax.all_gather(values, ('head', 'blk'), axis=0, tiled=True)]
    all_to_all x4, waiting for transfers between devices: 44.8 us -> 19.1 us  [exchange(): lax.all_to_all(values, 'blk', split_axis=0, concat_axis=0, tiled=True)]
    ppermute x24 -> x32, starting transfers between devices: 39.8 us -> 64.8 us  [ring_steps(): send_on = lambda values: lax.ppermute(values, 'blk', onward)]
    dynamic_update_slice x0 -> x27, local copies, waits for them, and re-layouts: none -> 19.8 us  [the longest x16 13.6 us: dense_gather(): lax.dynamic_update_slice(full, part.reshape(heads, 1, 1, rows, columns),...]
    ppermute x24 -> x32, waiting for transfers between devices: 177 us -> 194 us  [ring_steps(): send_on = lambda values: lax.ppermute(values, 'blk', onward)]
    ppermute x24 -> x32, starting transfers between devices: 27.5 us -> 21.8 us  [ring_steps(): send_back = lambda values: lax.ppermute(values, 'blk', back)]
  transfers between devices with their start and end apart: 65 -> 90, of which waited for: 26 -> 34; matrix products, arithmetic and copies ran while one was open for 17% -> 20% of each run, Pallas kernels for 16% -> 16%
where the time goes in v4:
time: 825 us; the launch traced here: 816 us
  waiting for transfers between devices  364 us (44%)
  Pallas kernels  146 us (18%)
  starting transfers between devices  115 us (14%)
  local copies, waits for them, and re-layouts  80.8 us (10%)
  other arithmetic  54.2 us (7%)
  matrix products  53.8 us (7%)
    ppermute x32, waiting for transfers between devices, ring_steps(): send_on = lambda values: lax.ppermute(values, 'blk', onward)  194 us
    pallas_call x5, Pallas kernels, expert_rows(): pl.pallas_call(functools.partial(expert_kernel, parts, rows, width, exper...  86.9 us
    ppermute x2, waiting for transfers between devices, from_heads(): lax.ppermute(values, 'head', [(k, (k + turn) % heads) for k in range(head...  86.3 us
    ppermute x32, starting transfers between devices, ring_steps(): send_on = lambda values: lax.ppermute(values, 'blk', onward)  64.8 us
    ppermute x2, waiting for transfers between devices, head_share(): other = lax.ppermute(share(turn), 'head', moved)  48 us
    dot_general x6, matrix products, matmul_tn(): lax.dot_general(left, right, (((0,), (0,)), ((), ())), preferred_element_...  38 us
    pallas_call x1, Pallas kernels, attend_backward(): pl.pallas_call(functools.partial(backward_kernel, group, steps), grid=(st...  29.2 us
    pallas_call x1, Pallas kernels, attend_forward(): pl.pallas_call(functools.partial(forward_kernel, group), grid=(steps,), i...  22.5 us
  transfers between devices with their start and end apart: 90, of which 34 were waited for; matrix products, arithmetic and copies ran while one was open for 20% of the time, Pallas kernels for 16%

profile of v4, /device:TPU:0, one launch (start us, length us, event | category | flops | bytes accessed | tf_op | source)
XLA Modules:
  0.0 815.8 jit_solution(7340594640336070361)
XLA Ops:
  28.9 3.9 broadcast_in_dim.117
  37.2 4.9 collective-permute-done.22
  44.3 3.3 collective-permute-done.23
  52.5 5.1 collective-permute-done.2
  62.4 10.2 %collective-permute-done.6 = bf16[96,2688]{1,0:T(8,128)(2,1)S(1)} collective-permute-done((bf16[96,2688]{1,0:T(8,128)(2,1)S(1)}, bf16[96,2688]{1,0:T(8,128)(2,1)S(1)}, u32[]{:S(2)}, u32[]{:S(2)}) %collective-permute-start.6) | collective-permute-done | bytes 516128 | tf_op jit(solution)/shard_map/ppermute | solution.py:359
  77.2 10.4 %collective-permute-done.10 = bf16[96,2688]{1,0:T(8,128)(2,1)S(1)} collective-permute-done((bf16[96,2688]{1,0:T(8,128)(2,1)S(1)}, bf16[96,2688]{1,0:T(8,128)(2,1)S(1)}, u32[]{:S(2)}, u32[]{:S(2)}) %collective-permute-start.10) | collective-permute-done | bytes 516128 | tf_op jit(solution)/shard_map/ppermute | solution.py:359
  108.0 7.6 project.1
  118.2 6.0 all-to-all-start
  130.5 34.3 %collective-permute-done.38.refs_2_ = bf16[256,1664]{1,0:T(8,128)(2,1)} collective-permute-done((bf16[256,1664]{1,0:T(8,128)(2,1)}, bf16[256,1664]{1,0:T(8,128)(2,1)}, u32[]{:S(2)}, u32[]{:S(2)}) %collective-permute-start.38) | collective-permute-done | bytes 852000 | tf_op jit(solution)/shard_map/ppermute | solution.py:359
  164.8 8.6 %collective-permute-start.39 = (bf16[256,1664]{1,0:T(8,128)(2,1)}, bf16[256,1664]{1,0:T(8,128)(2,1)}, u32[]{:S(2)}, u32[]{:S(2)}) collective-permute-start(bf16[256,1664]{1,0:T(8,128)(2,1)} %collective-permute-done.38.refs_2_), channel_id=1, source_target_pairs={{0,4},{1,5},{4,8},{5,9},{8,12},{9,13},{12,14},{13,15},{14,10},{15,... | collective-permute-start | bytes 2555912 | tf_op jit(solution)/shard_map/ppermute | solution.py:359
  177.0 14.6 %collective-permute-done.39.refs_2_ = bf16[256,1664]{1,0:T(8,128)(2,1)} collective-permute-done((bf16[256,1664]{1,0:T(8,128)(2,1)}, bf16[256,1664]{1,0:T(8,128)(2,1)}, u32[]{:S(2)}, u32[]{:S(2)}) %collective-permute-start.39) | collective-permute-done | bytes 852000 | tf_op jit(solution)/shard_map/ppermute | solution.py:359
  202.1 22.5 %attend_forward.1 = (bf16[2048,192]{1,0:T(8,128)(2,1)}, f32[8,64,768]{2,1,0:T(8,128)}, f32[8,1,768]{2,1,0:T(1,128)}) custom-call(bf16[2048,320]{1,0:T(8,128)(2,1)} %bitcast.226), custom_call_target="tpu_custom_call" | custom-call | tf_op jit(solution)/shard_map/attend_forward/pallas_call | solution.py:100
  226.8 4.6 all-to-all-start.1
  231.4 6.1 pad_maximum_fusion.refs_3_.refs_5_
  243.6 6.4 all-to-all-done.1
  250.9 4.1 multiply_reduce_fusion.4
  259.5 12.6 %expert_rows.5 = (bf16[256,1536]{1,0:T(8,128)(2,1)}, bf16[256,1664]{1,0:T(8,128)(2,1)}, bf16[2048,1536]{1,0:T(8,128)(2,1)}, bf16[2048,1536]{1,0:T(8,128)(2,1)}, ...) custom-call(s32[2]{0:T(128)} %pad_add_fusion.2.index_ref, bf16[256,1536]{1,0:T(8,128)(2,1)} %copy-done.15, ...), custom_call_target="tpu_custom_call" | custom-call | flops 4831838208 | bytes 17301504 | tf_op jit(solution)/shard_map/expert_rows/pallas_call | solution.py:284
  272.1 3.5 collective-permute-done.29.refs_0_
  279.1 20.5 %expert_rows.6 = (bf16[256,1536]{1,0:T(8,128)(2,1)}, bf16[256,1536]{1,0:T(8,128)(2,1)}, bf16[256,1664]{1,0:T(8,128)(2,1)}, bf16[256,1664]{1,0:T(8,128)(2,1)}, bf...) custom-call(s32[2]{0:T(128)} %pad_add_fusion.2.index_ref, ...), custom_call_target="tpu_custom_call", output_to_operand_aliasing={{4}: (8, {}), {5}: (9, {}), {6}: (10, {}), {7}: (11, {})} | custom-call | flops 9663676416 | bytes 25165824 | tf_op jit(solution)/shard_map/expert_rows/pallas_call | solution.py:284
  301.7 20.6 %expert_rows.7 = (bf16[256,1536]{1,0:T(8,128)(2,1)}, bf16[256,1536]{1,0:T(8,128)(2,1)}, bf16[256,1664]{1,0:T(8,128)(2,1)}, bf16[256,1664]{1,0:T(8,128)(2,1)}, bf...) custom-call(s32[2]{0:T(128)} %pad_add_fusion.2.index_ref, ...), custom_call_target="tpu_custom_call", output_to_operand_aliasing={{4}: (8, {}), {5}: (9, {}), {6}: (10, {}), {7}: (11, {})} | custom-call | flops 9663676416 | bytes 25165824 | tf_op jit(solution)/shard_map/expert_rows/pallas_call | solution.py:284
  326.4 20.5 %expert_rows.8 = (bf16[256,1536]{1,0:T(8,128)(2,1)}, bf16[256,1536]{1,0:T(8,128)(2,1)}, bf16[256,1664]{1,0:T(8,128)(2,1)}, bf16[256,1664]{1,0:T(8,128)(2,1)}, bf...) custom-call(s32[2]{0:T(128)} %pad_add_fusion.2.index_ref, ...), custom_call_target="tpu_custom_call", output_to_operand_aliasing={{4}: (8, {}), {5}: (9, {}), {6}: (10, {}), {7}: (11, {})} | custom-call | flops 9663676416 | bytes 25165824 | tf_op jit(solution)/shard_map/expert_rows/pallas_call | solution.py:284
  347.7 12.7 %expert_rows.9 = (bf16[128,1536]{1,0:T(8,128)(2,1)}, bf16[128,1536]{1,0:T(8,128)(2,1)}, bf16[128,1664]{1,0:T(8,128)(2,1)}, bf16[128,1664]{1,0:T(8,128)(2,1)}, bf...) custom-call(s32[2]{0:T(128)} %pad_add_fusion.2.index_ref, ...), custom_call_target="tpu_custom_call", output_to_operand_aliasing={{4}: (8, {}), {5}: (9, {}), {6}: (10, {}), {7}: (11, {})} | custom-call | flops 4831838208 | bytes 17301504 | tf_op jit(solution)/shard_map/expert_rows/pallas_call | solution.py:284
  362.6 8.6 %collective-permute-done.45 = bf16[128,1664]{1,0:T(8,128)(2,1)S(1)} collective-permute-done((bf16[128,1664]{1,0:T(8,128)(2,1)}, bf16[128,1664]{1,0:T(8,128)(2,1)S(1)}, u32[]{:S(2)}, u32[]{:S(2)}) %collective-permute-start.45) | collective-permute-done | bytes 426016 | tf_op jit(solution)/shard_map/ppermute | solution.py:359
  373.5 16.7 %collective-permute-done.46 = bf16[256,1664]{1,0:T(8,128)(2,1)S(1)} collective-permute-done((bf16[256,1664]{1,0:T(8,128)(2,1)S(1)}, bf16[256,1664]{1,0:T(8,128)(2,1)S(1)}, u32[]{:S(2)}, u32[]{:S(2)}) %collective-permute-start.46) | collective-permute-done | bytes 852000 | tf_op jit(solution)/shard_map/ppermute | solution.py:359
  392.7 16.5 %collective-permute-done.47 = bf16[256,1664]{1,0:T(8,128)(2,1)S(1)} collective-permute-done((bf16[256,1664]{1,0:T(8,128)(2,1)S(1)}, bf16[256,1664]{1,0:T(8,128)(2,1)S(1)}, u32[]{:S(2)}, u32[]{:S(2)}) %collective-permute-start.47) | collective-permute-done | bytes 852000 | tf_op jit(solution)/shard_map/ppermute | solution.py:359
  412.8 13.7 %collective-permute-done.48 = bf16[256,1664]{1,0:T(8,128)(2,1)S(1)} collective-permute-done((bf16[256,1664]{1,0:T(8,128)(2,1)S(1)}, bf16[256,1664]{1,0:T(8,128)(2,1)S(1)}, u32[]{:S(2)}, u32[]{:S(2)}) %collective-permute-start.48) | collective-permute-done | bytes 852000 | tf_op jit(solution)/shard_map/ppermute | solution.py:359
  437.1 4.1 collective-permute-done.53
  448.4 3.6 all-to-all-start.2
  452.0 3.6 bitcast_add_fusion.1
  457.9 12.7 %all-to-all-done.2 = bf16[16,128,192]{1,2,0:T(8,128)(2,1)S(1)} async-done(((bf16[16,128,192]{1,2,0:T(8,128)(2,1)}), bf16[16,128,192]{1,2,0:T(8,128)(2,1)S(1)}, u32[]{:S(2)}, u32[]{:S(2)}) %all-to-all-start.2) | async-done | bytes 786464 | tf_op jit(solution)/shard_map/all_to_all | solution.py:326
  477.6 9.9 %collective-permute-done.62 = bf16[1,8,48,1664]{3,2,1,0:T(8,128)(2,1)} collective-permute-done((bf16[1,8,48,1664]{3,2,1,0:T(8,128)(2,1)}, bf16[1,8,48,1664]{3,2,1,0:T(8,128)(2,1)}, u32[]{:S(2)}, u32[]{:S(2)}) %collective-permute-start.62) | collective-permute-done | bytes 1277984 | tf_op jit(solution)/shard_map/ppermute | solution.py:482
  491.2 8.0 collective-permute-done.63
  503.8 29.2 %attend_backward.1 = bf16[2048,320]{1,0:T(8,128)(2,1)} custom-call(bf16[2048,320]{1,0:T(8,128)(2,1)} %bitcast.227, bf16[2048,192]{1,0:T(8,128)(2,1)} %bitcast.243, f32[8,64,768]{2,1,0:T(8,128)} %get-tuple-element.104.flat_ref, f32[8,1,768]{2,1,0:T(1,128)} %get-tuple-element.105.lse_ref, f32[32,2048]{1,0:T(8,128)} %get-tuple-element.233.cos_ref, ...), custom_call_target="tpu_custom_call" | custom-call | tf_op jit(solution)/shard_map/attend_backward/pallas_call | solution.py:174
  536.5 3.9 all-to-all-start.3
  543.5 22.5 %collective-permute-done.65 = bf16[48,1664]{1,0:T(8,128)(2,1)S(1)} collective-permute-done((bf16[48,1664]{1,0:T(8,128)(2,1)S(1)}, bf16[48,1664]{1,0:T(8,128)(2,1)S(1)}, u32[]{:S(2)}, u32[]{:S(2)}) %collective-permute-start.65) | collective-permute-done | bytes 159776 | tf_op jit(solution)/shard_map/ppermute | solution.py:359
  566.0 10.5 %collective-permute-start.66 = (bf16[48,1664]{1,0:T(8,128)(2,1)S(1)}, bf16[48,1664]{1,0:T(8,128)(2,1)S(1)}, u32[]{:S(2)}, u32[]{:S(2)}) collective-permute-start(bf16[48,1664]{1,0:T(8,128)(2,1)S(1)} %get-tuple-element.224), channel_id=1, source_target_pairs={{0,4},{1,5},{4,8},{5,9},{8,12},{9,13},{12,14},{13,15},{14,10},{15,... | collective-permute-start | bytes 479240 | tf_op jit(solution)/shard_map/ppermute | solution.py:359
  576.6 8.0 convolution_convert_fusion.1
  586.3 6.3 convolution_convert_fusion
  592.6 6.4 select_bitcast_fusion
  599.6 8.5 %fusion.5 = bf16[1536,1024]{1,0:T(8,128)(2,1)} fusion(bf16[2048,1536]{1,0:T(8,128)(2,1)S(1)} %bitcast.217, bf16[2048,2048]{1,0:T(8,128)(2,1)S(1)} %bitcast.215), kind=kOutput, calls=%fused_computation.18 | convolution fusion | flops 6444023808 | bytes 13631488 | tf_op jit(solution)/shard_map/dot_general | solution.py:51
  608.1 7.7 multiply_reduce_fusion
  616.9 5.2 fusion.8
  627.0 8.4 %add_convert_fusion.1 = bf16[1536,1024]{1,0:T(8,128)(2,1)S(1)} fusion(bf16[1536,1024]{1,0:T(8,128)(2,1)} %collective-permute-done.82, bf16[2048,1536]{1,0:T(8,128)(2,1)S(1)} %bitcast.217, bf16[2048,2048]{1,0:T(8,128)(2,1)S(1)} %bitcast.215), kind=kOutput, calls=%fused_computation.4 | convolution fusion | flops 6447169536 | bytes 16777216 | tf_op jit(solution)/shard_map/dot_general | solution.py:51
  636.6 22.8 %collective-permute-done.85 = bf16[512,1536]{1,0:T(8,128)(2,1)S(1)} collective-permute-done((bf16[512,1536]{1,0:T(8,128)(2,1)S(1)}, bf16[512,1536]{1,0:T(8,128)(2,1)S(1)}, u32[]{:S(2)}, u32[]{:S(2)}) %collective-permute-start.85) | collective-permute-done | bytes 1572896 | tf_op jit(solution)/shard_map/ppermute | solution.py:332
  665.5 38.1 %collective-permute-done.73 = bf16[1,8,48,2688]{3,2,1,0:T(8,128)(2,1)S(1)} collective-permute-done((bf16[1,8,48,2688]{3,2,1,0:T(8,128)(2,1)S(1)}, bf16[1,8,48,2688]{3,2,1,0:T(8,128)(2,1)S(1)}, u32[]{:S(2)}, u32[]{:S(2)}) %collective-permute-start.73) | collective-permute-done | bytes 2064416 | tf_op jit(solution)/shard_map/ppermute | solution.py:482
  706.4 63.5 %collective-permute-done.83 = bf16[1536,1024]{1,0:T(8,128)(2,1)S(1)} collective-permute-done((bf16[1536,1024]{1,0:T(8,128)(2,1)S(1)}, bf16[1536,1024]{1,0:T(8,128)(2,1)S(1)}, u32[]{:S(2)}, u32[]{:S(2)}) %collective-permute-start.83) | collective-permute-done | bytes 3145760 | tf_op jit(solution)/shard_map/ppermute | solution.py:332
  776.5 3.5 slice_bitcast_fusion.2
  780.0 15.6 %collective-permute-done.75 = bf16[48,2688]{1,0:T(8,128)(2,1)S(1)} collective-permute-done((bf16[48,2688]{1,0:T(8,128)(2,1)S(1)}, bf16[48,2688]{1,0:T(8,128)(2,1)S(1)}, u32[]{:S(2)}, u32[]{:S(2)}) %collective-permute-start.75) | collective-permute-done | bytes 258080 | tf_op jit(solution)/shard_map/ppermute | solution.py:359
  (447 shorter events, 213.2 us)
Async XLA Ops:
  3.9 19.9 %collective-permute-start.17 = (bf16[48,1664]{1,0:T(8,128)(2,1)}, bf16[48,1664]{1,0:T(8,128)(2,1)}, u32[]{:S(2)}, u32[]{:S(2)}) collective-permute-start(bf16[48,1664]{1,0:T(8,128)(2,1)} %concatenate.48), channel_id=1, source_target_pairs={{0,4},{1,5},{4,8},{5,9},{8,12},{9,13},{12,14},{13,15},{14,10},{15,... | collective-permute-start | bytes 479240 | tf_op jit(solution)/shard_map/ppermute | solution.py:359
  11.1 117.5 %collective-permute-start.37 = (bf16[256,1664]{1,0:T(8,128)(2,1)}, bf16[256,1664]{1,0:T(8,128)(2,1)}, u32[]{:S(2)}, u32[]{:S(2)}) collective-permute-start(bf16[256,1664]{1,0:T(8,128)(2,1)} %concatenate.50.refs_1_), channel_id=1, source_target_pairs={{0,4},{1,5},{4,8},{5,9},{8,12},{9,13},{12,14},{13,15},{14,10},{15,... | collective-permute-start | bytes 2555912 | tf_op jit(solution)/shard_map/ppermute | solution.py:359
  13.1 117.1 %collective-permute-start.41 = (bf16[256,1664]{1,0:T(8,128)(2,1)}, bf16[256,1664]{1,0:T(8,128)(2,1)}, u32[]{:S(2)}, u32[]{:S(2)}) collective-permute-start(bf16[256,1664]{1,0:T(8,128)(2,1)} %concatenate.50.refs_1_), channel_id=1, source_target_pairs={{4,0},{5,1},{8,4},{9,5},{12,8},{13,9},{14,12},{15,13},{10,14},{11,... | collective-permute-start | bytes 2555912 | tf_op jit(solution)/shard_map/ppermute | solution.py:360
  28.8 28.8 %collective-permute-start.1 = (bf16[96,2688]{1,0:T(8,128)(2,1)S(1)}, bf16[96,2688]{1,0:T(8,128)(2,1)S(1)}, u32[]{:S(2)}, u32[]{:S(2)}) collective-permute-start(bf16[96,2688]{1,0:T(8,128)(2,1)S(1)} %bitcast.248), channel_id=1, source_target_pairs={{0,1},{1,0},{2,3},{3,2},{4,5},{5,4},{6,7},{7,6},{8,9},{9,8},{10,11... | collective-permute-start | bytes 1548296 | tf_op jit(solution)/shard_map/ppermute | solution.py:339
  96.3 135.1 %collective-permute-start.27 = (bf16[1,1536,1024]{2,1,0:T(8,128)(2,1)}, bf16[1,1536,1024]{2,1,0:T(8,128)(2,1)}, u32[]{:S(2)}, u32[]{:S(2)}) collective-permute-start(bf16[1,1536,1024]{2,1,0:T(8,128)(2,1)} %constant_dynamic-update-slice_fusion.2), channel_id=1, source_target_pairs={{0,1},{1,0},{2,3},{3,2},{4,5},{5,4},{6,7},{7,6},{8,9},{9,8},{10,11... | collective-permute-start | bytes 9437192 | tf_op jit(solution)/shard_map/ppermute | solution.py:339
  98.3 28.5 %collective-permute-start.25 = (bf16[8,48,1664]{2,1,0:T(8,128)(2,1)S(1)}, bf16[8,48,1664]{2,1,0:T(8,128)(2,1)S(1)}, u32[]{:S(2)}, u32[]{:S(2)}) collective-permute-start(bf16[8,48,1664]{2,1,0:T(8,128)(2,1)S(1)} %fusion.31), channel_id=1, source_target_pairs={{0,16},{16,0},{1,17},{17,1},{2,18},{18,2},{3,19},{19,3},{4,20},{20... | collective-permute-start | bytes 3833864 | tf_op jit(solution)/shard_map/ppermute | solution.py:429
  118.2 81.4 %all-to-all-start = ((bf16[16,128,320]{1,2,0:T(8,128)(2,1)}), bf16[16,128,320]{1,2,0:T(8,128)(2,1)}, u32[]{:S(2)}, u32[]{:S(2)}) async-start(bf16[16,128,320]{1,2,0:T(8,128)(2,1)} %copy.189), calls=%async_computation | async-start | bytes 2621440 | tf_op jit(solution)/shard_map/all_to_all | solution.py:326
  128.0 109.5 %collective-permute-start.26 = (bf16[2,8,48,1664]{3,2,1,0:T(8,128)(2,1)}, bf16[2,8,48,1664]{3,2,1,0:T(8,128)(2,1)}, u32[]{:S(2)}, u32[]{:S(2)}) collective-permute-start(bf16[2,8,48,1664]{3,2,1,0:T(8,128)(2,1)} %bitcast_dynamic-update-slice_fusion), channel_id=1, source_target_pairs={{0,1},{1,0},{2,3},{3,2},{4,5},{5,4},{6,7},{7,6},{8,9},{9,8},{10,11... | collective-permute-start | bytes 7667720 | tf_op jit(solution)/shard_map/ppermute | solution.py:339
  128.0 47.5 %collective-permute-start.28 = (bf16[1,512,1536]{2,1,0:T(8,128)(2,1)}, bf16[1,512,1536]{2,1,0:T(8,128)(2,1)}, u32[]{:S(2)}, u32[]{:S(2)}) collective-permute-start(bf16[1,512,1536]{2,1,0:T(8,128)(2,1)} %param.23), channel_id=1, source_target_pairs={{0,1},{1,0},{2,3},{3,2},{4,5},{5,4},{6,7},{7,6},{8,9},{9,8},{10,11... | collective-permute-start | bytes 4718600 | tf_op jit(solution)/shard_map/ppermute | solution.py:339
  128.5 36.3 %collective-permute-start.38 = (bf16[256,1664]{1,0:T(8,128)(2,1)}, bf16[256,1664]{1,0:T(8,128)(2,1)}, u32[]{:S(2)}, u32[]{:S(2)}) collective-permute-start(bf16[256,1664]{1,0:T(8,128)(2,1)} %collective-permute-done.37.refs_2_), channel_id=1, source_target_pairs={{0,4},{1,5},{4,8},{5,9},{8,12},{9,13},{12,14},{13,15},{14,10},{15,... | collective-permute-start | bytes 2555912 | tf_op jit(solution)/shard_map/ppermute | solution.py:359
  130.2 43.1 %collective-permute-start.42 = (bf16[256,1664]{1,0:T(8,128)(2,1)}, bf16[256,1664]{1,0:T(8,128)(2,1)}, u32[]{:S(2)}, u32[]{:S(2)}) collective-permute-start(bf16[256,1664]{1,0:T(8,128)(2,1)} %collective-permute-done.41.refs_3_), channel_id=1, source_target_pairs={{4,0},{5,1},{8,4},{9,5},{12,8},{13,9},{14,12},{15,13},{10,14},{11,... | collective-permute-start | bytes 2555912 | tf_op jit(solution)/shard_map/ppermute | solution.py:360
  164.8 26.8 %collective-permute-start.39 = (bf16[256,1664]{1,0:T(8,128)(2,1)}, bf16[256,1664]{1,0:T(8,128)(2,1)}, u32[]{:S(2)}, u32[]{:S(2)}) collective-permute-start(bf16[256,1664]{1,0:T(8,128)(2,1)} %collective-permute-done.38.refs_2_), channel_id=1, source_target_pairs={{0,4},{1,5},{4,8},{5,9},{8,12},{9,13},{12,14},{13,15},{14,10},{15,... | collective-permute-start | bytes 2555912 | tf_op jit(solution)/shard_map/ppermute | solution.py:359
  173.4 22.5 %collective-permute-start.43 = (bf16[256,1664]{1,0:T(8,128)(2,1)}, bf16[256,1664]{1,0:T(8,128)(2,1)}, u32[]{:S(2)}, u32[]{:S(2)}) collective-permute-start(bf16[256,1664]{1,0:T(8,128)(2,1)} %collective-permute-done.42.refs_3_), channel_id=1, source_target_pairs={{4,0},{5,1},{8,4},{9,5},{12,8},{13,9},{14,12},{15,13},{10,14},{11,... | collective-permute-start | bytes 2555912 | tf_op jit(solution)/shard_map/ppermute | solution.py:360
  193.4 153.5 %collective-permute-start.40 = (bf16[128,1664]{1,0:T(8,128)(2,1)}, bf16[128,1664]{1,0:T(8,128)(2,1)}, u32[]{:S(2)}, u32[]{:S(2)}) collective-permute-start(bf16[128,1664]{1,0:T(8,128)(2,1)} %slice.162), channel_id=1, source_target_pairs={{0,4},{1,5},{4,8},{5,9},{8,12},{9,13},{12,14},{13,15},{14,10},{15,... | collective-permute-start | bytes 1277960 | tf_op jit(solution)/shard_map/ppermute | solution.py:359
  197.7 149.2 %collective-permute-start.44 = (bf16[128,1664]{1,0:T(8,128)(2,1)}, bf16[128,1664]{1,0:T(8,128)(2,1)}, u32[]{:S(2)}, u32[]{:S(2)}) collective-permute-start(bf16[128,1664]{1,0:T(8,128)(2,1)} %slice.163), channel_id=1, source_target_pairs={{4,0},{5,1},{8,4},{9,5},{12,8},{13,9},{14,12},{15,13},{10,14},{11,... | collective-permute-start | bytes 1277960 | tf_op jit(solution)/shard_map/ppermute | solution.py:360
  226.8 23.2 %all-to-all-start.1 = ((bf16[16,128,192]{1,2,0:T(8,128)(2,1)}), bf16[16,128,192]{1,2,0:T(8,128)(2,1)S(1)}, u32[]{:S(2)}, u32[]{:S(2)}) async-start(bf16[16,128,192]{1,2,0:T(8,128)(2,1)} %copy.191), calls=%async_computation.1 | async-start | bytes 1572864 | tf_op jit(solution)/shard_map/all_to_all | solution.py:326
  255.6 20.0 %collective-permute-start.29 = (bf16[256,1536]{1,0:T(8,128)(2,1)S(1)}, bf16[256,1536]{1,0:T(8,128)(2,1)}, u32[]{:S(2)}, u32[]{:S(2)}) collective-permute-start(bf16[256,1536]{1,0:T(8,128)(2,1)S(1)} %multiply_convert_fusion.refs_0_), channel_id=1, source_target_pairs={{0,4},{1,5},{4,8},{5,9},{8,12},{9,13},{12,14},{13,15},{14,10},{15,... | collective-permute-start | bytes 2359304 | tf_op jit(solution)/shard_map/ppermute | solution.py:359
  257.7 20.5 %collective-permute-start.33 = (bf16[256,1536]{1,0:T(8,128)(2,1)S(1)}, bf16[256,1536]{1,0:T(8,128)(2,1)S(1)}, u32[]{:S(2)}, u32[]{:S(2)}) collective-permute-start(bf16[256,1536]{1,0:T(8,128)(2,1)S(1)} %multiply_convert_fusion.refs_0_), channel_id=1, source_target_pairs={{4,0},{5,1},{8,4},{9,5},{12,8},{13,9},{14,12},{15,13},{10,14},{11,... | collective-permute-start | bytes 2359304 | tf_op jit(solution)/shard_map/ppermute | solution.py:360
  275.6 24.0 %collective-permute-start.30 = (bf16[256,1536]{1,0:T(8,128)(2,1)}, bf16[256,1536]{1,0:T(8,128)(2,1)}, u32[]{:S(2)}, u32[]{:S(2)}) collective-permute-start(bf16[256,1536]{1,0:T(8,128)(2,1)} %collective-permute-done.29.refs_0_), channel_id=1, source_target_pairs={{0,4},{1,5},{4,8},{5,9},{8,12},{9,13},{12,14},{13,15},{14,10},{15,... | collective-permute-start | bytes 2359304 | tf_op jit(solution)/shard_map/ppermute | solution.py:359
  278.2 22.8 %collective-permute-start.34 = (bf16[256,1536]{1,0:T(8,128)(2,1)S(1)}, bf16[256,1536]{1,0:T(8,128)(2,1)}, u32[]{:S(2)}, u32[]{:S(2)}) collective-permute-start(bf16[256,1536]{1,0:T(8,128)(2,1)S(1)} %collective-permute-done.33.refs_1_), channel_id=1, source_target_pairs={{4,0},{5,1},{8,4},{9,5},{12,8},{13,9},{14,12},{15,13},{10,14},{11,... | collective-permute-start | bytes 2359304 | tf_op jit(solution)/shard_map/ppermute | solution.py:360
  299.6 22.7 %collective-permute-start.31 = (bf16[256,1536]{1,0:T(8,128)(2,1)}, bf16[256,1536]{1,0:T(8,128)(2,1)S(1)}, u32[]{:S(2)}, u32[]{:S(2)}) collective-permute-start(bf16[256,1536]{1,0:T(8,128)(2,1)} %collective-permute-done.30.refs_0_), channel_id=1, source_target_pairs={{0,4},{1,5},{4,8},{5,9},{8,12},{9,13},{12,14},{13,15},{14,10},{15,... | collective-permute-start | bytes 2359304 | tf_op jit(solution)/shard_map/ppermute | solution.py:359
  300.9 23.5 %collective-permute-start.35 = (bf16[256,1536]{1,0:T(8,128)(2,1)}, bf16[256,1536]{1,0:T(8,128)(2,1)S(1)}, u32[]{:S(2)}, u32[]{:S(2)}) collective-permute-start(bf16[256,1536]{1,0:T(8,128)(2,1)} %collective-permute-done.34.refs_1_), channel_id=1, source_target_pairs={{4,0},{5,1},{8,4},{9,5},{12,8},{13,9},{14,12},{15,13},{10,14},{11,... | collective-permute-start | bytes 2359304 | tf_op jit(solution)/shard_map/ppermute | solution.py:360
  323.1 23.8 %collective-permute-start.32 = (bf16[128,1536]{1,0:T(8,128)(2,1)}, bf16[128,1536]{1,0:T(8,128)(2,1)S(1)}, u32[]{:S(2)}, u32[]{:S(2)}) collective-permute-start(bf16[128,1536]{1,0:T(8,128)(2,1)} %slice.160), channel_id=1, source_target_pairs={{0,4},{1,5},{4,8},{5,9},{8,12},{9,13},{12,14},{13,15},{14,10},{15,... | collective-permute-start | bytes 1179656 | tf_op jit(solution)/shard_map/ppermute | solution.py:359
  325.3 21.7 %collective-permute-start.36 = (bf16[128,1536]{1,0:T(8,128)(2,1)}, bf16[128,1536]{1,0:T(8,128)(2,1)}, u32[]{:S(2)}, u32[]{:S(2)}) collective-permute-start(bf16[128,1536]{1,0:T(8,128)(2,1)} %slice.161), channel_id=1, source_target_pairs={{4,0},{5,1},{8,4},{9,5},{12,8},{13,9},{14,12},{15,13},{10,14},{11,... | collective-permute-start | bytes 1179656 | tf_op jit(solution)/shard_map/ppermute | solution.py:360
  372.5 19.0 %collective-permute-start.50 = (bf16[256,1664]{1,0:T(8,128)(2,1)S(1)}, bf16[256,1664]{1,0:T(8,128)(2,1)S(1)}, u32[]{:S(2)}, u32[]{:S(2)}) collective-permute-start(bf16[256,1664]{1,0:T(8,128)(2,1)S(1)} %pad_add_fusion), channel_id=1, source_target_pairs={{4,0},{5,1},{8,4},{9,5},{12,8},{13,9},{14,12},{15,13},{10,14},{11,... | collective-permute-start | bytes 2555912 | tf_op jit(solution)/shard_map/ppermute | solution.py:360
  448.4 22.3 %all-to-all-start.2 = ((bf16[16,128,192]{1,2,0:T(8,128)(2,1)}), bf16[16,128,192]{1,2,0:T(8,128)(2,1)S(1)}, u32[]{:S(2)}, u32[]{:S(2)}) async-start(bf16[16,128,192]{1,2,0:T(8,128)(2,1)} %bitcast.48), calls=%async_computation.2 | async-start | bytes 1572864 | tf_op jit(solution)/shard_map/all_to_all | solution.py:326
  456.8 30.7 %collective-permute-start.62 = (bf16[1,8,48,1664]{3,2,1,0:T(8,128)(2,1)}, bf16[1,8,48,1664]{3,2,1,0:T(8,128)(2,1)}, u32[]{:S(2)}, u32[]{:S(2)}) collective-permute-start(bf16[1,8,48,1664]{3,2,1,0:T(8,128)(2,1)} %constant_dynamic-slice_fusion), channel_id=1, source_target_pairs={{0,16},{16,0},{1,17},{17,1},{2,18},{18,2},{3,19},{19,3},{4,20},{20... | collective-permute-start | bytes 3833864 | tf_op jit(solution)/shard_map/ppermute | solution.py:482
  474.4 58.5 %collective-permute-start.56 = (bf16[256,1536]{1,0:T(8,128)(2,1)}, bf16[256,1536]{1,0:T(8,128)(2,1)S(1)}, u32[]{:S(2)}, u32[]{:S(2)}) collective-permute-start(bf16[256,1536]{1,0:T(8,128)(2,1)} %add.576), channel_id=1, source_target_pairs={{4,0},{5,1},{8,4},{9,5},{12,8},{13,9},{14,12},{15,13},{10,14},{11,... | collective-permute-start | bytes 2359304 | tf_op jit(solution)/shard_map/ppermute | solution.py:360
  476.5 56.4 %collective-permute-start.55 = (bf16[256,1536]{1,0:T(8,128)(2,1)}, bf16[256,1536]{1,0:T(8,128)(2,1)}, u32[]{:S(2)}, u32[]{:S(2)}) collective-permute-start(bf16[256,1536]{1,0:T(8,128)(2,1)} %add.575), channel_id=1, source_target_pairs={{0,4},{1,5},{4,8},{5,9},{8,12},{9,13},{12,14},{13,15},{14,10},{15,... | collective-permute-start | bytes 2359304 | tf_op jit(solution)/shard_map/ppermute | solution.py:359
  500.0 40.4 %collective-permute-start.64 = (bf16[48,1664]{1,0:T(8,128)(2,1)}, bf16[48,1664]{1,0:T(8,128)(2,1)S(1)}, u32[]{:S(2)}, u32[]{:S(2)}) collective-permute-start(bf16[48,1664]{1,0:T(8,128)(2,1)} %get-tuple-element.228), channel_id=1, source_target_pairs={{0,4},{1,5},{4,8},{5,9},{8,12},{9,13},{12,14},{13,15},{14,10},{15,... | collective-permute-start | bytes 479240 | tf_op jit(solution)/shard_map/ppermute | solution.py:359
  500.5 39.9 %collective-permute-start.68 = (bf16[48,1664]{1,0:T(8,128)(2,1)}, bf16[48,1664]{1,0:T(8,128)(2,1)}, u32[]{:S(2)}, u32[]{:S(2)}) collective-permute-start(bf16[48,1664]{1,0:T(8,128)(2,1)} %get-tuple-element.229), channel_id=1, source_target_pairs={{4,0},{5,1},{8,4},{9,5},{12,8},{13,9},{14,12},{15,13},{10,14},{11,... | collective-permute-start | bytes 479240 | tf_op jit(solution)/shard_map/ppermute | solution.py:360
  536.5 48.2 %all-to-all-start.3 = ((bf16[16,128,320]{1,2,0:T(8,128)(2,1)}), bf16[16,128,320]{1,2,0:T(8,128)(2,1)S(1)}, u32[]{:S(2)}, u32[]{:S(2)}) async-start(bf16[16,128,320]{1,2,0:T(8,128)(2,1)} %copy.203), calls=%async_computation.3 | async-start | bytes 2621440 | tf_op jit(solution)/shard_map/all_to_all | solution.py:326
  541.4 24.6 %collective-permute-start.65 = (bf16[48,1664]{1,0:T(8,128)(2,1)S(1)}, bf16[48,1664]{1,0:T(8,128)(2,1)S(1)}, u32[]{:S(2)}, u32[]{:S(2)}) collective-permute-start(bf16[48,1664]{1,0:T(8,128)(2,1)S(1)} %get-tuple-element.226), channel_id=1, source_target_pairs={{0,4},{1,5},{4,8},{5,9},{8,12},{9,13},{12,14},{13,15},{14,10},{15,... | collective-permute-start | bytes 479240 | tf_op jit(solution)/shard_map/ppermute | solution.py:359
  543.3 22.7 %collective-permute-start.69 = (bf16[48,1664]{1,0:T(8,128)(2,1)S(1)}, bf16[48,1664]{1,0:T(8,128)(2,1)S(1)}, u32[]{:S(2)}, u32[]{:S(2)}) collective-permute-start(bf16[48,1664]{1,0:T(8,128)(2,1)S(1)} %get-tuple-element.227), channel_id=1, source_target_pairs={{4,0},{5,1},{8,4},{9,5},{12,8},{13,9},{14,12},{15,13},{10,14},{11,... | collective-permute-start | bytes 479240 | tf_op jit(solution)/shard_map/ppermute | solution.py:360
  584.6 32.2 %collective-permute-start.84 = (bf16[512,1536]{1,0:T(8,128)(2,1)}, bf16[512,1536]{1,0:T(8,128)(2,1)}, u32[]{:S(2)}, u32[]{:S(2)}) collective-permute-start(bf16[512,1536]{1,0:T(8,128)(2,1)} %convolution_convert_fusion.1), channel_id=1, source_target_pairs={{0,1},{1,0},{2,3},{3,2},{4,5},{5,4},{6,7},{7,6},{8,9},{9,8},{10,11... | collective-permute-start | bytes 4718600 | tf_op jit(solution)/shard_map/ppermute | solution.py:339
  599.0 24.3 %collective-permute-start.71 = (bf16[2,8,48,2560]{3,2,1,0:T(8,128)(2,1)}, bf16[2,8,48,2560]{3,2,1,0:T(8,128)(2,1)}, u32[]{:S(2)}, u32[]{:S(2)}) collective-permute-start(bf16[2,8,48,2560]{3,2,1,0:T(8,128)(2,1)} %select_bitcast_fusion), channel_id=1, source_target_pairs={{0,1},{1,0},{2,3},{3,2},{4,5},{5,4},{6,7},{7,6},{8,9},{9,8},{10,11... | collective-permute-start | bytes 11796488 | tf_op jit(solution)/shard_map/ppermute | solution.py:339
  608.1 18.9 %collective-permute-start.82 = (bf16[1536,1024]{1,0:T(8,128)(2,1)}, bf16[1536,1024]{1,0:T(8,128)(2,1)}, u32[]{:S(2)}, u32[]{:S(2)}) collective-permute-start(bf16[1536,1024]{1,0:T(8,128)(2,1)} %fusion.5), channel_id=1, source_target_pairs={{0,1},{1,0},{2,3},{3,2},{4,5},{5,4},{6,7},{7,6},{8,9},{9,8},{10,11... | collective-permute-start | bytes 9437192 | tf_op jit(solution)/shard_map/ppermute | solution.py:339
  622.0 37.3 %collective-permute-start.85 = (bf16[512,1536]{1,0:T(8,128)(2,1)S(1)}, bf16[512,1536]{1,0:T(8,128)(2,1)S(1)}, u32[]{:S(2)}, u32[]{:S(2)}) collective-permute-start(bf16[512,1536]{1,0:T(8,128)(2,1)S(1)} %fusion.8), channel_id=1, source_target_pairs={{0,16},{16,0},{1,17},{17,1},{2,18},{18,2},{3,19},{19,3},{4,20},{20... | collective-permute-start | bytes 4718600 | tf_op jit(solution)/shard_map/ppermute | solution.py:332
  626.0 77.6 %collective-permute-start.73 = (bf16[1,8,48,2688]{3,2,1,0:T(8,128)(2,1)S(1)}, bf16[1,8,48,2688]{3,2,1,0:T(8,128)(2,1)S(1)}, u32[]{:S(2)}, u32[]{:S(2)}) collective-permute-start(bf16[1,8,48,2688]{3,2,1,0:T(8,128)(2,1)S(1)} %fusion.14), channel_id=1, source_target_pairs={{0,16},{16,0},{1,17},{17,1},{2,18},{18,2},{3,19},{19,3},{4,20},{20... | collective-permute-start | bytes 6193160 | tf_op jit(solution)/shard_map/ppermute | solution.py:482
  635.4 134.5 %collective-permute-start.83 = (bf16[1536,1024]{1,0:T(8,128)(2,1)S(1)}, bf16[1536,1024]{1,0:T(8,128)(2,1)S(1)}, u32[]{:S(2)}, u32[]{:S(2)}) collective-permute-start(bf16[1536,1024]{1,0:T(8,128)(2,1)S(1)} %add_convert_fusion.1), channel_id=1, source_target_pairs={{0,16},{16,0},{1,17},{17,1},{2,18},{18,2},{3,19},{19,3},{4,20},{20... | collective-permute-start | bytes 9437192 | tf_op jit(solution)/shard_map/ppermute | solution.py:332
  662.9 108.4 %collective-permute-start.57 = (bf16[256,1536]{1,0:T(8,128)(2,1)S(1)}, bf16[256,1536]{1,0:T(8,128)(2,1)S(1)}, u32[]{:S(2)}, u32[]{:S(2)}) collective-permute-start(bf16[256,1536]{1,0:T(8,128)(2,1)S(1)} %add.577), channel_id=1, source_target_pairs={{0,4},{1,5},{4,8},{5,9},{8,12},{9,13},{12,14},{13,15},{14,10},{15,... | collective-permute-start | bytes 2359304 | tf_op jit(solution)/shard_map/ppermute | solution.py:359
  665.3 108.4 %collective-permute-start.59 = (bf16[256,1536]{1,0:T(8,128)(2,1)S(1)}, bf16[256,1536]{1,0:T(8,128)(2,1)S(1)}, u32[]{:S(2)}, u32[]{:S(2)}) collective-permute-start(bf16[256,1536]{1,0:T(8,128)(2,1)S(1)} %add.580), channel_id=1, source_target_pairs={{4,0},{5,1},{8,4},{9,5},{12,8},{13,9},{14,12},{15,13},{10,14},{11,... | collective-permute-start | bytes 2359304 | tf_op jit(solution)/shard_map/ppermute | solution.py:360
  704.3 70.1 %collective-permute-start.78 = (bf16[48,1408]{1,0:T(8,128)(2,1)S(1)}, bf16[48,1408]{1,0:T(8,128)(2,1)S(1)}, u32[]{:S(2)}, u32[]{:S(2)}) collective-permute-start(bf16[48,1408]{1,0:T(8,128)(2,1)S(1)} %split.19), channel_id=1, source_target_pairs={{4,0},{5,1},{8,4},{9,5},{12,8},{13,9},{14,12},{15,13},{10,14},{11,... | collective-permute-start | bytes 405512 | tf_op jit(solution)/shard_map/ppermute | solution.py:360
  705.9 68.4 %collective-permute-start.74 = (bf16[48,1280]{1,0:T(8,128)(2,1)S(1)}, bf16[48,1280]{1,0:T(8,128)(2,1)S(1)}, u32[]{:S(2)}, u32[]{:S(2)}) collective-permute-start(bf16[48,1280]{1,0:T(8,128)(2,1)S(1)} %split.18), channel_id=1, source_target_pairs={{0,4},{1,5},{4,8},{5,9},{8,12},{9,13},{12,14},{13,15},{14,10},{15,... | collective-permute-start | bytes 368648 | tf_op jit(solution)/shard_map/ppermute | solution.py:359
  771.6 28.2 %collective-permute-start.58 = (bf16[256,1536]{1,0:T(8,128)(2,1)S(1)}, bf16[256,1536]{1,0:T(8,128)(2,1)S(1)}, u32[]{:S(2)}, u32[]{:S(2)}) collective-permute-start(bf16[256,1536]{1,0:T(8,128)(2,1)S(1)} %add.578), channel_id=1, source_target_pairs={{0,4},{1,5},{4,8},{5,9},{8,12},{9,13},{12,14},{13,15},{14,10},{15,... | collective-permute-start | bytes 2359304 | tf_op jit(solution)/shard_map/ppermute | solution.py:359
  773.9 25.9 %collective-permute-start.60 = (bf16[256,1536]{1,0:T(8,128)(2,1)S(1)}, bf16[256,1536]{1,0:T(8,128)(2,1)S(1)}, u32[]{:S(2)}, u32[]{:S(2)}) collective-permute-start(bf16[256,1536]{1,0:T(8,128)(2,1)S(1)} %add.581), channel_id=1, source_target_pairs={{4,0},{5,1},{8,4},{9,5},{12,8},{13,9},{14,12},{15,13},{10,14},{11,... | collective-permute-start | bytes 2359304 | tf_op jit(solution)/shard_map/ppermute | solution.py:360
  774.4 21.1 %collective-permute-start.75 = (bf16[48,2688]{1,0:T(8,128)(2,1)S(1)}, bf16[48,2688]{1,0:T(8,128)(2,1)S(1)}, u32[]{:S(2)}, u32[]{:S(2)}) collective-permute-start(bf16[48,2688]{1,0:T(8,128)(2,1)S(1)} %get-tuple-element.222), channel_id=1, source_target_pairs={{0,4},{1,5},{4,8},{5,9},{8,12},{9,13},{12,14},{13,15},{14,10},{15,... | collective-permute-start | bytes 774152 | tf_op jit(solution)/shard_map/ppermute | solution.py:359
  776.1 21.5 %collective-permute-start.79 = (bf16[48,2688]{1,0:T(8,128)(2,1)S(1)}, bf16[48,2688]{1,0:T(8,128)(2,1)S(1)}, u32[]{:S(2)}, u32[]{:S(2)}) collective-permute-start(bf16[48,2688]{1,0:T(8,128)(2,1)S(1)} %get-tuple-element.223), channel_id=1, source_target_pairs={{4,0},{5,1},{8,4},{9,5},{12,8},{13,9},{14,12},{15,13},{10,14},{11,... | collective-permute-start | bytes 774152 | tf_op jit(solution)/shard_map/ppermute | solution.py:360
  (105 other events, 1407.4 us)

commit v5 on v4

--- a/solution.py
+++ b/solution.py
@@ -51,17 +51,28 @@
     return lax.dot_general(left, right, (((0,), (0,)), ((), ())), preferred_element_type=jnp.float32)
 
 
-def wide(block, group):
-    flipped = block.T
-    return jnp.concatenate([flipped[h*HDIM:(h+1)*HDIM] for h in range(group)], axis=1)
-
-
-def tall(block, group):
-    return jnp.concatenate([block[:, h*HDIM:(h+1)*HDIM] for h in range(group)], axis=0)
-
-
-def narrow(values, group, rows):
-    return jnp.concatenate([values[:, h*rows:(h+1)*rows] for h in range(group)], axis=0).T
+def wide(ref, i, group):
+    blocks = [ref[2 * i], ref[2 * i + 1]] if i is not None else [ref[0], ref[1]]
+    pieces = [b[h * HDIM : (h + 1) * HDIM] for h in range(group) for b in blocks]
+    return jnp.concatenate(pieces, axis=1)
+
+
+def narrow(values, group, k):
+    starts = [h * BLOCK + k * LANES for h in range(group)]
+    return jnp.concatenate([values[:, s : s + LANES] for s in starts], axis=0)
+
+
+def spread(qkv_ref, start, row_ref, column_ref):
+    def step(b, carry):
+        here = pl.ds(pl.multiple_of(b * LANES, LANES), LANES)
+        piece = qkv_ref[b, start : start + HDIM]
+        if row_ref is not None:
+            row_ref[here, :] = piece.T
+        if column_ref is not None:
+            column_ref[:, here] = piece
+        return carry
+
+    lax.fori_loop(0, qkv_ref.shape[0], step, 0)
 
 
 def forward_kernel(group, qkv_ref, att_ref, flat_ref, lse_ref, key_sc, val_sc, acc_sc):
@@ -70,11 +81,10 @@
 
     @pl.when(i == 0)
     def _():
-        key_sc[...] = qkv_ref[:, lanes:lanes+HDIM]
-        val_sc[...] = qkv_ref[:, lanes+HDIM:lanes+2*HDIM].T
-
-    rows = pl.ds(pl.multiple_of(i*BLOCK, BLOCK), BLOCK)
-    query = wide(qkv_ref[rows, :lanes], group) * jnp.bfloat16(HDIM**-0.5)
+        spread(qkv_ref, lanes, key_sc, None)
+        spread(qkv_ref, lanes + HDIM, None, val_sc)
+
+    query = wide(qkv_ref, i, group) * jnp.bfloat16(HDIM**-0.5)
     acc_sc[...] = jnp.zeros_like(acc_sc)
 
     def step(j, carry):
@@ -91,20 +101,21 @@
     top, total = lax.fori_loop(0, i+1, step, (jnp.full((1,width), -1e30, jnp.float32), jnp.zeros((1,width), jnp.float32)))
     result = acc_sc[...] / total
     flat_ref[0] = result
-    att_ref[...] = narrow(result.astype(jnp.bfloat16), group, BLOCK)
+    for k in range(2):
+        att_ref[k] = narrow(result, group, k).astype(jnp.bfloat16)
     lse_ref[0] = top + jnp.log(total)
 
 
 def attend_forward(qkv, group):
-    total = qkv.shape[0]; steps = total//BLOCK; lanes = group*HDIM; width = group*BLOCK
+    count = qkv.shape[0]; total = count*LANES; steps = total//BLOCK; lanes = group*HDIM; width = group*BLOCK
     return pl.pallas_call(
         functools.partial(forward_kernel, group),
         grid=(steps,),
-        in_specs=[pl.BlockSpec((total, lanes+2*HDIM), lambda i: (0,0))],
-        out_specs=[pl.BlockSpec((BLOCK, lanes), lambda i: (i,0)),
+        in_specs=[pl.BlockSpec((count, lanes+2*HDIM, LANES), lambda i: (0,0,0))],
+        out_specs=[pl.BlockSpec((2, lanes, LANES), lambda i: (i,0,0)),
                    pl.BlockSpec((1, HDIM, width), lambda i: (i,0,0)),
                    pl.BlockSpec((1,1,width), lambda i: (i,0,0))],
-        out_shape=[jax.ShapeDtypeStruct((total, lanes), jnp.bfloat16),
+        out_shape=[jax.ShapeDtypeStruct((count, lanes, LANES), jnp.bfloat16),
                    jax.ShapeDtypeStruct((steps,HDIM,width), jnp.float32),
                    jax.ShapeDtypeStruct((steps,1,width), jnp.float32)],
         scratch_shapes=[pltpu.VMEM((total,HDIM), jnp.bfloat16), pltpu.VMEM((HDIM,total), jnp.bfloat16), pltpu.VMEM((HDIM,width), jnp.float32)],
@@ -125,18 +136,15 @@
 
     @pl.when(i == 0)
     def _():
-        key = qkv_ref[:, lanes:lanes+HDIM]
-        key_sc[...] = key
-        keyt_sc[...] = key.T
-        val_sc[...] = qkv_ref[:, lanes+HDIM:lanes+2*HDIM]
+        spread(qkv_ref, lanes, key_sc, keyt_sc)
+        spread(qkv_ref, lanes + HDIM, val_sc, None)
         dk_sc[...] = jnp.zeros_like(dk_sc)
         dv_sc[...] = jnp.zeros_like(dv_sc)
 
     rows = pl.ds(pl.multiple_of(i*BLOCK, BLOCK), BLOCK)
-    block = qkv_ref[rows, :lanes] * jnp.bfloat16(scale)
-    query_w, query_t = wide(block, group), tall(block, group)
-    grad = grad_ref[...]
-    grad_w, grad_t = wide(grad, group), tall(grad, group)
+    query_w = wide(qkv_ref, i, group) * jnp.bfloat16(scale)
+    grad_w = wide(grad_ref, None, group)
+    query_t, grad_t = query_w.T, grad_w.T
     lse = lse_ref[0]
     delta = jnp.sum(grad_w.astype(jnp.float32)*flat_ref[0], axis=0, keepdims=True)
     dq_sc[...] = jnp.zeros_like(dq_sc)
@@ -155,33 +163,36 @@
     lax.fori_loop(0, i+1, step, 0)
     cosine, sine = cos_ref[:, rows], sin_ref[:, rows]
     pieces = [unrotate(dq_sc[:, h*BLOCK:(h+1)*BLOCK]*scale, cosine, sine).astype(jnp.bfloat16) for h in range(group)]
-    out_ref[rows, :lanes] = jnp.concatenate(pieces, axis=0).T
+    for k in range(2):
+        columns = slice(k * LANES, (k + 1) * LANES)
+        out_ref[2 * i + k, :lanes] = jnp.concatenate([p[:, columns] for p in pieces], axis=0)
 
     @pl.when(i == steps-1)
     def _():
         def finish(j, carry):
             here = pl.ds(pl.multiple_of(j*BLOCK, BLOCK), BLOCK)
             turned = unrotate(dk_sc[here,:].T, cos_ref[:,here], sin_ref[:,here]).astype(jnp.bfloat16)
-            both = jnp.concatenate([turned, dv_sc[here,:].astype(jnp.bfloat16).T], axis=0).T
-            out_ref[here, lanes:lanes+2*HDIM] = both
+            both = jnp.concatenate([turned, dv_sc[here,:].astype(jnp.bfloat16).T], axis=0)
+            for k in range(2):
+                out_ref[2 * j + k, lanes:] = both[:, k * LANES : (k + 1) * LANES]
             return carry
 
         lax.fori_loop(0, steps, finish, 0)
 
 
 def attend_backward(qkv, grad, flat, lse, cosine, sine, group):
-    total = qkv.shape[0]; steps = total//BLOCK; lanes = group*HDIM; width = group*BLOCK
+    count = qkv.shape[0]; total = count*LANES; steps = total//BLOCK; lanes = group*HDIM; width = group*BLOCK
     return pl.pallas_call(
         functools.partial(backward_kernel, group, steps),
         grid=(steps,),
-        in_specs=[pl.BlockSpec((total, lanes+2*HDIM), lambda i: (0,0)),
-                  pl.BlockSpec((BLOCK, lanes), lambda i: (i,0)),
+        in_specs=[pl.BlockSpec((count, lanes+2*HDIM, LANES), lambda i: (0,0,0)),
+                  pl.BlockSpec((2, lanes, LANES), lambda i: (i,0,0)),
                   pl.BlockSpec((1, HDIM, width), lambda i: (i,0,0)),
                   pl.BlockSpec((1,1,width), lambda i: (i,0,0)),
                   pl.BlockSpec((HDIM//2, total), lambda i: (0,0)),
                   pl.BlockSpec((HDIM//2, total), lambda i: (0,0))],
-        out_specs=pl.BlockSpec((total, lanes+2*HDIM), lambda i: (0,0)),
-        out_shape=jax.ShapeDtypeStruct((total, lanes+2*HDIM), jnp.bfloat16),
+        out_specs=pl.BlockSpec((count, lanes+2*HDIM, LANES), lambda i: (0,0,0)),
+        out_shape=jax.ShapeDtypeStruct((count, lanes+2*HDIM, LANES), jnp.bfloat16),
         scratch_shapes=[pltpu.VMEM((total,HDIM), jnp.bfloat16), pltpu.VMEM((HDIM,total), jnp.bfloat16), pltpu.VMEM((total,HDIM), jnp.bfloat16),
                         pltpu.VMEM((HDIM,width), jnp.float32), pltpu.VMEM((total,HDIM), jnp.float32), pltpu.VMEM((total,HDIM), jnp.float32)],
         compiler_params=pltpu.CompilerParams(dimension_semantics=("arbitrary",)),
@@ -322,6 +333,10 @@
     return results[:parts], results[parts : 2 * parts], results[2 * parts :]
 
 
+def contract(equation, left, right):
+    return jnp.einsum(equation, left, right, preferred_element_type=jnp.float32)
+
+
 def exchange(values):
     return lax.all_to_all(values, "blk", split_axis=0, concat_axis=0, tiled=True)
 
@@ -485,7 +500,8 @@
 
 
 class DenseSum:
-    def __init__(self, values, label, heads_first=False):
+    def __init__(self, values, label, heads_first=False, staged=False):
+        self.staged = staged
         self.heads = lax.axis_size("head")
         self.chips = lax.axis_size("blk") // 2
         self.rows = values.shape[0] // (2 * self.heads * self.chips)
@@ -508,15 +524,35 @@
         piece = lax.dynamic_slice(self.mine, (0, chip, 0, 0), (heads, 1, self.rows, columns))
         return piece.reshape(heads * self.rows, columns)
 
+    def blocks(self, offsets):
+        if not self.heads_first:
+            return [self.block(offset) for offset in offsets]
+        columns = self.mine.shape[3]
+        taken = [
+            lax.dynamic_slice(
+                self.mine, (0, ring_chip(offset), 0, 0), (self.heads, 1, self.rows, columns)
+            )
+            for offset in offsets
+        ]
+        total = head_share(jnp.concatenate(taken, axis=1))
+        return [total[0, k].astype(jnp.bfloat16) for k in range(len(offsets))]
+
     def ring(self):
-        if self.heads_first:
-            self.mine = head_share(self.mine).astype(jnp.bfloat16)
-        pairs = [(self.block(-k), self.block(k)) for k in range(1, self.chips // 2)]
-        opposite = self.block(self.chips // 2)
+        far = self.chips // 2
+        if self.staged:
+            stages = [[far, 1 - far, far - 1]]
+            stages += [[-k, k] for k in reversed(range(1, far - 1))] + [[0]]
+        else:
+            stages = [list(range(1 - far, far + 1))]
+        found = {}
+        for offsets in stages:
+            found.update(zip(offsets, self.blocks(offsets)))
+        pairs = [(found[-k], found[k]) for k in range(1, far)]
+        opposite = found[far]
         axis = 1 if self.heads_first else 0
         half = opposite.shape[1] // 256 * 128 if axis else opposite.shape[0] // 2
         opposite = jnp.split(opposite, [half], axis=axis)
-        return RingSum(self.block(0), pairs, opposite, self.label, axis)
+        return RingSum(found[0], pairs, opposite, self.label, axis)
 
     def finish(self, total):
         return total if self.heads_first else head_share(total.astype(jnp.bfloat16))
@@ -538,7 +574,7 @@
         )
         part = (part * cosine_ref[...] + turned * sine_ref[...]).astype(jnp.bfloat16)
         for k in range(groups):
-            out_ref[s, k] = part[:, k * span : (k + 1) * span]
+            out_ref[s, k] = part[:, k * span : (k + 1) * span].T
 
 
 def project(normed, weights, positions, groups, group):
@@ -561,8 +597,8 @@
             table,
             table,
         ],
-        out_specs=pl.BlockSpec((rows // shard, 2, shard, span), lambda j: (0, j, 0, 0)),
-        out_shape=jax.ShapeDtypeStruct((rows // shard, groups, shard, span), jnp.bfloat16),
+        out_specs=pl.BlockSpec((rows // shard, 2, span, shard), lambda j: (0, j, 0, 0)),
+        out_shape=jax.ShapeDtypeStruct((rows // shard, groups, span, shard), jnp.bfloat16),
         compiler_params=pltpu.CompilerParams(dimension_semantics=("arbitrary",)),
         cost_estimate=pl.CostEstimate(
             flops=2 * rows * width * groups * span,
@@ -651,20 +687,19 @@
     packed = project(normed, full_mixed, positions, groups, group)
 
     def to_pairs(values, columns):
-        values = values.reshape(pairs, 1, shard, columns)
-        values = jnp.broadcast_to(values, (pairs, copies, shard, columns))
-        return exchange(values.reshape(blk_count, shard, columns)).reshape(seq_total, columns)
+        values = values.reshape(pairs, 1, columns, shard)
+        values = jnp.broadcast_to(values, (pairs, copies, columns, shard))
+        return exchange(values.reshape(blk_count, columns, shard))
 
     def to_tokens(values, columns):
-        values = exchange(values.reshape(blk_count, shard, columns))
-        values = values.reshape(pairs, copies, shard, columns)[:, 0]
-        values = values.reshape(seq_local, groups, shard, columns).transpose(0, 2, 1, 3)
-        return values.reshape(token_rows, groups * columns)
+        values = exchange(values).reshape(pairs, copies, columns, shard)[:, 0]
+        return values.reshape(seq_local, groups * columns, shard)
 
     pair_qkv = to_pairs(packed, span)
     pair_attended, flat, log_total = attend_forward(pair_qkv, group)
     attended = to_tokens(pair_attended, lanes)
-    branch = matmul(attended, full_out)[:, :width]
+    branch = contract("sqt,qd->std", attended, full_out)
+    branch = branch.reshape(token_rows, -1)[:, :width]
     middle = residual + branch
     inverse_two = rms_scale(middle)
     normed_two = (middle * inverse_two * gain_second).astype(jnp.bfloat16)
@@ -694,18 +729,18 @@
     )
     rows_all, grads_all, d_lin_all, hidden_all = buffers
     back_ring = RingSum(back_own[0], back_pairs, back_opposite, "back")
-    others = [
-        matmul_tn(rows_all, d_lin_all[:, 2 * units :]).astype(jnp.bfloat16),
-        matmul_tn(hidden_all[:, units:], grads_all).astype(jnp.bfloat16),
-    ]
-    others = [partner(part) for part in others]
-    mine = [
-        matmul_tn(rows_all, d_lin_all[:, : 2 * units]) + others[0].astype(jnp.float32),
-        matmul_tn(hidden_all[:, :units], grads_all) + others[1].astype(jnp.float32),
-    ]
-    mine = [part.astype(jnp.bfloat16) for part in mine]
+    lefts = [lambda half: rows_all, lambda half: hidden_all[:, half * units :][:, :units]]
+    rights = [lambda half: d_lin_all[:, 2 * half * units :][:, : 2 * units], lambda half: grads_all]
+    others, mine = [], []
+    for left, right in zip(lefts, rights):
+        others.append(partner(matmul_tn(left(1), right(1)).astype(jnp.bfloat16)))
+    for k, (left, right) in enumerate(zip(lefts, rights)):
+        total = matmul_tn(left(0), right(0)) + others[k].astype(jnp.float32)
+        mine.append(total.astype(jnp.bfloat16))
     back_sum = back_ring.total()
-    theirs = [from_heads(part) for part in mine]
+    theirs = []
+    for part in mine:
+        theirs.append(from_heads(part))
     mixed_ring = RingSum(mixed_own[0], mixed_pairs, mixed_opposite, "mixed")
     (mixed_ring.onward, mixed_ring.back), back_sum = lax.optimization_barrier(
         ((mixed_ring.onward, mixed_ring.back), back_sum)
@@ -721,18 +756,17 @@
     d_mid_norm, grad_gain_second = norm_back(middle, inverse_two, gain_second, d_normed_two)
     d_mid = d_out + d_mid_norm
     d_branch = jnp.pad(d_mid.astype(jnp.bfloat16), ((0, 0), (0, LANES)))
-    d_attended = matmul_nt(d_branch, full_out).astype(jnp.bfloat16)
+    d_branch = d_branch.reshape(seq_local, shard, -1)
+    d_attended = contract("qd,std->sqt", full_out, d_branch).astype(jnp.bfloat16)
     early = add_lanes(
-        matmul_tn(attended, d_branch),
+        contract("sqt,std->qd", attended, d_branch),
         jnp.concatenate([grad_router, grad_gain_second[:, None]], axis=1),
     ).astype(jnp.bfloat16)
     mixed_ring.land()
     d_attended, early, mixed_ring.onward, mixed_ring.back = lax.optimization_barrier(
         (d_attended, early, mixed_ring.onward, mixed_ring.back)
     )
-    pair_grad = to_pairs(
-        d_attended.reshape(seq_local, shard, groups, lanes).transpose(0, 2, 1, 3), lanes
-    )
+    pair_grad = to_pairs(d_attended, lanes)
     pair_grad, mixed_ring.onward, mixed_ring.back = lax.optimization_barrier(
         (pair_grad, mixed_ring.onward, mixed_ring.back)
     )
@@ -743,26 +777,29 @@
     )
     early = DenseSum(early, "early", True).total()
     mixed_ring.land()
-    pair_d, mixed_ring.onward, mixed_ring.back = lax.optimization_barrier(
-        (pair_d, mixed_ring.onward, mixed_ring.back)
-    )
-    mixed_ring.send()
     d_linear = to_tokens(pair_d, span)
-    mixed_ring.land()
     d_linear, early = lax.optimization_barrier((d_linear, early))
-    grad_mixed = matmul_tn(normed, d_linear).astype(jnp.bfloat16)
-    late = DenseSum(grad_mixed, "late", True)
-    d_normed = matmul_nt(jnp.pad(d_linear, ((0, 0), (0, LANES))), full_mixed)
+    grad_mixed = contract(
+        "stf,sct->fc", normed.reshape(seq_local, shard, width), d_linear
+    ).astype(jnp.bfloat16)
+    late = DenseSum(grad_mixed, "late", True, True)
+    d_normed = contract(
+        "sct,fc->stf", jnp.pad(d_linear, ((0, 0), (0, LANES), (0, 0))), full_mixed
+    ).reshape(token_rows, width)
     d_tok_norm, grad_gain_first = norm_back(residual, inverse_one, gain_first, d_normed)
     grad_tokens = (d_mid + d_tok_norm).reshape(seq_local, shard, width)
+    grad_gain_first, mixed_ring.onward, mixed_ring.back = lax.optimization_barrier(
+        (grad_gain_first, mixed_ring.onward, mixed_ring.back)
+    )
+    mixed_ring.send().land()
     late.append(jnp.pad(grad_gain_first[:, None].astype(jnp.bfloat16), ((0, 0), (0, LANES - 1))))
     late_ring = late.ring()
     sums = [
         functools.reduce(jnp.add, [v.astype(jnp.float32) for v in others], part.astype(jnp.float32))
         for part, others in zip(mine, theirs)
     ]
-    grad_gate_sum, grad_up_sum = sums[0][:, :units], sums[0][:, units:]
-    grad_down_sum = sums[1]
+    grad_gate_sum, grad_up_sum = sums[0][None, :, :units], sums[0][None, :, units:]
+    grad_down_sum = sums[1][None]
     out = (middle + mixed_ring.total()).reshape(seq_local, shard, width)
     late = late.finish(late_ring.total())
     late_mixed = late[:, : groups * span].reshape(part_rows, groups, span)
@@ -776,9 +813,9 @@
         early[:, :width],
         early[:, width + experts],
         early[:, width : width + experts],
-        grad_gate_sum[None],
-        grad_up_sum[None],
-        grad_down_sum[None],
+        grad_gate_sum,
+        grad_up_sum,
+        grad_down_sum,
     )
 
 

time: 825 us -> 802 us (0.972)
  waiting for transfers between devices: 364 us -> 334 us
  local copies, waits for them, and re-layouts: 80.8 us -> 63.7 us
  other arithmetic: 54.2 us -> 66.8 us
  matrix products: 53.8 us -> 62.3 us
    ppermute x2, waiting for transfers between devices: 86.3 us -> 67.2 us  [from_heads(): lax.ppermute(values, 'head', [(k, (k + turn) % heads) for k in range(head...]
    dynamic_update_slice x16, local copies, waits for them, and re-layouts: 13.6 us -> 0.81 us  [dense_gather(): lax.dynamic_update_slice(full, part.reshape(heads, 1, 1, rows, columns),...]
    all_to_all x4, waiting for transfers between devices: 19.1 us -> 6.64 us  [exchange(): lax.all_to_all(values, 'blk', split_axis=0, concat_axis=0, tiled=True)]
    dot_general x2 -> x5, matrix products: 9.32 us -> 20.2 us  [contract(): return jnp.einsum(equation, left, right, preferred_element_type=jnp.float32)]
    ppermute x32, waiting for transfers between devices: 194 us -> 184 us  [ring_steps(): send_on = lambda values: lax.ppermute(values, 'blk', onward)]
    ppermute x2 -> x5, waiting for transfers between devices: 48 us -> 44.8 us  [head_share(): other = lax.ppermute(share(turn), 'head', moved)]
    dot_general x6 -> x4, matrix products: 38 us -> 35.3 us  [matmul_tn(): lax.dot_general(left, right, (((0,), (0,)), ((), ())), preferred_element_...]
  transfers between devices with their start and end apart: 90 -> 93, of which waited for: 34 -> 38; matrix products, arithmetic and copies ran while one was open for 20% -> 20% of each run, Pallas kernels for 16% -> 17%
where the time goes in v5:
time: 802 us; the launch traced here: 792 us
  waiting for transfers between devices  334 us (42%)
  Pallas kernels  145 us (18%)
  starting transfers between devices  118 us (15%)
  other arithmetic  66.8 us (8%)
  local copies, waits for them, and re-layouts  63.7 us (8%)
  matrix products  62.3 us (8%)
    ppermute x32, waiting for transfers between devices, ring_steps(): send_on = lambda values: lax.ppermute(values, 'blk', onward)  184 us
    pallas_call x5, Pallas kernels, expert_rows(): pl.pallas_call(functools.partial(expert_kernel, parts, rows, width, exper...  86.7 us
    ppermute x2, waiting for transfers between devices, from_heads(): lax.ppermute(values, 'head', [(k, (k + turn) % heads) for k in range(head...  67.2 us
    ppermute x32, starting transfers between devices, ring_steps(): send_on = lambda values: lax.ppermute(values, 'blk', onward)  66.7 us
    ppermute x5, waiting for transfers between devices, head_share(): other = lax.ppermute(share(turn), 'head', moved)  44.8 us
    dot_general x4, matrix products, matmul_tn(): lax.dot_general(left, right, (((0,), (0,)), ((), ())), preferred_element_...  35.3 us
    pallas_call x1, Pallas kernels, attend_backward(): pl.pallas_call(functools.partial(backward_kernel, group, steps), grid=(st...  28.2 us
    ppermute x32, starting transfers between devices, ring_steps(): send_back = lambda values: lax.ppermute(values, 'blk', back)  22.8 us
  transfers between devices with their start and end apart: 93, of which 38 were waited for; matrix products, arithmetic and copies ran while one was open for 20% of the time, Pallas kernels for 17%

profile of v5, /device:TPU:0, one launch (start us, length us, event | category | flops | bytes accessed | tf_op | source)
XLA Modules:
  0.0 791.9 jit_solution(14124368799646765519)
XLA Ops:
  29.0 5.6 collective-permute-done.19
  36.6 4.9 collective-permute-done.22
  52.0 4.8 collective-permute-done.2
  60.1 10.9 %collective-permute-done.6 = bf16[96,2688]{1,0:T(8,128)(2,1)S(1)} collective-permute-done((bf16[96,2688]{1,0:T(8,128)(2,1)S(1)}, bf16[96,2688]{1,0:T(8,128)(2,1)S(1)}, u32[]{:S(2)}, u32[]{:S(2)}) %collective-permute-start.6) | collective-permute-done | bytes 516128 | tf_op jit(solution)/shard_map/ppermute | solution.py:374
  73.9 11.4 %collective-permute-done.10 = bf16[96,2688]{1,0:T(8,128)(2,1)S(1)} collective-permute-done((bf16[96,2688]{1,0:T(8,128)(2,1)S(1)}, bf16[96,2688]{1,0:T(8,128)(2,1)S(1)}, u32[]{:S(2)}, u32[]{:S(2)}) %collective-permute-start.10) | collective-permute-done | bytes 516128 | tf_op jit(solution)/shard_map/ppermute | solution.py:374
  89.2 4.8 collective-permute-done.14
  107.1 8.1 %project.1 = bf16[2,8,320,128]{3,2,1,0:T(8,128)(2,1)} custom-call(bf16[256,1536]{1,0:T(8,128)(2,1)} %multiply_convert_fusion.2.rows_ref, bf16[1536,2688]{1,0:T(8,128)(2,1)} %bitcast.241, f32[128,640]{1,0:T(8,128)} %concatenate.58.cosine_ref, f32[128,640]{1,0:T(8,128)} %concatenate.59.sine_ref), custom_call_target="tpu_custom_call" | custom-call | flops 2013265920 | bytes 7864320 | tf_op jit(solution)/shard_map/project/pallas_call | solution.py:591
  115.2 5.9 all-to-all-start
  128.2 33.5 %collective-permute-done.38.refs_2_ = bf16[256,1664]{1,0:T(8,128)(2,1)} collective-permute-done((bf16[256,1664]{1,0:T(8,128)(2,1)}, bf16[256,1664]{1,0:T(8,128)(2,1)}, u32[]{:S(2)}, u32[]{:S(2)}) %collective-permute-start.38) | collective-permute-done | bytes 852000 | tf_op jit(solution)/shard_map/ppermute | solution.py:374
  161.8 8.6 %collective-permute-start.39 = (bf16[256,1664]{1,0:T(8,128)(2,1)}, bf16[256,1664]{1,0:T(8,128)(2,1)}, u32[]{:S(2)}, u32[]{:S(2)}) collective-permute-start(bf16[256,1664]{1,0:T(8,128)(2,1)} %collective-permute-done.38.refs_2_), channel_id=1, source_target_pairs={{0,4},{1,5},{4,8},{5,9},{8,12},{9,13},{12,14},{13,15},{14,10},{15,... | collective-permute-start | bytes 2555912 | tf_op jit(solution)/shard_map/ppermute | solution.py:374
  174.0 14.6 %collective-permute-done.39.refs_2_ = bf16[256,1664]{1,0:T(8,128)(2,1)} collective-permute-done((bf16[256,1664]{1,0:T(8,128)(2,1)}, bf16[256,1664]{1,0:T(8,128)(2,1)}, u32[]{:S(2)}, u32[]{:S(2)}) %collective-permute-start.39) | collective-permute-done | bytes 852000 | tf_op jit(solution)/shard_map/ppermute | solution.py:374
  196.3 22.3 %attend_forward.1 = (bf16[16,192,128]{2,1,0:T(8,128)(2,1)}, f32[8,64,768]{2,1,0:T(8,128)}, f32[8,1,768]{2,1,0:T(1,128)}) custom-call(bf16[16,320,128]{2,1,0:T(8,128)(2,1)} %all-to-all-done.qkv_ref), custom_call_target="tpu_custom_call" | custom-call | tf_op jit(solution)/shard_map/attend_forward/pallas_call | solution.py:111
  218.6 5.2 all-to-all-start.1
  223.7 6.0 pad_maximum_fusion.refs_3_.refs_5_
  235.8 6.6 all-to-all-done.1
  244.7 4.1 multiply_reduce_fusion.4
  253.9 12.6 %expert_rows.5 = (bf16[256,1536]{1,0:T(8,128)(2,1)}, bf16[256,1664]{1,0:T(8,128)(2,1)}, bf16[2048,1536]{1,0:T(8,128)(2,1)}, bf16[2048,1536]{1,0:T(8,128)(2,1)}, ...) custom-call(s32[2]{0:T(128)} %pad_add_fusion.2.index_ref, bf16[256,1536]{1,0:T(8,128)(2,1)} %multiply_convert_fusion.1.refs_0_, ...), custom_call_target="tpu_custom_call" | custom-call | flops 4831838208 | bytes 17301504 | tf_op jit(solution)/shard_map/expert_rows/pallas_call | solution.py:295
  266.5 3.9 collective-permute-done.29.refs_0_
  273.0 20.6 %expert_rows.6 = (bf16[256,1536]{1,0:T(8,128)(2,1)}, bf16[256,1536]{1,0:T(8,128)(2,1)}, bf16[256,1664]{1,0:T(8,128)(2,1)}, bf16[256,1664]{1,0:T(8,128)(2,1)}, bf...) custom-call(s32[2]{0:T(128)} %pad_add_fusion.2.index_ref, ...), custom_call_target="tpu_custom_call", output_to_operand_aliasing={{4}: (8, {}), {5}: (9, {}), {6}: (10, {}), {7}: (11, {})} | custom-call | flops 9663676416 | bytes 25165824 | tf_op jit(solution)/shard_map/expert_rows/pallas_call | solution.py:295
  295.9 20.5 %expert_rows.7 = (bf16[256,1536]{1,0:T(8,128)(2,1)}, bf16[256,1536]{1,0:T(8,128)(2,1)}, bf16[256,1664]{1,0:T(8,128)(2,1)}, bf16[256,1664]{1,0:T(8,128)(2,1)}, bf...) custom-call(s32[2]{0:T(128)} %pad_add_fusion.2.index_ref, ...), custom_call_target="tpu_custom_call", output_to_operand_aliasing={{4}: (8, {}), {5}: (9, {}), {6}: (10, {}), {7}: (11, {})} | custom-call | flops 9663676416 | bytes 25165824 | tf_op jit(solution)/shard_map/expert_rows/pallas_call | solution.py:295
  322.1 20.5 %expert_rows.8 = (bf16[256,1536]{1,0:T(8,128)(2,1)}, bf16[256,1536]{1,0:T(8,128)(2,1)}, bf16[256,1664]{1,0:T(8,128)(2,1)}, bf16[256,1664]{1,0:T(8,128)(2,1)}, bf...) custom-call(s32[2]{0:T(128)} %pad_add_fusion.2.index_ref, ...), custom_call_target="tpu_custom_call", output_to_operand_aliasing={{4}: (8, {}), {5}: (9, {}), {6}: (10, {}), {7}: (11, {})} | custom-call | flops 9663676416 | bytes 25165824 | tf_op jit(solution)/shard_map/expert_rows/pallas_call | solution.py:295
  343.5 12.6 %expert_rows.9 = (bf16[128,1536]{1,0:T(8,128)(2,1)}, bf16[128,1536]{1,0:T(8,128)(2,1)}, bf16[128,1664]{1,0:T(8,128)(2,1)}, bf16[128,1664]{1,0:T(8,128)(2,1)}, bf...) custom-call(s32[2]{0:T(128)} %pad_add_fusion.2.index_ref, ...), custom_call_target="tpu_custom_call", output_to_operand_aliasing={{4}: (8, {}), {5}: (9, {}), {6}: (10, {}), {7}: (11, {})} | custom-call | flops 4831838208 | bytes 17301504 | tf_op jit(solution)/shard_map/expert_rows/pallas_call | solution.py:295
  358.2 8.6 %collective-permute-done.45 = bf16[128,1664]{1,0:T(8,128)(2,1)S(1)} collective-permute-done((bf16[128,1664]{1,0:T(8,128)(2,1)}, bf16[128,1664]{1,0:T(8,128)(2,1)S(1)}, u32[]{:S(2)}, u32[]{:S(2)}) %collective-permute-start.45) | collective-permute-done | bytes 426016 | tf_op jit(solution)/shard_map/ppermute | solution.py:374
  370.3 16.6 %collective-permute-done.46 = bf16[256,1664]{1,0:T(8,128)(2,1)S(1)} collective-permute-done((bf16[256,1664]{1,0:T(8,128)(2,1)S(1)}, bf16[256,1664]{1,0:T(8,128)(2,1)S(1)}, u32[]{:S(2)}, u32[]{:S(2)}) %collective-permute-start.46) | collective-permute-done | bytes 852000 | tf_op jit(solution)/shard_map/ppermute | solution.py:374
  389.5 16.5 %collective-permute-done.47 = bf16[256,1664]{1,0:T(8,128)(2,1)S(1)} collective-permute-done((bf16[256,1664]{1,0:T(8,128)(2,1)S(1)}, bf16[256,1664]{1,0:T(8,128)(2,1)S(1)}, u32[]{:S(2)}, u32[]{:S(2)}) %collective-permute-start.47) | collective-permute-done | bytes 852000 | tf_op jit(solution)/shard_map/ppermute | solution.py:374
  411.0 12.2 %collective-permute-done.48 = bf16[256,1664]{1,0:T(8,128)(2,1)S(1)} collective-permute-done((bf16[256,1664]{1,0:T(8,128)(2,1)S(1)}, bf16[256,1664]{1,0:T(8,128)(2,1)S(1)}, u32[]{:S(2)}, u32[]{:S(2)}) %collective-permute-start.48) | collective-permute-done | bytes 852000 | tf_op jit(solution)/shard_map/ppermute | solution.py:374
  437.2 5.0 fusion.13
  449.3 5.1 collective-permute-done.55
  462.5 9.7 %fusion.6 = bf16[1536,1024]{1,0:T(8,128)(2,1)} fusion(bf16[2048,1536]{1,0:T(8,128)(2,1)S(1)} %bitcast.235, bf16[2048,2048]{1,0:T(8,128)(2,1)} %get-tuple-element.121), kind=kOutput, calls=%fused_computation.25 | convolution fusion | flops 6444023808 | bytes 13631488 | tf_op jit(solution)/shard_map/dot_general | solution.py:51
  478.1 13.3 %collective-permute-done.56 = bf16[1,8,48,1664]{3,2,1,0:T(8,128)(2,1)} collective-permute-done((bf16[1,8,48,1664]{3,2,1,0:T(8,128)(2,1)}, bf16[1,8,48,1664]{3,2,1,0:T(8,128)(2,1)}, u32[]{:S(2)}, u32[]{:S(2)}) %collective-permute-start.56) | collective-permute-done | bytes 1277984 | tf_op jit(solution)/shard_map/ppermute | solution.py:497
  501.4 8.0 %convolution_convert_fusion = bf16[512,1536]{1,0:T(8,128)(2,1)} fusion(bf16[2048,1536]{1,0:T(8,128)(2,1)} %get-tuple-element.123, bf16[2048,1024]{1,0:T(8,128)(2,1)} %get-tuple-element.122), kind=kOutput, calls=%fused_computation.31 | convolution fusion | flops 3222011904 | bytes 9961472 | tf_op jit(solution)/shard_map/dot_general | solution.py:51
  510.4 28.2 %attend_backward.1 = bf16[16,320,128]{2,1,0:T(8,128)(2,1)} custom-call(bf16[16,320,128]{2,1,0:T(8,128)(2,1)} %all-to-all-done.qkv_ref, bf16[16,192,128]{2,1,0:T(8,128)(2,1)} %copy-done.15, f32[8,64,768]{2,1,0:T(8,128)} %get-tuple-element.104.flat_ref, f32[8,1,768]{2,1,0:T(1,128)} %get-tuple-element.105.lse_ref, f32[32,2048]{1,0:T(8,128)} %get-tuple-element.227.cos_ref, ...), custom_call_target="tpu_custom_call" | custom-call | tf_op jit(solution)/shard_map/attend_backward/pallas_call | solution.py:185
  538.6 4.4 all-to-all-start.3
  546.2 11.9 %add_convert_fusion = bf16[1536,1024]{1,0:T(8,128)(2,1)} fusion(bf16[1536,1024]{1,0:T(8,128)(2,1)} %collective-permute-done.85, bf16[2048,1536]{1,0:T(8,128)(2,1)} %get-tuple-element.120, bf16[2048,2048]{1,0:T(8,128)(2,1)} %get-tuple-element.121), kind=kOutput, calls=%fused_computation.14 | convolution fusion | flops 6447169536 | bytes 16777216 | tf_op jit(solution)/shard_map/dot_general | solution.py:51
  558.6 10.1 %collective-permute-done.59 = bf16[48,1664]{1,0:T(8,128)(2,1)S(1)} collective-permute-done((bf16[48,1664]{1,0:T(8,128)(2,1)S(1)}, bf16[48,1664]{1,0:T(8,128)(2,1)S(1)}, u32[]{:S(2)}, u32[]{:S(2)}) %collective-permute-start.59) | collective-permute-done | bytes 159776 | tf_op jit(solution)/shard_map/ppermute | solution.py:374
  569.7 10.5 %collective-permute-start.60 = (bf16[48,1664]{1,0:T(8,128)(2,1)S(1)}, bf16[48,1664]{1,0:T(8,128)(2,1)S(1)}, u32[]{:S(2)}, u32[]{:S(2)}) collective-permute-start(bf16[48,1664]{1,0:T(8,128)(2,1)S(1)} %get-tuple-element.212), channel_id=1, source_target_pairs={{0,4},{1,5},{4,8},{5,9},{8,12},{9,13},{12,14},{13,15},{14,10},{15,... | collective-permute-start | bytes 479240 | tf_op jit(solution)/shard_map/ppermute | solution.py:374
  580.5 5.7 fusion.9
  594.7 67.2 %collective-permute-done.88 = bf16[512,1536]{1,0:T(8,128)(2,1)} collective-permute-done((bf16[512,1536]{1,0:T(8,128)(2,1)}, bf16[512,1536]{1,0:T(8,128)(2,1)}, u32[]{:S(2)}, u32[]{:S(2)}) %collective-permute-start.88) | collective-permute-done | bytes 1572896 | tf_op jit(solution)/shard_map/ppermute | solution.py:347
  661.9 4.0 add_bitcast_fusion
  670.3 4.3 convert_add_fusion
  680.9 6.0 multiply_reduce_fusion
  699.6 12.3 %collective-permute-done.67 = bf16[256,1536]{1,0:T(8,128)(2,1)} collective-permute-done((bf16[256,1536]{1,0:T(8,128)(2,1)}, bf16[256,1536]{1,0:T(8,128)(2,1)}, u32[]{:S(2)}, u32[]{:S(2)}) %collective-permute-start.67) | collective-permute-done | bytes 786464 | tf_op jit(solution)/shard_map/ppermute | solution.py:374
  717.3 4.8 bitcast_add_fusion.1
  724.9 17.9 %collective-permute-done.74 = bf16[1,3,48,2688]{3,2,1,0:T(8,128)(2,1)S(1)} collective-permute-done((bf16[1,3,48,2688]{3,2,1,0:T(8,128)(2,1)S(1)}, bf16[1,3,48,2688]{3,2,1,0:T(8,128)(2,1)S(1)}, u32[]{:S(2)}, u32[]{:S(2)}) %collective-permute-start.74) | collective-permute-done | bytes 774176 | tf_op jit(solution)/shard_map/ppermute | solution.py:497
  745.2 5.5 collective-permute-done.75
  751.5 11.6 %collective-permute-done.77 = bf16[1,2,48,2688]{3,2,1,0:T(8,128)(2,1)S(1)} collective-permute-done((bf16[1,2,48,2688]{3,2,1,0:T(8,128)(2,1)S(1)}, bf16[1,2,48,2688]{3,2,1,0:T(8,128)(2,1)S(1)}, u32[]{:S(2)}, u32[]{:S(2)}) %collective-permute-start.77) | collective-permute-done | bytes 516128 | tf_op jit(solution)/shard_map/ppermute | solution.py:497
  764.8 6.2 collective-permute-done.82
  776.1 3.8 collective-permute-done.78
  (428 shorter events, 232.4 us)
Async XLA Ops:
  3.9 19.4 %collective-permute-start.17 = (bf16[48,1664]{1,0:T(8,128)(2,1)}, bf16[48,1664]{1,0:T(8,128)(2,1)}, u32[]{:S(2)}, u32[]{:S(2)}) collective-permute-start(bf16[48,1664]{1,0:T(8,128)(2,1)} %concatenate.60), channel_id=1, source_target_pairs={{0,4},{1,5},{4,8},{5,9},{8,12},{9,13},{12,14},{13,15},{14,10},{15,... | collective-permute-start | bytes 479240 | tf_op jit(solution)/shard_map/ppermute | solution.py:374
  10.5 115.7 %collective-permute-start.37 = (bf16[256,1664]{1,0:T(8,128)(2,1)}, bf16[256,1664]{1,0:T(8,128)(2,1)}, u32[]{:S(2)}, u32[]{:S(2)}) collective-permute-start(bf16[256,1664]{1,0:T(8,128)(2,1)} %concatenate.62.refs_1_), channel_id=1, source_target_pairs={{0,4},{1,5},{4,8},{5,9},{8,12},{9,13},{12,14},{13,15},{14,10},{15,... | collective-permute-start | bytes 2555912 | tf_op jit(solution)/shard_map/ppermute | solution.py:374
  12.5 115.3 %collective-permute-start.41 = (bf16[256,1664]{1,0:T(8,128)(2,1)}, bf16[256,1664]{1,0:T(8,128)(2,1)}, u32[]{:S(2)}, u32[]{:S(2)}) collective-permute-start(bf16[256,1664]{1,0:T(8,128)(2,1)} %concatenate.62.refs_1_), channel_id=1, source_target_pairs={{4,0},{5,1},{8,4},{9,5},{12,8},{13,9},{14,12},{15,13},{10,14},{11,... | collective-permute-start | bytes 2555912 | tf_op jit(solution)/shard_map/ppermute | solution.py:375
  28.3 28.5 %collective-permute-start.1 = (bf16[96,2688]{1,0:T(8,128)(2,1)S(1)}, bf16[96,2688]{1,0:T(8,128)(2,1)S(1)}, u32[]{:S(2)}, u32[]{:S(2)}) collective-permute-start(bf16[96,2688]{1,0:T(8,128)(2,1)S(1)} %bitcast.257), channel_id=1, source_target_pairs={{0,1},{1,0},{2,3},{3,2},{4,5},{5,4},{6,7},{7,6},{8,9},{9,8},{10,11... | collective-permute-start | bytes 1548296 | tf_op jit(solution)/shard_map/ppermute | solution.py:354
  94.0 129.8 %collective-permute-start.27 = (bf16[1,1536,1024]{2,1,0:T(8,128)(2,1)}, bf16[1,1536,1024]{2,1,0:T(8,128)(2,1)}, u32[]{:S(2)}, u32[]{:S(2)}) collective-permute-start(bf16[1,1536,1024]{2,1,0:T(8,128)(2,1)} %constant_dynamic-update-slice_fusion.2), channel_id=1, source_target_pairs={{0,1},{1,0},{2,3},{3,2},{4,5},{5,4},{6,7},{7,6},{8,9},{9,8},{10,11... | collective-permute-start | bytes 9437192 | tf_op jit(solution)/shard_map/ppermute | solution.py:354
  95.9 28.7 %collective-permute-start.25 = (bf16[8,48,1664]{2,1,0:T(8,128)(2,1)S(1)}, bf16[8,48,1664]{2,1,0:T(8,128)(2,1)S(1)}, u32[]{:S(2)}, u32[]{:S(2)}) collective-permute-start(bf16[8,48,1664]{2,1,0:T(8,128)(2,1)S(1)} %fusion.51), channel_id=1, source_target_pairs={{0,16},{16,0},{1,17},{17,1},{2,18},{18,2},{3,19},{19,3},{4,20},{20... | collective-permute-start | bytes 3833864 | tf_op jit(solution)/shard_map/ppermute | solution.py:444
  115.2 81.1 %all-to-all-start = ((bf16[16,320,128]{2,1,0:T(8,128)(2,1)}), bf16[16,320,128]{2,1,0:T(8,128)(2,1)}, u32[]{:S(2)}, u32[]{:S(2)}) async-start(bf16[16,320,128]{2,1,0:T(8,128)(2,1)} %bitcast.254), calls=%async_computation | async-start | bytes 2621440 | tf_op jit(solution)/shard_map/all_to_all | solution.py:341
  125.7 104.1 %collective-permute-start.26 = (bf16[2,8,48,1664]{3,2,1,0:T(8,128)(2,1)}, bf16[2,8,48,1664]{3,2,1,0:T(8,128)(2,1)}, u32[]{:S(2)}, u32[]{:S(2)}) collective-permute-start(bf16[2,8,48,1664]{3,2,1,0:T(8,128)(2,1)} %bitcast_dynamic-update-slice_fusion), channel_id=1, source_target_pairs={{0,1},{1,0},{2,3},{3,2},{4,5},{5,4},{6,7},{7,6},{8,9},{9,8},{10,11... | collective-permute-start | bytes 7667720 | tf_op jit(solution)/shard_map/ppermute | solution.py:354
  125.7 46.7 %collective-permute-start.28 = (bf16[1,512,1536]{2,1,0:T(8,128)(2,1)}, bf16[1,512,1536]{2,1,0:T(8,128)(2,1)}, u32[]{:S(2)}, u32[]{:S(2)}) collective-permute-start(bf16[1,512,1536]{2,1,0:T(8,128)(2,1)} %param.23), channel_id=1, source_target_pairs={{0,1},{1,0},{2,3},{3,2},{4,5},{5,4},{6,7},{7,6},{8,9},{9,8},{10,11... | collective-permute-start | bytes 4718600 | tf_op jit(solution)/shard_map/ppermute | solution.py:354
  126.2 35.5 %collective-permute-start.38 = (bf16[256,1664]{1,0:T(8,128)(2,1)}, bf16[256,1664]{1,0:T(8,128)(2,1)}, u32[]{:S(2)}, u32[]{:S(2)}) collective-permute-start(bf16[256,1664]{1,0:T(8,128)(2,1)} %collective-permute-done.37.refs_2_), channel_id=1, source_target_pairs={{0,4},{1,5},{4,8},{5,9},{8,12},{9,13},{12,14},{13,15},{14,10},{15,... | collective-permute-start | bytes 2555912 | tf_op jit(solution)/shard_map/ppermute | solution.py:374
  127.8 42.5 %collective-permute-start.42 = (bf16[256,1664]{1,0:T(8,128)(2,1)}, bf16[256,1664]{1,0:T(8,128)(2,1)}, u32[]{:S(2)}, u32[]{:S(2)}) collective-permute-start(bf16[256,1664]{1,0:T(8,128)(2,1)} %collective-permute-done.41.refs_3_), channel_id=1, source_target_pairs={{4,0},{5,1},{8,4},{9,5},{12,8},{13,9},{14,12},{15,13},{10,14},{11,... | collective-permute-start | bytes 2555912 | tf_op jit(solution)/shard_map/ppermute | solution.py:375
  161.8 26.8 %collective-permute-start.39 = (bf16[256,1664]{1,0:T(8,128)(2,1)}, bf16[256,1664]{1,0:T(8,128)(2,1)}, u32[]{:S(2)}, u32[]{:S(2)}) collective-permute-start(bf16[256,1664]{1,0:T(8,128)(2,1)} %collective-permute-done.38.refs_2_), channel_id=1, source_target_pairs={{0,4},{1,5},{4,8},{5,9},{8,12},{9,13},{12,14},{13,15},{14,10},{15,... | collective-permute-start | bytes 2555912 | tf_op jit(solution)/shard_map/ppermute | solution.py:374
  170.3 22.5 %collective-permute-start.43 = (bf16[256,1664]{1,0:T(8,128)(2,1)}, bf16[256,1664]{1,0:T(8,128)(2,1)}, u32[]{:S(2)}, u32[]{:S(2)}) collective-permute-start(bf16[256,1664]{1,0:T(8,128)(2,1)} %collective-permute-done.42.refs_3_), channel_id=1, source_target_pairs={{4,0},{5,1},{8,4},{9,5},{12,8},{13,9},{14,12},{15,13},{10,14},{11,... | collective-permute-start | bytes 2555912 | tf_op jit(solution)/shard_map/ppermute | solution.py:375
  190.3 152.3 %collective-permute-start.40 = (bf16[128,1664]{1,0:T(8,128)(2,1)}, bf16[128,1664]{1,0:T(8,128)(2,1)}, u32[]{:S(2)}, u32[]{:S(2)}) collective-permute-start(bf16[128,1664]{1,0:T(8,128)(2,1)} %slice.237), channel_id=1, source_target_pairs={{0,4},{1,5},{4,8},{5,9},{8,12},{9,13},{12,14},{13,15},{14,10},{15,... | collective-permute-start | bytes 1277960 | tf_op jit(solution)/shard_map/ppermute | solution.py:374
  194.6 148.0 %collective-permute-start.44 = (bf16[128,1664]{1,0:T(8,128)(2,1)}, bf16[128,1664]{1,0:T(8,128)(2,1)}, u32[]{:S(2)}, u32[]{:S(2)}) collective-permute-start(bf16[128,1664]{1,0:T(8,128)(2,1)} %slice.238), channel_id=1, source_target_pairs={{4,0},{5,1},{8,4},{9,5},{12,8},{13,9},{14,12},{15,13},{10,14},{11,... | collective-permute-start | bytes 1277960 | tf_op jit(solution)/shard_map/ppermute | solution.py:375
  218.6 23.9 %all-to-all-start.1 = ((bf16[16,192,128]{2,1,0:T(8,128)(2,1)}), bf16[16,192,128]{2,1,0:T(8,128)(2,1)}, u32[]{:S(2)}, u32[]{:S(2)}) async-start(bf16[16,192,128]{2,1,0:T(8,128)(2,1)} %get-tuple-element.68), calls=%async_computation.1 | async-start | bytes 1572864 | tf_op jit(solution)/shard_map/all_to_all | solution.py:341
  250.1 20.3 %collective-permute-start.29 = (bf16[256,1536]{1,0:T(8,128)(2,1)}, bf16[256,1536]{1,0:T(8,128)(2,1)}, u32[]{:S(2)}, u32[]{:S(2)}) collective-permute-start(bf16[256,1536]{1,0:T(8,128)(2,1)} %multiply_convert_fusion.1.refs_0_), channel_id=1, source_target_pairs={{0,4},{1,5},{4,8},{5,9},{8,12},{9,13},{12,14},{13,15},{14,10},{15,... | collective-permute-start | bytes 2359304 | tf_op jit(solution)/shard_map/ppermute | solution.py:374
  252.1 20.7 %collective-permute-start.33 = (bf16[256,1536]{1,0:T(8,128)(2,1)}, bf16[256,1536]{1,0:T(8,128)(2,1)}, u32[]{:S(2)}, u32[]{:S(2)}) collective-permute-start(bf16[256,1536]{1,0:T(8,128)(2,1)} %multiply_convert_fusion.1.refs_0_), channel_id=1, source_target_pairs={{4,0},{5,1},{8,4},{9,5},{12,8},{13,9},{14,12},{15,13},{10,14},{11,... | collective-permute-start | bytes 2359304 | tf_op jit(solution)/shard_map/ppermute | solution.py:375
  270.3 23.3 %collective-permute-start.30 = (bf16[256,1536]{1,0:T(8,128)(2,1)}, bf16[256,1536]{1,0:T(8,128)(2,1)}, u32[]{:S(2)}, u32[]{:S(2)}) collective-permute-start(bf16[256,1536]{1,0:T(8,128)(2,1)} %collective-permute-done.29.refs_0_), channel_id=1, source_target_pairs={{0,4},{1,5},{4,8},{5,9},{8,12},{9,13},{12,14},{13,15},{14,10},{15,... | collective-permute-start | bytes 2359304 | tf_op jit(solution)/shard_map/ppermute | solution.py:374
  272.8 22.8 %collective-permute-start.34 = (bf16[256,1536]{1,0:T(8,128)(2,1)}, bf16[256,1536]{1,0:T(8,128)(2,1)}, u32[]{:S(2)}, u32[]{:S(2)}) collective-permute-start(bf16[256,1536]{1,0:T(8,128)(2,1)} %collective-permute-done.33.refs_1_), channel_id=1, source_target_pairs={{4,0},{5,1},{8,4},{9,5},{12,8},{13,9},{14,12},{15,13},{10,14},{11,... | collective-permute-start | bytes 2359304 | tf_op jit(solution)/shard_map/ppermute | solution.py:375
  293.6 22.7 %collective-permute-start.31 = (bf16[256,1536]{1,0:T(8,128)(2,1)}, bf16[256,1536]{1,0:T(8,128)(2,1)}, u32[]{:S(2)}, u32[]{:S(2)}) collective-permute-start(bf16[256,1536]{1,0:T(8,128)(2,1)} %collective-permute-done.30.refs_0_), channel_id=1, source_target_pairs={{0,4},{1,5},{4,8},{5,9},{8,12},{9,13},{12,14},{13,15},{14,10},{15,... | collective-permute-start | bytes 2359304 | tf_op jit(solution)/shard_map/ppermute | solution.py:374
  295.6 24.5 %collective-permute-start.35 = (bf16[256,1536]{1,0:T(8,128)(2,1)}, bf16[256,1536]{1,0:T(8,128)(2,1)}, u32[]{:S(2)}, u32[]{:S(2)}) collective-permute-start(bf16[256,1536]{1,0:T(8,128)(2,1)} %collective-permute-done.34.refs_1_), channel_id=1, source_target_pairs={{4,0},{5,1},{8,4},{9,5},{12,8},{13,9},{14,12},{15,13},{10,14},{11,... | collective-permute-start | bytes 2359304 | tf_op jit(solution)/shard_map/ppermute | solution.py:375
  318.1 24.5 %collective-permute-start.32 = (bf16[128,1536]{1,0:T(8,128)(2,1)}, bf16[128,1536]{1,0:T(8,128)(2,1)S(1)}, u32[]{:S(2)}, u32[]{:S(2)}) collective-permute-start(bf16[128,1536]{1,0:T(8,128)(2,1)} %slice.235), channel_id=1, source_target_pairs={{0,4},{1,5},{4,8},{5,9},{8,12},{9,13},{12,14},{13,15},{14,10},{15,... | collective-permute-start | bytes 1179656 | tf_op jit(solution)/shard_map/ppermute | solution.py:374
  321.9 20.8 %collective-permute-start.36 = (bf16[128,1536]{1,0:T(8,128)(2,1)}, bf16[128,1536]{1,0:T(8,128)(2,1)S(1)}, u32[]{:S(2)}, u32[]{:S(2)}) collective-permute-start(bf16[128,1536]{1,0:T(8,128)(2,1)} %slice.236), channel_id=1, source_target_pairs={{4,0},{5,1},{8,4},{9,5},{12,8},{13,9},{14,12},{15,13},{10,14},{11,... | collective-permute-start | bytes 1179656 | tf_op jit(solution)/shard_map/ppermute | solution.py:375
  368.0 18.9 %collective-permute-start.46 = (bf16[256,1664]{1,0:T(8,128)(2,1)S(1)}, bf16[256,1664]{1,0:T(8,128)(2,1)S(1)}, u32[]{:S(2)}, u32[]{:S(2)}) collective-permute-start(bf16[256,1664]{1,0:T(8,128)(2,1)S(1)} %pad_add_fusion.1), channel_id=1, source_target_pairs={{0,4},{1,5},{4,8},{5,9},{8,12},{9,13},{12,14},{13,15},{14,10},{15,... | collective-permute-start | bytes 2555912 | tf_op jit(solution)/shard_map/ppermute | solution.py:374
  369.9 19.0 %collective-permute-start.50 = (bf16[256,1664]{1,0:T(8,128)(2,1)S(1)}, bf16[256,1664]{1,0:T(8,128)(2,1)S(1)}, u32[]{:S(2)}, u32[]{:S(2)}) collective-permute-start(bf16[256,1664]{1,0:T(8,128)(2,1)S(1)} %pad_add_fusion), channel_id=1, source_target_pairs={{4,0},{5,1},{8,4},{9,5},{12,8},{13,9},{14,12},{15,13},{10,14},{11,... | collective-permute-start | bytes 2555912 | tf_op jit(solution)/shard_map/ppermute | solution.py:375
  387.1 18.9 %collective-permute-start.47 = (bf16[256,1664]{1,0:T(8,128)(2,1)S(1)}, bf16[256,1664]{1,0:T(8,128)(2,1)S(1)}, u32[]{:S(2)}, u32[]{:S(2)}) collective-permute-start(bf16[256,1664]{1,0:T(8,128)(2,1)S(1)} %add.597), channel_id=1, source_target_pairs={{0,4},{1,5},{4,8},{5,9},{8,12},{9,13},{12,14},{13,15},{14,10},{15,... | collective-permute-start | bytes 2555912 | tf_op jit(solution)/shard_map/ppermute | solution.py:374
  389.1 18.9 %collective-permute-start.51 = (bf16[256,1664]{1,0:T(8,128)(2,1)S(1)}, bf16[256,1664]{1,0:T(8,128)(2,1)S(1)}, u32[]{:S(2)}, u32[]{:S(2)}) collective-permute-start(bf16[256,1664]{1,0:T(8,128)(2,1)S(1)} %add.601), channel_id=1, source_target_pairs={{4,0},{5,1},{8,4},{9,5},{12,8},{13,9},{14,12},{15,13},{10,14},{11,... | collective-permute-start | bytes 2555912 | tf_op jit(solution)/shard_map/ppermute | solution.py:375
  461.0 30.4 %collective-permute-start.56 = (bf16[1,8,48,1664]{3,2,1,0:T(8,128)(2,1)}, bf16[1,8,48,1664]{3,2,1,0:T(8,128)(2,1)}, u32[]{:S(2)}, u32[]{:S(2)}) collective-permute-start(bf16[1,8,48,1664]{3,2,1,0:T(8,128)(2,1)} %constant_dynamic-slice_fusion.1), channel_id=1, source_target_pairs={{0,16},{16,0},{1,17},{17,1},{2,18},{18,2},{3,19},{19,3},{4,20},{20... | collective-permute-start | bytes 3833864 | tf_op jit(solution)/shard_map/ppermute | solution.py:497
  472.2 74.0 %collective-permute-start.85 = (bf16[1536,1024]{1,0:T(8,128)(2,1)}, bf16[1536,1024]{1,0:T(8,128)(2,1)}, u32[]{:S(2)}, u32[]{:S(2)}) collective-permute-start(bf16[1536,1024]{1,0:T(8,128)(2,1)} %fusion.6), channel_id=1, source_target_pairs={{0,1},{1,0},{2,3},{3,2},{4,5},{5,4},{6,7},{7,6},{8,9},{9,8},{10,11... | collective-permute-start | bytes 9437192 | tf_op jit(solution)/shard_map/ppermute | solution.py:354
  474.5 35.0 %all-to-all-start.2 = ((bf16[16,192,128]{2,1,0:T(8,128)(2,1)}), bf16[16,192,128]{2,1,0:T(8,128)(2,1)S(1)}, u32[]{:S(2)}, u32[]{:S(2)}) async-start(bf16[16,192,128]{2,1,0:T(8,128)(2,1)} %bitcast.50), calls=%async_computation.2 | async-start | bytes 1572864 | tf_op jit(solution)/shard_map/all_to_all | solution.py:341
  498.7 44.3 %collective-permute-start.58 = (bf16[48,1664]{1,0:T(8,128)(2,1)S(1)}, bf16[48,1664]{1,0:T(8,128)(2,1)S(1)}, u32[]{:S(2)}, u32[]{:S(2)}) collective-permute-start(bf16[48,1664]{1,0:T(8,128)(2,1)S(1)} %get-tuple-element.216), channel_id=1, source_target_pairs={{0,4},{1,5},{4,8},{5,9},{8,12},{9,13},{12,14},{13,15},{14,10},{15,... | collective-permute-start | bytes 479240 | tf_op jit(solution)/shard_map/ppermute | solution.py:374
  501.4 41.6 %collective-permute-start.62 = (bf16[48,1664]{1,0:T(8,128)(2,1)S(1)}, bf16[48,1664]{1,0:T(8,128)(2,1)S(1)}, u32[]{:S(2)}, u32[]{:S(2)}) collective-permute-start(bf16[48,1664]{1,0:T(8,128)(2,1)S(1)} %get-tuple-element.217), channel_id=1, source_target_pairs={{4,0},{5,1},{8,4},{9,5},{12,8},{13,9},{14,12},{15,13},{10,14},{11,... | collective-permute-start | bytes 479240 | tf_op jit(solution)/shard_map/ppermute | solution.py:375
  509.5 71.0 %collective-permute-start.87 = (bf16[512,1536]{1,0:T(8,128)(2,1)}, bf16[512,1536]{1,0:T(8,128)(2,1)}, u32[]{:S(2)}, u32[]{:S(2)}) collective-permute-start(bf16[512,1536]{1,0:T(8,128)(2,1)} %convolution_convert_fusion), channel_id=1, source_target_pairs={{0,1},{1,0},{2,3},{3,2},{4,5},{5,4},{6,7},{7,6},{8,9},{9,8},{10,11... | collective-permute-start | bytes 4718600 | tf_op jit(solution)/shard_map/ppermute | solution.py:354
  538.6 49.2 %all-to-all-start.3 = ((bf16[16,320,128]{2,1,0:T(8,128)(2,1)}), bf16[16,320,128]{2,1,0:T(8,128)(2,1)S(1)}, u32[]{:S(2)}, u32[]{:S(2)}) async-start(bf16[16,320,128]{2,1,0:T(8,128)(2,1)} %attend_backward.1), calls=%async_computation.3 | async-start | bytes 2621440 | tf_op jit(solution)/shard_map/all_to_all | solution.py:341
  544.1 24.6 %collective-permute-start.59 = (bf16[48,1664]{1,0:T(8,128)(2,1)S(1)}, bf16[48,1664]{1,0:T(8,128)(2,1)S(1)}, u32[]{:S(2)}, u32[]{:S(2)}) collective-permute-start(bf16[48,1664]{1,0:T(8,128)(2,1)S(1)} %get-tuple-element.214), channel_id=1, source_target_pairs={{0,4},{1,5},{4,8},{5,9},{8,12},{9,13},{12,14},{13,15},{14,10},{15,... | collective-permute-start | bytes 479240 | tf_op jit(solution)/shard_map/ppermute | solution.py:374
  546.1 22.6 %collective-permute-start.63 = (bf16[48,1664]{1,0:T(8,128)(2,1)S(1)}, bf16[48,1664]{1,0:T(8,128)(2,1)S(1)}, u32[]{:S(2)}, u32[]{:S(2)}) collective-permute-start(bf16[48,1664]{1,0:T(8,128)(2,1)S(1)} %get-tuple-element.215), channel_id=1, source_target_pairs={{4,0},{5,1},{8,4},{9,5},{12,8},{13,9},{14,12},{15,13},{10,14},{11,... | collective-permute-start | bytes 479240 | tf_op jit(solution)/shard_map/ppermute | solution.py:375
  558.0 112.3 %collective-permute-start.86 = (bf16[1536,1024]{1,0:T(8,128)(2,1)}, bf16[1536,1024]{1,0:T(8,128)(2,1)}, u32[]{:S(2)}, u32[]{:S(2)}) collective-permute-start(bf16[1536,1024]{1,0:T(8,128)(2,1)} %add_convert_fusion), channel_id=1, source_target_pairs={{0,16},{16,0},{1,17},{17,1},{2,18},{18,2},{3,19},{19,3},{4,20},{20... | collective-permute-start | bytes 9437192 | tf_op jit(solution)/shard_map/ppermute | solution.py:347
  586.2 75.7 %collective-permute-start.88 = (bf16[512,1536]{1,0:T(8,128)(2,1)}, bf16[512,1536]{1,0:T(8,128)(2,1)}, u32[]{:S(2)}, u32[]{:S(2)}) collective-permute-start(bf16[512,1536]{1,0:T(8,128)(2,1)} %fusion.9), channel_id=1, source_target_pairs={{0,16},{16,0},{1,17},{17,1},{2,18},{18,2},{3,19},{19,3},{4,20},{20... | collective-permute-start | bytes 4718600 | tf_op jit(solution)/shard_map/ppermute | solution.py:347
  594.7 122.6 %collective-permute-start.71 = (bf16[2,8,48,2560]{3,2,1,0:T(8,128)(2,1)}, bf16[2,8,48,2560]{3,2,1,0:T(8,128)(2,1)}, u32[]{:S(2)}, u32[]{:S(2)}) collective-permute-start(bf16[2,8,48,2560]{3,2,1,0:T(8,128)(2,1)} %select_bitcast_fusion), channel_id=1, source_target_pairs={{0,1},{1,0},{2,3},{3,2},{4,5},{5,4},{6,7},{7,6},{8,9},{9,8},{10,11... | collective-permute-start | bytes 11796488 | tf_op jit(solution)/shard_map/ppermute | solution.py:354
  667.0 19.9 %collective-permute-start.66 = (bf16[256,1536]{1,0:T(8,128)(2,1)}, bf16[256,1536]{1,0:T(8,128)(2,1)}, u32[]{:S(2)}, u32[]{:S(2)}) collective-permute-start(bf16[256,1536]{1,0:T(8,128)(2,1)} %add.624), channel_id=1, source_target_pairs={{4,0},{5,1},{8,4},{9,5},{12,8},{13,9},{14,12},{15,13},{10,14},{11,... | collective-permute-start | bytes 2359304 | tf_op jit(solution)/shard_map/ppermute | solution.py:375
  670.3 18.1 %collective-permute-start.65 = (bf16[256,1536]{1,0:T(8,128)(2,1)}, bf16[256,1536]{1,0:T(8,128)(2,1)}, u32[]{:S(2)}, u32[]{:S(2)}) collective-permute-start(bf16[256,1536]{1,0:T(8,128)(2,1)} %add.623), channel_id=1, source_target_pairs={{0,4},{1,5},{4,8},{5,9},{8,12},{9,13},{12,14},{13,15},{14,10},{15,... | collective-permute-start | bytes 2359304 | tf_op jit(solution)/shard_map/ppermute | solution.py:374
  691.7 20.3 %collective-permute-start.67 = (bf16[256,1536]{1,0:T(8,128)(2,1)}, bf16[256,1536]{1,0:T(8,128)(2,1)}, u32[]{:S(2)}, u32[]{:S(2)}) collective-permute-start(bf16[256,1536]{1,0:T(8,128)(2,1)} %add.625), channel_id=1, source_target_pairs={{0,4},{1,5},{4,8},{5,9},{8,12},{9,13},{12,14},{13,15},{14,10},{15,... | collective-permute-start | bytes 2359304 | tf_op jit(solution)/shard_map/ppermute | solution.py:374
  694.2 20.0 %collective-permute-start.69 = (bf16[256,1536]{1,0:T(8,128)(2,1)}, bf16[256,1536]{1,0:T(8,128)(2,1)}, u32[]{:S(2)}, u32[]{:S(2)}) collective-permute-start(bf16[256,1536]{1,0:T(8,128)(2,1)} %add.628), channel_id=1, source_target_pairs={{4,0},{5,1},{8,4},{9,5},{12,8},{13,9},{14,12},{15,13},{10,14},{11,... | collective-permute-start | bytes 2359304 | tf_op jit(solution)/shard_map/ppermute | solution.py:375
  713.3 69.8 %collective-permute-start.68 = (bf16[256,1536]{1,0:T(8,128)(2,1)S(1)}, bf16[256,1536]{1,0:T(8,128)(2,1)S(1)}, u32[]{:S(2)}, u32[]{:S(2)}) collective-permute-start(bf16[256,1536]{1,0:T(8,128)(2,1)S(1)} %add.626), channel_id=1, source_target_pairs={{0,4},{1,5},{4,8},{5,9},{8,12},{9,13},{12,14},{13,15},{14,10},{15,... | collective-permute-start | bytes 2359304 | tf_op jit(solution)/shard_map/ppermute | solution.py:374
  715.5 67.6 %collective-permute-start.70 = (bf16[256,1536]{1,0:T(8,128)(2,1)S(1)}, bf16[256,1536]{1,0:T(8,128)(2,1)S(1)}, u32[]{:S(2)}, u32[]{:S(2)}) collective-permute-start(bf16[256,1536]{1,0:T(8,128)(2,1)S(1)} %add.629), channel_id=1, source_target_pairs={{4,0},{5,1},{8,4},{9,5},{12,8},{13,9},{14,12},{15,13},{10,14},{11,... | collective-permute-start | bytes 2359304 | tf_op jit(solution)/shard_map/ppermute | solution.py:375
  722.6 20.2 %collective-permute-start.74 = (bf16[1,3,48,2688]{3,2,1,0:T(8,128)(2,1)S(1)}, bf16[1,3,48,2688]{3,2,1,0:T(8,128)(2,1)S(1)}, u32[]{:S(2)}, u32[]{:S(2)}) collective-permute-start(bf16[1,3,48,2688]{3,2,1,0:T(8,128)(2,1)S(1)} %constant_dynamic-slice_fusion), channel_id=1, source_target_pairs={{0,16},{16,0},{1,17},{17,1},{2,18},{18,2},{3,19},{19,3},{4,20},{20... | collective-permute-start | bytes 2322440 | tf_op jit(solution)/shard_map/ppermute | solution.py:497
  723.2 61.5 %collective-permute-start.73 = (bf16[1,1,48,2688]{3,2,1,0:T(8,128)(2,1)S(1)}, bf16[1,1,48,2688]{3,2,1,0:T(8,128)(2,1)S(1)}, u32[]{:S(2)}, u32[]{:S(2)}) collective-permute-start(bf16[1,1,48,2688]{3,2,1,0:T(8,128)(2,1)S(1)} %fusion.34), channel_id=1, source_target_pairs={{0,16},{16,0},{1,17},{17,1},{2,18},{18,2},{3,19},{19,3},{4,20},{20... | collective-permute-start | bytes 774152 | tf_op jit(solution)/shard_map/ppermute | solution.py:497
  (92 other events, 1378.1 us)

commit v6 on v5

--- a/solution.py
+++ b/solution.py
@@ -12,6 +12,9 @@
 TOP = 8
 BLOCK = 256
 LANES = 128
+HEAD = "head"
+BLK = "blk"
+ORDERED = ("arbitrary",)
 
 highest = lax.Precision.HIGHEST
 theta_base = 10000.0
@@ -119,8 +122,8 @@
                    jax.ShapeDtypeStruct((steps,HDIM,width), jnp.float32),
                    jax.ShapeDtypeStruct((steps,1,width), jnp.float32)],
         scratch_shapes=[pltpu.VMEM((total,HDIM), jnp.bfloat16), pltpu.VMEM((HDIM,total), jnp.bfloat16), pltpu.VMEM((HDIM,width), jnp.float32)],
-        compiler_params=pltpu.CompilerParams(dimension_semantics=("arbitrary",)),
-        name="attend_forward",
+        compiler_params=pltpu.CompilerParams(dimension_semantics=ORDERED),
+        name="forward",
     )(qkv)
 
 
@@ -195,8 +198,8 @@
         out_shape=jax.ShapeDtypeStruct((count, lanes+2*HDIM, LANES), jnp.bfloat16),
         scratch_shapes=[pltpu.VMEM((total,HDIM), jnp.bfloat16), pltpu.VMEM((HDIM,total), jnp.bfloat16), pltpu.VMEM((total,HDIM), jnp.bfloat16),
                         pltpu.VMEM((HDIM,width), jnp.float32), pltpu.VMEM((total,HDIM), jnp.float32), pltpu.VMEM((total,HDIM), jnp.float32)],
-        compiler_params=pltpu.CompilerParams(dimension_semantics=("arbitrary",)),
-        name="attend_backward",
+        compiler_params=pltpu.CompilerParams(dimension_semantics=ORDERED),
+        name="backward",
     )(qkv, grad, flat, lse, cosine, sine)
 
 
@@ -322,7 +325,7 @@
         ),
         out_shape=shapes,
         input_output_aliases={first + k: 2 * parts + k for k in range(4)} if chained else {},
-        compiler_params=pltpu.CompilerParams(dimension_semantics=("arbitrary",)),
+        compiler_params=pltpu.CompilerParams(dimension_semantics=ORDERED),
         cost_estimate=pl.CostEstimate(
             flops=rows * width * units * 24,
             bytes_accessed=12 * width * units + 20 * rows * width,
@@ -338,20 +341,20 @@
 
 
 def exchange(values):
-    return lax.all_to_all(values, "blk", split_axis=0, concat_axis=0, tiled=True)
+    return lax.all_to_all(values, BLK, split_axis=0, concat_axis=0, tiled=True)
 
 
 def from_heads(values):
-    heads = lax.axis_size("head")
+    heads = lax.axis_size(HEAD)
     return [
-        lax.ppermute(values, "head", [(k, (k + turn) % heads) for k in range(heads)])
+        lax.ppermute(values, HEAD, [(k, (k + turn) % heads) for k in range(heads)])
         for turn in range(1, heads)
     ]
 
 
 def partner(values):
-    count = lax.axis_size("blk")
-    return lax.ppermute(values, "blk", [(k, k ^ 1) for k in range(count)])
+    count = lax.axis_size(BLK)
+    return lax.ppermute(values, BLK, [(k, k ^ 1) for k in range(count)])
 
 
 def after(values, *earlier):
@@ -359,7 +362,7 @@
 
 
 def ring_order():
-    half = lax.axis_size("blk") // 4
+    half = lax.axis_size(BLK) // 4
     return [2 * k for k in range(half)] + [2 * k + 1 for k in reversed(range(half))]
 
 
@@ -371,8 +374,8 @@
         for core in range(2):
             onward.append((2 * chip + core, 2 * following + core))
             back.append((2 * following + core, 2 * chip + core))
-    send_on = lambda values: lax.ppermute(values, "blk", onward)
-    send_back = lambda values: lax.ppermute(values, "blk", back)
+    send_on = lambda values: lax.ppermute(values, BLK, onward)
+    send_back = lambda values: lax.ppermute(values, BLK, back)
     return len(order), send_on, send_back
 
 
@@ -427,22 +430,22 @@
 
 
 def ring_chip(offset):
-    chips = lax.axis_size("blk") // 2
-    chip = lax.axis_index("blk") // 2
+    chips = lax.axis_size(BLK) // 2
+    chip = lax.axis_index(BLK) // 2
     place = jnp.where(chip % 2 == 0, chip // 2, chips - 1 - chip // 2)
     target = (place + offset) % chips
     return jnp.where(target < chips // 2, 2 * target, 2 * (chips - 1 - target) + 1)
 
 
 def all_heads(values):
-    heads = lax.axis_size("head")
-    head = lax.axis_index("head")
+    heads = lax.axis_size(HEAD)
+    head = lax.axis_index(HEAD)
     place = lambda found, at: lax.dynamic_update_index_in_dim(result, found, at, 0)
     result = jnp.zeros((heads, *values.shape), values.dtype)
     result = place(values, head)
     for turn in range(1, heads):
         other = lax.ppermute(
-            values, "head", [(k, (k + turn) % heads) for k in range(heads)]
+            values, HEAD, [(k, (k + turn) % heads) for k in range(heads)]
         )
         result = place(other, (head - turn) % heads)
     return result
@@ -457,9 +460,9 @@
 
 
 def dense_gather(shard):
-    chips = lax.axis_size("blk") // 2
-    heads = lax.axis_size("head")
-    core = lax.axis_index("blk") % 2
+    chips = lax.axis_size(BLK) // 2
+    heads = lax.axis_size(HEAD)
+    core = lax.axis_index(BLK) % 2
     rows, columns = shard.shape
     block = all_heads(shard).reshape(heads * rows, columns)
     full = jnp.zeros((heads, chips, 2, rows, columns), shard.dtype)
@@ -472,21 +475,21 @@
 
 
 def dense_gather_late(shard):
-    chips = lax.axis_size("blk") // 2
+    chips = lax.axis_size(BLK) // 2
     rows, columns = shard.shape
     found = jnp.zeros((chips, rows, columns), shard.dtype)
     for offset, piece in ring_pieces(shard, 1):
         found = lax.dynamic_update_slice(found, piece[None], (ring_chip(offset), 0, 0))
     found = all_heads(found)
     other = partner(found)
-    even = lax.axis_index("blk") % 2 == 0
+    even = lax.axis_index(BLK) % 2 == 0
     pair = [jnp.where(even, found, other), jnp.where(even, other, found)]
     return jnp.stack(pair, axis=2).reshape(-1, columns)
 
 
 def head_share(values):
-    heads, rows = lax.axis_size("head"), values.shape[0] // lax.axis_size("head")
-    head = lax.axis_index("head")
+    heads, rows = lax.axis_size(HEAD), values.shape[0] // lax.axis_size(HEAD)
+    head = lax.axis_index(HEAD)
     start = (0,) * (values.ndim - 1)
     share = lambda turn: lax.dynamic_slice(
         values, ((head + turn) % heads * rows, *start), (rows, *values.shape[1:])
@@ -494,7 +497,7 @@
     result = share(0).astype(jnp.float32)
     for turn in range(1, heads):
         moved = [(k, (k + turn) % heads) for k in range(heads)]
-        other = lax.ppermute(share(turn), "head", moved)
+        other = lax.ppermute(share(turn), HEAD, moved)
         result = result + other.astype(jnp.float32)
     return result
 
@@ -502,11 +505,11 @@
 class DenseSum:
     def __init__(self, values, label, heads_first=False, staged=False):
         self.staged = staged
-        self.heads = lax.axis_size("head")
-        self.chips = lax.axis_size("blk") // 2
+        self.heads = lax.axis_size(HEAD)
+        self.chips = lax.axis_size(BLK) // 2
         self.rows = values.shape[0] // (2 * self.heads * self.chips)
         self.label, self.heads_first = label, heads_first
-        self.index = lax.axis_index("blk")
+        self.index = lax.axis_index(BLK)
         self.mine = self.core_sum(values)
 
     def core_sum(self, values):
@@ -599,7 +602,7 @@
         ],
         out_specs=pl.BlockSpec((rows // shard, 2, span, shard), lambda j: (0, j, 0, 0)),
         out_shape=jax.ShapeDtypeStruct((rows // shard, groups, span, shard), jnp.bfloat16),
-        compiler_params=pltpu.CompilerParams(dimension_semantics=("arbitrary",)),
+        compiler_params=pltpu.CompilerParams(dimension_semantics=ORDERED),
         cost_estimate=pl.CostEstimate(
             flops=2 * rows * width * groups * span,
             bytes_accessed=2 * width * groups * span,
@@ -638,8 +641,8 @@
 ):
     seq_local, shard, width = tokens.shape
     token_rows = seq_local * shard
-    blk_index = lax.axis_index("blk")
-    blk_count = lax.axis_size("blk")
+    blk_index = lax.axis_index(BLK)
+    blk_count = lax.axis_size(BLK)
     seq_total = blk_count * shard
     part_rows = w_query.shape[0]
     groups = w_key.shape[1] // HDIM
@@ -821,37 +824,37 @@
 
 def solution(mesh):
     placed = (
-        P("head", "blk", None),
-        P(("head", "blk")),
-        P(("head", "blk"), None),
-        P(("head", "blk"), None),
-        P(("head", "blk"), None),
-        P(("head", "blk"), None),
-        P(("head", "blk")),
-        P(("head", "blk"), None),
-        P("blk", None, None),
-        P("blk", None, None),
-        P("blk", None, None),
-        P("head", "blk", None),
-        P("head", "blk", None),
+        P(HEAD, BLK, None),
+        P((HEAD, BLK)),
+        P((HEAD, BLK), None),
+        P((HEAD, BLK), None),
+        P((HEAD, BLK), None),
+        P((HEAD, BLK), None),
+        P((HEAD, BLK)),
+        P((HEAD, BLK), None),
+        P(BLK, None, None),
+        P(BLK, None, None),
+        P(BLK, None, None),
+        P(HEAD, BLK, None),
+        P(HEAD, BLK, None),
     )
     return jax.shard_map(
         layer,
         mesh=mesh,
         in_specs=placed,
         out_specs=(
-            P("head", "blk", None),
-            P("head", "blk", None),
-            P(("head", "blk")),
-            P(("head", "blk"), None),
-            P(("head", "blk"), None),
-            P(("head", "blk"), None),
-            P(("head", "blk"), None),
-            P(("head", "blk")),
-            P(("head", "blk"), None),
-            P("blk", None, None),
-            P("blk", None, None),
-            P("blk", None, None),
+            P(HEAD, BLK, None),
+            P(HEAD, BLK, None),
+            P((HEAD, BLK)),
+            P((HEAD, BLK), None),
+            P((HEAD, BLK), None),
+            P((HEAD, BLK), None),
+            P((HEAD, BLK), None),
+            P((HEAD, BLK)),
+            P((HEAD, BLK), None),
+            P(BLK, None, None),
+            P(BLK, None, None),
+            P(BLK, None, None),
         ),
         check_vma=False,
     )

time: 802 us -> 802 us (level)
  no operation moved by 1% of the time
where the time goes in v6:
time: 802 us; the launch traced here: 792 us
  waiting for transfers between devices  334 us (42%)
  Pallas kernels  145 us (18%)
  starting transfers between devices  118 us (15%)
  other arithmetic  66.8 us (8%)
  local copies, waits for them, and re-layouts  63.7 us (8%)
  matrix products  62.3 us (8%)
    ppermute x32, waiting for transfers between devices, ring_steps(): send_on = lambda values: lax.ppermute(values, BLK, onward)  184 us
    pallas_call x5, Pallas kernels, expert_rows(): pl.pallas_call(functools.partial(expert_kernel, parts, rows, width, exper...  86.7 us
    ppermute x2, waiting for transfers between devices, from_heads(): lax.ppermute(values, HEAD, [(k, (k + turn) % heads) for k in range(heads)])  67.2 us
    ppermute x32, starting transfers between devices, ring_steps(): send_on = lambda values: lax.ppermute(values, BLK, onward)  66.7 us
    ppermute x5, waiting for transfers between devices, head_share(): other = lax.ppermute(share(turn), HEAD, moved)  44.8 us
    dot_general x4, matrix products, matmul_tn(): lax.dot_general(left, right, (((0,), (0,)), ((), ())), preferred_element_...  35.3 us
    pallas_call x1, Pallas kernels, attend_backward(): pl.pallas_call(functools.partial(backward_kernel, group, steps), grid=(st...  28.2 us
    ppermute x32, starting transfers between devices, ring_steps(): send_back = lambda values: lax.ppermute(values, BLK, back)  22.8 us
  transfers between devices with their start and end apart: 93, of which 38 were waited for; matrix products, arithmetic and copies ran while one was open for 20% of the time, Pallas kernels for 17%

profile of v6, /device:TPU:0, one launch (start us, length us, event | category | flops | bytes accessed | tf_op | source)
XLA Modules:
  0.0 791.9 jit_solution(14124368799646765519)
XLA Ops:
  29.0 5.6 collective-permute-done.19
  36.6 4.9 collective-permute-done.22
  52.0 4.8 collective-permute-done.2
  60.1 10.9 %collective-permute-done.6 = bf16[96,2688]{1,0:T(8,128)(2,1)S(1)} collective-permute-done((bf16[96,2688]{1,0:T(8,128)(2,1)S(1)}, bf16[96,2688]{1,0:T(8,128)(2,1)S(1)}, u32[]{:S(2)}, u32[]{:S(2)}) %collective-permute-start.6) | collective-permute-done | bytes 516128 | tf_op jit(solution)/shard_map/ppermute | solution.py:377
  73.9 11.4 %collective-permute-done.10 = bf16[96,2688]{1,0:T(8,128)(2,1)S(1)} collective-permute-done((bf16[96,2688]{1,0:T(8,128)(2,1)S(1)}, bf16[96,2688]{1,0:T(8,128)(2,1)S(1)}, u32[]{:S(2)}, u32[]{:S(2)}) %collective-permute-start.10) | collective-permute-done | bytes 516128 | tf_op jit(solution)/shard_map/ppermute | solution.py:377
  89.2 4.8 collective-permute-done.14
  107.1 8.1 %project.1 = bf16[2,8,320,128]{3,2,1,0:T(8,128)(2,1)} custom-call(bf16[256,1536]{1,0:T(8,128)(2,1)} %multiply_convert_fusion.2.rows_ref, bf16[1536,2688]{1,0:T(8,128)(2,1)} %bitcast.241, f32[128,640]{1,0:T(8,128)} %concatenate.58.cosine_ref, f32[128,640]{1,0:T(8,128)} %concatenate.59.sine_ref), custom_call_target="tpu_custom_call" | custom-call | flops 2013265920 | bytes 7864320 | tf_op jit(solution)/shard_map/project/pallas_call | solution.py:594
  115.2 5.9 all-to-all-start
  128.2 33.5 %collective-permute-done.38.refs_2_ = bf16[256,1664]{1,0:T(8,128)(2,1)} collective-permute-done((bf16[256,1664]{1,0:T(8,128)(2,1)}, bf16[256,1664]{1,0:T(8,128)(2,1)}, u32[]{:S(2)}, u32[]{:S(2)}) %collective-permute-start.38) | collective-permute-done | bytes 852000 | tf_op jit(solution)/shard_map/ppermute | solution.py:377
  161.8 8.6 %collective-permute-start.39 = (bf16[256,1664]{1,0:T(8,128)(2,1)}, bf16[256,1664]{1,0:T(8,128)(2,1)}, u32[]{:S(2)}, u32[]{:S(2)}) collective-permute-start(bf16[256,1664]{1,0:T(8,128)(2,1)} %collective-permute-done.38.refs_2_), channel_id=1, source_target_pairs={{0,4},{1,5},{4,8},{5,9},{8,12},{9,13},{12,14},{13,15},{14,10},{15,... | collective-permute-start | bytes 2555912 | tf_op jit(solution)/shard_map/ppermute | solution.py:377
  174.0 14.6 %collective-permute-done.39.refs_2_ = bf16[256,1664]{1,0:T(8,128)(2,1)} collective-permute-done((bf16[256,1664]{1,0:T(8,128)(2,1)}, bf16[256,1664]{1,0:T(8,128)(2,1)}, u32[]{:S(2)}, u32[]{:S(2)}) %collective-permute-start.39) | collective-permute-done | bytes 852000 | tf_op jit(solution)/shard_map/ppermute | solution.py:377
  196.3 22.3 %forward.1 = (bf16[16,192,128]{2,1,0:T(8,128)(2,1)}, f32[8,64,768]{2,1,0:T(8,128)}, f32[8,1,768]{2,1,0:T(1,128)}) custom-call(bf16[16,320,128]{2,1,0:T(8,128)(2,1)} %all-to-all-done.qkv_ref), custom_call_target="tpu_custom_call" | custom-call | tf_op jit(solution)/shard_map/forward/pallas_call | solution.py:114
  218.6 5.2 all-to-all-start.1
  223.7 6.0 pad_maximum_fusion.refs_3_.refs_5_
  235.8 6.6 all-to-all-done.1
  244.7 4.1 multiply_reduce_fusion.4
  253.9 12.6 %expert_rows.5 = (bf16[256,1536]{1,0:T(8,128)(2,1)}, bf16[256,1664]{1,0:T(8,128)(2,1)}, bf16[2048,1536]{1,0:T(8,128)(2,1)}, bf16[2048,1536]{1,0:T(8,128)(2,1)}, ...) custom-call(s32[2]{0:T(128)} %pad_add_fusion.2.index_ref, bf16[256,1536]{1,0:T(8,128)(2,1)} %multiply_convert_fusion.1.refs_0_, ...), custom_call_target="tpu_custom_call" | custom-call | flops 4831838208 | bytes 17301504 | tf_op jit(solution)/shard_map/expert_rows/pallas_call | solution.py:298
  266.5 3.9 collective-permute-done.29.refs_0_
  273.0 20.6 %expert_rows.6 = (bf16[256,1536]{1,0:T(8,128)(2,1)}, bf16[256,1536]{1,0:T(8,128)(2,1)}, bf16[256,1664]{1,0:T(8,128)(2,1)}, bf16[256,1664]{1,0:T(8,128)(2,1)}, bf...) custom-call(s32[2]{0:T(128)} %pad_add_fusion.2.index_ref, ...), custom_call_target="tpu_custom_call", output_to_operand_aliasing={{4}: (8, {}), {5}: (9, {}), {6}: (10, {}), {7}: (11, {})} | custom-call | flops 9663676416 | bytes 25165824 | tf_op jit(solution)/shard_map/expert_rows/pallas_call | solution.py:298
  295.9 20.5 %expert_rows.7 = (bf16[256,1536]{1,0:T(8,128)(2,1)}, bf16[256,1536]{1,0:T(8,128)(2,1)}, bf16[256,1664]{1,0:T(8,128)(2,1)}, bf16[256,1664]{1,0:T(8,128)(2,1)}, bf...) custom-call(s32[2]{0:T(128)} %pad_add_fusion.2.index_ref, ...), custom_call_target="tpu_custom_call", output_to_operand_aliasing={{4}: (8, {}), {5}: (9, {}), {6}: (10, {}), {7}: (11, {})} | custom-call | flops 9663676416 | bytes 25165824 | tf_op jit(solution)/shard_map/expert_rows/pallas_call | solution.py:298
  322.1 20.5 %expert_rows.8 = (bf16[256,1536]{1,0:T(8,128)(2,1)}, bf16[256,1536]{1,0:T(8,128)(2,1)}, bf16[256,1664]{1,0:T(8,128)(2,1)}, bf16[256,1664]{1,0:T(8,128)(2,1)}, bf...) custom-call(s32[2]{0:T(128)} %pad_add_fusion.2.index_ref, ...), custom_call_target="tpu_custom_call", output_to_operand_aliasing={{4}: (8, {}), {5}: (9, {}), {6}: (10, {}), {7}: (11, {})} | custom-call | flops 9663676416 | bytes 25165824 | tf_op jit(solution)/shard_map/expert_rows/pallas_call | solution.py:298
  343.5 12.6 %expert_rows.9 = (bf16[128,1536]{1,0:T(8,128)(2,1)}, bf16[128,1536]{1,0:T(8,128)(2,1)}, bf16[128,1664]{1,0:T(8,128)(2,1)}, bf16[128,1664]{1,0:T(8,128)(2,1)}, bf...) custom-call(s32[2]{0:T(128)} %pad_add_fusion.2.index_ref, ...), custom_call_target="tpu_custom_call", output_to_operand_aliasing={{4}: (8, {}), {5}: (9, {}), {6}: (10, {}), {7}: (11, {})} | custom-call | flops 4831838208 | bytes 17301504 | tf_op jit(solution)/shard_map/expert_rows/pallas_call | solution.py:298
  358.2 8.6 %collective-permute-done.45 = bf16[128,1664]{1,0:T(8,128)(2,1)S(1)} collective-permute-done((bf16[128,1664]{1,0:T(8,128)(2,1)}, bf16[128,1664]{1,0:T(8,128)(2,1)S(1)}, u32[]{:S(2)}, u32[]{:S(2)}) %collective-permute-start.45) | collective-permute-done | bytes 426016 | tf_op jit(solution)/shard_map/ppermute | solution.py:377
  370.3 16.6 %collective-permute-done.46 = bf16[256,1664]{1,0:T(8,128)(2,1)S(1)} collective-permute-done((bf16[256,1664]{1,0:T(8,128)(2,1)S(1)}, bf16[256,1664]{1,0:T(8,128)(2,1)S(1)}, u32[]{:S(2)}, u32[]{:S(2)}) %collective-permute-start.46) | collective-permute-done | bytes 852000 | tf_op jit(solution)/shard_map/ppermute | solution.py:377
  389.5 16.5 %collective-permute-done.47 = bf16[256,1664]{1,0:T(8,128)(2,1)S(1)} collective-permute-done((bf16[256,1664]{1,0:T(8,128)(2,1)S(1)}, bf16[256,1664]{1,0:T(8,128)(2,1)S(1)}, u32[]{:S(2)}, u32[]{:S(2)}) %collective-permute-start.47) | collective-permute-done | bytes 852000 | tf_op jit(solution)/shard_map/ppermute | solution.py:377
  411.0 12.2 %collective-permute-done.48 = bf16[256,1664]{1,0:T(8,128)(2,1)S(1)} collective-permute-done((bf16[256,1664]{1,0:T(8,128)(2,1)S(1)}, bf16[256,1664]{1,0:T(8,128)(2,1)S(1)}, u32[]{:S(2)}, u32[]{:S(2)}) %collective-permute-start.48) | collective-permute-done | bytes 852000 | tf_op jit(solution)/shard_map/ppermute | solution.py:377
  437.2 5.0 fusion.13
  449.3 5.1 collective-permute-done.55
  462.5 9.7 %fusion.6 = bf16[1536,1024]{1,0:T(8,128)(2,1)} fusion(bf16[2048,1536]{1,0:T(8,128)(2,1)S(1)} %bitcast.235, bf16[2048,2048]{1,0:T(8,128)(2,1)} %get-tuple-element.121), kind=kOutput, calls=%fused_computation.25 | convolution fusion | flops 6444023808 | bytes 13631488 | tf_op jit(solution)/shard_map/dot_general | solution.py:54
  478.1 13.3 %collective-permute-done.56 = bf16[1,8,48,1664]{3,2,1,0:T(8,128)(2,1)} collective-permute-done((bf16[1,8,48,1664]{3,2,1,0:T(8,128)(2,1)}, bf16[1,8,48,1664]{3,2,1,0:T(8,128)(2,1)}, u32[]{:S(2)}, u32[]{:S(2)}) %collective-permute-start.56) | collective-permute-done | bytes 1277984 | tf_op jit(solution)/shard_map/ppermute | solution.py:500
  501.4 8.0 %convolution_convert_fusion = bf16[512,1536]{1,0:T(8,128)(2,1)} fusion(bf16[2048,1536]{1,0:T(8,128)(2,1)} %get-tuple-element.123, bf16[2048,1024]{1,0:T(8,128)(2,1)} %get-tuple-element.122), kind=kOutput, calls=%fused_computation.31 | convolution fusion | flops 3222011904 | bytes 9961472 | tf_op jit(solution)/shard_map/dot_general | solution.py:54
  510.4 28.2 %backward.1 = bf16[16,320,128]{2,1,0:T(8,128)(2,1)} custom-call(bf16[16,320,128]{2,1,0:T(8,128)(2,1)} %all-to-all-done.qkv_ref, bf16[16,192,128]{2,1,0:T(8,128)(2,1)} %copy-done.15, f32[8,64,768]{2,1,0:T(8,128)} %get-tuple-element.104.flat_ref, f32[8,1,768]{2,1,0:T(1,128)} %get-tuple-element.105.lse_ref, f32[32,2048]{1,0:T(8,128)} %get-tuple-element.227.cos_ref, ...), custom_call_target="tpu_custom_call" | custom-call | tf_op jit(solution)/shard_map/backward/pallas_call | solution.py:188
  538.6 4.4 all-to-all-start.3
  546.2 11.9 %add_convert_fusion = bf16[1536,1024]{1,0:T(8,128)(2,1)} fusion(bf16[1536,1024]{1,0:T(8,128)(2,1)} %collective-permute-done.85, bf16[2048,1536]{1,0:T(8,128)(2,1)} %get-tuple-element.120, bf16[2048,2048]{1,0:T(8,128)(2,1)} %get-tuple-element.121), kind=kOutput, calls=%fused_computation.14 | convolution fusion | flops 6447169536 | bytes 16777216 | tf_op jit(solution)/shard_map/dot_general | solution.py:54
  558.6 10.1 %collective-permute-done.59 = bf16[48,1664]{1,0:T(8,128)(2,1)S(1)} collective-permute-done((bf16[48,1664]{1,0:T(8,128)(2,1)S(1)}, bf16[48,1664]{1,0:T(8,128)(2,1)S(1)}, u32[]{:S(2)}, u32[]{:S(2)}) %collective-permute-start.59) | collective-permute-done | bytes 159776 | tf_op jit(solution)/shard_map/ppermute | solution.py:377
  569.7 10.5 %collective-permute-start.60 = (bf16[48,1664]{1,0:T(8,128)(2,1)S(1)}, bf16[48,1664]{1,0:T(8,128)(2,1)S(1)}, u32[]{:S(2)}, u32[]{:S(2)}) collective-permute-start(bf16[48,1664]{1,0:T(8,128)(2,1)S(1)} %get-tuple-element.212), channel_id=1, source_target_pairs={{0,4},{1,5},{4,8},{5,9},{8,12},{9,13},{12,14},{13,15},{14,10},{15,... | collective-permute-start | bytes 479240 | tf_op jit(solution)/shard_map/ppermute | solution.py:377
  580.5 5.7 fusion.9
  594.7 67.2 %collective-permute-done.88 = bf16[512,1536]{1,0:T(8,128)(2,1)} collective-permute-done((bf16[512,1536]{1,0:T(8,128)(2,1)}, bf16[512,1536]{1,0:T(8,128)(2,1)}, u32[]{:S(2)}, u32[]{:S(2)}) %collective-permute-start.88) | collective-permute-done | bytes 1572896 | tf_op jit(solution)/shard_map/ppermute | solution.py:350
  661.9 4.0 add_bitcast_fusion
  670.3 4.3 convert_add_fusion
  680.9 6.0 multiply_reduce_fusion
  699.6 12.3 %collective-permute-done.67 = bf16[256,1536]{1,0:T(8,128)(2,1)} collective-permute-done((bf16[256,1536]{1,0:T(8,128)(2,1)}, bf16[256,1536]{1,0:T(8,128)(2,1)}, u32[]{:S(2)}, u32[]{:S(2)}) %collective-permute-start.67) | collective-permute-done | bytes 786464 | tf_op jit(solution)/shard_map/ppermute | solution.py:377
  717.3 4.8 bitcast_add_fusion.1
  724.9 17.9 %collective-permute-done.74 = bf16[1,3,48,2688]{3,2,1,0:T(8,128)(2,1)S(1)} collective-permute-done((bf16[1,3,48,2688]{3,2,1,0:T(8,128)(2,1)S(1)}, bf16[1,3,48,2688]{3,2,1,0:T(8,128)(2,1)S(1)}, u32[]{:S(2)}, u32[]{:S(2)}) %collective-permute-start.74) | collective-permute-done | bytes 774176 | tf_op jit(solution)/shard_map/ppermute | solution.py:500
  745.2 5.5 collective-permute-done.75
  751.5 11.6 %collective-permute-done.77 = bf16[1,2,48,2688]{3,2,1,0:T(8,128)(2,1)S(1)} collective-permute-done((bf16[1,2,48,2688]{3,2,1,0:T(8,128)(2,1)S(1)}, bf16[1,2,48,2688]{3,2,1,0:T(8,128)(2,1)S(1)}, u32[]{:S(2)}, u32[]{:S(2)}) %collective-permute-start.77) | collective-permute-done | bytes 516128 | tf_op jit(solution)/shard_map/ppermute | solution.py:500
  764.8 6.2 collective-permute-done.82
  776.1 3.8 collective-permute-done.78
  (428 shorter events, 232.4 us)
Async XLA Ops:
  3.9 19.4 %collective-permute-start.17 = (bf16[48,1664]{1,0:T(8,128)(2,1)}, bf16[48,1664]{1,0:T(8,128)(2,1)}, u32[]{:S(2)}, u32[]{:S(2)}) collective-permute-start(bf16[48,1664]{1,0:T(8,128)(2,1)} %concatenate.60), channel_id=1, source_target_pairs={{0,4},{1,5},{4,8},{5,9},{8,12},{9,13},{12,14},{13,15},{14,10},{15,... | collective-permute-start | bytes 479240 | tf_op jit(solution)/shard_map/ppermute | solution.py:377
  10.5 115.7 %collective-permute-start.37 = (bf16[256,1664]{1,0:T(8,128)(2,1)}, bf16[256,1664]{1,0:T(8,128)(2,1)}, u32[]{:S(2)}, u32[]{:S(2)}) collective-permute-start(bf16[256,1664]{1,0:T(8,128)(2,1)} %concatenate.62.refs_1_), channel_id=1, source_target_pairs={{0,4},{1,5},{4,8},{5,9},{8,12},{9,13},{12,14},{13,15},{14,10},{15,... | collective-permute-start | bytes 2555912 | tf_op jit(solution)/shard_map/ppermute | solution.py:377
  12.5 115.3 %collective-permute-start.41 = (bf16[256,1664]{1,0:T(8,128)(2,1)}, bf16[256,1664]{1,0:T(8,128)(2,1)}, u32[]{:S(2)}, u32[]{:S(2)}) collective-permute-start(bf16[256,1664]{1,0:T(8,128)(2,1)} %concatenate.62.refs_1_), channel_id=1, source_target_pairs={{4,0},{5,1},{8,4},{9,5},{12,8},{13,9},{14,12},{15,13},{10,14},{11,... | collective-permute-start | bytes 2555912 | tf_op jit(solution)/shard_map/ppermute | solution.py:378
  28.3 28.5 %collective-permute-start.1 = (bf16[96,2688]{1,0:T(8,128)(2,1)S(1)}, bf16[96,2688]{1,0:T(8,128)(2,1)S(1)}, u32[]{:S(2)}, u32[]{:S(2)}) collective-permute-start(bf16[96,2688]{1,0:T(8,128)(2,1)S(1)} %bitcast.257), channel_id=1, source_target_pairs={{0,1},{1,0},{2,3},{3,2},{4,5},{5,4},{6,7},{7,6},{8,9},{9,8},{10,11... | collective-permute-start | bytes 1548296 | tf_op jit(solution)/shard_map/ppermute | solution.py:357
  94.0 129.8 %collective-permute-start.27 = (bf16[1,1536,1024]{2,1,0:T(8,128)(2,1)}, bf16[1,1536,1024]{2,1,0:T(8,128)(2,1)}, u32[]{:S(2)}, u32[]{:S(2)}) collective-permute-start(bf16[1,1536,1024]{2,1,0:T(8,128)(2,1)} %constant_dynamic-update-slice_fusion.2), channel_id=1, source_target_pairs={{0,1},{1,0},{2,3},{3,2},{4,5},{5,4},{6,7},{7,6},{8,9},{9,8},{10,11... | collective-permute-start | bytes 9437192 | tf_op jit(solution)/shard_map/ppermute | solution.py:357
  95.9 28.7 %collective-permute-start.25 = (bf16[8,48,1664]{2,1,0:T(8,128)(2,1)S(1)}, bf16[8,48,1664]{2,1,0:T(8,128)(2,1)S(1)}, u32[]{:S(2)}, u32[]{:S(2)}) collective-permute-start(bf16[8,48,1664]{2,1,0:T(8,128)(2,1)S(1)} %fusion.51), channel_id=1, source_target_pairs={{0,16},{16,0},{1,17},{17,1},{2,18},{18,2},{3,19},{19,3},{4,20},{20... | collective-permute-start | bytes 3833864 | tf_op jit(solution)/shard_map/ppermute | solution.py:447
  115.2 81.1 %all-to-all-start = ((bf16[16,320,128]{2,1,0:T(8,128)(2,1)}), bf16[16,320,128]{2,1,0:T(8,128)(2,1)}, u32[]{:S(2)}, u32[]{:S(2)}) async-start(bf16[16,320,128]{2,1,0:T(8,128)(2,1)} %bitcast.254), calls=%async_computation | async-start | bytes 2621440 | tf_op jit(solution)/shard_map/all_to_all | solution.py:344
  125.7 104.1 %collective-permute-start.26 = (bf16[2,8,48,1664]{3,2,1,0:T(8,128)(2,1)}, bf16[2,8,48,1664]{3,2,1,0:T(8,128)(2,1)}, u32[]{:S(2)}, u32[]{:S(2)}) collective-permute-start(bf16[2,8,48,1664]{3,2,1,0:T(8,128)(2,1)} %bitcast_dynamic-update-slice_fusion), channel_id=1, source_target_pairs={{0,1},{1,0},{2,3},{3,2},{4,5},{5,4},{6,7},{7,6},{8,9},{9,8},{10,11... | collective-permute-start | bytes 7667720 | tf_op jit(solution)/shard_map/ppermute | solution.py:357
  125.7 46.7 %collective-permute-start.28 = (bf16[1,512,1536]{2,1,0:T(8,128)(2,1)}, bf16[1,512,1536]{2,1,0:T(8,128)(2,1)}, u32[]{:S(2)}, u32[]{:S(2)}) collective-permute-start(bf16[1,512,1536]{2,1,0:T(8,128)(2,1)} %param.23), channel_id=1, source_target_pairs={{0,1},{1,0},{2,3},{3,2},{4,5},{5,4},{6,7},{7,6},{8,9},{9,8},{10,11... | collective-permute-start | bytes 4718600 | tf_op jit(solution)/shard_map/ppermute | solution.py:357
  126.2 35.5 %collective-permute-start.38 = (bf16[256,1664]{1,0:T(8,128)(2,1)}, bf16[256,1664]{1,0:T(8,128)(2,1)}, u32[]{:S(2)}, u32[]{:S(2)}) collective-permute-start(bf16[256,1664]{1,0:T(8,128)(2,1)} %collective-permute-done.37.refs_2_), channel_id=1, source_target_pairs={{0,4},{1,5},{4,8},{5,9},{8,12},{9,13},{12,14},{13,15},{14,10},{15,... | collective-permute-start | bytes 2555912 | tf_op jit(solution)/shard_map/ppermute | solution.py:377
  127.8 42.5 %collective-permute-start.42 = (bf16[256,1664]{1,0:T(8,128)(2,1)}, bf16[256,1664]{1,0:T(8,128)(2,1)}, u32[]{:S(2)}, u32[]{:S(2)}) collective-permute-start(bf16[256,1664]{1,0:T(8,128)(2,1)} %collective-permute-done.41.refs_3_), channel_id=1, source_target_pairs={{4,0},{5,1},{8,4},{9,5},{12,8},{13,9},{14,12},{15,13},{10,14},{11,... | collective-permute-start | bytes 2555912 | tf_op jit(solution)/shard_map/ppermute | solution.py:378
  161.8 26.8 %collective-permute-start.39 = (bf16[256,1664]{1,0:T(8,128)(2,1)}, bf16[256,1664]{1,0:T(8,128)(2,1)}, u32[]{:S(2)}, u32[]{:S(2)}) collective-permute-start(bf16[256,1664]{1,0:T(8,128)(2,1)} %collective-permute-done.38.refs_2_), channel_id=1, source_target_pairs={{0,4},{1,5},{4,8},{5,9},{8,12},{9,13},{12,14},{13,15},{14,10},{15,... | collective-permute-start | bytes 2555912 | tf_op jit(solution)/shard_map/ppermute | solution.py:377
  170.3 22.5 %collective-permute-start.43 = (bf16[256,1664]{1,0:T(8,128)(2,1)}, bf16[256,1664]{1,0:T(8,128)(2,1)}, u32[]{:S(2)}, u32[]{:S(2)}) collective-permute-start(bf16[256,1664]{1,0:T(8,128)(2,1)} %collective-permute-done.42.refs_3_), channel_id=1, source_target_pairs={{4,0},{5,1},{8,4},{9,5},{12,8},{13,9},{14,12},{15,13},{10,14},{11,... | collective-permute-start | bytes 2555912 | tf_op jit(solution)/shard_map/ppermute | solution.py:378
  190.3 152.3 %collective-permute-start.40 = (bf16[128,1664]{1,0:T(8,128)(2,1)}, bf16[128,1664]{1,0:T(8,128)(2,1)}, u32[]{:S(2)}, u32[]{:S(2)}) collective-permute-start(bf16[128,1664]{1,0:T(8,128)(2,1)} %slice.237), channel_id=1, source_target_pairs={{0,4},{1,5},{4,8},{5,9},{8,12},{9,13},{12,14},{13,15},{14,10},{15,... | collective-permute-start | bytes 1277960 | tf_op jit(solution)/shard_map/ppermute | solution.py:377
  194.6 148.0 %collective-permute-start.44 = (bf16[128,1664]{1,0:T(8,128)(2,1)}, bf16[128,1664]{1,0:T(8,128)(2,1)}, u32[]{:S(2)}, u32[]{:S(2)}) collective-permute-start(bf16[128,1664]{1,0:T(8,128)(2,1)} %slice.238), channel_id=1, source_target_pairs={{4,0},{5,1},{8,4},{9,5},{12,8},{13,9},{14,12},{15,13},{10,14},{11,... | collective-permute-start | bytes 1277960 | tf_op jit(solution)/shard_map/ppermute | solution.py:378
  218.6 23.9 %all-to-all-start.1 = ((bf16[16,192,128]{2,1,0:T(8,128)(2,1)}), bf16[16,192,128]{2,1,0:T(8,128)(2,1)}, u32[]{:S(2)}, u32[]{:S(2)}) async-start(bf16[16,192,128]{2,1,0:T(8,128)(2,1)} %get-tuple-element.68), calls=%async_computation.1 | async-start | bytes 1572864 | tf_op jit(solution)/shard_map/all_to_all | solution.py:344
  250.1 20.3 %collective-permute-start.29 = (bf16[256,1536]{1,0:T(8,128)(2,1)}, bf16[256,1536]{1,0:T(8,128)(2,1)}, u32[]{:S(2)}, u32[]{:S(2)}) collective-permute-start(bf16[256,1536]{1,0:T(8,128)(2,1)} %multiply_convert_fusion.1.refs_0_), channel_id=1, source_target_pairs={{0,4},{1,5},{4,8},{5,9},{8,12},{9,13},{12,14},{13,15},{14,10},{15,... | collective-permute-start | bytes 2359304 | tf_op jit(solution)/shard_map/ppermute | solution.py:377
  252.1 20.7 %collective-permute-start.33 = (bf16[256,1536]{1,0:T(8,128)(2,1)}, bf16[256,1536]{1,0:T(8,128)(2,1)}, u32[]{:S(2)}, u32[]{:S(2)}) collective-permute-start(bf16[256,1536]{1,0:T(8,128)(2,1)} %multiply_convert_fusion.1.refs_0_), channel_id=1, source_target_pairs={{4,0},{5,1},{8,4},{9,5},{12,8},{13,9},{14,12},{15,13},{10,14},{11,... | collective-permute-start | bytes 2359304 | tf_op jit(solution)/shard_map/ppermute | solution.py:378
  270.3 23.3 %collective-permute-start.30 = (bf16[256,1536]{1,0:T(8,128)(2,1)}, bf16[256,1536]{1,0:T(8,128)(2,1)}, u32[]{:S(2)}, u32[]{:S(2)}) collective-permute-start(bf16[256,1536]{1,0:T(8,128)(2,1)} %collective-permute-done.29.refs_0_), channel_id=1, source_target_pairs={{0,4},{1,5},{4,8},{5,9},{8,12},{9,13},{12,14},{13,15},{14,10},{15,... | collective-permute-start | bytes 2359304 | tf_op jit(solution)/shard_map/ppermute | solution.py:377
  272.8 22.8 %collective-permute-start.34 = (bf16[256,1536]{1,0:T(8,128)(2,1)}, bf16[256,1536]{1,0:T(8,128)(2,1)}, u32[]{:S(2)}, u32[]{:S(2)}) collective-permute-start(bf16[256,1536]{1,0:T(8,128)(2,1)} %collective-permute-done.33.refs_1_), channel_id=1, source_target_pairs={{4,0},{5,1},{8,4},{9,5},{12,8},{13,9},{14,12},{15,13},{10,14},{11,... | collective-permute-start | bytes 2359304 | tf_op jit(solution)/shard_map/ppermute | solution.py:378
  293.6 22.7 %collective-permute-start.31 = (bf16[256,1536]{1,0:T(8,128)(2,1)}, bf16[256,1536]{1,0:T(8,128)(2,1)}, u32[]{:S(2)}, u32[]{:S(2)}) collective-permute-start(bf16[256,1536]{1,0:T(8,128)(2,1)} %collective-permute-done.30.refs_0_), channel_id=1, source_target_pairs={{0,4},{1,5},{4,8},{5,9},{8,12},{9,13},{12,14},{13,15},{14,10},{15,... | collective-permute-start | bytes 2359304 | tf_op jit(solution)/shard_map/ppermute | solution.py:377
  295.6 24.5 %collective-permute-start.35 = (bf16[256,1536]{1,0:T(8,128)(2,1)}, bf16[256,1536]{1,0:T(8,128)(2,1)}, u32[]{:S(2)}, u32[]{:S(2)}) collective-permute-start(bf16[256,1536]{1,0:T(8,128)(2,1)} %collective-permute-done.34.refs_1_), channel_id=1, source_target_pairs={{4,0},{5,1},{8,4},{9,5},{12,8},{13,9},{14,12},{15,13},{10,14},{11,... | collective-permute-start | bytes 2359304 | tf_op jit(solution)/shard_map/ppermute | solution.py:378
  318.1 24.5 %collective-permute-start.32 = (bf16[128,1536]{1,0:T(8,128)(2,1)}, bf16[128,1536]{1,0:T(8,128)(2,1)S(1)}, u32[]{:S(2)}, u32[]{:S(2)}) collective-permute-start(bf16[128,1536]{1,0:T(8,128)(2,1)} %slice.235), channel_id=1, source_target_pairs={{0,4},{1,5},{4,8},{5,9},{8,12},{9,13},{12,14},{13,15},{14,10},{15,... | collective-permute-start | bytes 1179656 | tf_op jit(solution)/shard_map/ppermute | solution.py:377
  321.9 20.8 %collective-permute-start.36 = (bf16[128,1536]{1,0:T(8,128)(2,1)}, bf16[128,1536]{1,0:T(8,128)(2,1)S(1)}, u32[]{:S(2)}, u32[]{:S(2)}) collective-permute-start(bf16[128,1536]{1,0:T(8,128)(2,1)} %slice.236), channel_id=1, source_target_pairs={{4,0},{5,1},{8,4},{9,5},{12,8},{13,9},{14,12},{15,13},{10,14},{11,... | collective-permute-start | bytes 1179656 | tf_op jit(solution)/shard_map/ppermute | solution.py:378
  368.0 18.9 %collective-permute-start.46 = (bf16[256,1664]{1,0:T(8,128)(2,1)S(1)}, bf16[256,1664]{1,0:T(8,128)(2,1)S(1)}, u32[]{:S(2)}, u32[]{:S(2)}) collective-permute-start(bf16[256,1664]{1,0:T(8,128)(2,1)S(1)} %pad_add_fusion.1), channel_id=1, source_target_pairs={{0,4},{1,5},{4,8},{5,9},{8,12},{9,13},{12,14},{13,15},{14,10},{15,... | collective-permute-start | bytes 2555912 | tf_op jit(solution)/shard_map/ppermute | solution.py:377
  369.9 19.0 %collective-permute-start.50 = (bf16[256,1664]{1,0:T(8,128)(2,1)S(1)}, bf16[256,1664]{1,0:T(8,128)(2,1)S(1)}, u32[]{:S(2)}, u32[]{:S(2)}) collective-permute-start(bf16[256,1664]{1,0:T(8,128)(2,1)S(1)} %pad_add_fusion), channel_id=1, source_target_pairs={{4,0},{5,1},{8,4},{9,5},{12,8},{13,9},{14,12},{15,13},{10,14},{11,... | collective-permute-start | bytes 2555912 | tf_op jit(solution)/shard_map/ppermute | solution.py:378
  387.1 18.9 %collective-permute-start.47 = (bf16[256,1664]{1,0:T(8,128)(2,1)S(1)}, bf16[256,1664]{1,0:T(8,128)(2,1)S(1)}, u32[]{:S(2)}, u32[]{:S(2)}) collective-permute-start(bf16[256,1664]{1,0:T(8,128)(2,1)S(1)} %add.597), channel_id=1, source_target_pairs={{0,4},{1,5},{4,8},{5,9},{8,12},{9,13},{12,14},{13,15},{14,10},{15,... | collective-permute-start | bytes 2555912 | tf_op jit(solution)/shard_map/ppermute | solution.py:377
  389.1 18.9 %collective-permute-start.51 = (bf16[256,1664]{1,0:T(8,128)(2,1)S(1)}, bf16[256,1664]{1,0:T(8,128)(2,1)S(1)}, u32[]{:S(2)}, u32[]{:S(2)}) collective-permute-start(bf16[256,1664]{1,0:T(8,128)(2,1)S(1)} %add.601), channel_id=1, source_target_pairs={{4,0},{5,1},{8,4},{9,5},{12,8},{13,9},{14,12},{15,13},{10,14},{11,... | collective-permute-start | bytes 2555912 | tf_op jit(solution)/shard_map/ppermute | solution.py:378
  461.0 30.4 %collective-permute-start.56 = (bf16[1,8,48,1664]{3,2,1,0:T(8,128)(2,1)}, bf16[1,8,48,1664]{3,2,1,0:T(8,128)(2,1)}, u32[]{:S(2)}, u32[]{:S(2)}) collective-permute-start(bf16[1,8,48,1664]{3,2,1,0:T(8,128)(2,1)} %constant_dynamic-slice_fusion.1), channel_id=1, source_target_pairs={{0,16},{16,0},{1,17},{17,1},{2,18},{18,2},{3,19},{19,3},{4,20},{20... | collective-permute-start | bytes 3833864 | tf_op jit(solution)/shard_map/ppermute | solution.py:500
  472.2 74.0 %collective-permute-start.85 = (bf16[1536,1024]{1,0:T(8,128)(2,1)}, bf16[1536,1024]{1,0:T(8,128)(2,1)}, u32[]{:S(2)}, u32[]{:S(2)}) collective-permute-start(bf16[1536,1024]{1,0:T(8,128)(2,1)} %fusion.6), channel_id=1, source_target_pairs={{0,1},{1,0},{2,3},{3,2},{4,5},{5,4},{6,7},{7,6},{8,9},{9,8},{10,11... | collective-permute-start | bytes 9437192 | tf_op jit(solution)/shard_map/ppermute | solution.py:357
  474.5 35.0 %all-to-all-start.2 = ((bf16[16,192,128]{2,1,0:T(8,128)(2,1)}), bf16[16,192,128]{2,1,0:T(8,128)(2,1)S(1)}, u32[]{:S(2)}, u32[]{:S(2)}) async-start(bf16[16,192,128]{2,1,0:T(8,128)(2,1)} %bitcast.50), calls=%async_computation.2 | async-start | bytes 1572864 | tf_op jit(solution)/shard_map/all_to_all | solution.py:344
  498.7 44.3 %collective-permute-start.58 = (bf16[48,1664]{1,0:T(8,128)(2,1)S(1)}, bf16[48,1664]{1,0:T(8,128)(2,1)S(1)}, u32[]{:S(2)}, u32[]{:S(2)}) collective-permute-start(bf16[48,1664]{1,0:T(8,128)(2,1)S(1)} %get-tuple-element.216), channel_id=1, source_target_pairs={{0,4},{1,5},{4,8},{5,9},{8,12},{9,13},{12,14},{13,15},{14,10},{15,... | collective-permute-start | bytes 479240 | tf_op jit(solution)/shard_map/ppermute | solution.py:377
  501.4 41.6 %collective-permute-start.62 = (bf16[48,1664]{1,0:T(8,128)(2,1)S(1)}, bf16[48,1664]{1,0:T(8,128)(2,1)S(1)}, u32[]{:S(2)}, u32[]{:S(2)}) collective-permute-start(bf16[48,1664]{1,0:T(8,128)(2,1)S(1)} %get-tuple-element.217), channel_id=1, source_target_pairs={{4,0},{5,1},{8,4},{9,5},{12,8},{13,9},{14,12},{15,13},{10,14},{11,... | collective-permute-start | bytes 479240 | tf_op jit(solution)/shard_map/ppermute | solution.py:378
  509.5 71.0 %collective-permute-start.87 = (bf16[512,1536]{1,0:T(8,128)(2,1)}, bf16[512,1536]{1,0:T(8,128)(2,1)}, u32[]{:S(2)}, u32[]{:S(2)}) collective-permute-start(bf16[512,1536]{1,0:T(8,128)(2,1)} %convolution_convert_fusion), channel_id=1, source_target_pairs={{0,1},{1,0},{2,3},{3,2},{4,5},{5,4},{6,7},{7,6},{8,9},{9,8},{10,11... | collective-permute-start | bytes 4718600 | tf_op jit(solution)/shard_map/ppermute | solution.py:357
  538.6 49.2 %all-to-all-start.3 = ((bf16[16,320,128]{2,1,0:T(8,128)(2,1)}), bf16[16,320,128]{2,1,0:T(8,128)(2,1)S(1)}, u32[]{:S(2)}, u32[]{:S(2)}) async-start(bf16[16,320,128]{2,1,0:T(8,128)(2,1)} %backward.1), calls=%async_computation.3 | async-start | bytes 2621440 | tf_op jit(solution)/shard_map/all_to_all | solution.py:344
  544.1 24.6 %collective-permute-start.59 = (bf16[48,1664]{1,0:T(8,128)(2,1)S(1)}, bf16[48,1664]{1,0:T(8,128)(2,1)S(1)}, u32[]{:S(2)}, u32[]{:S(2)}) collective-permute-start(bf16[48,1664]{1,0:T(8,128)(2,1)S(1)} %get-tuple-element.214), channel_id=1, source_target_pairs={{0,4},{1,5},{4,8},{5,9},{8,12},{9,13},{12,14},{13,15},{14,10},{15,... | collective-permute-start | bytes 479240 | tf_op jit(solution)/shard_map/ppermute | solution.py:377
  546.1 22.6 %collective-permute-start.63 = (bf16[48,1664]{1,0:T(8,128)(2,1)S(1)}, bf16[48,1664]{1,0:T(8,128)(2,1)S(1)}, u32[]{:S(2)}, u32[]{:S(2)}) collective-permute-start(bf16[48,1664]{1,0:T(8,128)(2,1)S(1)} %get-tuple-element.215), channel_id=1, source_target_pairs={{4,0},{5,1},{8,4},{9,5},{12,8},{13,9},{14,12},{15,13},{10,14},{11,... | collective-permute-start | bytes 479240 | tf_op jit(solution)/shard_map/ppermute | solution.py:378
  558.0 112.3 %collective-permute-start.86 = (bf16[1536,1024]{1,0:T(8,128)(2,1)}, bf16[1536,1024]{1,0:T(8,128)(2,1)}, u32[]{:S(2)}, u32[]{:S(2)}) collective-permute-start(bf16[1536,1024]{1,0:T(8,128)(2,1)} %add_convert_fusion), channel_id=1, source_target_pairs={{0,16},{16,0},{1,17},{17,1},{2,18},{18,2},{3,19},{19,3},{4,20},{20... | collective-permute-start | bytes 9437192 | tf_op jit(solution)/shard_map/ppermute | solution.py:350
  586.2 75.7 %collective-permute-start.88 = (bf16[512,1536]{1,0:T(8,128)(2,1)}, bf16[512,1536]{1,0:T(8,128)(2,1)}, u32[]{:S(2)}, u32[]{:S(2)}) collective-permute-start(bf16[512,1536]{1,0:T(8,128)(2,1)} %fusion.9), channel_id=1, source_target_pairs={{0,16},{16,0},{1,17},{17,1},{2,18},{18,2},{3,19},{19,3},{4,20},{20... | collective-permute-start | bytes 4718600 | tf_op jit(solution)/shard_map/ppermute | solution.py:350
  594.7 122.6 %collective-permute-start.71 = (bf16[2,8,48,2560]{3,2,1,0:T(8,128)(2,1)}, bf16[2,8,48,2560]{3,2,1,0:T(8,128)(2,1)}, u32[]{:S(2)}, u32[]{:S(2)}) collective-permute-start(bf16[2,8,48,2560]{3,2,1,0:T(8,128)(2,1)} %select_bitcast_fusion), channel_id=1, source_target_pairs={{0,1},{1,0},{2,3},{3,2},{4,5},{5,4},{6,7},{7,6},{8,9},{9,8},{10,11... | collective-permute-start | bytes 11796488 | tf_op jit(solution)/shard_map/ppermute | solution.py:357
  667.0 19.9 %collective-permute-start.66 = (bf16[256,1536]{1,0:T(8,128)(2,1)}, bf16[256,1536]{1,0:T(8,128)(2,1)}, u32[]{:S(2)}, u32[]{:S(2)}) collective-permute-start(bf16[256,1536]{1,0:T(8,128)(2,1)} %add.624), channel_id=1, source_target_pairs={{4,0},{5,1},{8,4},{9,5},{12,8},{13,9},{14,12},{15,13},{10,14},{11,... | collective-permute-start | bytes 2359304 | tf_op jit(solution)/shard_map/ppermute | solution.py:378
  670.3 18.1 %collective-permute-start.65 = (bf16[256,1536]{1,0:T(8,128)(2,1)}, bf16[256,1536]{1,0:T(8,128)(2,1)}, u32[]{:S(2)}, u32[]{:S(2)}) collective-permute-start(bf16[256,1536]{1,0:T(8,128)(2,1)} %add.623), channel_id=1, source_target_pairs={{0,4},{1,5},{4,8},{5,9},{8,12},{9,13},{12,14},{13,15},{14,10},{15,... | collective-permute-start | bytes 2359304 | tf_op jit(solution)/shard_map/ppermute | solution.py:377
  691.7 20.3 %collective-permute-start.67 = (bf16[256,1536]{1,0:T(8,128)(2,1)}, bf16[256,1536]{1,0:T(8,128)(2,1)}, u32[]{:S(2)}, u32[]{:S(2)}) collective-permute-start(bf16[256,1536]{1,0:T(8,128)(2,1)} %add.625), channel_id=1, source_target_pairs={{0,4},{1,5},{4,8},{5,9},{8,12},{9,13},{12,14},{13,15},{14,10},{15,... | collective-permute-start | bytes 2359304 | tf_op jit(solution)/shard_map/ppermute | solution.py:377
  694.2 20.0 %collective-permute-start.69 = (bf16[256,1536]{1,0:T(8,128)(2,1)}, bf16[256,1536]{1,0:T(8,128)(2,1)}, u32[]{:S(2)}, u32[]{:S(2)}) collective-permute-start(bf16[256,1536]{1,0:T(8,128)(2,1)} %add.628), channel_id=1, source_target_pairs={{4,0},{5,1},{8,4},{9,5},{12,8},{13,9},{14,12},{15,13},{10,14},{11,... | collective-permute-start | bytes 2359304 | tf_op jit(solution)/shard_map/ppermute | solution.py:378
  713.3 69.8 %collective-permute-start.68 = (bf16[256,1536]{1,0:T(8,128)(2,1)S(1)}, bf16[256,1536]{1,0:T(8,128)(2,1)S(1)}, u32[]{:S(2)}, u32[]{:S(2)}) collective-permute-start(bf16[256,1536]{1,0:T(8,128)(2,1)S(1)} %add.626), channel_id=1, source_target_pairs={{0,4},{1,5},{4,8},{5,9},{8,12},{9,13},{12,14},{13,15},{14,10},{15,... | collective-permute-start | bytes 2359304 | tf_op jit(solution)/shard_map/ppermute | solution.py:377
  715.5 67.6 %collective-permute-start.70 = (bf16[256,1536]{1,0:T(8,128)(2,1)S(1)}, bf16[256,1536]{1,0:T(8,128)(2,1)S(1)}, u32[]{:S(2)}, u32[]{:S(2)}) collective-permute-start(bf16[256,1536]{1,0:T(8,128)(2,1)S(1)} %add.629), channel_id=1, source_target_pairs={{4,0},{5,1},{8,4},{9,5},{12,8},{13,9},{14,12},{15,13},{10,14},{11,... | collective-permute-start | bytes 2359304 | tf_op jit(solution)/shard_map/ppermute | solution.py:378
  722.6 20.2 %collective-permute-start.74 = (bf16[1,3,48,2688]{3,2,1,0:T(8,128)(2,1)S(1)}, bf16[1,3,48,2688]{3,2,1,0:T(8,128)(2,1)S(1)}, u32[]{:S(2)}, u32[]{:S(2)}) collective-permute-start(bf16[1,3,48,2688]{3,2,1,0:T(8,128)(2,1)S(1)} %constant_dynamic-slice_fusion), channel_id=1, source_target_pairs={{0,16},{16,0},{1,17},{17,1},{2,18},{18,2},{3,19},{19,3},{4,20},{20... | collective-permute-start | bytes 2322440 | tf_op jit(solution)/shard_map/ppermute | solution.py:500
  723.2 61.5 %collective-permute-start.73 = (bf16[1,1,48,2688]{3,2,1,0:T(8,128)(2,1)S(1)}, bf16[1,1,48,2688]{3,2,1,0:T(8,128)(2,1)S(1)}, u32[]{:S(2)}, u32[]{:S(2)}) collective-permute-start(bf16[1,1,48,2688]{3,2,1,0:T(8,128)(2,1)S(1)} %fusion.34), channel_id=1, source_target_pairs={{0,16},{16,0},{1,17},{17,1},{2,18},{18,2},{3,19},{19,3},{4,20},{20... | collective-permute-start | bytes 774152 | tf_op jit(solution)/shard_map/ppermute | solution.py:500
  (92 other events, 1378.1 us)

commit v7 on v6

--- a/solution.py
+++ b/solution.py
@@ -766,8 +766,8 @@
         jnp.concatenate([grad_router, grad_gain_second[:, None]], axis=1),
     ).astype(jnp.bfloat16)
     mixed_ring.land()
-    d_attended, early, mixed_ring.onward, mixed_ring.back = lax.optimization_barrier(
-        (d_attended, early, mixed_ring.onward, mixed_ring.back)
+    d_attended, mixed_ring.onward, mixed_ring.back = lax.optimization_barrier(
+        (d_attended, mixed_ring.onward, mixed_ring.back)
     )
     pair_grad = to_pairs(d_attended, lanes)
     pair_grad, mixed_ring.onward, mixed_ring.back = lax.optimization_barrier(
@@ -781,7 +781,6 @@
     early = DenseSum(early, "early", True).total()
     mixed_ring.land()
     d_linear = to_tokens(pair_d, span)
-    d_linear, early = lax.optimization_barrier((d_linear, early))
     grad_mixed = contract(
         "stf,sct->fc", normed.reshape(seq_local, shard, width), d_linear
     ).astype(jnp.bfloat16)
@@ -794,8 +793,11 @@
     grad_gain_first, mixed_ring.onward, mixed_ring.back = lax.optimization_barrier(
         (grad_gain_first, mixed_ring.onward, mixed_ring.back)
     )
+    late.append(jnp.pad(grad_gain_first[:, None].astype(jnp.bfloat16), ((0, 0), (0, LANES - 1))))
+    late.mine, mixed_ring.onward, mixed_ring.back = lax.optimization_barrier(
+        (late.mine, mixed_ring.onward, mixed_ring.back)
+    )
     mixed_ring.send().land()
-    late.append(jnp.pad(grad_gain_first[:, None].astype(jnp.bfloat16), ((0, 0), (0, LANES - 1))))
     late_ring = late.ring()
     sums = [
         functools.reduce(jnp.add, [v.astype(jnp.float32) for v in others], part.astype(jnp.float32))

time: 802 us -> 754 us (0.940)
  waiting for transfers between devices: 334 us -> 290 us
    ppermute x2, waiting for transfers between devices: 67.2 us -> 28.4 us  [from_heads(): lax.ppermute(values, HEAD, [(k, (k + turn) % heads) for k in range(heads)])]
    ppermute x32, waiting for transfers between devices: 184 us -> 158 us  [ring_steps(): send_on = lambda values: lax.ppermute(values, BLK, onward)]
    ppermute x5, waiting for transfers between devices: 44.8 us -> 61.2 us  [head_share(): other = lax.ppermute(share(turn), HEAD, moved)]
    ppermute x32, starting transfers between devices: 66.7 us -> 57.7 us  [ring_steps(): send_on = lambda values: lax.ppermute(values, BLK, onward)]
  transfers between devices with their start and end apart: 93 -> 93, of which waited for: 38 -> 35; matrix products, arithmetic and copies ran while one was open for 20% -> 23% of each run, Pallas kernels for 17% -> 18%
where the time goes in v7:
time: 754 us; the launch traced here: 744 us
  waiting for transfers between devices  290 us (38%)
  Pallas kernels  145 us (19%)
  starting transfers between devices  112 us (15%)
  other arithmetic  71.6 us (9%)
  local copies, waits for them, and re-layouts  63.9 us (8%)
  matrix products  59 us (8%)
    ppermute x32, waiting for transfers between devices, ring_steps(): send_on = lambda values: lax.ppermute(values, BLK, onward)  158 us
    pallas_call x5, Pallas kernels, expert_rows(): pl.pallas_call(functools.partial(expert_kernel, parts, rows, width, exper...  86.7 us
    ppermute x5, waiting for transfers between devices, head_share(): other = lax.ppermute(share(turn), HEAD, moved)  61.2 us
    ppermute x32, starting transfers between devices, ring_steps(): send_on = lambda values: lax.ppermute(values, BLK, onward)  57.7 us
    dot_general x4, matrix products, matmul_tn(): lax.dot_general(left, right, (((0,), (0,)), ((), ())), preferred_element_...  29.7 us
    ppermute x2, waiting for transfers between devices, from_heads(): lax.ppermute(values, HEAD, [(k, (k + turn) % heads) for k in range(heads)])  28.4 us
    pallas_call x1, Pallas kernels, attend_backward(): pl.pallas_call(functools.partial(backward_kernel, group, steps), grid=(st...  28.2 us
    ppermute x32, waiting for transfers between devices, ring_steps(): send_back = lambda values: lax.ppermute(values, BLK, back)  25.7 us
  transfers between devices with their start and end apart: 93, of which 35 were waited for; matrix products, arithmetic and copies ran while one was open for 23% of the time, Pallas kernels for 18%

profile of v7, /device:TPU:0, one launch (start us, length us, event | category | flops | bytes accessed | tf_op | source)
XLA Modules:
  0.0 744.2 jit_solution(10803154739584657611)
XLA Ops:
  28.9 5.6 collective-permute-done.19
  36.6 4.9 collective-permute-done.22
  51.9 4.8 collective-permute-done.2
  60.1 10.9 %collective-permute-done.6 = bf16[96,2688]{1,0:T(8,128)(2,1)S(1)} collective-permute-done((bf16[96,2688]{1,0:T(8,128)(2,1)S(1)}, bf16[96,2688]{1,0:T(8,128)(2,1)S(1)}, u32[]{:S(2)}, u32[]{:S(2)}) %collective-permute-start.6) | collective-permute-done | bytes 516128 | tf_op jit(solution)/shard_map/ppermute | solution.py:377
  73.9 11.4 %collective-permute-done.10 = bf16[96,2688]{1,0:T(8,128)(2,1)S(1)} collective-permute-done((bf16[96,2688]{1,0:T(8,128)(2,1)S(1)}, bf16[96,2688]{1,0:T(8,128)(2,1)S(1)}, u32[]{:S(2)}, u32[]{:S(2)}) %collective-permute-start.10) | collective-permute-done | bytes 516128 | tf_op jit(solution)/shard_map/ppermute | solution.py:377
  89.2 4.8 collective-permute-done.14
  107.1 8.1 %project.1 = bf16[2,8,320,128]{3,2,1,0:T(8,128)(2,1)} custom-call(bf16[256,1536]{1,0:T(8,128)(2,1)} %multiply_convert_fusion.2.rows_ref, bf16[1536,2688]{1,0:T(8,128)(2,1)} %bitcast.247, f32[128,640]{1,0:T(8,128)} %concatenate.58.cosine_ref, f32[128,640]{1,0:T(8,128)} %concatenate.59.sine_ref), custom_call_target="tpu_custom_call" | custom-call | flops 2013265920 | bytes 7864320 | tf_op jit(solution)/shard_map/project/pallas_call | solution.py:594
  115.2 5.9 all-to-all-start
  128.2 33.5 %collective-permute-done.38.refs_2_ = bf16[256,1664]{1,0:T(8,128)(2,1)} collective-permute-done((bf16[256,1664]{1,0:T(8,128)(2,1)}, bf16[256,1664]{1,0:T(8,128)(2,1)}, u32[]{:S(2)}, u32[]{:S(2)}) %collective-permute-start.38) | collective-permute-done | bytes 852000 | tf_op jit(solution)/shard_map/ppermute | solution.py:377
  161.7 8.6 %collective-permute-start.39 = (bf16[256,1664]{1,0:T(8,128)(2,1)}, bf16[256,1664]{1,0:T(8,128)(2,1)}, u32[]{:S(2)}, u32[]{:S(2)}) collective-permute-start(bf16[256,1664]{1,0:T(8,128)(2,1)} %collective-permute-done.38.refs_2_), channel_id=1, source_target_pairs={{0,4},{1,5},{4,8},{5,9},{8,12},{9,13},{12,14},{13,15},{14,10},{15,... | collective-permute-start | bytes 2555912 | tf_op jit(solution)/shard_map/ppermute | solution.py:377
  174.0 14.6 %collective-permute-done.39.refs_2_ = bf16[256,1664]{1,0:T(8,128)(2,1)} collective-permute-done((bf16[256,1664]{1,0:T(8,128)(2,1)}, bf16[256,1664]{1,0:T(8,128)(2,1)}, u32[]{:S(2)}, u32[]{:S(2)}) %collective-permute-start.39) | collective-permute-done | bytes 852000 | tf_op jit(solution)/shard_map/ppermute | solution.py:377
  196.3 22.3 %forward.1 = (bf16[16,192,128]{2,1,0:T(8,128)(2,1)}, f32[8,64,768]{2,1,0:T(8,128)}, f32[8,1,768]{2,1,0:T(1,128)}) custom-call(bf16[16,320,128]{2,1,0:T(8,128)(2,1)} %all-to-all-done.qkv_ref), custom_call_target="tpu_custom_call" | custom-call | tf_op jit(solution)/shard_map/forward/pallas_call | solution.py:114
  218.5 5.1 all-to-all-start.1
  223.7 6.0 pad_maximum_fusion.refs_3_.refs_5_
  236.8 5.5 all-to-all-done.1
  244.6 4.1 multiply_reduce_fusion.4
  253.9 12.6 %expert_rows.5 = (bf16[256,1536]{1,0:T(8,128)(2,1)}, bf16[256,1664]{1,0:T(8,128)(2,1)}, bf16[2048,1536]{1,0:T(8,128)(2,1)}, bf16[2048,1536]{1,0:T(8,128)(2,1)}, ...) custom-call(s32[2]{0:T(128)} %pad_add_fusion.2.index_ref, bf16[256,1536]{1,0:T(8,128)(2,1)} %multiply_convert_fusion.1.refs_0_, ...), custom_call_target="tpu_custom_call" | custom-call | flops 4831838208 | bytes 17301504 | tf_op jit(solution)/shard_map/expert_rows/pallas_call | solution.py:298
  266.5 3.8 collective-permute-done.29.refs_0_
  273.0 20.5 %expert_rows.6 = (bf16[256,1536]{1,0:T(8,128)(2,1)}, bf16[256,1536]{1,0:T(8,128)(2,1)}, bf16[256,1664]{1,0:T(8,128)(2,1)}, bf16[256,1664]{1,0:T(8,128)(2,1)}, bf...) custom-call(s32[2]{0:T(128)} %pad_add_fusion.2.index_ref, ...), custom_call_target="tpu_custom_call", output_to_operand_aliasing={{4}: (8, {}), {5}: (9, {}), {6}: (10, {}), {7}: (11, {})} | custom-call | flops 9663676416 | bytes 25165824 | tf_op jit(solution)/shard_map/expert_rows/pallas_call | solution.py:298
  295.8 20.5 %expert_rows.7 = (bf16[256,1536]{1,0:T(8,128)(2,1)}, bf16[256,1536]{1,0:T(8,128)(2,1)}, bf16[256,1664]{1,0:T(8,128)(2,1)}, bf16[256,1664]{1,0:T(8,128)(2,1)}, bf...) custom-call(s32[2]{0:T(128)} %pad_add_fusion.2.index_ref, ...), custom_call_target="tpu_custom_call", output_to_operand_aliasing={{4}: (8, {}), {5}: (9, {}), {6}: (10, {}), {7}: (11, {})} | custom-call | flops 9663676416 | bytes 25165824 | tf_op jit(solution)/shard_map/expert_rows/pallas_call | solution.py:298
  322.2 20.5 %expert_rows.8 = (bf16[256,1536]{1,0:T(8,128)(2,1)}, bf16[256,1536]{1,0:T(8,128)(2,1)}, bf16[256,1664]{1,0:T(8,128)(2,1)}, bf16[256,1664]{1,0:T(8,128)(2,1)}, bf...) custom-call(s32[2]{0:T(128)} %pad_add_fusion.2.index_ref, ...), custom_call_target="tpu_custom_call", output_to_operand_aliasing={{4}: (8, {}), {5}: (9, {}), {6}: (10, {}), {7}: (11, {})} | custom-call | flops 9663676416 | bytes 25165824 | tf_op jit(solution)/shard_map/expert_rows/pallas_call | solution.py:298
  343.5 12.6 %expert_rows.9 = (bf16[128,1536]{1,0:T(8,128)(2,1)}, bf16[128,1536]{1,0:T(8,128)(2,1)}, bf16[128,1664]{1,0:T(8,128)(2,1)}, bf16[128,1664]{1,0:T(8,128)(2,1)}, bf...) custom-call(s32[2]{0:T(128)} %pad_add_fusion.2.index_ref, ...), custom_call_target="tpu_custom_call", output_to_operand_aliasing={{4}: (8, {}), {5}: (9, {}), {6}: (10, {}), {7}: (11, {})} | custom-call | flops 4831838208 | bytes 17301504 | tf_op jit(solution)/shard_map/expert_rows/pallas_call | solution.py:298
  358.2 8.6 %collective-permute-done.45 = bf16[128,1664]{1,0:T(8,128)(2,1)S(1)} collective-permute-done((bf16[128,1664]{1,0:T(8,128)(2,1)}, bf16[128,1664]{1,0:T(8,128)(2,1)S(1)}, u32[]{:S(2)}, u32[]{:S(2)}) %collective-permute-start.45) | collective-permute-done | bytes 426016 | tf_op jit(solution)/shard_map/ppermute | solution.py:377
  374.1 13.8 %collective-permute-done.46 = bf16[256,1664]{1,0:T(8,128)(2,1)} collective-permute-done((bf16[256,1664]{1,0:T(8,128)(2,1)}, bf16[256,1664]{1,0:T(8,128)(2,1)}, u32[]{:S(2)}, u32[]{:S(2)}) %collective-permute-start.46) | collective-permute-done | bytes 852000 | tf_op jit(solution)/shard_map/ppermute | solution.py:377
  393.9 6.4 convolution_convert_fusion
  400.3 8.1 %collective-permute-done.47 = bf16[256,1664]{1,0:T(8,128)(2,1)S(1)} collective-permute-done((bf16[256,1664]{1,0:T(8,128)(2,1)S(1)}, bf16[256,1664]{1,0:T(8,128)(2,1)S(1)}, u32[]{:S(2)}, u32[]{:S(2)}) %collective-permute-start.47) | collective-permute-done | bytes 852000 | tf_op jit(solution)/shard_map/ppermute | solution.py:377
  413.0 8.3 %fusion.6 = bf16[1536,1024]{1,0:T(8,128)(2,1)} fusion(bf16[2048,1536]{1,0:T(8,128)(2,1)S(1)} %bitcast.239, bf16[2048,2048]{1,0:T(8,128)(2,1)S(1)} %bitcast.235), kind=kOutput, calls=%fused_computation.17 | convolution fusion | flops 6444023808 | bytes 13631488 | tf_op jit(solution)/shard_map/dot_general | solution.py:54
  421.3 4.3 collective-permute-done.48
  435.7 3.5 fusion.48
  448.2 5.1 fusion.13
  453.3 9.3 %add_convert_fusion = bf16[1536,1024]{1,0:T(8,128)(2,1)} fusion(bf16[1536,1024]{1,0:T(8,128)(2,1)} %collective-permute-done.85, bf16[2048,1536]{1,0:T(8,128)(2,1)S(1)} %bitcast.241, bf16[2048,2048]{1,0:T(8,128)(2,1)S(1)} %bitcast.237), kind=kOutput, calls=%fused_computation.5 | convolution fusion | flops 6447169536 | bytes 16777216 | tf_op jit(solution)/shard_map/dot_general | solution.py:54
  468.5 4.3 all-to-all-start.2
  472.8 3.8 bitcast_add_fusion.2
  480.5 5.7 fusion.9
  491.5 28.2 %backward.1 = bf16[16,320,128]{2,1,0:T(8,128)(2,1)} custom-call(bf16[16,320,128]{2,1,0:T(8,128)(2,1)} %all-to-all-done.qkv_ref, bf16[16,192,128]{2,1,0:T(8,128)(2,1)} %all-to-all-done.2.grad_ref, f32[8,64,768]{2,1,0:T(8,128)} %get-tuple-element.104.flat_ref, f32[8,1,768]{2,1,0:T(1,128)} %get-tuple-element.105.lse_ref, ...), custom_call_target="tpu_custom_call" | custom-call | tf_op jit(solution)/shard_map/backward/pallas_call | solution.py:188
  519.7 5.4 all-to-all-start.3
  525.1 36.2 %collective-permute-done.76 = bf16[1,8,48,1664]{3,2,1,0:T(8,128)(2,1)} collective-permute-done((bf16[1,8,48,1664]{3,2,1,0:T(8,128)(2,1)}, bf16[1,8,48,1664]{3,2,1,0:T(8,128)(2,1)}, u32[]{:S(2)}, u32[]{:S(2)}) %collective-permute-start.76) | collective-permute-done | bytes 1277984 | tf_op jit(solution)/shard_map/ppermute | solution.py:500
  565.4 28.4 %collective-permute-done.88 = bf16[512,1536]{1,0:T(8,128)(2,1)S(1)} collective-permute-done((bf16[512,1536]{1,0:T(8,128)(2,1)}, bf16[512,1536]{1,0:T(8,128)(2,1)S(1)}, u32[]{:S(2)}, u32[]{:S(2)}) %collective-permute-start.88) | collective-permute-done | bytes 1572896 | tf_op jit(solution)/shard_map/ppermute | solution.py:350
  603.7 6.9 convert_add_fusion
  610.6 11.7 %collective-permute-done.78 = bf16[48,1664]{1,0:T(8,128)(2,1)S(1)} collective-permute-done((bf16[48,1664]{1,0:T(8,128)(2,1)S(1)}, bf16[48,1664]{1,0:T(8,128)(2,1)S(1)}, u32[]{:S(2)}, u32[]{:S(2)}) %collective-permute-start.78) | collective-permute-done | bytes 159776 | tf_op jit(solution)/shard_map/ppermute | solution.py:377
  624.7 3.9 bitcast_convert_fusion
  633.0 3.6 slice_bitcast_fusion.2
  642.6 6.3 multiply_reduce_fusion.1
  654.4 4.8 bitcast_add_fusion.1
  667.3 13.1 %collective-permute-done.64 = bf16[1,3,48,2688]{3,2,1,0:T(8,128)(2,1)S(1)} collective-permute-done((bf16[1,3,48,2688]{3,2,1,0:T(8,128)(2,1)S(1)}, bf16[1,3,48,2688]{3,2,1,0:T(8,128)(2,1)S(1)}, u32[]{:S(2)}, u32[]{:S(2)}) %collective-permute-start.64) | collective-permute-done | bytes 774176 | tf_op jit(solution)/shard_map/ppermute | solution.py:500
  689.5 12.0 %collective-permute-done.67 = bf16[1,2,48,2688]{3,2,1,0:T(8,128)(2,1)S(1)} collective-permute-done((bf16[1,2,48,2688]{3,2,1,0:T(8,128)(2,1)S(1)}, bf16[1,2,48,2688]{3,2,1,0:T(8,128)(2,1)S(1)}, u32[]{:S(2)}, u32[]{:S(2)}) %collective-permute-start.67) | collective-permute-done | bytes 516128 | tf_op jit(solution)/shard_map/ppermute | solution.py:500
  714.7 13.0 %collective-permute-done.68 = bf16[48,2688]{1,0:T(8,128)(2,1)S(1)} collective-permute-done((bf16[48,2688]{1,0:T(8,128)(2,1)S(1)}, bf16[48,2688]{1,0:T(8,128)(2,1)S(1)}, u32[]{:S(2)}, u32[]{:S(2)}) %collective-permute-start.68) | collective-permute-done | bytes 258080 | tf_op jit(solution)/shard_map/ppermute | solution.py:377
  727.7 5.2 collective-permute-done.73
  (442 shorter events, 235.7 us)
Async XLA Ops:
  3.9 19.4 %collective-permute-start.17 = (bf16[48,1664]{1,0:T(8,128)(2,1)}, bf16[48,1664]{1,0:T(8,128)(2,1)}, u32[]{:S(2)}, u32[]{:S(2)}) collective-permute-start(bf16[48,1664]{1,0:T(8,128)(2,1)} %concatenate.60), channel_id=1, source_target_pairs={{0,4},{1,5},{4,8},{5,9},{8,12},{9,13},{12,14},{13,15},{14,10},{15,... | collective-permute-start | bytes 479240 | tf_op jit(solution)/shard_map/ppermute | solution.py:377
  10.5 115.7 %collective-permute-start.37 = (bf16[256,1664]{1,0:T(8,128)(2,1)}, bf16[256,1664]{1,0:T(8,128)(2,1)}, u32[]{:S(2)}, u32[]{:S(2)}) collective-permute-start(bf16[256,1664]{1,0:T(8,128)(2,1)} %concatenate.62.refs_1_), channel_id=1, source_target_pairs={{0,4},{1,5},{4,8},{5,9},{8,12},{9,13},{12,14},{13,15},{14,10},{15,... | collective-permute-start | bytes 2555912 | tf_op jit(solution)/shard_map/ppermute | solution.py:377
  12.5 115.3 %collective-permute-start.41 = (bf16[256,1664]{1,0:T(8,128)(2,1)}, bf16[256,1664]{1,0:T(8,128)(2,1)}, u32[]{:S(2)}, u32[]{:S(2)}) collective-permute-start(bf16[256,1664]{1,0:T(8,128)(2,1)} %concatenate.62.refs_1_), channel_id=1, source_target_pairs={{4,0},{5,1},{8,4},{9,5},{12,8},{13,9},{14,12},{15,13},{10,14},{11,... | collective-permute-start | bytes 2555912 | tf_op jit(solution)/shard_map/ppermute | solution.py:378
  28.2 28.5 %collective-permute-start.1 = (bf16[96,2688]{1,0:T(8,128)(2,1)S(1)}, bf16[96,2688]{1,0:T(8,128)(2,1)S(1)}, u32[]{:S(2)}, u32[]{:S(2)}) collective-permute-start(bf16[96,2688]{1,0:T(8,128)(2,1)S(1)} %bitcast.258), channel_id=1, source_target_pairs={{0,1},{1,0},{2,3},{3,2},{4,5},{5,4},{6,7},{7,6},{8,9},{9,8},{10,11... | collective-permute-start | bytes 1548296 | tf_op jit(solution)/shard_map/ppermute | solution.py:357
  93.9 129.7 %collective-permute-start.27 = (bf16[1,1536,1024]{2,1,0:T(8,128)(2,1)}, bf16[1,1536,1024]{2,1,0:T(8,128)(2,1)}, u32[]{:S(2)}, u32[]{:S(2)}) collective-permute-start(bf16[1,1536,1024]{2,1,0:T(8,128)(2,1)} %constant_dynamic-update-slice_fusion.2), channel_id=1, source_target_pairs={{0,1},{1,0},{2,3},{3,2},{4,5},{5,4},{6,7},{7,6},{8,9},{9,8},{10,11... | collective-permute-start | bytes 9437192 | tf_op jit(solution)/shard_map/ppermute | solution.py:357
  95.8 28.7 %collective-permute-start.25 = (bf16[8,48,1664]{2,1,0:T(8,128)(2,1)S(1)}, bf16[8,48,1664]{2,1,0:T(8,128)(2,1)S(1)}, u32[]{:S(2)}, u32[]{:S(2)}) collective-permute-start(bf16[8,48,1664]{2,1,0:T(8,128)(2,1)S(1)} %fusion.42), channel_id=1, source_target_pairs={{0,16},{16,0},{1,17},{17,1},{2,18},{18,2},{3,19},{19,3},{4,20},{20... | collective-permute-start | bytes 3833864 | tf_op jit(solution)/shard_map/ppermute | solution.py:447
  115.2 81.1 %all-to-all-start = ((bf16[16,320,128]{2,1,0:T(8,128)(2,1)}), bf16[16,320,128]{2,1,0:T(8,128)(2,1)}, u32[]{:S(2)}, u32[]{:S(2)}) async-start(bf16[16,320,128]{2,1,0:T(8,128)(2,1)} %bitcast.254), calls=%async_computation | async-start | bytes 2621440 | tf_op jit(solution)/shard_map/all_to_all | solution.py:344
  125.7 104.0 %collective-permute-start.26 = (bf16[2,8,48,1664]{3,2,1,0:T(8,128)(2,1)}, bf16[2,8,48,1664]{3,2,1,0:T(8,128)(2,1)}, u32[]{:S(2)}, u32[]{:S(2)}) collective-permute-start(bf16[2,8,48,1664]{3,2,1,0:T(8,128)(2,1)} %bitcast_dynamic-update-slice_fusion), channel_id=1, source_target_pairs={{0,1},{1,0},{2,3},{3,2},{4,5},{5,4},{6,7},{7,6},{8,9},{9,8},{10,11... | collective-permute-start | bytes 7667720 | tf_op jit(solution)/shard_map/ppermute | solution.py:357
  125.7 46.8 %collective-permute-start.28 = (bf16[1,512,1536]{2,1,0:T(8,128)(2,1)}, bf16[1,512,1536]{2,1,0:T(8,128)(2,1)}, u32[]{:S(2)}, u32[]{:S(2)}) collective-permute-start(bf16[1,512,1536]{2,1,0:T(8,128)(2,1)} %param.23), channel_id=1, source_target_pairs={{0,1},{1,0},{2,3},{3,2},{4,5},{5,4},{6,7},{7,6},{8,9},{9,8},{10,11... | collective-permute-start | bytes 4718600 | tf_op jit(solution)/shard_map/ppermute | solution.py:357
  126.2 35.6 %collective-permute-start.38 = (bf16[256,1664]{1,0:T(8,128)(2,1)}, bf16[256,1664]{1,0:T(8,128)(2,1)}, u32[]{:S(2)}, u32[]{:S(2)}) collective-permute-start(bf16[256,1664]{1,0:T(8,128)(2,1)} %collective-permute-done.37.refs_2_), channel_id=1, source_target_pairs={{0,4},{1,5},{4,8},{5,9},{8,12},{9,13},{12,14},{13,15},{14,10},{15,... | collective-permute-start | bytes 2555912 | tf_op jit(solution)/shard_map/ppermute | solution.py:377
  127.8 42.5 %collective-permute-start.42 = (bf16[256,1664]{1,0:T(8,128)(2,1)}, bf16[256,1664]{1,0:T(8,128)(2,1)}, u32[]{:S(2)}, u32[]{:S(2)}) collective-permute-start(bf16[256,1664]{1,0:T(8,128)(2,1)} %collective-permute-done.41.refs_3_), channel_id=1, source_target_pairs={{4,0},{5,1},{8,4},{9,5},{12,8},{13,9},{14,12},{15,13},{10,14},{11,... | collective-permute-start | bytes 2555912 | tf_op jit(solution)/shard_map/ppermute | solution.py:378
  161.7 26.8 %collective-permute-start.39 = (bf16[256,1664]{1,0:T(8,128)(2,1)}, bf16[256,1664]{1,0:T(8,128)(2,1)}, u32[]{:S(2)}, u32[]{:S(2)}) collective-permute-start(bf16[256,1664]{1,0:T(8,128)(2,1)} %collective-permute-done.38.refs_2_), channel_id=1, source_target_pairs={{0,4},{1,5},{4,8},{5,9},{8,12},{9,13},{12,14},{13,15},{14,10},{15,... | collective-permute-start | bytes 2555912 | tf_op jit(solution)/shard_map/ppermute | solution.py:377
  170.3 22.5 %collective-permute-start.43 = (bf16[256,1664]{1,0:T(8,128)(2,1)}, bf16[256,1664]{1,0:T(8,128)(2,1)}, u32[]{:S(2)}, u32[]{:S(2)}) collective-permute-start(bf16[256,1664]{1,0:T(8,128)(2,1)} %collective-permute-done.42.refs_3_), channel_id=1, source_target_pairs={{4,0},{5,1},{8,4},{9,5},{12,8},{13,9},{14,12},{15,13},{10,14},{11,... | collective-permute-start | bytes 2555912 | tf_op jit(solution)/shard_map/ppermute | solution.py:378
  190.3 152.3 %collective-permute-start.40 = (bf16[128,1664]{1,0:T(8,128)(2,1)}, bf16[128,1664]{1,0:T(8,128)(2,1)}, u32[]{:S(2)}, u32[]{:S(2)}) collective-permute-start(bf16[128,1664]{1,0:T(8,128)(2,1)} %slice.237), channel_id=1, source_target_pairs={{0,4},{1,5},{4,8},{5,9},{8,12},{9,13},{12,14},{13,15},{14,10},{15,... | collective-permute-start | bytes 1277960 | tf_op jit(solution)/shard_map/ppermute | solution.py:377
  194.6 148.0 %collective-permute-start.44 = (bf16[128,1664]{1,0:T(8,128)(2,1)}, bf16[128,1664]{1,0:T(8,128)(2,1)}, u32[]{:S(2)}, u32[]{:S(2)}) collective-permute-start(bf16[128,1664]{1,0:T(8,128)(2,1)} %slice.238), channel_id=1, source_target_pairs={{4,0},{5,1},{8,4},{9,5},{12,8},{13,9},{14,12},{15,13},{10,14},{11,... | collective-permute-start | bytes 1277960 | tf_op jit(solution)/shard_map/ppermute | solution.py:378
  218.5 23.8 %all-to-all-start.1 = ((bf16[16,192,128]{2,1,0:T(8,128)(2,1)}), bf16[16,192,128]{2,1,0:T(8,128)(2,1)}, u32[]{:S(2)}, u32[]{:S(2)}) async-start(bf16[16,192,128]{2,1,0:T(8,128)(2,1)} %get-tuple-element.68), calls=%async_computation.1 | async-start | bytes 1572864 | tf_op jit(solution)/shard_map/all_to_all | solution.py:344
  250.1 20.3 %collective-permute-start.29 = (bf16[256,1536]{1,0:T(8,128)(2,1)}, bf16[256,1536]{1,0:T(8,128)(2,1)}, u32[]{:S(2)}, u32[]{:S(2)}) collective-permute-start(bf16[256,1536]{1,0:T(8,128)(2,1)} %multiply_convert_fusion.1.refs_0_), channel_id=1, source_target_pairs={{0,4},{1,5},{4,8},{5,9},{8,12},{9,13},{12,14},{13,15},{14,10},{15,... | collective-permute-start | bytes 2359304 | tf_op jit(solution)/shard_map/ppermute | solution.py:377
  252.2 20.7 %collective-permute-start.33 = (bf16[256,1536]{1,0:T(8,128)(2,1)}, bf16[256,1536]{1,0:T(8,128)(2,1)}, u32[]{:S(2)}, u32[]{:S(2)}) collective-permute-start(bf16[256,1536]{1,0:T(8,128)(2,1)} %multiply_convert_fusion.1.refs_0_), channel_id=1, source_target_pairs={{4,0},{5,1},{8,4},{9,5},{12,8},{13,9},{14,12},{15,13},{10,14},{11,... | collective-permute-start | bytes 2359304 | tf_op jit(solution)/shard_map/ppermute | solution.py:378
  270.4 23.2 %collective-permute-start.30 = (bf16[256,1536]{1,0:T(8,128)(2,1)}, bf16[256,1536]{1,0:T(8,128)(2,1)}, u32[]{:S(2)}, u32[]{:S(2)}) collective-permute-start(bf16[256,1536]{1,0:T(8,128)(2,1)} %collective-permute-done.29.refs_0_), channel_id=1, source_target_pairs={{0,4},{1,5},{4,8},{5,9},{8,12},{9,13},{12,14},{13,15},{14,10},{15,... | collective-permute-start | bytes 2359304 | tf_op jit(solution)/shard_map/ppermute | solution.py:377
  272.8 22.8 %collective-permute-start.34 = (bf16[256,1536]{1,0:T(8,128)(2,1)}, bf16[256,1536]{1,0:T(8,128)(2,1)}, u32[]{:S(2)}, u32[]{:S(2)}) collective-permute-start(bf16[256,1536]{1,0:T(8,128)(2,1)} %collective-permute-done.33.refs_1_), channel_id=1, source_target_pairs={{4,0},{5,1},{8,4},{9,5},{12,8},{13,9},{14,12},{15,13},{10,14},{11,... | collective-permute-start | bytes 2359304 | tf_op jit(solution)/shard_map/ppermute | solution.py:378
  293.5 22.8 %collective-permute-start.31 = (bf16[256,1536]{1,0:T(8,128)(2,1)}, bf16[256,1536]{1,0:T(8,128)(2,1)}, u32[]{:S(2)}, u32[]{:S(2)}) collective-permute-start(bf16[256,1536]{1,0:T(8,128)(2,1)} %collective-permute-done.30.refs_0_), channel_id=1, source_target_pairs={{0,4},{1,5},{4,8},{5,9},{8,12},{9,13},{12,14},{13,15},{14,10},{15,... | collective-permute-start | bytes 2359304 | tf_op jit(solution)/shard_map/ppermute | solution.py:377
  295.6 24.5 %collective-permute-start.35 = (bf16[256,1536]{1,0:T(8,128)(2,1)}, bf16[256,1536]{1,0:T(8,128)(2,1)}, u32[]{:S(2)}, u32[]{:S(2)}) collective-permute-start(bf16[256,1536]{1,0:T(8,128)(2,1)} %collective-permute-done.34.refs_1_), channel_id=1, source_target_pairs={{4,0},{5,1},{8,4},{9,5},{12,8},{13,9},{14,12},{15,13},{10,14},{11,... | collective-permute-start | bytes 2359304 | tf_op jit(solution)/shard_map/ppermute | solution.py:378
  318.1 24.5 %collective-permute-start.32 = (bf16[128,1536]{1,0:T(8,128)(2,1)}, bf16[128,1536]{1,0:T(8,128)(2,1)S(1)}, u32[]{:S(2)}, u32[]{:S(2)}) collective-permute-start(bf16[128,1536]{1,0:T(8,128)(2,1)} %slice.235), channel_id=1, source_target_pairs={{0,4},{1,5},{4,8},{5,9},{8,12},{9,13},{12,14},{13,15},{14,10},{15,... | collective-permute-start | bytes 1179656 | tf_op jit(solution)/shard_map/ppermute | solution.py:377
  321.9 20.7 %collective-permute-start.36 = (bf16[128,1536]{1,0:T(8,128)(2,1)}, bf16[128,1536]{1,0:T(8,128)(2,1)S(1)}, u32[]{:S(2)}, u32[]{:S(2)}) collective-permute-start(bf16[128,1536]{1,0:T(8,128)(2,1)} %slice.236), channel_id=1, source_target_pairs={{4,0},{5,1},{8,4},{9,5},{12,8},{13,9},{14,12},{15,13},{10,14},{11,... | collective-permute-start | bytes 1179656 | tf_op jit(solution)/shard_map/ppermute | solution.py:378
  400.3 78.4 %collective-permute-start.87 = (bf16[512,1536]{1,0:T(8,128)(2,1)}, bf16[512,1536]{1,0:T(8,128)(2,1)}, u32[]{:S(2)}, u32[]{:S(2)}) collective-permute-start(bf16[512,1536]{1,0:T(8,128)(2,1)} %convolution_convert_fusion), channel_id=1, source_target_pairs={{0,1},{1,0},{2,3},{3,2},{4,5},{5,4},{6,7},{7,6},{8,9},{9,8},{10,11... | collective-permute-start | bytes 4718600 | tf_op jit(solution)/shard_map/ppermute | solution.py:357
  421.3 32.0 %collective-permute-start.85 = (bf16[1536,1024]{1,0:T(8,128)(2,1)}, bf16[1536,1024]{1,0:T(8,128)(2,1)}, u32[]{:S(2)}, u32[]{:S(2)}) collective-permute-start(bf16[1536,1024]{1,0:T(8,128)(2,1)} %fusion.6), channel_id=1, source_target_pairs={{0,1},{1,0},{2,3},{3,2},{4,5},{5,4},{6,7},{7,6},{8,9},{9,8},{10,11... | collective-permute-start | bytes 9437192 | tf_op jit(solution)/shard_map/ppermute | solution.py:357
  446.0 26.8 %collective-permute-start.75 = (bf16[2,8,48,1664]{3,2,1,0:T(8,128)(2,1)}, bf16[2,8,48,1664]{3,2,1,0:T(8,128)(2,1)}, u32[]{:S(2)}, u32[]{:S(2)}) collective-permute-start(bf16[2,8,48,1664]{3,2,1,0:T(8,128)(2,1)} %select_bitcast_fusion.1), channel_id=1, source_target_pairs={{0,1},{1,0},{2,3},{3,2},{4,5},{5,4},{6,7},{7,6},{8,9},{9,8},{10,11... | collective-permute-start | bytes 7667720 | tf_op jit(solution)/shard_map/ppermute | solution.py:357
  462.6 141.1 %collective-permute-start.86 = (bf16[1536,1024]{1,0:T(8,128)(2,1)}, bf16[1536,1024]{1,0:T(8,128)(2,1)}, u32[]{:S(2)}, u32[]{:S(2)}) collective-permute-start(bf16[1536,1024]{1,0:T(8,128)(2,1)} %add_convert_fusion), channel_id=1, source_target_pairs={{0,16},{16,0},{1,17},{17,1},{2,18},{18,2},{3,19},{19,3},{4,20},{20... | collective-permute-start | bytes 9437192 | tf_op jit(solution)/shard_map/ppermute | solution.py:350
  468.5 23.0 %all-to-all-start.2 = ((bf16[16,192,128]{2,1,0:T(8,128)(2,1)}), bf16[16,192,128]{2,1,0:T(8,128)(2,1)}, u32[]{:S(2)}, u32[]{:S(2)}) async-start(bf16[16,192,128]{2,1,0:T(8,128)(2,1)} %bitcast.257), calls=%async_computation.2 | async-start | bytes 1572864 | tf_op jit(solution)/shard_map/all_to_all | solution.py:344
  478.2 83.1 %collective-permute-start.76 = (bf16[1,8,48,1664]{3,2,1,0:T(8,128)(2,1)}, bf16[1,8,48,1664]{3,2,1,0:T(8,128)(2,1)}, u32[]{:S(2)}, u32[]{:S(2)}) collective-permute-start(bf16[1,8,48,1664]{3,2,1,0:T(8,128)(2,1)} %constant_dynamic-slice_fusion), channel_id=1, source_target_pairs={{0,16},{16,0},{1,17},{17,1},{2,18},{18,2},{3,19},{19,3},{4,20},{20... | collective-permute-start | bytes 3833864 | tf_op jit(solution)/shard_map/ppermute | solution.py:500
  486.2 107.7 %collective-permute-start.88 = (bf16[512,1536]{1,0:T(8,128)(2,1)}, bf16[512,1536]{1,0:T(8,128)(2,1)S(1)}, u32[]{:S(2)}, u32[]{:S(2)}) collective-permute-start(bf16[512,1536]{1,0:T(8,128)(2,1)} %fusion.9), channel_id=1, source_target_pairs={{0,16},{16,0},{1,17},{17,1},{2,18},{18,2},{3,19},{19,3},{4,20},{20... | collective-permute-start | bytes 4718600 | tf_op jit(solution)/shard_map/ppermute | solution.py:350
  519.7 105.0 %all-to-all-start.3 = ((bf16[16,320,128]{2,1,0:T(8,128)(2,1)}), bf16[16,320,128]{2,1,0:T(8,128)(2,1)}, u32[]{:S(2)}, u32[]{:S(2)}) async-start(bf16[16,320,128]{2,1,0:T(8,128)(2,1)} %backward.1), calls=%async_computation.3 | async-start | bytes 2621440 | tf_op jit(solution)/shard_map/all_to_all | solution.py:344
  563.4 38.2 %collective-permute-start.81 = (bf16[48,896]{1,0:T(8,128)(2,1)S(1)}, bf16[48,896]{1,0:T(8,128)(2,1)S(1)}, u32[]{:S(2)}, u32[]{:S(2)}) collective-permute-start(bf16[48,896]{1,0:T(8,128)(2,1)S(1)} %split.19), channel_id=1, source_target_pairs={{4,0},{5,1},{8,4},{9,5},{12,8},{13,9},{14,12},{15,13},{10,14},{11,... | collective-permute-start | bytes 258056 | tf_op jit(solution)/shard_map/ppermute | solution.py:378
  564.3 37.3 %collective-permute-start.77 = (bf16[48,768]{1,0:T(8,128)(2,1)S(1)}, bf16[48,768]{1,0:T(8,128)(2,1)S(1)}, u32[]{:S(2)}, u32[]{:S(2)}) collective-permute-start(bf16[48,768]{1,0:T(8,128)(2,1)S(1)} %split.18), channel_id=1, source_target_pairs={{0,4},{1,5},{4,8},{5,9},{8,12},{9,13},{12,14},{13,15},{14,10},{15,... | collective-permute-start | bytes 221192 | tf_op jit(solution)/shard_map/ppermute | solution.py:377
  598.5 50.5 %collective-permute-start.57 = (bf16[256,1536]{1,0:T(8,128)(2,1)}, bf16[256,1536]{1,0:T(8,128)(2,1)}, u32[]{:S(2)}, u32[]{:S(2)}) collective-permute-start(bf16[256,1536]{1,0:T(8,128)(2,1)} %add.609), channel_id=1, source_target_pairs={{4,0},{5,1},{8,4},{9,5},{12,8},{13,9},{14,12},{15,13},{10,14},{11,... | collective-permute-start | bytes 2359304 | tf_op jit(solution)/shard_map/ppermute | solution.py:378
  600.4 48.6 %collective-permute-start.56 = (bf16[256,1536]{1,0:T(8,128)(2,1)}, bf16[256,1536]{1,0:T(8,128)(2,1)}, u32[]{:S(2)}, u32[]{:S(2)}) collective-permute-start(bf16[256,1536]{1,0:T(8,128)(2,1)} %add.608), channel_id=1, source_target_pairs={{0,4},{1,5},{4,8},{5,9},{8,12},{9,13},{12,14},{13,15},{14,10},{15,... | collective-permute-start | bytes 2359304 | tf_op jit(solution)/shard_map/ppermute | solution.py:377
  601.6 20.7 %collective-permute-start.78 = (bf16[48,1664]{1,0:T(8,128)(2,1)S(1)}, bf16[48,1664]{1,0:T(8,128)(2,1)S(1)}, u32[]{:S(2)}, u32[]{:S(2)}) collective-permute-start(bf16[48,1664]{1,0:T(8,128)(2,1)S(1)} %get-tuple-element.217), channel_id=1, source_target_pairs={{0,4},{1,5},{4,8},{5,9},{8,12},{9,13},{12,14},{13,15},{14,10},{15,... | collective-permute-start | bytes 479240 | tf_op jit(solution)/shard_map/ppermute | solution.py:377
  602.1 20.3 %collective-permute-start.82 = (bf16[48,1664]{1,0:T(8,128)(2,1)S(1)}, bf16[48,1664]{1,0:T(8,128)(2,1)S(1)}, u32[]{:S(2)}, u32[]{:S(2)}) collective-permute-start(bf16[48,1664]{1,0:T(8,128)(2,1)S(1)} %get-tuple-element.218), channel_id=1, source_target_pairs={{4,0},{5,1},{8,4},{9,5},{12,8},{13,9},{14,12},{15,13},{10,14},{11,... | collective-permute-start | bytes 479240 | tf_op jit(solution)/shard_map/ppermute | solution.py:378
  633.0 21.4 %collective-permute-start.55 = (bf16[2,8,48,2560]{3,2,1,0:T(8,128)(2,1)}, bf16[2,8,48,2560]{3,2,1,0:T(8,128)(2,1)}, u32[]{:S(2)}, u32[]{:S(2)}) collective-permute-start(bf16[2,8,48,2560]{3,2,1,0:T(8,128)(2,1)} %select_bitcast_fusion), channel_id=1, source_target_pairs={{0,1},{1,0},{2,3},{3,2},{4,5},{5,4},{6,7},{7,6},{8,9},{9,8},{10,11... | collective-permute-start | bytes 11796488 | tf_op jit(solution)/shard_map/ppermute | solution.py:357
  660.1 20.2 %collective-permute-start.64 = (bf16[1,3,48,2688]{3,2,1,0:T(8,128)(2,1)S(1)}, bf16[1,3,48,2688]{3,2,1,0:T(8,128)(2,1)S(1)}, u32[]{:S(2)}, u32[]{:S(2)}) collective-permute-start(bf16[1,3,48,2688]{3,2,1,0:T(8,128)(2,1)S(1)} %constant_dynamic-slice_fusion.5), channel_id=1, source_target_pairs={{0,16},{16,0},{1,17},{17,1},{2,18},{18,2},{3,19},{19,3},{4,20},{20... | collective-permute-start | bytes 2322440 | tf_op jit(solution)/shard_map/ppermute | solution.py:500
  662.5 51.2 %collective-permute-start.69 = (bf16[1,2,48,2688]{3,2,1,0:T(8,128)(2,1)S(1)}, bf16[1,2,48,2688]{3,2,1,0:T(8,128)(2,1)S(1)}, u32[]{:S(2)}, u32[]{:S(2)}) collective-permute-start(bf16[1,2,48,2688]{3,2,1,0:T(8,128)(2,1)S(1)} %fusion.18), channel_id=1, source_target_pairs={{0,16},{16,0},{1,17},{17,1},{2,18},{18,2},{3,19},{19,3},{4,20},{20... | collective-permute-start | bytes 1548296 | tf_op jit(solution)/shard_map/ppermute | solution.py:500
  663.1 38.3 %collective-permute-start.67 = (bf16[1,2,48,2688]{3,2,1,0:T(8,128)(2,1)S(1)}, bf16[1,2,48,2688]{3,2,1,0:T(8,128)(2,1)S(1)}, u32[]{:S(2)}, u32[]{:S(2)}) collective-permute-start(bf16[1,2,48,2688]{3,2,1,0:T(8,128)(2,1)S(1)} %fusion.20), channel_id=1, source_target_pairs={{0,16},{16,0},{1,17},{17,1},{2,18},{18,2},{3,19},{19,3},{4,20},{20... | collective-permute-start | bytes 1548296 | tf_op jit(solution)/shard_map/ppermute | solution.py:500
  666.1 36.3 %collective-permute-start.59 = (bf16[256,1536]{1,0:T(8,128)(2,1)S(1)}, bf16[256,1536]{1,0:T(8,128)(2,1)S(1)}, u32[]{:S(2)}, u32[]{:S(2)}) collective-permute-start(bf16[256,1536]{1,0:T(8,128)(2,1)S(1)} %add.611), channel_id=1, source_target_pairs={{0,4},{1,5},{4,8},{5,9},{8,12},{9,13},{12,14},{13,15},{14,10},{15,... | collective-permute-start | bytes 2359304 | tf_op jit(solution)/shard_map/ppermute | solution.py:377
  687.3 19.6 %collective-permute-start.61 = (bf16[256,1536]{1,0:T(8,128)(2,1)S(1)}, bf16[256,1536]{1,0:T(8,128)(2,1)S(1)}, u32[]{:S(2)}, u32[]{:S(2)}) collective-permute-start(bf16[256,1536]{1,0:T(8,128)(2,1)S(1)} %add.614), channel_id=1, source_target_pairs={{4,0},{5,1},{8,4},{9,5},{12,8},{13,9},{14,12},{15,13},{10,14},{11,... | collective-permute-start | bytes 2359304 | tf_op jit(solution)/shard_map/ppermute | solution.py:378
  688.2 20.0 %collective-permute-start.66 = (bf16[48,2688]{1,0:T(8,128)(2,1)S(1)}, bf16[48,2688]{1,0:T(8,128)(2,1)S(1)}, u32[]{:S(2)}, u32[]{:S(2)}) collective-permute-start(bf16[48,2688]{1,0:T(8,128)(2,1)S(1)} %get-tuple-element.219), channel_id=1, source_target_pairs={{0,4},{1,5},{4,8},{5,9},{8,12},{9,13},{12,14},{13,15},{14,10},{15,... | collective-permute-start | bytes 774152 | tf_op jit(solution)/shard_map/ppermute | solution.py:377
  702.4 34.2 %collective-permute-start.63 = (bf16[1,1,48,2688]{3,2,1,0:T(8,128)(2,1)S(1)}, bf16[1,1,48,2688]{3,2,1,0:T(8,128)(2,1)S(1)}, u32[]{:S(2)}, u32[]{:S(2)}) collective-permute-start(bf16[1,1,48,2688]{3,2,1,0:T(8,128)(2,1)S(1)} %constant_dynamic-slice_fusion.9), channel_id=1, source_target_pairs={{0,16},{16,0},{1,17},{17,1},{2,18},{18,2},{3,19},{19,3},{4,20},{20... | collective-permute-start | bytes 774152 | tf_op jit(solution)/shard_map/ppermute | solution.py:500
  706.9 28.2 %collective-permute-start.60 = (bf16[256,1536]{1,0:T(8,128)(2,1)S(1)}, bf16[256,1536]{1,0:T(8,128)(2,1)S(1)}, u32[]{:S(2)}, u32[]{:S(2)}) collective-permute-start(bf16[256,1536]{1,0:T(8,128)(2,1)S(1)} %add.612), channel_id=1, source_target_pairs={{0,4},{1,5},{4,8},{5,9},{8,12},{9,13},{12,14},{13,15},{14,10},{15,... | collective-permute-start | bytes 2359304 | tf_op jit(solution)/shard_map/ppermute | solution.py:377
  708.3 26.8 %collective-permute-start.62 = (bf16[256,1536]{1,0:T(8,128)(2,1)S(1)}, bf16[256,1536]{1,0:T(8,128)(2,1)S(1)}, u32[]{:S(2)}, u32[]{:S(2)}) collective-permute-start(bf16[256,1536]{1,0:T(8,128)(2,1)S(1)} %add.615), channel_id=1, source_target_pairs={{4,0},{5,1},{8,4},{9,5},{12,8},{13,9},{14,12},{15,13},{10,14},{11,... | collective-permute-start | bytes 2359304 | tf_op jit(solution)/shard_map/ppermute | solution.py:378
  (97 other events, 1456.0 us)
